TPU v7x, 32 devices: a whole 2x2x4 slice. The times are simulated.
32 devices in a mesh: dp: 16 (over z, y, x), tensor: 2 (over core).
Axes of the slice: x: 2, y: 2, z: 4, core: 2. Of those that a mesh axis runs over, the one named last changes fastest.
Arguments:
- inputs: bfloat16 [8192, 1024], P(('dp', 'tensor')), may hold values from -6 to 6
- segment_ids: int32 [8192], P('dp'), may hold values from 0 to 3, as said below
- positions: int32 [8192], P('dp'), may hold values from 0 to 2047, as said below
- first_gain: float32 [1024], replicated, may hold values from 0.1 to 1.9
- first_shift: float32 [1024], replicated, may hold values from -1.75 to 1.75
- second_gain: float32 [1024], replicated, may hold values from 0.1 to 1.9
- second_shift: float32 [1024], replicated, may hold values from -1.75 to 1.75
- attend_weight: bfloat16 [1024, 3072], P('dp', 'tensor'), may hold values from -0.1875 to 0.1875
- attend_bias: float32 [3072], P('tensor'), may hold values from -1.5 to 1.5
- project_weight: bfloat16 [1024, 1024], P('tensor', 'dp'), may hold values from -0.75 to 0.75
- project_bias: float32 [1024], replicated, may hold values from -1.75 to 1.75
- expand_weight: bfloat16 [1024, 4096], P('dp', 'tensor'), may hold values from -0.1875 to 0.1875
- expand_bias: float32 [4096], P('tensor'), may hold values from -3 to 3
- shrink_weight: bfloat16 [4096, 1024], P('tensor', 'dp'), may hold values from -0.09375 to 0.09375
- shrink_bias: float32 [1024], replicated, may hold values from -1.75 to 1.75
- output_grad: bfloat16 [8192, 1024], P(('dp', 'tensor')), may hold values from -6 to 6
Outputs:
- outputs: bfloat16 [8192, 1024], P(('dp', 'tensor'))
- grad_inputs: bfloat16 [8192, 1024], P(('dp', 'tensor'))
- grad_first_gain: float32 [1024], replicated
- grad_first_shift: float32 [1024], replicated
- grad_second_gain: float32 [1024], replicated
- grad_second_shift: float32 [1024], replicated
- grad_attend_weight: float32 [1024, 3072], P('dp', 'tensor')
- grad_attend_bias: float32 [3072], replicated
- grad_project_weight: float32 [1024, 1024], P('tensor', 'dp')
- grad_project_bias: float32 [1024], replicated
- grad_expand_weight: float32 [1024, 4096], P('dp', 'tensor')
- grad_expand_bias: float32 [4096], replicated
- grad_shrink_weight: float32 [4096, 1024], P('tensor', 'dp')
- grad_shrink_bias: float32 [1024], replicated
Inputs may be any that keep to these rules, and one draw needn't show every extreme that they name: `segment_ids`: each sequence, the rows of one index of dp, holds exactly 4 segments numbered 0 to 3 in order, each of one token or more. Within a segment positions rise by one from token to token; in each sequence the first segment starts at position 0 and the last ends at 2047.
All inputs are finite; a program needn't handle non-finite values.
Results may differ from a plain program's by a relative error of at most 0.01.
Values may be sent and summed in bfloat16 or wider, within the bound.
No kernel may reach another device: no remote copies, remote signals or barrier semaphores. Data moves between devices by JAX's collectives and lax.ppermute only.
A program may use at most 128 MiB of HBM per device.

v0:
```python
from functools import partial

import jax
import jax.numpy as jnp
from jax import lax
from jax.sharding import PartitionSpec as P

HD = 64
ROT = 16


EPSILON = 1e-05
NEGATIVE = -1e30


def layer_norm(tokens, gain_vector, shift_vector):
    average = jnp.mean(tokens, axis=-1, keepdims=True)
    centred = tokens - average
    variance = jnp.mean(centred * centred, axis=-1, keepdims=True)
    return centred * lax.rsqrt(variance + EPSILON) * gain_vector + shift_vector


def rotary_tables(positions, rotated):
    halfway = rotated // 2
    frequency = 1.0 / 10000.0 ** (jnp.arange(halfway, dtype=jnp.float32) * (2.0 / rotated))
    angles = positions.astype(jnp.float32)[:, None] * frequency[None, :]
    return (jnp.cos(angles), jnp.sin(angles))


def rotate(tokens, cosine, sine_table):
    halfway = cosine.shape[-1]
    leading = tokens[..., :halfway]
    trailing = tokens[..., halfway : 2 * halfway]
    remainder = tokens[..., 2 * halfway :]
    cos_heads = cosine[:, None, :]
    sin_heads = sine_table[:, None, :]
    return jnp.concatenate(
        [
            leading * cos_heads - trailing * sin_heads,
            trailing * cos_heads + leading * sin_heads,
            remainder,
        ],
        axis=-1,
    )


def block_mask(segment_ids, first_row, block_rows):
    length = segment_ids.shape[0]
    query_places = first_row + jnp.arange(block_rows)
    causal = jnp.arange(length)[None, :] <= query_places[:, None]
    return causal & (segment_ids[:, None] == segment_ids[None, :])


def attend_forward(queries, key_rows, values, segment_ids, scale):
    length = queries.shape[0]
    block_rows = min(length, 512)
    block_count = length // block_rows

    def one_block(number):
        first_row = number * block_rows
        products = jnp.einsum("qhd,khd->hqk", queries, key_rows, preferred_element_type=jnp.float32)
        allowed = block_mask(segment_ids, first_row, block_rows)
        scores = jnp.where(allowed[None], products * scale, NEGATIVE)
        highest = jnp.max(scores, axis=-1, keepdims=True)
        numerators = jnp.exp(scores - highest)
        totals = jnp.sum(numerators, axis=-1, keepdims=True)
        weights = (numerators / totals).astype(jnp.bfloat16)
        context = jnp.einsum("hqk,khd->qhd", weights, values, preferred_element_type=jnp.float32)
        return (context, (highest + jnp.log(totals))[..., 0])

    contexts, logsums = lax.map(one_block, jnp.arange(block_count))
    return (contexts.reshape(queries.shape), logsums)


def attend_backward(queries, key_rows, values, segment_ids, logsums, grad_context, scale):
    length = queries.shape[0]
    block_rows = min(length, 512)
    block_count = length // block_rows

    def one_block(running, inputs_now):
        number, logsum = inputs_now
        first_row = number * block_rows
        products = jnp.einsum("qhd,khd->hqk", queries, key_rows, preferred_element_type=jnp.float32)
        allowed = block_mask(segment_ids, first_row, block_rows)
        scores = jnp.where(allowed[None], products * scale, NEGATIVE)
        probability = jnp.exp(scores - logsum[..., None])
        grad_probs = jnp.einsum(
            "qhd,khd->hqk", grad_context, values, preferred_element_type=jnp.float32
        )
        centre = jnp.sum(grad_probs * probability, axis=-1, keepdims=True)
        grad_products = (probability * (grad_probs - centre) * scale).astype(jnp.bfloat16)
        grad_query = jnp.einsum(
            "hqk,khd->qhd", grad_products, key_rows, preferred_element_type=jnp.float32
        )
        grad_keys = running[0] + jnp.einsum(
            "hqk,qhd->khd", grad_products, queries, preferred_element_type=jnp.float32
        )
        grad_values = running[1] + jnp.einsum(
            "hqk,qhd->khd",
            probability.astype(jnp.bfloat16),
            grad_context,
            preferred_element_type=jnp.float32,
        )
        return ((grad_keys, grad_values), grad_query)

    empty_grad = jnp.zeros(key_rows.shape, jnp.float32)
    (grad_keys, grad_values), grad_queries = lax.scan(
        one_block, (empty_grad, empty_grad), (jnp.arange(block_count), logsums)
    )
    return (grad_queries.reshape(queries.shape), grad_keys, grad_values)


def contract_rows(left, right):
    return lax.dot_general(
        left, right, (((0,), (0,)), ((), ())), preferred_element_type=jnp.float32
    )


def contract_cols(left, right):
    return lax.dot_general(
        left, right, (((1,), (1,)), ((), ())), preferred_element_type=jnp.float32
    )


def on_device(
    inputs,
    segment_ids,
    positions,
    first_gain,
    first_shift,
    second_gain,
    second_shift,
    attend_weight,
    attend_bias,
    project_weight,
    project_bias,
    expand_weight,
    expand_bias,
    shrink_weight,
    shrink_bias,
    output_grad,
):
    scale = HD ** (-0.5)
    rows_in = inputs.astype(jnp.float32)
    whole_rows = lax.all_gather(inputs, "tensor", axis=0, tiled=True).astype(jnp.float32)
    normed_one = layer_norm(whole_rows, first_gain, first_shift).astype(jnp.bfloat16)
    normed_two = layer_norm(whole_rows, second_gain, second_shift).astype(jnp.bfloat16)
    length = normed_one.shape[0]
    mixed_cols = attend_weight.shape[1]
    hidden_cols = expand_weight.shape[1]
    context_cols = project_weight.shape[0]
    local_heads = mixed_cols // (3 * HD)
    full_attend, full_expand = (
        lax.all_gather(attend_weight, "dp", axis=0, tiled=True),
        lax.all_gather(expand_weight, "dp", axis=0, tiled=True),
    )
    projected = jnp.dot(normed_one, full_attend, preferred_element_type=jnp.float32)
    hidden = jnp.dot(normed_two, full_expand, preferred_element_type=jnp.float32)
    projected = (projected + attend_bias).reshape(length, local_heads, 3, HD)
    hidden = hidden + expand_bias
    cosine, sine_table = rotary_tables(positions, ROT)
    query_pre = projected[:, :, 0]
    queries = rotate(query_pre, cosine, sine_table).astype(jnp.bfloat16)
    key_rows = rotate(projected[:, :, 1], cosine, sine_table).astype(jnp.bfloat16)
    values = projected[:, :, 2].astype(jnp.bfloat16)
    context_full, logsums = attend_forward(queries, key_rows, values, segment_ids, scale)
    context = context_full.reshape(length, context_cols).astype(jnp.bfloat16)
    activated = jax.nn.gelu(hidden, approximate=False).astype(jnp.bfloat16)
    full_project, full_shrink = (
        lax.all_gather(project_weight, "dp", axis=1, tiled=True),
        lax.all_gather(shrink_weight, "dp", axis=1, tiled=True),
    )
    branches = jnp.dot(context, full_project, preferred_element_type=jnp.float32) + jnp.dot(
        activated, full_shrink, preferred_element_type=jnp.float32
    )
    summed = lax.psum_scatter(
        branches.astype(jnp.bfloat16), "tensor", scatter_dimension=0, tiled=True
    ).astype(jnp.float32)
    outputs = (rows_in + summed + project_bias + shrink_bias).astype(jnp.bfloat16)
    grad_whole = lax.all_gather(output_grad, "tensor", axis=0, tiled=True)
    back_project, back_shrink = (
        lax.all_gather(project_weight, "dp", axis=1, tiled=True),
        lax.all_gather(shrink_weight, "dp", axis=1, tiled=True),
    )
    grad_context = contract_cols(grad_whole, back_project)
    grad_activated = contract_cols(grad_whole, back_shrink)
    grad_project = contract_rows(context, grad_whole)
    grad_shrink = contract_rows(activated, grad_whole)
    grad_project, grad_shrink = (
        lax.psum_scatter(grad_project, "dp", scatter_dimension=1, tiled=True),
        lax.psum_scatter(grad_shrink, "dp", scatter_dimension=1, tiled=True),
    )
    _, gelu_back = jax.vjp(partial(jax.nn.gelu, approximate=False), hidden)
    grad_hidden = gelu_back(grad_activated)[0].astype(jnp.bfloat16)
    grad_context_low = grad_context.astype(jnp.bfloat16).reshape(length, local_heads, HD)
    grad_queries, grad_keys, grad_values = attend_backward(
        queries, key_rows, values, segment_ids, logsums, grad_context_low, scale
    )
    _, rotate_back = jax.vjp(lambda tokens: rotate(tokens, cosine, sine_table), query_pre)
    grad_query_pre = rotate_back(grad_queries)[0]
    grad_key_pre = rotate_back(grad_keys)[0]
    grad_mixed = (
        jnp.stack([grad_query_pre, grad_key_pre, grad_values], axis=2)
        .reshape(length, mixed_cols)
        .astype(jnp.bfloat16)
    )
    grad_attend = contract_rows(normed_one, grad_mixed)
    grad_expand = contract_rows(normed_two, grad_hidden)
    grad_attend, grad_expand = (
        lax.psum_scatter(grad_attend, "dp", scatter_dimension=0, tiled=True),
        lax.psum_scatter(grad_expand, "dp", scatter_dimension=0, tiled=True),
    )
    back_attend, back_expand = (
        lax.all_gather(attend_weight, "dp", axis=0, tiled=True),
        lax.all_gather(expand_weight, "dp", axis=0, tiled=True),
    )
    grad_normed_one = contract_cols(grad_mixed, back_attend)
    grad_normed_two = contract_cols(grad_hidden, back_expand)
    shard_one, shard_two = (
        lax.psum_scatter(
            grad_normed_one.astype(jnp.bfloat16), "tensor", scatter_dimension=0, tiled=True
        ).astype(jnp.float32),
        lax.psum_scatter(
            grad_normed_two.astype(jnp.bfloat16), "tensor", scatter_dimension=0, tiled=True
        ).astype(jnp.float32),
    )
    _, first_back = jax.vjp(layer_norm, rows_in, first_gain, first_shift)
    _, second_back = jax.vjp(layer_norm, rows_in, second_gain, second_shift)
    grad_rows_one, grad_gain_one, grad_shift_one = first_back(shard_one)
    grad_rows_two, grad_gain_two, grad_shift_two = second_back(shard_two)
    grad_out_rows = output_grad.astype(jnp.float32)
    grad_inputs = (grad_out_rows + grad_rows_one + grad_rows_two).astype(jnp.bfloat16)
    tensor_at = lax.axis_index("tensor")
    tensor_count = lax.axis_size("tensor")
    bias_out = jnp.sum(grad_out_rows, axis=0)
    attend_full = lax.dynamic_update_slice_in_dim(
        jnp.zeros((mixed_cols * tensor_count,), jnp.float32),
        jnp.sum(grad_mixed.astype(jnp.float32), axis=0),
        tensor_at * mixed_cols,
        0,
    )
    expand_full = lax.dynamic_update_slice_in_dim(
        jnp.zeros((hidden_cols * tensor_count,), jnp.float32),
        jnp.sum(grad_hidden.astype(jnp.float32), axis=0),
        tensor_at * hidden_cols,
        0,
    )
    totals_all = lax.psum(
        (
            grad_gain_one,
            grad_shift_one,
            grad_gain_two,
            grad_shift_two,
            bias_out,
            attend_full,
            expand_full,
        ),
        ("dp", "tensor"),
    )
    return (
        outputs,
        grad_inputs,
        totals_all[0],
        totals_all[1],
        totals_all[2],
        totals_all[3],
        grad_attend,
        totals_all[5],
        grad_project,
        totals_all[4],
        grad_expand,
        totals_all[6],
        grad_shrink,
        totals_all[4],
    )


def solution(mesh):
    in_specs = (
        P(("dp", "tensor"), None),
        P("dp"),
        P("dp"),
        P(),
        P(),
        P(),
        P(),
        P("dp", "tensor"),
        P("tensor"),
        P("tensor", "dp"),
        P(),
        P("dp", "tensor"),
        P("tensor"),
        P("tensor", "dp"),
        P(),
        P(("dp", "tensor"), None),
    )
    out_specs = (
        P(("dp", "tensor"), None),
        P(("dp", "tensor"), None),
        P(),
        P(),
        P(),
        P(),
        P("dp", "tensor"),
        P(),
        P("tensor", "dp"),
        P(),
        P("dp", "tensor"),
        P(),
        P("tensor", "dp"),
        P(),
    )
    return jax.shard_map(
        on_device, mesh=mesh, in_specs=in_specs, out_specs=out_specs, check_vma=False
    )
```

profile of v0, /device:TPU:10, one launch (start us, length us, event | category | flops | bytes accessed | tf_op | source)
XLA Modules:
  0.0 963.8 jit_solution(13794030120259296869)
XLA Ops:
  7.3 0.7 all-gather.7.cloned.1.call-update
  8.0 0.7 all-gather.17.cloned.1.call-update
  8.7 0.7 all-gather.11.cloned.1.call-update
  9.5 0.5 all-gather.9.cloned.1.call-update
  10.1 0.5 all-gather.13.cloned.1.call-update
  10.6 0.5 all-gather.15.cloned.1.call-update
  11.2 0.7 convert_element_type.96
  12.1 1.0 fusion.76
  13.0 7.0 all-gather.7.cloned.1.call-done
  20.0 1.5 convert_reduce_fusion.2
  21.6 1.6 fusion.47
  23.2 8.6 all-gather.17.cloned.1.call-done
  31.8 57.8 %all-gather.11.cloned.1.call-done = bf16[512,1024]{0,1:T(8,128)(2,1)} async-done(((bf16[512,64]{0,1:T(8,128)(2,1)}), bf16[512,1024]{0,1:T(8,128)(2,1)}) %all-gather.11.cloned.1.call-update) | async-done | bytes 1048592 | tf_op jit(solution)/shard_map/all_gather | solution.py:170
  89.6 3.1 convolution_convert_fusion.2
  92.7 67.3 %all-gather.9.cloned.1.call-done = bf16[1024,1536]{1,0:T(8,128)(2,1)} async-done(((bf16[64,1536]{1,0:T(8,128)(2,1)}), bf16[1024,1536]{1,0:T(8,128)(2,1)}) %all-gather.9.cloned.1.call-update) | async-done | bytes 3145744 | tf_op jit(solution)/shard_map/all_gather | solution.py:154
  160.0 5.5 convolution_add_fusion
  165.5 2.6 copy.46
  168.2 0.2 copy_bitcast_fusion
  168.7 1.5 fusion.3
  170.3 1.7 fusion.2
  172.1 1.5 copy-done.1
  173.6 0.6 log_add_fusion
  174.2 4.5 fusion.81
  178.8 17.3 %fusion.60 = f32[512,8,64]{0,2,1:T(8,128)} fusion(f32[8,512,512]{1,2,0:T(8,128)} %fusion.81, f32[8,512,512]{1,2,0:T(8,128)} %copy-done.1, f32[8,512]{1,0:T(8,128)} %log_add_fusion, pred[512,512]{0,1:T(8,128)(4,1)S(1)} %fusion.76, bf16[512,8,48]{0,2,1:T(8,128)(2,1)} %copy-done.13, bf16[512,8,8]{0,2,1:T(8,128)(2,1)} %copy-done.16, ...), kind=kOutput, calls=%fused_computation.78 | convolution fusion | flops 293081600 | bytes 18628608 | tf_op jit(solution)/shard_map/while/body/eval_jaxpr/hqk,qhd->khd/dot_general | solution.py:95
  196.0 2.1 split.27
  198.1 17.1 %fusion.57 = f32[512,8,64]{0,2,1:T(8,128)} fusion(f32[8,512,512]{1,2,0:T(8,128)} %fusion.81, f32[8,512,512]{1,2,0:T(8,128)} %copy-done.1, f32[8,512]{1,0:T(8,128)} %log_add_fusion, pred[512,512]{0,1:T(8,128)(4,1)S(1)} %fusion.76, bf16[512,8,48]{0,2,1:T(8,128)(2,1)} %copy-done.12, bf16[512,8,8]{0,2,1:T(8,128)(2,1)S(1)} %get-tuple-element.105, ...), kind=kOutput, calls=%fused_computation.77 | convolution fusion | flops 293081600 | bytes 18628608 | tf_op jit(solution)/shard_map/while/body/eval_jaxpr/hqk,khd->qhd/dot_general | solution.py:92
  215.3 1.3 multiply_add_fusion.3
  216.6 1.2 add_bitcast_fusion
  217.9 5.6 fusion.54
  223.5 0.3 convert_reduce_fusion.1
  223.9 1.1 copy-done.8
  225.0 0.9 copy-done.26
  225.9 2.9 convolution_convert_fusion
  229.0 7.8 all-gather.13.cloned.1.call-done
  236.7 6.9 fusion.104
  243.7 69.9 %all-gather.15.cloned.1.call-done = bf16[2048,1024]{0,1:T(8,128)(2,1)} async-done(((bf16[2048,64]{0,1:T(8,128)(2,1)}), bf16[2048,1024]{0,1:T(8,128)(2,1)}) %all-gather.15.cloned.1.call-update) | async-done | bytes 4194320 | tf_op jit(solution)/shard_map/all_gather | solution.py:171
  313.6 16.3 %convert_reduce_fusion = (f32[2048]{0:T(1024)S(1)}, bf16[512,2048]{1,0:T(8,128)(2,1)S(1)}, f32[512,2048]{1,0:T(8,128)}) fusion(f32[512,2048]{1,0:T(8,128)} %fusion.104, f32[2048]{0:T(1024)S(1)} %copy-done.20, bf16[512,1024]{1,0:T(8,128)(2,1)} %all-gather.17.cloned.1.call-done, bf16[2048,1024]{0,1:T(8,128)(2,1)} %all-gather.15.cloned.1.call-done), kind=kOutput, calls=%fused_computation.15 | convolution fusion | flops 2226124800 | bytes 15745024 | tf_op jit(solution)/shard_map/dot_general | solution.py:120
  329.9 1.3 copy-done.30
  331.2 3.3 convolution_convert_fusion.1
  334.6 0.2 reduce-scatter.8.cloned.1.call-start
  334.8 5.9 fusion.63
  340.7 0.3 copy-done.3
  341.0 1.0 multiply_convert_fusion.1
  342.1 1.2 copy-done.24
  343.3 2.4 fusion.111
  345.7 1.8 add_convert_fusion.1
  347.6 3.5 fusion.112
  351.2 6.1 fusion.106
  357.4 6.8 fusion.113
  364.3 0.3 reduce-scatter.18.cloned.1.call-start
  364.5 1.4 copy-done.31
  365.9 5.9 fusion.102
  371.9 1.0 copy-done
  373.1 0.3 dynamic_update_slice.14
  373.4 0.3 dynamic_update_slice.15
  373.8 1.9 fusion.69
  375.6 2.3 fusion.75
  378.0 3.1 convert_reduce_fusion.6
  381.1 41.4 %all-reduce.6 = (f32[1024]{0:T(1024)}, f32[1024]{0:T(1024)}, f32[1024]{0:T(1024)}, f32[1024]{0:T(1024)}, f32[3072]{0:T(1024)}, /*index=5*/f32[1024]{0:T(1024)S(1)}, f32[4096]{0:T(1024)}) all-reduce(f32[1024]{0:T(1024)S(1)} %get-tuple-element.70, ...), channel_id=1, replica_groups=mesh['dp'=16,'tensor'=2] {'dp','tensor'}, use_global_device_ids=true, to_apply=%region_15.16 | all-reduce | flops 12288 | bytes 98304 | tf_op jit(solution)/shard_map/psum | solution.py:248
  422.6 8.5 reduce-scatter.16.cloned.1.call-done
  431.1 158.8 %reduce-scatter.14.cloned.1.call-done = f32[64,1536]{1,0:T(8,128)} async-done(((f32[1024,1536]{1,0:T(8,128)}), f32[64,1536]{1,0:T(8,128)}) %reduce-scatter.14.cloned.1.call-update) | async-done | bytes 393232 | tf_op jit(solution)/shard_map/reduce_scatter | solution.py:210
  589.9 183.3 %reduce-scatter.20.cloned.1.call-done = f32[2048,64]{0,1:T(8,128)} async-done(((f32[2048,1024]{0,1:T(8,128)}), f32[2048,64]{0,1:T(8,128)}) %reduce-scatter.20.cloned.1.call-update) | async-done | bytes 524304 | tf_op jit(solution)/shard_map/reduce_scatter | solution.py:191
  773.2 183.2 %reduce-scatter.18.cloned.1.call-done = f32[64,2048]{1,0:T(8,128)} async-done(((f32[1024,2048]{1,0:T(8,128)}), f32[64,2048]{1,0:T(8,128)}) %reduce-scatter.18.cloned.1.call-update) | async-done | bytes 524304 | tf_op jit(solution)/shard_map/reduce_scatter | solution.py:211
  956.4 0.6 copy.73
  (99 shorter events, 1.7 us)
Async XLA Ops:
  7.2 152.8 %copy-start.17 = (f32[1024]{0:T(1024)S(1)}, f32[1024]{0:T(1024)}, u32[]{:S(2)}) copy-start(f32[1024]{0:T(1024)} %param.19) | copy-start | bytes 12292
  7.2 152.8 %copy-start.28 = (f32[1024]{0:T(1024)S(1)}, f32[1024]{0:T(1024)}, u32[]{:S(2)}) copy-start(f32[1024]{0:T(1024)} %param.20) | copy-start | bytes 12292
  7.2 152.8 %copy-start.27 = (f32[1536]{0:T(1024)S(1)}, f32[1536]{0:T(1024)}, u32[]{:S(2)}) copy-start(f32[1536]{0:T(1024)} %param.24) | copy-start | bytes 18436
  7.2 12.8 %all-gather.7.cloned.1.call-start = ((), (), s32[]{:S(2)}) async-start(), calls=%async_computation.7 | async-start | bytes 1572864 | tf_op jit(solution)/shard_map/all_gather | solution.py:145
  7.9 23.9 %all-gather.17.cloned.1.call-start = ((), (), s32[]{:S(2)}) async-start(), calls=%async_computation.13 | async-start | bytes 1572864 | tf_op jit(solution)/shard_map/all_gather | solution.py:180
  8.7 80.9 %all-gather.11.cloned.1.call-start = ((), (), s32[]{:S(2)}) async-start(), calls=%async_computation.9 | async-start | bytes 1114112 | tf_op jit(solution)/shard_map/all_gather | solution.py:170
  9.4 150.6 %all-gather.9.cloned.1.call-start = ((), (), s32[]{:S(2)}) async-start(), calls=%async_computation.8 | async-start | bytes 3342336 | tf_op jit(solution)/shard_map/all_gather | solution.py:154
  10.0 226.7 %all-gather.13.cloned.1.call-start = ((), (), s32[]{:S(2)}) async-start(), calls=%async_computation.10 | async-start | bytes 4456448 | tf_op jit(solution)/shard_map/all_gather | solution.py:155
  10.6 303.0 %all-gather.15.cloned.1.call-start = ((), (), s32[]{:S(2)}) async-start(), calls=%async_computation.11 | async-start | bytes 4456448 | tf_op jit(solution)/shard_map/all_gather | solution.py:171
  11.2 362.5 %reduce-scatter.10.cloned.1.call-start = ((), (), s32[]{:S(2)}) async-start(), calls=%async_computation.14 | async-start | bytes 1572864 | tf_op jit(solution)/shard_map/reduce_scatter | solution.py:220
  20.0 140.0 %copy-start.4 = (bf16[512,1024]{1,0:T(8,128)(2,1)S(1)}, bf16[512,1024]{1,0:T(8,128)(2,1)}, u32[]{:S(2)}) copy-start(bf16[512,1024]{1,0:T(8,128)(2,1)} %all-gather.7.cloned.1.call-done) | copy-start | bytes 3145732
  168.5 1.7 copy-start.12
  168.6 1.7 copy-start.13
  168.7 1.6 copy-start.14
  168.7 1.6 copy-start.15
  168.7 1.6 copy-start.16
  170.3 3.3 copy-start.1
  170.3 3.9 copy-start.10
  215.3 2.5 slice-start
  215.3 2.6 copy-start.11
  215.3 2.6 copy-start.19
  223.5 2.5 copy-start.26
  223.9 1.1 copy-start.8
  225.9 10.8 %copy-start.18 = (f32[1024]{0:T(1024)S(1)}, f32[1024]{0:T(1024)}, u32[]{:S(2)}) copy-start(f32[1024]{0:T(1024)} %param.21) | copy-start | bytes 12292
  225.9 10.8 %copy-start.29 = (f32[1024]{0:T(1024)S(1)}, f32[1024]{0:T(1024)}, u32[]{:S(2)}) copy-start(f32[1024]{0:T(1024)} %param.22) | copy-start | bytes 12292
  228.9 84.7 %copy-start.20 = (f32[2048]{0:T(1024)S(1)}, f32[2048]{0:T(1024)}, u32[]{:S(2)}) copy-start(f32[2048]{0:T(1024)} %param.28) | copy-start | bytes 24580
  228.9 144.8 %reduce-scatter.12.cloned.1.call-start = ((), (), s32[]{:S(2)}) async-start(), calls=%async_computation.15 | async-start | bytes 1572864 | tf_op jit(solution)/shard_map/reduce_scatter | solution.py:223
  313.6 17.6 %copy-start.25 = (bf16[1024,2048]{1,0:T(8,128)(2,1)S(1)}, bf16[1024,2048]{1,0:T(8,128)(2,1)}, u32[]{:S(2)}) copy-start(bf16[1024,2048]{1,0:T(8,128)(2,1)} %all-gather.13.cloned.1.call-done) | copy-start | bytes 12582916
  329.9 1.3 copy-start.30
  334.6 43.4 %reduce-scatter.8.cloned.1.call-start = ((), (), s32[]{:S(2)}) async-start(), calls=%async_computation.12 | async-start | bytes 1572864 | tf_op jit(solution)/shard_map/reduce_scatter | solution.py:176
  334.8 5.9 copy-start.2
  334.8 6.2 copy-start.3
  340.7 5.0 copy-start.6
  341.0 2.3 copy-start.24
  343.3 2.4 copy-start.9
  347.5 3.7 copy-start.5
  347.5 83.6 %reduce-scatter.16.cloned.1.call-start = ((), (), s32[]{:S(2)}) async-start(), calls=%async_computation.17 | async-start | bytes 2228224 | tf_op jit(solution)/shard_map/reduce_scatter | solution.py:190
  351.1 238.8 %reduce-scatter.14.cloned.1.call-start = ((), (), s32[]{:S(2)}) async-start(), calls=%async_computation.16 | async-start | bytes 6684672 | tf_op jit(solution)/shard_map/reduce_scatter | solution.py:210
  357.4 415.9 %reduce-scatter.20.cloned.1.call-start = ((), (), s32[]{:S(2)}) async-start(), calls=%async_computation.19 | async-start | bytes 8912896 | tf_op jit(solution)/shard_map/reduce_scatter | solution.py:191
  364.2 1.7 copy-start.31
  364.3 592.2 %reduce-scatter.18.cloned.1.call-start = ((), (), s32[]{:S(2)}) async-start(), calls=%async_computation.18 | async-start | bytes 8912896 | tf_op jit(solution)/shard_map/reduce_scatter | solution.py:211
  371.8 1.0 copy-start
  371.8 6.1 copy-start.7
  371.8 6.1 copy-start.21
  371.8 6.1 copy-start.22
  422.6 534.5 %copy-start.23 = (f32[1024]{0:T(1024)}, f32[1024]{0:T(1024)S(1)}, u32[]{:S(2)}) copy-start(f32[1024]{0:T(1024)S(1)} %get-tuple-element.141) | copy-start | bytes 12292
Sparse Core Ops, SparseCore 0:
  9.6 10.4 all-gather.6
  21.6 10.1 all-gather.16
  34.6 54.9 all-gather.10
  92.2 67.7 all-gather.8
  162.6 74.0 all-gather.12
  239.4 74.2 all-gather.14
  315.9 7.3 reduce-scatter.9
  334.7 7.3 reduce-scatter.11
  347.6 7.4 reduce-scatter.7
  357.8 73.1 reduce-scatter.15
  436.9 152.9 reduce-scatter.13
  592.6 180.5 reduce-scatter.19
  776.1 180.2 reduce-scatter.17
where the time goes:
time: 968 us; the launch traced here: 964 us
  waiting for transfers between devices  756 us (78%)
  matrix products  117 us (12%)
  blocking collectives  41.4 us (4%)
  other arithmetic  18.7 us (2%)
  local copies, waits for them, and re-layouts  15.5 us (2%)
  between operations  14.6 us (2%)
    reduce_scatter x1, waiting for transfers between devices, on_device(): lax.psum_scatter(grad_shrink, 'dp', scatter_dimension=1, tiled=True)  183 us
    reduce_scatter x1, waiting for transfers between devices, on_device(): lax.psum_scatter(grad_expand, 'dp', scatter_dimension=0, tiled=True)  183 us
    reduce_scatter x1, waiting for transfers between devices, on_device(): lax.psum_scatter(grad_attend, 'dp', scatter_dimension=0, tiled=True)  159 us
    all_gather x1, waiting for transfers between devices, on_device(): lax.all_gather(shrink_weight, 'dp', axis=1, tiled=True)  69.9 us
    all_gather x1, waiting for transfers between devices, on_device(): lax.all_gather(attend_weight, 'dp', axis=0, tiled=True)  67.3 us
    all_gather x1, waiting for transfers between devices, on_device(): lax.all_gather(project_weight, 'dp', axis=1, tiled=True)  57.8 us
    psum x1, blocking collectives, on_device(): lax.psum((grad_gain_one, grad_shift_one, grad_gain_two, grad_shift_two, b...  41.4 us
    dot_general x4, matrix products, contract_cols(): lax.dot_general(left, right, (((1,), (1,)), ((), ())), preferred_element_...  25.6 us
  transfers between devices with their start and end apart: 13, of which 10 were waited for; matrix products, arithmetic and copies ran while one was open for 15% of the time, Pallas kernels for 0%

commit v1 on v0

v1 whole, which is shorter than its diff:
```python
import jax
import jax.numpy as jnp
import numpy as np
from jax import lax
from jax.experimental import pallas as pl
from jax.experimental.pallas import tpu as pltpu
from jax.sharding import PartitionSpec as P


HD = 64
ROT = 16
QUAD = 4
TABLE_ROWS = 32
EPSILON = 1e-05
NEGATIVE = -1e30
QUERY_BLOCK = 256
ROW_CHUNK = 32
ATTEND_GROUPS = ((0,), (1, 2), (3,))
MLP_GROUPS = ((3,), (1,), (2, 0))
F32 = jnp.float32
BF16 = jnp.bfloat16


HBM = pl.BlockSpec(memory_space=pltpu.HBM)
VMEM = pl.BlockSpec(memory_space=pltpu.VMEM)
SMEM = pl.BlockSpec(memory_space=pltpu.SMEM)


def dot_nn(left, right):
    return lax.dot_general(left, right, (((1,), (0,)), ((), ())), preferred_element_type=F32)


def dot_nt(left, right):
    return lax.dot_general(left, right, (((1,), (1,)), ((), ())), preferred_element_type=F32)


def dot_tn(left, right):
    return lax.dot_general(left, right, (((0,), (0,)), ((), ())), preferred_element_type=F32)


def xor_pairs(n_dp, bits):
    return [(index, index ^ bits) for index in range(n_dp)]


def swap_cores(value):
    return lax.ppermute(value, "tensor", [(0, 1), (1, 0)])


def low_parts(value, number):
    parts = []
    for _ in range(number):
        part = lax.reduce_precision(value, 8, 7)
        parts.append(part.astype(BF16))
        value = value - part
    return parts


def pack_body(meta, attend, project, expand, shrink, *outs):
    first, second = outs[:QUAD], outs[QUAD:]
    quarter = meta[1]
    heads = attend.shape[1] // QUAD
    context = project.shape[1] // QUAD
    hidden = expand.shape[1] // QUAD
    for j in range(QUAD):
        at = quarter ^ j
        first[j][:, :heads] = attend[:, pl.ds(pl.multiple_of(at * heads, 128), heads)]
        first[j][:, heads:] = project[:, pl.ds(pl.multiple_of(at * context, 128), context)]
        second[j][0] = expand[:, pl.ds(pl.multiple_of(at * hidden, 128), hidden)]
        second[j][1] = shrink[:, pl.ds(pl.multiple_of(at * hidden, 128), hidden)]


def pack_weights(meta, attend, project, expand, shrink):
    rows = attend.shape[0]
    width = (attend.shape[1] + project.shape[1]) // QUAD
    hidden = expand.shape[1] // QUAD
    parts = pl.pallas_call(
        pack_body,
        in_specs=[SMEM] + [VMEM] * 4,
        out_specs=[VMEM] * (2 * QUAD),
        out_shape=[jax.ShapeDtypeStruct((rows, width), BF16)] * QUAD
        + [jax.ShapeDtypeStruct((2, rows, hidden), BF16)] * QUAD,
        name="pack_weights",
    )(meta, attend, project, expand, shrink)
    return parts[:QUAD], parts[QUAD:]


def join_body(*refs):
    parts, message = refs[:-1], refs[-1]
    at = 0
    for part in parts:
        message[at : at + part.shape[0]] = part[...]
        at += part.shape[0]


def join_message(*parts):
    rows = sum(part.shape[0] for part in parts)
    return pl.pallas_call(
        join_body,
        in_specs=[VMEM] * len(parts),
        out_specs=VMEM,
        out_shape=jax.ShapeDtypeStruct((rows, parts[0].shape[1]), BF16),
        name="join_message",
    )(*parts)


def unpack_attend_body(meta, own, *refs):
    received, (attend, project) = refs[:3], refs[3:]
    quarter = meta[1]
    heads = attend.shape[1] // QUAD
    context = project.shape[1] // QUAD
    for j in range(QUAD):
        piece = own[...] if j == 0 else received[j - 1][...].astype(F32)
        at = quarter ^ j
        attend[:, pl.ds(pl.multiple_of(at * heads, 128), heads)] = piece[:, :heads]
        project[:, pl.ds(pl.multiple_of(at * context, 128), context)] = piece[:, heads:]


def unpack_attend(meta, own, received, attend_cols, project_cols):
    rows = own.shape[0]
    return pl.pallas_call(
        unpack_attend_body,
        in_specs=[SMEM] + [VMEM] * 4,
        out_specs=[VMEM] * 2,
        out_shape=[
            jax.ShapeDtypeStruct((rows, attend_cols), F32),
            jax.ShapeDtypeStruct((rows, project_cols), F32),
        ],
        name="unpack_attend",
    )(meta, own, *received)


def unpack_mlp_body(meta, own, *refs):
    received, (expand, shrink) = refs[:3], refs[3:]
    quarter = meta[1]
    hidden = expand.shape[1] // QUAD
    for j in range(QUAD):
        piece = own if j == 0 else received[j - 1]
        lanes = pl.ds(pl.multiple_of((quarter ^ j) * hidden, 128), hidden)
        expand[:, lanes] = piece[0].astype(F32)
        shrink[:, lanes] = piece[1].astype(F32)


def unpack_mlp(meta, own, received, hidden_cols):
    rows = own.shape[1]
    return pl.pallas_call(
        unpack_mlp_body,
        in_specs=[SMEM] + [VMEM] * 4,
        out_specs=[VMEM] * 2,
        out_shape=[jax.ShapeDtypeStruct((rows, hidden_cols), F32)] * 2,
        name="unpack_mlp",
    )(meta, own, *received)


def row_chunks(length):
    return [slice(c * ROW_CHUNK, (c + 1) * ROW_CHUNK) for c in range(length // ROW_CHUNK)]


def column_chunks(features):
    return [slice(c * 256, (c + 1) * 256) for c in range(features // 256)]


def wait_bytes(view, sem):
    pltpu.make_async_copy(view, view, sem).wait()


def widen(tile, features):
    return jnp.concatenate([tile] * (features // 128), axis=1)


def fold_rows(value):
    return jnp.sum(value.reshape(value.shape[0] // 8, 8, value.shape[1]), axis=0)


def fold_lanes(value):
    tiles = [value[:, k * 128 : (k + 1) * 128] for k in range(value.shape[1] // 128)]
    while len(tiles) > 1:
        tiles = [sum(tiles[k : k + 2]) for k in range(0, len(tiles), 2)]
    return tiles[0]


def normalize(x, gain, shift, norm_s, hat_s):
    length, features = x.shape
    share = np.float32(1.0 / features)

    def some_rows(number, carry):
        for part in range(4):
            at = pl.multiple_of((number * 4 + part) * ROW_CHUNK, ROW_CHUNK)
            rows = pl.ds(at, ROW_CHUNK)
            tokens = x[rows, :].astype(F32)
            centred = tokens - jnp.sum(fold_lanes(tokens), axis=-1, keepdims=True) * share
            variance = jnp.sum(fold_lanes(centred * centred), axis=-1, keepdims=True) * share
            scaled = centred * lax.rsqrt(variance + EPSILON)
            hat_s[rows, :] = scaled
            norm_s[rows, :] = (scaled * gain[...] + shift[...]).astype(BF16)
        return carry

    lax.fori_loop(0, length // (4 * ROW_CHUNK), some_rows, 0)


def rotate_rows(part, cosine, sine):
    half = ROT // 2
    lead, trail = part[:half], part[half:ROT]
    return jnp.concatenate(
        [lead * cosine - trail * sine, trail * cosine + lead * sine, part[ROT:]], axis=0
    )


class Attend:
    picks = (None,)
    turns = True

    @staticmethod
    def scratch(length, features, width):
        return {
            "mask": pltpu.VMEM((length // QUERY_BLOCK, length, QUERY_BLOCK), F32),
            "q": pltpu.VMEM((2, 2 * HD, length), BF16),
            "d": pltpu.VMEM((2, 2 * HD, length), BF16),
            "kv": pltpu.VMEM((2, length, 2 * HD), BF16),
            "kvt": pltpu.VMEM((2, 2 * HD, length), BF16),
            "dq": pltpu.VMEM((2, HD, length), F32),
            "dk": pltpu.VMEM((2, HD, length), F32),
            "dv": pltpu.VMEM((2, HD, length), F32),
            "ctxt": pltpu.VMEM((2 * HD, length), BF16),
            "ctx": pltpu.VMEM((length, 2 * HD), BF16),
            "gmt": pltpu.VMEM((6 * HD, length), BF16),
            "gm": pltpu.VMEM((length, 6 * HD), BF16),
        }

    @staticmethod
    def bias_shape(width):
        return (6 * HD, 128)

    @staticmethod
    def cost(length, features, width):
        return 6 * length * features * width + 14 * length * length * 2 * HD, 2 * length**2

    @staticmethod
    def compute(m, norm, cot, w, bias, bias_sums, table):
        length = norm.shape[0]
        heads = 6 * HD
        scale = np.float32(HD ** (-0.5))
        values = sum(table[k * 8 : (k + 1) * 8, :].astype(F32) for k in range(3))
        cosine, sine = values[:, :length], values[:, length:]
        start = table[24:25, :length].astype(F32) * 256.0 + table[24:25, length:].astype(F32)
        for block in range(length // QUERY_BLOCK):
            width = (block + 1) * QUERY_BLOCK
            lanes = slice(block * QUERY_BLOCK, width)
            key_at = lax.broadcasted_iota(jnp.int32, (width, QUERY_BLOCK), 0)
            query_at = lax.broadcasted_iota(jnp.int32, (width, QUERY_BLOCK), 1)
            first = start[:, lanes].astype(jnp.int32)
            allowed = (key_at >= first) & (key_at <= query_at + block * QUERY_BLOCK)
            m["mask"][block, :width, :] = jnp.where(allowed, 0.0, NEGATIVE)

        projected = dot_nt(w[:heads, :], norm[...]) + widen(bias[...], length)
        grad_context = dot_nt(w[heads:, :], cot[...]).astype(BF16)
        nothing = jnp.zeros((HD, length), BF16)
        for h in range(2):
            query, key, value = [
                projected[(3 * h + k) * HD : (3 * h + k + 1) * HD] for k in range(3)
            ]
            m["q"][h, :HD, :] = (rotate_rows(query, cosine, sine) * scale).astype(BF16)
            m["q"][h, HD:, :] = nothing
            m["d"][h, :HD, :] = nothing
            m["d"][h, HD:, :] = grad_context[h * HD : (h + 1) * HD]
            both = jnp.concatenate([rotate_rows(key, cosine, sine), value], axis=0).astype(BF16)
            m["kvt"][h] = both
            m["kv"][h] = both.T

        for block in reversed(range(length // QUERY_BLOCK)):
            width = (block + 1) * QUERY_BLOCK
            lanes = slice(block * QUERY_BLOCK, width)
            for h in range(2):
                key_value = m["kv"][h, :width, :]
                scores = dot_nn(key_value, m["q"][h, :, lanes]) + m["mask"][block, :width, :]
                highest = jnp.max(scores, axis=0, keepdims=True)
                numerators = jnp.exp(scores - highest)
                weights = numerators * (1.0 / jnp.sum(numerators, axis=0, keepdims=True))
                weights_low = weights.astype(BF16)
                context = dot_nn(m["kvt"][h, HD:, :width], weights_low)
                m["ctxt"][h * HD : (h + 1) * HD, lanes] = context.astype(BF16)
                grad_probs = dot_nn(key_value, m["d"][h, :, lanes])
                centre = jnp.sum(grad_probs * weights, axis=0, keepdims=True)
                grad_products = (weights * (grad_probs - centre)).astype(BF16)
                grad_query = dot_nn(m["kvt"][h, :HD, :width], grad_products)
                m["dq"][h, :, lanes] = grad_query * scale
                grad_key = dot_nt(m["q"][h, :HD, lanes], grad_products)
                grad_value = dot_nt(m["d"][h, HD:, lanes], weights_low)
                if width == length:
                    m["dk"][h] = grad_key
                    m["dv"][h] = grad_value
                else:
                    m["dk"][h, :, :width] += grad_key
                    m["dv"][h, :, :width] += grad_value

        for h in range(2):
            parts = [
                rotate_rows(m["dq"][h], cosine, -sine),
                rotate_rows(m["dk"][h], cosine, -sine),
                m["dv"][h],
            ]
            for k, part in enumerate(parts):
                rows = slice((3 * h + k) * HD, (3 * h + k + 1) * HD)
                low = part.astype(BF16)
                m["gmt"][rows, :] = low
                bias_sums[rows, :] += fold_lanes(low.astype(F32))
        m["gm"][...] = m["gmt"][...].T
        m["ctx"][...] = m["ctxt"][...].T

    @staticmethod
    def accumulate(m, norm, cot, total):
        heads = 6 * HD
        total[0, :heads, :] += dot_nn(m["gmt"][...], norm[...])
        total[0, heads:, :] += dot_nn(m["ctxt"][...], cot[...])

    @staticmethod
    def forward_out(m, w, cols):
        return dot_nn(m["ctx"][...], w[6 * HD :, cols])

    @staticmethod
    def backward_out(m, w, cols):
        return dot_nn(m["gm"][...], w[: 6 * HD, cols])


class Mlp:
    picks = (0, 1)
    turns = False

    @staticmethod
    def scratch(length, features, width):
        return {
            "hid": pltpu.VMEM((2, length, width), F32),
            "act": pltpu.VMEM((length, width), BF16),
            "dh": pltpu.VMEM((length, width), BF16),
        }

    @staticmethod
    def bias_shape(width):
        return (8, width)

    @staticmethod
    def cost(length, features, width):
        return 12 * length * features * width, 2 * length * width

    @staticmethod
    def compute(m, norm, cot, w, bias, bias_sums, table):
        m["hid"][0] = dot_nn(norm[...], w[0]) + bias[...]
        m["hid"][1] = dot_nn(cot[...], w[1])
        for rows in row_chunks(norm.shape[0]):
            hid = m["hid"][0, rows, :]
            below = 0.5 + 0.5 * lax.erf(hid * np.float32(0.5**0.5))
            slope = below + hid * jnp.exp(-0.5 * (hid * hid)) * np.float32((2 * np.pi) ** -0.5)
            m["act"][rows, :] = (hid * below).astype(BF16)
            grad_hid = (slope * m["hid"][1, rows, :]).astype(BF16)
            m["dh"][rows, :] = grad_hid
            bias_sums[...] += fold_rows(grad_hid.astype(F32))

    @staticmethod
    def accumulate(m, norm, cot, total):
        total[0] += dot_tn(m["dh"][...], norm[...])
        total[1] += dot_tn(m["act"][...], cot[...])

    @staticmethod
    def forward_out(m, w, cols):
        return dot_nt(m["act"][...], w[1, cols, :])

    @staticmethod
    def backward_out(m, w, cols):
        return dot_nt(m["dh"][...], w[0, cols, :])


def branch_body(kind, names, n_seq, count, is_first, is_last, places, *refs):
    refs = list(refs)
    take = lambda number: [refs.pop(0) for _ in range(number)]
    (meta, gain, shift, bias) = take(4)
    messages = [take(2) for _ in range(n_seq)]
    partials = [take(2) for _ in places or ()]
    reads_turned = kind.turns and not is_first
    blocks = take(1 if reads_turned else count)
    carried = [] if is_first else take(3)
    out_hbm, grad_hbm, sums, bias_sums = take(4)
    if is_last:
        grad_send, grad_keep = take(2)
    else:
        (total_hbm,) = take(1)
        if kind.turns:
            (turned_hbm,) = take(1) if is_first else (None,)
    x_s, d_s, tab_s, w_s, total, norm_s, hat_s, out_st, grad_st = take(9)
    wt_s = take(1)[0] if kind.turns else None
    turned = take(1)[0] if is_last else None
    m = dict(zip(names, take(len(names))))
    token_sem, table_sem, weight_sem, part_sem, out_sem, total_sem = take(6)

    length, features = x_s.shape[1:]
    half = length // 2
    mine = pl.multiple_of(meta[0] * half, half)
    other = pl.multiple_of((1 - meta[0]) * half, half)
    rows = features // (QUAD * count)

    weight_copies = []
    if reads_turned:
        weight_copies.append(pltpu.make_async_copy(blocks[0], wt_s, weight_sem.at[0, 0, 0]))
    else:
        for k in range(count):
            for j in range(QUAD):
                place = (meta[2] ^ k) * (QUAD * rows) + (meta[1] ^ j) * rows
                for number, pick in enumerate(kind.picks):
                    source = blocks[k].at[j] if pick is None else blocks[k].at[j, pick]
                    target = w_s.at[number, pl.ds(pl.multiple_of(place, rows), rows)]
                    weight_copies.append(
                        pltpu.make_async_copy(source, target, weight_sem.at[number, k, j])
                    )
    for i in range(n_seq):
        for target, first, which in ((x_s, 0, 0), (d_s, half, 1)):
            for number, place in enumerate((mine, other)):
                pltpu.make_async_copy(
                    messages[i][number].at[pl.ds(first, half)],
                    target.at[i, pl.ds(place, half)],
                    token_sem.at[i, which, number],
                ).start()
        if kind.turns:
            pltpu.make_async_copy(
                messages[i][0].at[pl.ds(2 * half, TABLE_ROWS)], tab_s.at[i], table_sem.at[i]
            ).start()
        if i == 0:
            for copy in weight_copies:
                copy.start()
        if places:
            for number, stage in enumerate((out_st, grad_st)):
                pltpu.make_async_copy(
                    partials[i][number].at[places[i]], stage.at[i], part_sem.at[i, number]
                ).start()
    if is_first:
        total[...] = jnp.zeros_like(total)
        sums[...] = jnp.zeros_like(sums)
        bias_sums[...] = jnp.zeros_like(bias_sums)
    else:
        load = pltpu.make_async_copy(carried[0], total, total_sem.at[0])
        load.start()
        sums[...] = carried[1][...]
        bias_sums[...] = carried[2][...]
    saves = []
    if not is_last:
        saves.append(pltpu.make_async_copy(total, total_hbm, total_sem.at[1]))
        if kind.turns and is_first:
            keep = pltpu.make_async_copy(wt_s, turned_hbm, total_sem.at[2])

    def stores(stage, i, which):
        if not places:
            target = (out_hbm, grad_hbm)[which]
            return [pltpu.make_async_copy(stage.at[i], target.at[i], out_sem.at[i, which, 0])]
        return [
            pltpu.make_async_copy(
                stage.at[i, pl.ds(place, half)], target.at[i, which], out_sem.at[i, which, number]
            )
            for number, (place, target) in enumerate(((mine, out_hbm), (other, grad_hbm)))
        ]

    def one_sequence(i, carry):
        for number in range(2):
            wait_bytes(x_s.at[i, pl.ds(0, half)], token_sem.at[i, 0, number])
        normalize(x_s.at[i], gain, shift, norm_s, hat_s)
        if kind.turns:
            wait_bytes(tab_s.at[i], table_sem.at[i])
        for number in range(2):
            wait_bytes(d_s.at[i, pl.ds(0, half)], token_sem.at[i, 1, number])

        @pl.when(i == 0)
        def _():
            for copy in weight_copies:
                copy.wait()
            if kind.turns and is_first:
                for cols in column_chunks(features):
                    wt_s[:, cols] = w_s[0, cols, :].T
                if not is_last:
                    keep.start()

        cot = d_s.at[i]
        w = wt_s if kind.turns else w_s
        kind.compute(m, norm_s, cot, w, bias, bias_sums, tab_s.at[i])
        if not is_first:

            @pl.when(i == 0)
            def _():
                load.wait()

        kind.accumulate(m, norm_s, cot, total)
        if not is_last:

            @pl.when(i == n_seq - 1)
            def _():
                for copy in saves:
                    copy.start()

        if places:
            wait_bytes(out_st.at[i], part_sem.at[i, 0])
            wait_bytes(grad_st.at[i], part_sem.at[i, 1])
        for cols in column_chunks(features):
            out = kind.forward_out(m, w, cols)
            if places:
                out = out + out_st[i, :, cols].astype(F32)
            out_st[i, :, cols] = out.astype(BF16)
        for copy in stores(out_st, i, 0):
            copy.start()
        for cols in column_chunks(features):
            grad = kind.backward_out(m, w, cols)
            sums[0:8, cols] += fold_rows(grad * hat_s[:, cols])
            sums[8:16, cols] += fold_rows(grad)
            whole = grad * gain[:, cols]
            if places:
                whole = whole + grad_st[i, :, cols].astype(F32)
            grad_st[i, :, cols] = whole.astype(BF16)
        for copy in stores(grad_st, i, 1):
            copy.start()
        return carry

    if n_seq == 1:
        one_sequence(0, 0)
    else:
        lax.fori_loop(0, n_seq, one_sequence, 0)
    if is_last:
        for number, pick in enumerate(kind.picks):
            for cols in column_chunks(features):
                turned[cols, :] = total[number, :, cols].T
            for k in range(count):
                for j in range(QUAD):
                    place = (meta[2] ^ k) * (QUAD * rows) + (meta[1] ^ j) * rows
                    piece = turned[pl.ds(pl.multiple_of(place, rows), rows), :]
                    at = (k // 2, j) if pick is None else (k // 2, j, pick)
                    if k % 2:
                        grad_send[at] = piece.astype(BF16)
                    else:
                        grad_keep[at] = piece
    for copy in saves:
        copy.wait()
    if kind.turns and is_first and not is_last:
        keep.wait()
    for i in range(n_seq):
        for copy in stores(out_st, i, 0) + stores(grad_st, i, 1):
            copy.wait()


def branch(kind, meta, gain, shift, bias, messages, partials, blocks, carried, is_last):
    n_seq, count, is_first = len(messages), len(blocks), carried is None
    half = (messages[0][0].shape[0] - TABLE_ROWS) // 2
    features = messages[0][0].shape[1]
    length = 2 * half
    width = blocks[0].shape[-1]
    n_pick = len(kind.picks)
    operands = [meta, gain, shift, bias]
    specs = [SMEM] + [VMEM] * 3
    for pair in list(messages) + [part[:2] for part in partials]:
        operands += list(pair)
        specs += [HBM] * 2
    places = [part[2] for part in partials]
    if kind.turns and not is_first:
        operands += [carried[3]]
        specs += [HBM]
    else:
        operands += list(blocks)
        specs += [HBM] * count
    if not is_first:
        operands += list(carried[:3])
        specs += [HBM, VMEM, VMEM]
    if places:
        shapes = [jax.ShapeDtypeStruct((n_seq, 2, half, features), BF16)] * 2
    else:
        shapes = [jax.ShapeDtypeStruct((n_seq, length, features), BF16)] * 2
    shapes += [
        jax.ShapeDtypeStruct((16, features), F32),
        jax.ShapeDtypeStruct(kind.bias_shape(width), F32),
    ]
    out_specs = [HBM, HBM, VMEM, VMEM]
    if is_last:
        piece = (count // 2,) + blocks[0].shape
        shapes += [jax.ShapeDtypeStruct(piece, BF16), jax.ShapeDtypeStruct(piece, F32)]
        out_specs += [VMEM] * 2
    else:
        shapes += [jax.ShapeDtypeStruct((n_pick, width, features), F32)]
        out_specs += [HBM]
        if kind.turns and is_first:
            shapes += [jax.ShapeDtypeStruct((width, features), BF16)]
            out_specs += [HBM]
    scratch = [
        pltpu.VMEM((n_seq, length, features), BF16),
        pltpu.VMEM((n_seq, length, features), BF16),
        pltpu.VMEM((n_seq, TABLE_ROWS, features), BF16),
        pltpu.VMEM((n_pick, features, width), BF16),
        pltpu.VMEM((n_pick, width, features), F32),
        pltpu.VMEM((length, features), BF16),
        pltpu.VMEM((length, features), F32),
        pltpu.VMEM((n_seq, length, features), BF16),
        pltpu.VMEM((n_seq, length, features), BF16),
    ]
    if kind.turns:
        scratch += [pltpu.VMEM((width, features), BF16)]
    if is_last:
        scratch += [pltpu.VMEM((features, width), F32)]
    named = kind.scratch(length, features, width)
    scratch += list(named.values())
    scratch += [
        pltpu.SemaphoreType.DMA((n_seq, 2, 2)),
        pltpu.SemaphoreType.DMA((n_seq,)),
        pltpu.SemaphoreType.DMA((n_pick, count, QUAD)),
        pltpu.SemaphoreType.DMA((n_seq, 2)),
        pltpu.SemaphoreType.DMA((n_seq, 2, 2)),
        pltpu.SemaphoreType.DMA((3,)),
    ]
    flops, transcendentals = kind.cost(length, features, width)
    names = tuple(named)

    def body(*refs):
        branch_body(kind, names, n_seq, count, is_first, is_last, places, *refs)

    call = pl.pallas_call(
        body,
        in_specs=specs,
        out_specs=out_specs,
        out_shape=shapes,
        scratch_shapes=scratch,
        cost_estimate=pl.CostEstimate(
            flops=n_seq * flops,
            bytes_accessed=n_seq * 8 * length * features + 10 * n_pick * width * features,
            transcendentals=n_seq * transcendentals,
        ),
    )
    results = call(*operands)
    sums = results[2:4]
    if is_last:
        return results[:2], sums, results[4:]
    turned = () if not kind.turns else (results[5] if is_first else carried[3],)
    return results[:2], sums, (results[4], *sums, *turned)


def finish_body(x, d, own, p1, p2, p3, first_bias, second_bias, out, grad):
    tokens = x[...].astype(F32)
    branches = own[0].astype(F32) + p1[0].astype(F32) + p2[0].astype(F32) + p3[0].astype(F32)
    out[...] = (tokens + branches + first_bias[...] + second_bias[...]).astype(BF16)
    back = own[1].astype(F32) + p1[1].astype(F32) + p2[1].astype(F32) + p3[1].astype(F32)
    average = jnp.mean(tokens, axis=-1, keepdims=True)
    centred = tokens - average
    inverse = lax.rsqrt(jnp.mean(centred * centred, axis=-1, keepdims=True) + EPSILON)
    scaled = centred * inverse
    level = jnp.mean(back, axis=-1, keepdims=True)
    along = jnp.mean(back * scaled, axis=-1, keepdims=True)
    grad[...] = (d[...].astype(F32) + (back - level - scaled * along) * inverse).astype(BF16)


def finish(x, d, own, parts, first_bias, second_bias):
    rows, features = x.shape
    block = min(rows, 64)
    flat = pl.BlockSpec((block, features), lambda i: (i, 0))
    pair = pl.BlockSpec((2, block, features), lambda i: (0, i, 0))
    row = pl.BlockSpec((1, features), lambda i: (0, 0))
    return pl.pallas_call(
        finish_body,
        grid=(rows // block,),
        in_specs=[flat, flat, pair, pair, pair, pair, row, row],
        out_specs=[flat, flat],
        out_shape=[jax.ShapeDtypeStruct((rows, features), BF16)] * 2,
        name="finish",
    )(x, d, own, *parts, first_bias, second_bias)


def on_device(
    n_dp,
    inputs,
    segment_ids,
    positions,
    first_gain,
    first_shift,
    second_gain,
    second_shift,
    attend_weight,
    attend_bias,
    project_weight,
    project_bias,
    expand_weight,
    expand_bias,
    shrink_weight,
    shrink_bias,
    output_grad,
):
    count = n_dp // QUAD
    features = inputs.shape[1]
    attend_cols, hidden_cols = attend_weight.shape[1], expand_weight.shape[1]
    project_cols = project_weight.shape[0]
    core = lax.axis_index("tensor").astype(jnp.int32)
    dp_at = lax.axis_index("dp").astype(jnp.int32)
    quarter = dp_at % QUAD
    meta = jnp.stack([core, quarter, dp_at // QUAD])

    def to_quad(value, j):
        return lax.ppermute(value, "dp", xor_pairs(n_dp, j))

    def to_layer(value, bits):
        return lax.ppermute(value, "dp", xor_pairs(n_dp, bits * QUAD))

    def gather_layers(block):
        blocks = {0: block}
        bit = count // 2
        while bit:
            for k in sorted(blocks):
                blocks[k | bit] = to_layer(blocks[k], bit)
            bit //= 2
        return [blocks[k] for k in range(count)]

    halfway = ROT // 2
    frequency = 1.0 / 10000.0 ** (jnp.arange(halfway, dtype=F32) * (2.0 / ROT))
    angles = frequency[:, None] * positions.astype(F32)[None, :]
    earlier = segment_ids[None, :] < segment_ids[:, None]
    start = jnp.sum(earlier.astype(jnp.int32), axis=1)
    start = jnp.concatenate([start // 256, start % 256]).astype(BF16)
    turns = jnp.concatenate([jnp.cos(angles), jnp.sin(angles)], axis=1)
    message = join_message(
        inputs, output_grad, *low_parts(turns, 3), jnp.broadcast_to(start[None], turns.shape)
    )

    first_pack, second_pack = pack_weights(
        meta, attend_weight, project_weight.T, expand_weight, shrink_weight.T
    )
    second_parts = [second_pack[0]]
    second_parts += [to_quad(second_pack[j], j) for j in range(1, QUAD)]
    second_blocks = gather_layers(jnp.stack(second_parts))
    first_parts = [first_pack[0]] + [to_quad(first_pack[j], j) for j in range(1, QUAD)]
    first_blocks = gather_layers(jnp.stack(first_parts))

    whole = [message] + [to_quad(message, j) for j in range(1, QUAD)]
    messages = [(value, swap_cores(value)) for value in whole]

    one_row = lambda vector: vector[None, :]
    bias_part = lax.dynamic_index_in_dim(
        attend_bias.reshape(QUAD, attend_cols // QUAD), quarter, 0, False
    )
    bias_part = jnp.broadcast_to(bias_part[:, None], (attend_cols // QUAD, 128))
    hidden_part = lax.dynamic_index_in_dim(
        expand_bias.reshape(QUAD, hidden_cols // QUAD), quarter, 0, True
    )

    carried, partials = None, {}
    for group in ATTEND_GROUPS:
        results = branch(
            Attend,
            meta,
            one_row(first_gain),
            one_row(first_shift),
            bias_part,
            [messages[s] for s in group],
            [],
            first_blocks,
            carried,
            group is ATTEND_GROUPS[-1],
        )
        (out_part, grad_part), attend_sums, carried = results
        for place, s in enumerate(group):
            partials[s] = (out_part, grad_part, place)
    attend_send, attend_keep = carried

    carried, sums_of = None, {}
    for group in MLP_GROUPS:
        results = branch(
            Mlp,
            meta,
            one_row(second_gain),
            one_row(second_shift),
            hidden_part,
            [messages[s] for s in group],
            [partials[s] for s in group],
            second_blocks,
            carried,
            group is MLP_GROUPS[-1],
        )
        (mine, other), mlp_sums, carried = results
        other = swap_cores(other)
        for place, s in enumerate(group):
            both = mine[place].astype(F32) + other[place].astype(F32)
            sums_of[s] = both.astype(BF16)
    mlp_send, mlp_keep = carried

    parts = [to_quad(sums_of[j], j) for j in range(1, QUAD)]
    outputs, grad_inputs = finish(
        inputs, output_grad, sums_of[0], parts, one_row(project_bias), one_row(shrink_bias)
    )

    def reduce_layers(send, keep):
        bit = 1
        while True:
            total = to_layer(send, bit).astype(F32) + keep
            if total.shape[0] == 1:
                break
            send, keep = total[1::2].astype(BF16), total[0::2]
            bit *= 2
        parts = [to_quad(total[0, j].astype(BF16), j) for j in range(1, QUAD)]
        return total[0, 0], parts

    own, received = reduce_layers(mlp_send, mlp_keep)
    grad_expand, grad_shrink = unpack_mlp(meta, own, received, hidden_cols)
    own, received = reduce_layers(attend_send, attend_keep)
    grad_attend, grad_project = unpack_attend(meta, own, received, attend_cols, project_cols)

    place = core * QUAD + quarter
    attend_full = lax.dynamic_update_slice_in_dim(
        jnp.zeros((2 * attend_cols,), F32),
        jnp.sum(attend_sums[1], axis=1),
        place * (attend_cols // QUAD),
        0,
    )
    hidden_full = lax.dynamic_update_slice_in_dim(
        jnp.zeros((2 * hidden_cols,), F32),
        jnp.sum(mlp_sums[1], axis=0),
        place * (hidden_cols // QUAD),
        0,
    )
    vector = jnp.concatenate(
        [
            jnp.sum(attend_sums[0].reshape(2, 8, features), axis=1).reshape(-1),
            jnp.sum(mlp_sums[0].reshape(2, 8, features), axis=1).reshape(-1),
            jnp.sum(output_grad.astype(F32), axis=0),
            attend_full,
            hidden_full,
        ]
    ).reshape(-1, 128)
    vector = vector + swap_cores(vector)
    bit = 1
    while bit < n_dp:
        vector = vector + lax.ppermute(vector, "dp", xor_pairs(n_dp, bit))
        bit *= 2
    vector = vector.reshape(-1)
    pieces, at = [], 0
    for size in [features] * 5 + [2 * attend_cols, 2 * hidden_cols]:
        pieces.append(vector[at : at + size])
        at += size
    return (
        outputs,
        grad_inputs,
        pieces[0],
        pieces[1],
        pieces[2],
        pieces[3],
        grad_attend,
        pieces[5],
        grad_project.T,
        pieces[4],
        grad_expand,
        pieces[6],
        grad_shrink.T,
        pieces[4],
    )


def solution(mesh):
    n_dp = mesh.shape["dp"]
    assert mesh.shape["tensor"] == 2 and n_dp % QUAD == 0 and n_dp & (n_dp - 1) == 0
    rows = P(("dp", "tensor"), None)
    in_specs = (
        rows,
        P("dp"),
        P("dp"),
        P(),
        P(),
        P(),
        P(),
        P("dp", "tensor"),
        P("tensor"),
        P("tensor", "dp"),
        P(),
        P("dp", "tensor"),
        P("tensor"),
        P("tensor", "dp"),
        P(),
        rows,
    )
    out_specs = (
        rows,
        rows,
        P(),
        P(),
        P(),
        P(),
        P("dp", "tensor"),
        P(),
        P("tensor", "dp"),
        P(),
        P("dp", "tensor"),
        P(),
        P("tensor", "dp"),
        P(),
    )

    def program(*args):
        return on_device(n_dp, *args)

    return jax.shard_map(
        program, mesh=mesh, in_specs=in_specs, out_specs=out_specs, check_vma=False
    )
```

time: 968 us -> 337 us (0.35)
  waiting for transfers between devices: 756 us -> 166 us
  matrix products: 117 us -> 0 us
  Pallas kernels: 0 us -> 92.8 us
  starting transfers between devices: 0.9 us -> 48 us
  blocking collectives: 41.4 us -> 0 us
  between operations: 14.6 us -> 1.09 us
    reduce_scatter x7 -> x0, waiting for transfers between devices: 534 us -> none  [the longest x1 183 us: on_device(): lax.psum_scatter(grad_shrink, 'dp', scatter_dimension=1, tiled=True)]
    all_gather x6 -> x0, waiting for transfers between devices: 218 us -> none  [the longest x1 69.9 us: on_device(): lax.all_gather(shrink_weight, 'dp', axis=1, tiled=True)]
    ppermute x0 -> x40, waiting for transfers between devices: none -> 166 us  [the longest x18 86.8 us: to_quad(): return lax.ppermute(value, 'dp', xor_pairs(n_dp, j))]
    dot_general x18 -> x0, matrix products: 117 us -> none  [the longest x4 25.6 us: contract_cols(): lax.dot_general(left, right, (((1,), (1,)), ((), ())), preferred_element_...]
    pallas_call x0 -> x11, Pallas kernels: none -> 92.8 us  [the longest x6 79.5 us: branch(): results = call(*operands)]
    ppermute x0 -> x40, starting transfers between devices: none -> 48 us  [the longest x18 21.4 us: to_quad(): return lax.ppermute(value, 'dp', xor_pairs(n_dp, j))]
    psum x1 -> x0, blocking collectives: 41.4 us -> none  [on_device(): lax.psum((grad_gain_one, grad_shift_one, grad_gain_two, grad_shift_two, b...]
  transfers between devices with their start and end apart: 13 -> 40, of which waited for: 10 -> 20; matrix products, arithmetic and copies ran while one was open for 15% -> 5% of each run, Pallas kernels for 0% -> 14%
where the time goes in v1:
time: 337 us; the launch traced here: 333 us
  waiting for transfers between devices  166 us (49%)
  Pallas kernels  92.8 us (28%)
  starting transfers between devices  48 us (14%)
  other arithmetic  13.7 us (4%)
  local copies, waits for them, and re-layouts  12.3 us (4%)
    ppermute x18, waiting for transfers between devices, to_quad(): return lax.ppermute(value, 'dp', xor_pairs(n_dp, j))  86.8 us
    pallas_call x6, Pallas kernels, branch(): results = call(*operands)  79.5 us
    ppermute x10, waiting for transfers between devices, to_layer(): return lax.ppermute(value, 'dp', xor_pairs(n_dp, bits * QUAD))  65.4 us
    ppermute x18, starting transfers between devices, to_quad(): return lax.ppermute(value, 'dp', xor_pairs(n_dp, j))  21.4 us
    ppermute x10, starting transfers between devices, to_layer(): return lax.ppermute(value, 'dp', xor_pairs(n_dp, bits * QUAD))  17.1 us
    ppermute x4, waiting for transfers between devices, on_device(): vector = vector + lax.ppermute(vector, 'dp', xor_pairs(n_dp, bit))  12.1 us
    ppermute x4, starting transfers between devices, on_device(): vector = vector + lax.ppermute(vector, 'dp', xor_pairs(n_dp, bit))  8.4 us
  transfers between devices with their start and end apart: 40, of which 20 were waited for; matrix products, arithmetic and copies ran while one was open for 5% of the time, Pallas kernels for 14%

profile of v1, /device:TPU:10, one launch (start us, length us, event | category | flops | bytes accessed | tf_op | source)
XLA Modules:
  0.0 333.4 jit_solution(2509641234899409945)
XLA Ops:
  0.7 1.0 convert_reduce_fusion.1
  3.8 2.4 join_message.1.refs_4_.refs_6_
  6.7 1.5 collective-permute-start
  8.2 1.4 collective-permute-start.17
  10.2 2.1 pack_weights.1
  12.9 1.5 collective-permute-start.6
  14.4 43.6 %collective-permute-done.5 = bf16[64,512]{1,0:T(8,128)(2,1)S(1)} collective-permute-done((bf16[64,512]{1,0:T(8,128)(2,1)}, bf16[64,512]{1,0:T(8,128)(2,1)S(1)}, u32[]{:S(2)}, u32[]{:S(2)}) %collective-permute-start.5) | collective-permute-done | bytes 65568 | tf_op jit(solution)/shard_map/ppermute | solution.py:693
  58.0 1.5 collective-permute-start.7
  59.5 1.5 collective-permute-start.11
  60.9 2.6 collective-permute-done.7
  63.6 1.5 collective-permute-start.12
  65.1 0.9 pad_maximum_fusion.1.refs_6_
  66.0 2.7 collective-permute-start.9
  68.7 2.0 collective-permute-start.13
  70.7 4.1 %collective-permute-done.13 = bf16[2,64,512]{2,1,0:T(8,128)(2,1)S(1)} collective-permute-done((bf16[2,64,512]{2,1,0:T(8,128)(2,1)}, bf16[2,64,512]{2,1,0:T(8,128)(2,1)S(1)}, u32[]{:S(2)}, u32[]{:S(2)}) %collective-permute-start.13) | collective-permute-done | bytes 131104 | tf_op jit(solution)/shard_map/ppermute | solution.py:693
  74.8 2.5 collective-permute-done.9.refs_8_
  77.3 1.4 collective-permute-start.8
  79.2 5.6 %collective-permute-done.8.refs_7_ = bf16[4,64,512]{2,1,0:T(8,128)(2,1)S(1)} collective-permute-done((bf16[4,64,512]{2,1,0:T(8,128)(2,1)S(1)}, bf16[4,64,512]{2,1,0:T(8,128)(2,1)S(1)}, u32[]{:S(2)}, u32[]{:S(2)}) %collective-permute-start.8) | collective-permute-done | bytes 262176 | tf_op jit(solution)/shard_map/ppermute | solution.py:696
  84.8 1.1 collective-permute-start.10
  85.9 1.0 pad_maximum_fusion.refs_8_.refs_12_
  86.9 4.6 %collective-permute-done.10.refs_9_ = bf16[4,64,512]{2,1,0:T(8,128)(2,1)S(1)} collective-permute-done((bf16[4,64,512]{2,1,0:T(8,128)(2,1)S(1)}, bf16[4,64,512]{2,1,0:T(8,128)(2,1)S(1)}, u32[]{:S(2)}, u32[]{:S(2)}) %collective-permute-start.10) | collective-permute-done | bytes 262176 | tf_op jit(solution)/shard_map/ppermute | solution.py:696
  92.1 3.4 %collective-permute-start.15 = (bf16[4,2,64,512]{3,2,1,0:T(8,128)(2,1)S(1)}, bf16[4,2,64,512]{3,2,1,0:T(8,128)(2,1)}, u32[]{:S(2)}, u32[]{:S(2)}) collective-permute-start(bf16[4,2,64,512]{3,2,1,0:T(8,128)(2,1)S(1)} %pad_maximum_fusion.refs_8_.refs_12_), channel_id=1, source_target_pairs={{0,16},{2,18},{4,20},{6,22},{8,24},{10,26},{12,28},{14,30},{16,0},... | collective-permute-start | bytes 1572872 | tf_op jit(solution)/shard_map/ppermute | solution.py:696
  96.9 18.7 %collective-permute-done.15.refs_10_.refs_14_ = bf16[4,2,64,512]{3,2,1,0:T(8,128)(2,1)} collective-permute-done((bf16[4,2,64,512]{3,2,1,0:T(8,128)(2,1)S(1)}, bf16[4,2,64,512]{3,2,1,0:T(8,128)(2,1)}, u32[]{:S(2)}, u32[]{:S(2)}) %collective-permute-start.15) | collective-permute-done | bytes 524320 | tf_op jit(solution)/shard_map/ppermute | solution.py:696
  115.7 1.7 collective-permute-start.14
  118.5 11.1 %shard_map.263 = (bf16[1,512,1024]{2,1,0:T(8,128)(2,1)}, bf16[1,512,1024]{2,1,0:T(8,128)(2,1)}, f32[16,1024]{1,0:T(8,128)}, f32[384,128]{1,0:T(8,128)}, f32[1,51...) custom-call(s32[3]{0:T(128)} %pad_add_fusion.meta.refs_0_, f32[1,1024]{1,0:T(1,128)} %bitcast.96, f32[1,1024]{1,0:T(1,128)} %bitcast.99, ...), custom_call_target="tpu_custom_call" | custom-call | flops 2080374784 | bytes 9437184 | tf_op jit(solution)/shard_map/pallas_call | solution.py:626
  129.7 1.0 copy-done.5
  130.7 17.9 %shard_map.264 = (bf16[2,512,1024]{2,1,0:T(8,128)(2,1)}, bf16[2,512,1024]{2,1,0:T(8,128)(2,1)}, f32[16,1024]{1,0:T(8,128)}, f32[384,128]{1,0:T(8,128)}, f32[1,512,1024]{2,1,0:T(8,128)}) custom-call(s32[3]{0:T(128)} %pad_add_fusion.meta.refs_0_, f32[1,1024]{1,0:T(1,128)} %bitcast.97, f32[1,1024]{1,0:T(1,128)} %bitcast.100, ...), custom_call_target="tpu_custom_call" | custom-call | flops 4160749568 | bytes 13631488 | tf_op jit(solution)/shard_map/pallas_call | solution.py:626
  148.7 12.2 %shard_map.265 = (bf16[1,512,1024]{2,1,0:T(8,128)(2,1)}, bf16[1,512,1024]{2,1,0:T(8,128)(2,1)}, f32[16,1024]{1,0:T(8,128)}, f32[384,128]{1,0:T(8,128)}, bf16[2,4...) custom-call(s32[3]{0:T(128)} %pad_add_fusion.meta.refs_0_, f32[1,1024]{1,0:T(1,128)} %bitcast.98, f32[1,1024]{1,0:T(1,128)} %bitcast.101, ...), custom_call_target="tpu_custom_call" | custom-call | flops 2080374784 | bytes 9437184 | tf_op jit(solution)/shard_map/pallas_call | solution.py:626
  160.9 1.1 reduce_sum.58
  161.9 0.9 bitcast_reduce_fusion.1
  163.6 10.0 %shard_map.266 = (bf16[1,2,256,1024]{3,2,1,0:T(8,128)(2,1)}, bf16[1,2,256,1024]{3,2,1,0:T(8,128)(2,1)}, f32[16,1024]{1,0:T(8,128)}, f32[8,512]{1,0:T(8,128)}, f32[2,512,1024]{2,1,0:T(8,128)}) custom-call(s32[3]{0:T(128)} %pad_add_fusion.meta.refs_0_, f32[1,1024]{1,0:T(1,128)} %bitcast.86, f32[1,1024]{1,0:T(1,128)} %bitcast.89, ...), custom_call_target="tpu_custom_call" | custom-call | flops 3221225472 | bytes 14680064 | tf_op jit(solution)/shard_map/pallas_call | solution.py:626
  173.6 10.5 %shard_map.267 = (bf16[1,2,256,1024]{3,2,1,0:T(8,128)(2,1)}, bf16[1,2,256,1024]{3,2,1,0:T(8,128)(2,1)}, f32[16,1024]{1,0:T(8,128)}, f32[8,512]{1,0:T(8,128)}, f32[2,512,1024]{2,1,0:T(8,128)}) custom-call(s32[3]{0:T(128)} %pad_add_fusion.meta.refs_0_, f32[1,1024]{1,0:T(1,128)} %bitcast.87, f32[1,1024]{1,0:T(1,128)} %bitcast.90, ...), custom_call_target="tpu_custom_call" | custom-call | flops 3221225472 | bytes 14680064 | tf_op jit(solution)/shard_map/pallas_call | solution.py:626
  184.2 17.8 %shard_map.268 = (bf16[2,2,256,1024]{3,2,1,0:T(8,128)(2,1)}, bf16[2,2,256,1024]{3,2,1,0:T(8,128)(2,1)}, f32[16,1024]{1,0:T(8,128)}, f32[8,512]{1,0:T(8,128)}, bf...) custom-call(s32[3]{0:T(128)} %pad_add_fusion.meta.refs_0_, f32[1,1024]{1,0:T(1,128)} %bitcast.88, ...), custom_call_target="tpu_custom_call" | custom-call | flops 6442450944 | bytes 18874368 | tf_op jit(solution)/shard_map/pallas_call | solution.py:626
  202.7 0.9 bitcast_reduce_fusion
  204.5 1.2 collective-permute-done.25
  205.7 2.1 collective-permute-start.26
  207.9 1.7 collective-permute-start.30
  210.0 1.0 collective-permute-start.27
  210.9 3.2 collective-permute-done.27
  214.1 1.7 collective-permute-start.28
  215.9 6.7 %collective-permute-done.28 = f32[96,128]{1,0:T(8,128)S(1)} collective-permute-done((f32[96,128]{1,0:T(8,128)S(1)}, f32[96,128]{1,0:T(8,128)S(1)}, u32[]{:S(2)}, u32[]{:S(2)}) %collective-permute-start.28) | collective-permute-done | bytes 49184 | tf_op jit(solution)/shard_map/ppermute | solution.py:825
  222.6 3.5 %collective-permute-start.29 = (f32[96,128]{1,0:T(8,128)S(1)}, f32[96,128]{1,0:T(8,128)S(1)}, u32[]{:S(2)}, u32[]{:S(2)}) collective-permute-start(f32[96,128]{1,0:T(8,128)S(1)} %add.87), channel_id=1, source_target_pairs={{0,16},{2,18},{4,20},{6,22},{8,24},{10,26},{12,28},{14,30},{16,0},... | collective-permute-start | bytes 147464 | tf_op jit(solution)/shard_map/ppermute | solution.py:825
  226.9 1.8 collective-permute-done.29
  229.6 3.0 collective-permute-start.31
  233.7 21.6 %collective-permute-done.31 = bf16[1,4,64,512]{3,2,1,0:T(8,128)(2,1)S(1)} collective-permute-done((bf16[1,4,64,512]{3,2,1,0:T(8,128)(2,1)S(1)}, bf16[1,4,64,512]{3,2,1,0:T(8,128)(2,1)S(1)}, u32[]{:S(2)}, u32[]{:S(2)}) %collective-permute-start.31) | collective-permute-done | bytes 262176 | tf_op jit(solution)/shard_map/ppermute | solution.py:696
  256.0 1.7 collective-permute-start.36
  258.8 1.4 fusion.3
  260.2 1.7 collective-permute-start.24
  262.0 2.3 fusion.2
  264.3 1.1 collective-permute-start.22
  265.5 1.0 collective-permute-start.34
  266.5 12.4 %collective-permute-done.36 = bf16[1,4,2,64,512]{4,3,2,1,0:T(8,128)(2,1)S(1)} collective-permute-done((bf16[1,4,2,64,512]{4,3,2,1,0:T(8,128)(2,1)S(1)}, bf16[1,4,2,64,512]{4,3,2,1,0:T(8,128)(2,1)S(1)}, u32[]{:S(2)}, u32[]{:S(2)}) %collective-permute-start.36) | collective-permute-done | bytes 524320 | tf_op jit(solution)/shard_map/ppermute | solution.py:696
  278.9 0.9 collective-permute-start.33
  280.7 25.2 %collective-permute-done.34.refs_2_ = bf16[64,512]{1,0:T(8,128)(2,1)S(1)} collective-permute-done((bf16[64,512]{1,0:T(8,128)(2,1)S(1)}, bf16[64,512]{1,0:T(8,128)(2,1)S(1)}, u32[]{:S(2)}, u32[]{:S(2)}) %collective-permute-start.34) | collective-permute-done | bytes 65568 | tf_op jit(solution)/shard_map/ppermute | solution.py:693
  305.9 0.9 collective-permute-start.32
  306.8 5.9 %collective-permute-done.33.refs_1_ = bf16[64,512]{1,0:T(8,128)(2,1)S(1)} collective-permute-done((bf16[64,512]{1,0:T(8,128)(2,1)S(1)}, bf16[64,512]{1,0:T(8,128)(2,1)S(1)}, u32[]{:S(2)}, u32[]{:S(2)}) %collective-permute-start.33) | collective-permute-done | bytes 65568 | tf_op jit(solution)/shard_map/ppermute | solution.py:693
  312.7 1.5 collective-permute-start.39
  314.8 1.8 unpack_attend.1
  316.6 0.9 collective-permute-start.38
  317.5 2.2 collective-permute-done.39.refs_2_
  322.2 2.5 collective-permute-done.37.refs_0_
  324.8 2.2 unpack_mlp.1
  327.0 1.0 copy-done.8
  327.9 4.8 %finish.1 = (bf16[256,1024]{1,0:T(8,128)(2,1)}, bf16[256,1024]{1,0:T(8,128)(2,1)}) custom-call(bf16[256,1024]{1,0:T(8,128)(2,1)} %x.1, bf16[256,1024]{1,0:T(8,128)(2,1)} %d.1, bf16[2,256,1024]{2,1,0:T(8,128)(2,1)} %get-tuple-element.113.own, bf16[2,256,1024]{2,1,0:T(8,128)(2,1)} %copy-done.8, bf16[2,256,1024]{2,1,0:T(8,128)(2,1)} %collective-permute-done.22.p2, ...), custom_call_target="tpu_custom_call" | custom-call | tf_op jit(solution)/shard_map/finish/pallas_call | solution.py:654
  (125 shorter events, 19.8 us)
Async XLA Ops:
  3.8 91.8 %copy-start.17 = (f32[1536]{0:T(1024)S(1)}, f32[1536]{0:T(1024)}, u32[]{:S(2)}) copy-start(f32[1536]{0:T(1024)} %param.24) | copy-start | bytes 18436
  3.8 93.1 %copy-start = (bf16[256,1024]{1,0:T(8,128)(2,1)S(1)}, bf16[256,1024]{1,0:T(8,128)(2,1)}, u32[]{:S(2)}) copy-start(bf16[256,1024]{1,0:T(8,128)(2,1)} %d.1) | copy-start | bytes 1572868
  6.1 72.5 %collective-permute-start.3 = (bf16[544,1024]{1,0:T(8,128)(2,1)}, bf16[544,1024]{1,0:T(8,128)(2,1)S(1)}, u32[]{:S(2)}, u32[]{:S(2)}) collective-permute-start(bf16[544,1024]{1,0:T(8,128)(2,1)} %join_message.1.refs_4_.refs_6_), channel_id=1, source_target_pairs={{0,2},{2,0},{4,6},{6,4},{8,10},{10,8},{12,14},{14,12},{16,18},{18,... | collective-permute-start | bytes 3342344 | tf_op jit(solution)/shard_map/ppermute | solution.py:693
  6.7 72.0 %collective-permute-start = (bf16[544,1024]{1,0:T(8,128)(2,1)}, bf16[544,1024]{1,0:T(8,128)(2,1)}, u32[]{:S(2)}, u32[]{:S(2)}) collective-permute-start(bf16[544,1024]{1,0:T(8,128)(2,1)} %join_message.1.refs_4_.refs_6_), channel_id=1, source_target_pairs={{0,4},{2,6},{4,0},{6,2},{8,12},{10,14},{12,8},{14,10},{16,20},{18,... | collective-permute-start | bytes 3342344 | tf_op jit(solution)/shard_map/ppermute | solution.py:693
  8.2 77.7 %collective-permute-start.17 = (bf16[544,1024]{1,0:T(8,128)(2,1)}, bf16[544,1024]{1,0:T(8,128)(2,1)}, u32[]{:S(2)}, u32[]{:S(2)}) collective-permute-start(bf16[544,1024]{1,0:T(8,128)(2,1)} %join_message.1.refs_4_.refs_6_), channel_id=1, source_target_pairs={{0,6},{2,4},{4,2},{6,0},{8,14},{10,12},{12,10},{14,8},{16,22},{18,... | collective-permute-start | bytes 3342344 | tf_op jit(solution)/shard_map/ppermute | solution.py:693
  12.3 45.6 %collective-permute-start.5 = (bf16[64,512]{1,0:T(8,128)(2,1)}, bf16[64,512]{1,0:T(8,128)(2,1)S(1)}, u32[]{:S(2)}, u32[]{:S(2)}) collective-permute-start(bf16[64,512]{1,0:T(8,128)(2,1)} %get-tuple-element.62), channel_id=1, source_target_pairs={{0,2},{2,0},{4,6},{6,4},{8,10},{10,8},{12,14},{14,12},{16,18},{18,... | collective-permute-start | bytes 196616 | tf_op jit(solution)/shard_map/ppermute | solution.py:693
  12.9 46.6 %collective-permute-start.6 = (bf16[64,512]{1,0:T(8,128)(2,1)}, bf16[64,512]{1,0:T(8,128)(2,1)S(1)}, u32[]{:S(2)}, u32[]{:S(2)}) collective-permute-start(bf16[64,512]{1,0:T(8,128)(2,1)} %get-tuple-element.63), channel_id=1, source_target_pairs={{0,4},{2,6},{4,0},{6,2},{8,12},{10,14},{12,8},{14,10},{16,20},{18,... | collective-permute-start | bytes 196616 | tf_op jit(solution)/shard_map/ppermute | solution.py:693
  58.0 5.6 %collective-permute-start.7 = (bf16[64,512]{1,0:T(8,128)(2,1)}, bf16[64,512]{1,0:T(8,128)(2,1)S(1)}, u32[]{:S(2)}, u32[]{:S(2)}) collective-permute-start(bf16[64,512]{1,0:T(8,128)(2,1)} %get-tuple-element.64), channel_id=1, source_target_pairs={{0,6},{2,4},{4,2},{6,0},{8,14},{10,12},{12,10},{14,8},{16,22},{18,... | collective-permute-start | bytes 196616 | tf_op jit(solution)/shard_map/ppermute | solution.py:693
  59.5 6.5 %collective-permute-start.11 = (bf16[2,64,512]{2,1,0:T(8,128)(2,1)}, bf16[2,64,512]{2,1,0:T(8,128)(2,1)S(1)}, u32[]{:S(2)}, u32[]{:S(2)}) collective-permute-start(bf16[2,64,512]{2,1,0:T(8,128)(2,1)} %get-tuple-element.74), channel_id=1, source_target_pairs={{0,2},{2,0},{4,6},{6,4},{8,10},{10,8},{12,14},{14,12},{16,18},{18,... | collective-permute-start | bytes 393224 | tf_op jit(solution)/shard_map/ppermute | solution.py:693
  63.6 5.2 %collective-permute-start.12 = (bf16[2,64,512]{2,1,0:T(8,128)(2,1)}, bf16[2,64,512]{2,1,0:T(8,128)(2,1)S(1)}, u32[]{:S(2)}, u32[]{:S(2)}) collective-permute-start(bf16[2,64,512]{2,1,0:T(8,128)(2,1)} %get-tuple-element.75), channel_id=1, source_target_pairs={{0,4},{2,6},{4,0},{6,2},{8,12},{10,14},{12,8},{14,10},{16,20},{18,... | collective-permute-start | bytes 393224 | tf_op jit(solution)/shard_map/ppermute | solution.py:693
  66.0 52.6 %copy-start.11 = (bf16[4,64,512]{2,1,0:T(8,128)(2,1)}, bf16[4,64,512]{2,1,0:T(8,128)(2,1)S(1)}, u32[]{:S(2)}) copy-start(bf16[4,64,512]{2,1,0:T(8,128)(2,1)S(1)} %pad_maximum_fusion.1.refs_6_) | copy-start | bytes 786436
  66.0 11.3 %collective-permute-start.9 = (bf16[4,64,512]{2,1,0:T(8,128)(2,1)S(1)}, bf16[4,64,512]{2,1,0:T(8,128)(2,1)S(1)}, u32[]{:S(2)}, u32[]{:S(2)}) collective-permute-start(bf16[4,64,512]{2,1,0:T(8,128)(2,1)S(1)} %pad_maximum_fusion.1.refs_6_), channel_id=1, source_target_pairs={{0,16},{2,18},{4,20},{6,22},{8,24},{10,26},{12,28},{14,30},{16,0},... | collective-permute-start | bytes 786440 | tf_op jit(solution)/shard_map/ppermute | solution.py:696
  68.7 6.1 %collective-permute-start.13 = (bf16[2,64,512]{2,1,0:T(8,128)(2,1)}, bf16[2,64,512]{2,1,0:T(8,128)(2,1)S(1)}, u32[]{:S(2)}, u32[]{:S(2)}) collective-permute-start(bf16[2,64,512]{2,1,0:T(8,128)(2,1)} %get-tuple-element.76), channel_id=1, source_target_pairs={{0,6},{2,4},{4,2},{6,0},{8,14},{10,12},{12,10},{14,8},{16,22},{18,... | collective-permute-start | bytes 393224 | tf_op jit(solution)/shard_map/ppermute | solution.py:693
  74.8 42.6 %collective-permute-start.2 = (bf16[544,1024]{1,0:T(8,128)(2,1)}, bf16[544,1024]{1,0:T(8,128)(2,1)}, u32[]{:S(2)}, u32[]{:S(2)}) collective-permute-start(bf16[544,1024]{1,0:T(8,128)(2,1)} %join_message.1.refs_4_.refs_6_), channel_id=1, source_target_pairs={{0,1},{1,0},{2,3},{3,2},{4,5},{5,4},{6,7},{7,6},{8,9},{9,8},{10,11... | collective-permute-start | bytes 3342344 | tf_op jit(solution)/shard_map/ppermute | solution.py:46
  77.3 9.6 %copy-start.20 = (bf16[4,64,512]{2,1,0:T(8,128)(2,1)}, bf16[4,64,512]{2,1,0:T(8,128)(2,1)S(1)}, u32[]{:S(2)}) copy-start(bf16[4,64,512]{2,1,0:T(8,128)(2,1)S(1)} %collective-permute-done.9.refs_8_) | copy-start | bytes 786436
  77.3 7.5 %collective-permute-start.8 = (bf16[4,64,512]{2,1,0:T(8,128)(2,1)S(1)}, bf16[4,64,512]{2,1,0:T(8,128)(2,1)S(1)}, u32[]{:S(2)}, u32[]{:S(2)}) collective-permute-start(bf16[4,64,512]{2,1,0:T(8,128)(2,1)S(1)} %pad_maximum_fusion.1.refs_6_), channel_id=1, source_target_pairs={{0,8},{2,10},{4,12},{6,14},{8,0},{10,2},{12,4},{14,6},{16,24},{18,... | collective-permute-start | bytes 786440 | tf_op jit(solution)/shard_map/ppermute | solution.py:696
  78.7 51.0 %copy-start.4 = (bf16[544,1024]{1,0:T(8,128)(2,1)}, bf16[544,1024]{1,0:T(8,128)(2,1)S(1)}, u32[]{:S(2)}) copy-start(bf16[544,1024]{1,0:T(8,128)(2,1)S(1)} %collective-permute-done.3.refs_4_) | copy-start | bytes 3342340
  78.7 51.0 %collective-permute-start.4 = (bf16[544,1024]{1,0:T(8,128)(2,1)S(1)}, bf16[544,1024]{1,0:T(8,128)(2,1)S(1)}, u32[]{:S(2)}, u32[]{:S(2)}) collective-permute-start(bf16[544,1024]{1,0:T(8,128)(2,1)S(1)} %collective-permute-done.3.refs_4_), channel_id=1, source_target_pairs={{0,1},{1,0},{2,3},{3,2},{4,5},{5,4},{6,7},{7,6},{8,9},{9,8},{10,11... | collective-permute-start | bytes 3342344 | tf_op jit(solution)/shard_map/ppermute | solution.py:46
  78.7 51.0 %collective-permute-start.1 = (bf16[544,1024]{1,0:T(8,128)(2,1)}, bf16[544,1024]{1,0:T(8,128)(2,1)}, u32[]{:S(2)}, u32[]{:S(2)}) collective-permute-start(bf16[544,1024]{1,0:T(8,128)(2,1)} %collective-permute-done.refs_6_.refs_4_), channel_id=1, source_target_pairs={{0,1},{1,0},{2,3},{3,2},{4,5},{5,4},{6,7},{7,6},{8,9},{9,8},{10,11... | collective-permute-start | bytes 3342344 | tf_op jit(solution)/shard_map/ppermute | solution.py:46
  84.8 1.1 copy-start.21
  84.8 6.6 %collective-permute-start.10 = (bf16[4,64,512]{2,1,0:T(8,128)(2,1)S(1)}, bf16[4,64,512]{2,1,0:T(8,128)(2,1)S(1)}, u32[]{:S(2)}, u32[]{:S(2)}) collective-permute-start(bf16[4,64,512]{2,1,0:T(8,128)(2,1)S(1)} %collective-permute-done.9.refs_8_), channel_id=1, source_target_pairs={{0,8},{2,10},{4,12},{6,14},{8,0},{10,2},{12,4},{14,6},{16,24},{18,... | collective-permute-start | bytes 786440 | tf_op jit(solution)/shard_map/ppermute | solution.py:696
  85.9 62.8 %collective-permute-start.18 = (bf16[544,1024]{1,0:T(8,128)(2,1)}, bf16[544,1024]{1,0:T(8,128)(2,1)}, u32[]{:S(2)}, u32[]{:S(2)}) collective-permute-start(bf16[544,1024]{1,0:T(8,128)(2,1)} %collective-permute-done.17.refs_4_), channel_id=1, source_target_pairs={{0,1},{1,0},{2,3},{3,2},{4,5},{5,4},{6,7},{7,6},{8,9},{9,8},{10,11... | collective-permute-start | bytes 3342344 | tf_op jit(solution)/shard_map/ppermute | solution.py:46
  86.9 42.8 %copy-start.2 = (bf16[4,2,64,512]{3,2,1,0:T(8,128)(2,1)}, bf16[4,2,64,512]{3,2,1,0:T(8,128)(2,1)S(1)}, u32[]{:S(2)}) copy-start(bf16[4,2,64,512]{3,2,1,0:T(8,128)(2,1)S(1)} %pad_maximum_fusion.refs_8_.refs_12_) | copy-start | bytes 1572868
  91.4 0.7 copy-start.22
  92.1 23.5 %collective-permute-start.15 = (bf16[4,2,64,512]{3,2,1,0:T(8,128)(2,1)S(1)}, bf16[4,2,64,512]{3,2,1,0:T(8,128)(2,1)}, u32[]{:S(2)}, u32[]{:S(2)}) collective-permute-start(bf16[4,2,64,512]{3,2,1,0:T(8,128)(2,1)S(1)} %pad_maximum_fusion.refs_8_.refs_12_), channel_id=1, source_target_pairs={{0,16},{2,18},{4,20},{6,22},{8,24},{10,26},{12,28},{14,30},{16,0},... | collective-permute-start | bytes 1572872 | tf_op jit(solution)/shard_map/ppermute | solution.py:696
  115.7 47.1 %collective-permute-start.14 = (bf16[4,2,64,512]{3,2,1,0:T(8,128)(2,1)S(1)}, bf16[4,2,64,512]{3,2,1,0:T(8,128)(2,1)S(1)}, u32[]{:S(2)}, u32[]{:S(2)}) collective-permute-start(bf16[4,2,64,512]{3,2,1,0:T(8,128)(2,1)S(1)} %pad_maximum_fusion.refs_8_.refs_12_), channel_id=1, source_target_pairs={{0,8},{2,10},{4,12},{6,14},{8,0},{10,2},{12,4},{14,6},{16,24},{18,... | collective-permute-start | bytes 1572872 | tf_op jit(solution)/shard_map/ppermute | solution.py:696
  117.4 45.5 %collective-permute-start.16 = (bf16[4,2,64,512]{3,2,1,0:T(8,128)(2,1)}, bf16[4,2,64,512]{3,2,1,0:T(8,128)(2,1)}, u32[]{:S(2)}, u32[]{:S(2)}) collective-permute-start(bf16[4,2,64,512]{3,2,1,0:T(8,128)(2,1)} %collective-permute-done.15.refs_10_.refs_14_), channel_id=1, source_target_pairs={{0,8},{2,10},{4,12},{6,14},{8,0},{10,2},{12,4},{14,6},{16,24},{18,... | collective-permute-start | bytes 1572872 | tf_op jit(solution)/shard_map/ppermute | solution.py:696
  129.7 1.0 copy-start.5
  162.8 0.8 copy-start.10
  184.2 23.7 %copy-start.19 = (bf16[2,4,64,512]{3,2,1,0:T(8,128)(2,1)S(1)}, bf16[2,4,64,512]{3,2,1,0:T(8,128)(2,1)}, u32[]{:S(2)}) copy-start(bf16[2,4,64,512]{3,2,1,0:T(8,128)(2,1)} %get-tuple-element.100) | copy-start | bytes 1572868
  184.2 42.3 %copy-start.18 = (bf16[1,2,256,1024]{3,2,1,0:T(8,128)(2,1)S(1)}, bf16[1,2,256,1024]{3,2,1,0:T(8,128)(2,1)}, u32[]{:S(2)}) copy-start(bf16[1,2,256,1024]{3,2,1,0:T(8,128)(2,1)} %get-tuple-element.93) | copy-start | bytes 3145732
  184.2 45.2 %copy-start.9 = (f32[2,4,64,512]{3,2,1,0:T(8,128)S(1)}, f32[2,4,64,512]{3,2,1,0:T(8,128)}, u32[]{:S(2)}) copy-start(f32[2,4,64,512]{3,2,1,0:T(8,128)} %get-tuple-element.101) | copy-start | bytes 3145732
  204.4 1.3 collective-permute-start.25
  205.7 4.2 %collective-permute-start.26 = (f32[96,128]{1,0:T(8,128)S(1)}, f32[96,128]{1,0:T(8,128)S(1)}, u32[]{:S(2)}, u32[]{:S(2)}) collective-permute-start(f32[96,128]{1,0:T(8,128)S(1)} %bitcast_add_fusion), channel_id=1, source_target_pairs={{0,2},{2,0},{4,6},{6,4},{8,10},{10,8},{12,14},{14,12},{16,18},{18,... | collective-permute-start | bytes 147464 | tf_op jit(solution)/shard_map/ppermute | solution.py:825
  207.9 21.5 %collective-permute-start.30 = (bf16[2,4,64,512]{3,2,1,0:T(8,128)(2,1)S(1)}, bf16[2,4,64,512]{3,2,1,0:T(8,128)(2,1)S(1)}, u32[]{:S(2)}, u32[]{:S(2)}) collective-permute-start(bf16[2,4,64,512]{3,2,1,0:T(8,128)(2,1)S(1)} %copy-done.19), channel_id=1, source_target_pairs={{0,8},{2,10},{4,12},{6,14},{8,0},{10,2},{12,4},{14,6},{16,24},{18,... | collective-permute-start | bytes 1572872 | tf_op jit(solution)/shard_map/ppermute | solution.py:696
  210.0 4.2 %collective-permute-start.27 = (f32[96,128]{1,0:T(8,128)S(1)}, f32[96,128]{1,0:T(8,128)S(1)}, u32[]{:S(2)}, u32[]{:S(2)}) collective-permute-start(f32[96,128]{1,0:T(8,128)S(1)} %fusion.11), channel_id=1, source_target_pairs={{0,4},{2,6},{4,0},{6,2},{8,12},{10,14},{12,8},{14,10},{16,20},{18,... | collective-permute-start | bytes 147464 | tf_op jit(solution)/shard_map/ppermute | solution.py:825
  214.1 8.5 %collective-permute-start.28 = (f32[96,128]{1,0:T(8,128)S(1)}, f32[96,128]{1,0:T(8,128)S(1)}, u32[]{:S(2)}, u32[]{:S(2)}) collective-permute-start(f32[96,128]{1,0:T(8,128)S(1)} %add.86), channel_id=1, source_target_pairs={{0,8},{2,10},{4,12},{6,14},{8,0},{10,2},{12,4},{14,6},{16,24},{18,... | collective-permute-start | bytes 147464 | tf_op jit(solution)/shard_map/ppermute | solution.py:825
  222.6 6.1 %collective-permute-start.29 = (f32[96,128]{1,0:T(8,128)S(1)}, f32[96,128]{1,0:T(8,128)S(1)}, u32[]{:S(2)}, u32[]{:S(2)}) collective-permute-start(f32[96,128]{1,0:T(8,128)S(1)} %add.87), channel_id=1, source_target_pairs={{0,16},{2,18},{4,20},{6,22},{8,24},{10,26},{12,28},{14,30},{16,0},... | collective-permute-start | bytes 147464 | tf_op jit(solution)/shard_map/ppermute | solution.py:825
  226.1 29.3 %collective-permute-start.35 = (bf16[2,4,2,64,512]{4,3,2,1,0:T(8,128)(2,1)}, bf16[2,4,2,64,512]{4,3,2,1,0:T(8,128)(2,1)S(1)}, u32[]{:S(2)}, u32[]{:S(2)}) collective-permute-start(bf16[2,4,2,64,512]{4,3,2,1,0:T(8,128)(2,1)} %get-tuple-element.104), channel_id=1, source_target_pairs={{0,8},{2,10},{4,12},{6,14},{8,0},{10,2},{12,4},{14,6},{16,24},{18,... | collective-permute-start | bytes 3145736 | tf_op jit(solution)/shard_map/ppermute | solution.py:696
  226.4 31.3 %collective-permute-start.20 = (bf16[1,2,256,1024]{3,2,1,0:T(8,128)(2,1)}, bf16[1,2,256,1024]{3,2,1,0:T(8,128)(2,1)S(1)}, u32[]{:S(2)}, u32[]{:S(2)}) collective-permute-start(bf16[1,2,256,1024]{3,2,1,0:T(8,128)(2,1)} %get-tuple-element.91), channel_id=1, source_target_pairs={{0,1},{1,0},{2,3},{3,2},{4,5},{5,4},{6,7},{7,6},{8,9},{9,8},{10,11... | collective-permute-start | bytes 3145736 | tf_op jit(solution)/shard_map/ppermute | solution.py:46
  226.4 32.4 %collective-permute-start.23 = (bf16[1,2,256,1024]{3,2,1,0:T(8,128)(2,1)S(1)}, bf16[1,2,256,1024]{3,2,1,0:T(8,128)(2,1)S(1)}, u32[]{:S(2)}, u32[]{:S(2)}) collective-permute-start(bf16[1,2,256,1024]{3,2,1,0:T(8,128)(2,1)S(1)} %copy-done.18), channel_id=1, source_target_pairs={{0,1},{1,0},{2,3},{3,2},{4,5},{5,4},{6,7},{7,6},{8,9},{9,8},{10,11... | collective-permute-start | bytes 3145736 | tf_op jit(solution)/shard_map/ppermute | solution.py:46
  228.7 33.3 %collective-permute-start.19 = (bf16[2,2,256,1024]{3,2,1,0:T(8,128)(2,1)}, bf16[2,2,256,1024]{3,2,1,0:T(8,128)(2,1)S(1)}, u32[]{:S(2)}, u32[]{:S(2)}) collective-permute-start(bf16[2,2,256,1024]{3,2,1,0:T(8,128)(2,1)} %get-tuple-element.89), channel_id=1, source_target_pairs={{0,1},{1,0},{2,3},{3,2},{4,5},{5,4},{6,7},{7,6},{8,9},{9,8},{10,11... | collective-permute-start | bytes 6291464 | tf_op jit(solution)/shard_map/ppermute | solution.py:46
  229.4 26.1 %copy-start.3 = (f32[2,4,2,64,512]{4,3,2,1,0:T(8,128)S(1)}, f32[2,4,2,64,512]{4,3,2,1,0:T(8,128)}, u32[]{:S(2)}) copy-start(f32[2,4,2,64,512]{4,3,2,1,0:T(8,128)} %get-tuple-element.105) | copy-start | bytes 6291460
  229.6 25.8 %collective-permute-start.31 = (bf16[1,4,64,512]{3,2,1,0:T(8,128)(2,1)S(1)}, bf16[1,4,64,512]{3,2,1,0:T(8,128)(2,1)S(1)}, u32[]{:S(2)}, u32[]{:S(2)}) collective-permute-start(bf16[1,4,64,512]{3,2,1,0:T(8,128)(2,1)S(1)} %slice.177), channel_id=1, source_target_pairs={{0,16},{2,18},{4,20},{6,22},{8,24},{10,26},{12,28},{14,30},{16,0},... | collective-permute-start | bytes 786440 | tf_op jit(solution)/shard_map/ppermute | solution.py:696
  233.1 99.6 %copy-start.16 = (f32[1024]{0:T(1024)}, f32[1024]{0:T(1024)S(1)}, u32[]{:S(2)}) copy-start(f32[1024]{0:T(1024)S(1)} %get-tuple-element.159) | copy-start | bytes 12292
  255.5 2.2 copy-start.7
  255.9 2.9 copy-start.6
  256.0 22.9 %collective-permute-start.36 = (bf16[1,4,2,64,512]{4,3,2,1,0:T(8,128)(2,1)S(1)}, bf16[1,4,2,64,512]{4,3,2,1,0:T(8,128)(2,1)S(1)}, u32[]{:S(2)}, u32[]{:S(2)}) collective-permute-start(bf16[1,4,2,64,512]{4,3,2,1,0:T(8,128)(2,1)S(1)} %slice.176), channel_id=1, source_target_pairs={{0,16},{2,18},{4,20},{6,22},{8,24},{10,26},{12,28},{14,30},{16,0},... | collective-permute-start | bytes 1572872 | tf_op jit(solution)/shard_map/ppermute | solution.py:696
  258.1 3.9 %copy-start.1 = (bf16[2,2,256,1024]{3,2,1,0:T(8,128)(2,1)S(1)}, bf16[2,2,256,1024]{3,2,1,0:T(8,128)(2,1)}, u32[]{:S(2)}) copy-start(bf16[2,2,256,1024]{3,2,1,0:T(8,128)(2,1)} %get-tuple-element.88) | copy-start | bytes 6291460
  258.1 68.8 %collective-permute-start.21 = (bf16[2,256,1024]{2,1,0:T(8,128)(2,1)S(1)}, bf16[2,256,1024]{2,1,0:T(8,128)(2,1)S(1)}, u32[]{:S(2)}, u32[]{:S(2)}) collective-permute-start(bf16[2,256,1024]{2,1,0:T(8,128)(2,1)S(1)} %fusion.1), channel_id=1, source_target_pairs={{0,2},{2,0},{4,6},{6,4},{8,10},{10,8},{12,14},{14,12},{16,18},{18,... | collective-permute-start | bytes 3145736 | tf_op jit(solution)/shard_map/ppermute | solution.py:693
  260.2 66.7 %collective-permute-start.24 = (bf16[2,256,1024]{2,1,0:T(8,128)(2,1)}, bf16[2,256,1024]{2,1,0:T(8,128)(2,1)}, u32[]{:S(2)}, u32[]{:S(2)}) collective-permute-start(bf16[2,256,1024]{2,1,0:T(8,128)(2,1)} %fusion.3), channel_id=1, source_target_pairs={{0,6},{2,4},{4,2},{6,0},{8,14},{10,12},{12,10},{14,8},{16,22},{18,... | collective-permute-start | bytes 3145736 | tf_op jit(solution)/shard_map/ppermute | solution.py:693
  264.3 62.6 %collective-permute-start.22 = (bf16[2,256,1024]{2,1,0:T(8,128)(2,1)}, bf16[2,256,1024]{2,1,0:T(8,128)(2,1)}, u32[]{:S(2)}, u32[]{:S(2)}) collective-permute-start(bf16[2,256,1024]{2,1,0:T(8,128)(2,1)} %get-tuple-element.112), channel_id=1, source_target_pairs={{0,4},{2,6},{4,0},{6,2},{8,12},{10,14},{12,8},{14,10},{16,20},{18,... | collective-permute-start | bytes 3145736 | tf_op jit(solution)/shard_map/ppermute | solution.py:693
  265.5 40.5 %collective-permute-start.34 = (bf16[64,512]{1,0:T(8,128)(2,1)S(1)}, bf16[64,512]{1,0:T(8,128)(2,1)S(1)}, u32[]{:S(2)}, u32[]{:S(2)}) collective-permute-start(bf16[64,512]{1,0:T(8,128)(2,1)S(1)} %get-tuple-element.117), channel_id=1, source_target_pairs={{0,6},{2,4},{4,2},{6,0},{8,14},{10,12},{12,10},{14,8},{16,22},{18,... | collective-permute-start | bytes 196616 | tf_op jit(solution)/shard_map/ppermute | solution.py:693
  278.9 33.8 %collective-permute-start.33 = (bf16[64,512]{1,0:T(8,128)(2,1)S(1)}, bf16[64,512]{1,0:T(8,128)(2,1)S(1)}, u32[]{:S(2)}, u32[]{:S(2)}) collective-permute-start(bf16[64,512]{1,0:T(8,128)(2,1)S(1)} %get-tuple-element.118), channel_id=1, source_target_pairs={{0,4},{2,6},{4,0},{6,2},{8,12},{10,14},{12,8},{14,10},{16,20},{18,... | collective-permute-start | bytes 196616 | tf_op jit(solution)/shard_map/ppermute | solution.py:693
  305.9 8.9 %copy-start.14 = (bf16[64,512]{1,0:T(8,128)(2,1)}, bf16[64,512]{1,0:T(8,128)(2,1)S(1)}, u32[]{:S(2)}) copy-start(bf16[64,512]{1,0:T(8,128)(2,1)S(1)} %collective-permute-done.34.refs_2_) | copy-start | bytes 196612
  305.9 8.9 %collective-permute-start.32 = (bf16[64,512]{1,0:T(8,128)(2,1)S(1)}, bf16[64,512]{1,0:T(8,128)(2,1)}, u32[]{:S(2)}, u32[]{:S(2)}) collective-permute-start(bf16[64,512]{1,0:T(8,128)(2,1)S(1)} %get-tuple-element.119), channel_id=1, source_target_pairs={{0,2},{2,0},{4,6},{6,4},{8,10},{10,8},{12,14},{14,12},{16,18},{18,... | collective-permute-start | bytes 196616 | tf_op jit(solution)/shard_map/ppermute | solution.py:693
  312.7 2.1 copy-start.15
  312.7 7.0 %collective-permute-start.39 = (bf16[2,64,512]{2,1,0:T(8,128)(2,1)}, bf16[2,64,512]{2,1,0:T(8,128)(2,1)S(1)}, u32[]{:S(2)}, u32[]{:S(2)}) collective-permute-start(bf16[2,64,512]{2,1,0:T(8,128)(2,1)} %get-tuple-element.114), channel_id=1, source_target_pairs={{0,6},{2,4},{4,2},{6,0},{8,14},{10,12},{12,10},{14,8},{16,22},{18,... | collective-permute-start | bytes 393224 | tf_op jit(solution)/shard_map/ppermute | solution.py:693
  316.6 5.0 %collective-permute-start.38 = (bf16[2,64,512]{2,1,0:T(8,128)(2,1)S(1)}, bf16[2,64,512]{2,1,0:T(8,128)(2,1)S(1)}, u32[]{:S(2)}, u32[]{:S(2)}) collective-permute-start(bf16[2,64,512]{2,1,0:T(8,128)(2,1)S(1)} %get-tuple-element.115), channel_id=1, source_target_pairs={{0,4},{2,6},{4,0},{6,2},{8,12},{10,14},{12,8},{14,10},{16,20},{18,... | collective-permute-start | bytes 393224 | tf_op jit(solution)/shard_map/ppermute | solution.py:693
  319.7 5.1 %copy-start.12 = (bf16[2,64,512]{2,1,0:T(8,128)(2,1)}, bf16[2,64,512]{2,1,0:T(8,128)(2,1)S(1)}, u32[]{:S(2)}) copy-start(bf16[2,64,512]{2,1,0:T(8,128)(2,1)S(1)} %collective-permute-done.39.refs_2_) | copy-start | bytes 393220
  319.7 5.1 %collective-permute-start.37 = (bf16[2,64,512]{2,1,0:T(8,128)(2,1)S(1)}, bf16[2,64,512]{2,1,0:T(8,128)(2,1)}, u32[]{:S(2)}, u32[]{:S(2)}) collective-permute-start(bf16[2,64,512]{2,1,0:T(8,128)(2,1)S(1)} %get-tuple-element.116), channel_id=1, source_target_pairs={{0,2},{2,0},{4,6},{6,4},{8,10},{10,8},{12,14},{14,12},{16,18},{18,... | collective-permute-start | bytes 393224 | tf_op jit(solution)/shard_map/ppermute | solution.py:693
  321.6 0.7 copy-start.13
  326.9 1.0 copy-start.8

commit v2 on v1

--- a/solution.py
+++ b/solution.py
@@ -16,7 +16,7 @@
 QUERY_BLOCK = 256
 ROW_CHUNK = 32
 ATTEND_GROUPS = ((0,), (1, 2), (3,))
-MLP_GROUPS = ((3,), (1,), (2, 0))
+MLP_GROUPS = ((3,), (1, 2), (0,))
 F32 = jnp.float32
 BF16 = jnp.bfloat16
 
@@ -103,6 +103,84 @@
     )(*parts)
 
 
+def sum_layers_body(keep, *refs):
+    received, outs = refs[:-QUAD], refs[-QUAD:]
+    for j in range(QUAD):
+        total = keep[j]
+        for part in received:
+            total = total + part[j].astype(F32)
+        outs[j][...] = total.astype(outs[j].dtype)
+
+
+def sum_layers(keep, received):
+    shape = keep.shape[1:]
+    return pl.pallas_call(
+        sum_layers_body,
+        in_specs=[VMEM] * (1 + len(received)),
+        out_specs=[VMEM] * QUAD,
+        out_shape=[jax.ShapeDtypeStruct(shape, BF16 if j else F32) for j in range(QUAD)],
+        name="sum_layers",
+    )(keep, *received)
+
+
+def add_body(place, mine, other, out, mine_s, other_s, out_s, sems):
+    def copies(which):
+        pairs = ((mine, mine_s), (other, other_s))
+        return [
+            pltpu.make_async_copy(source.at[place, which], target.at[which], sems.at[which, n])
+            for n, (source, target) in enumerate(pairs)
+        ]
+
+    saves = [
+        pltpu.make_async_copy(out_s.at[which], out.at[which], sems.at[which, 2]) for which in (0, 1)
+    ]
+    for which in (0, 1):
+        for copy in copies(which):
+            copy.start()
+    for which in (0, 1):
+        for copy in copies(which):
+            copy.wait()
+        out_s[which] = (mine_s[which].astype(F32) + other_s[which].astype(F32)).astype(BF16)
+        saves[which].start()
+    for save in saves:
+        save.wait()
+
+
+def add_halves(mine, other, place):
+    shape = mine.shape[1:]
+    return pl.pallas_call(
+        lambda *refs: add_body(place, *refs),
+        in_specs=[HBM] * 2,
+        out_specs=HBM,
+        out_shape=jax.ShapeDtypeStruct(shape, BF16),
+        scratch_shapes=[pltpu.VMEM(shape, BF16)] * 3 + [pltpu.SemaphoreType.DMA((2, 3))],
+        name="add_halves",
+    )(mine, other)
+
+
+def split_body(*refs):
+    count = len(refs) - 8
+    totals = [ref[...] for ref in refs[:count]]
+    while len(totals) > 1:
+        totals = [first + second for first, second in zip(totals[::2], totals[1::2])]
+    at = 0
+    for number, out in enumerate(refs[count:]):
+        at -= out.shape[0] if number == 5 else 0
+        out[...] = totals[0][at : at + out.shape[0]]
+        at += out.shape[0]
+
+
+def split_vector(vectors, sizes):
+    pieces = pl.pallas_call(
+        split_body,
+        in_specs=[VMEM] * len(vectors),
+        out_specs=[VMEM] * len(sizes),
+        out_shape=[jax.ShapeDtypeStruct((size // 128, 128), F32) for size in sizes],
+        name="split_vector",
+    )(*vectors)
+    return [piece.reshape(-1) for piece in pieces]
+
+
 def unpack_attend_body(meta, own, *refs):
     received, (attend, project) = refs[:3], refs[3:]
     quarter = meta[1]
@@ -217,6 +295,10 @@
             "d": pltpu.VMEM((2, 2 * HD, length), BF16),
             "kv": pltpu.VMEM((2, length, 2 * HD), BF16),
             "kvt": pltpu.VMEM((2, 2 * HD, length), BF16),
+            "score": pltpu.VMEM((2, length, QUERY_BLOCK), F32),
+            "gprob": pltpu.VMEM((2, length, QUERY_BLOCK), F32),
+            "weight": pltpu.VMEM((2, length, QUERY_BLOCK), BF16),
+            "gprod": pltpu.VMEM((2, length, QUERY_BLOCK), BF16),
             "dq": pltpu.VMEM((2, HD, length), F32),
             "dk": pltpu.VMEM((2, HD, length), F32),
             "dv": pltpu.VMEM((2, HD, length), F32),
@@ -266,31 +348,57 @@
             m["kvt"][h] = both
             m["kv"][h] = both.T
 
-        for block in reversed(range(length // QUERY_BLOCK)):
+        items = [
+            (block, h) for block in reversed(range(length // QUERY_BLOCK)) for h in range(2)
+        ]
+
+        def place(item):
+            block = items[item][0]
             width = (block + 1) * QUERY_BLOCK
-            lanes = slice(block * QUERY_BLOCK, width)
-            for h in range(2):
-                key_value = m["kv"][h, :width, :]
-                scores = dot_nn(key_value, m["q"][h, :, lanes]) + m["mask"][block, :width, :]
-                highest = jnp.max(scores, axis=0, keepdims=True)
-                numerators = jnp.exp(scores - highest)
-                weights = numerators * (1.0 / jnp.sum(numerators, axis=0, keepdims=True))
-                weights_low = weights.astype(BF16)
-                context = dot_nn(m["kvt"][h, HD:, :width], weights_low)
-                m["ctxt"][h * HD : (h + 1) * HD, lanes] = context.astype(BF16)
-                grad_probs = dot_nn(key_value, m["d"][h, :, lanes])
-                centre = jnp.sum(grad_probs * weights, axis=0, keepdims=True)
-                grad_products = (weights * (grad_probs - centre)).astype(BF16)
-                grad_query = dot_nn(m["kvt"][h, :HD, :width], grad_products)
-                m["dq"][h, :, lanes] = grad_query * scale
-                grad_key = dot_nt(m["q"][h, :HD, lanes], grad_products)
-                grad_value = dot_nt(m["d"][h, HD:, lanes], weights_low)
-                if width == length:
-                    m["dk"][h] = grad_key
-                    m["dv"][h] = grad_value
-                else:
-                    m["dk"][h, :, :width] += grad_key
-                    m["dv"][h, :, :width] += grad_value
+            return *items[item], width, slice(block * QUERY_BLOCK, width)
+
+        def products(item):
+            _, h, width, lanes = place(item)
+            key_value = m["kv"][h, :width, :]
+            m["score"][item % 2, :width, :] = dot_nn(key_value, m["q"][h, :, lanes])
+            m["gprob"][item % 2, :width, :] = dot_nn(key_value, m["d"][h, :, lanes])
+
+        def softmax(item):
+            block, _, width, _ = place(item)
+            scores = m["score"][item % 2, :width, :] + m["mask"][block, :width, :]
+            highest = jnp.max(scores, axis=0, keepdims=True)
+            numerators = jnp.exp(scores - highest)
+            weights = numerators * (1.0 / jnp.sum(numerators, axis=0, keepdims=True))
+            grad_probs = m["gprob"][item % 2, :width, :]
+            centre = jnp.sum(grad_probs * weights, axis=0, keepdims=True)
+            m["weight"][item % 2, :width, :] = weights.astype(BF16)
+            m["gprod"][item % 2, :width, :] = (weights * (grad_probs - centre)).astype(BF16)
+
+        def results(item):
+            _, h, width, lanes = place(item)
+            weights_low = m["weight"][item % 2, :width, :]
+            grad_products = m["gprod"][item % 2, :width, :]
+            context = dot_nn(m["kvt"][h, HD:, :width], weights_low)
+            m["ctxt"][h * HD : (h + 1) * HD, lanes] = context.astype(BF16)
+            grad_query = dot_nn(m["kvt"][h, :HD, :width], grad_products)
+            m["dq"][h, :, lanes] = grad_query * scale
+            grad_key = dot_nt(m["q"][h, :HD, lanes], grad_products)
+            grad_value = dot_nt(m["d"][h, HD:, lanes], weights_low)
+            if width == length:
+                m["dk"][h] = grad_key
+                m["dv"][h] = grad_value
+            else:
+                m["dk"][h, :, :width] += grad_key
+                m["dv"][h, :, :width] += grad_value
+
+        products(0)
+        for item in range(len(items)):
+            if item + 1 < len(items):
+                products(item + 1)
+            if item:
+                results(item - 1)
+            softmax(item)
+        results(len(items) - 1)
 
         for h in range(2):
             parts = [
@@ -379,7 +487,7 @@
     carried = [] if is_first else take(3)
     out_hbm, grad_hbm, sums, bias_sums = take(4)
     if is_last:
-        grad_send, grad_keep = take(2)
+        grads = take(count)
     else:
         (total_hbm,) = take(1)
         if kind.turns:
@@ -409,14 +517,17 @@
                     weight_copies.append(
                         pltpu.make_async_copy(source, target, weight_sem.at[number, k, j])
                     )
-    for i in range(n_seq):
-        for target, first, which in ((x_s, 0, 0), (d_s, half, 1)):
-            for number, place in enumerate((mine, other)):
-                pltpu.make_async_copy(
-                    messages[i][number].at[pl.ds(first, half)],
-                    target.at[i, pl.ds(place, half)],
-                    token_sem.at[i, which, number],
-                ).start()
+
+    def start_message(i, target, first, which):
+        for number, place in enumerate((mine, other)):
+            pltpu.make_async_copy(
+                messages[i][number].at[pl.ds(first, half)],
+                target.at[i, pl.ds(place, half)],
+                token_sem.at[i, which, number],
+            ).start()
+
+    def start_rest(i):
+        start_message(i, d_s, half, 1)
         if kind.turns:
             pltpu.make_async_copy(
                 messages[i][0].at[pl.ds(2 * half, TABLE_ROWS)], tab_s.at[i], table_sem.at[i]
@@ -424,18 +535,21 @@
         if i == 0:
             for copy in weight_copies:
                 copy.start()
+
+    def start_partials(i):
         if places:
             for number, stage in enumerate((out_st, grad_st)):
                 pltpu.make_async_copy(
                     partials[i][number].at[places[i]], stage.at[i], part_sem.at[i, number]
                 ).start()
+
+    start_message(0, x_s, 0, 0)
     if is_first:
         total[...] = jnp.zeros_like(total)
         sums[...] = jnp.zeros_like(sums)
         bias_sums[...] = jnp.zeros_like(bias_sums)
     else:
         load = pltpu.make_async_copy(carried[0], total, total_sem.at[0])
-        load.start()
         sums[...] = carried[1][...]
         bias_sums[...] = carried[2][...]
     saves = []
@@ -458,6 +572,11 @@
     def one_sequence(i, carry):
         for number in range(2):
             wait_bytes(x_s.at[i, pl.ds(0, half)], token_sem.at[i, 0, number])
+
+        @pl.when(i == 0)
+        def _():
+            start_rest(0)
+
         normalize(x_s.at[i], gain, shift, norm_s, hat_s)
         if kind.turns:
             wait_bytes(tab_s.at[i], table_sem.at[i])
@@ -468,6 +587,13 @@
         def _():
             for copy in weight_copies:
                 copy.wait()
+            if not is_first:
+                load.start()
+            for later in range(1, n_seq):
+                start_message(later, x_s, 0, 0)
+                start_rest(later)
+            for later in range(n_seq):
+                start_partials(later)
             if kind.turns and is_first:
                 for cols in column_chunks(features):
                     wt_s[:, cols] = w_s[0, cols, :].T
@@ -525,11 +651,8 @@
                 for j in range(QUAD):
                     place = (meta[2] ^ k) * (QUAD * rows) + (meta[1] ^ j) * rows
                     piece = turned[pl.ds(pl.multiple_of(place, rows), rows), :]
-                    at = (k // 2, j) if pick is None else (k // 2, j, pick)
-                    if k % 2:
-                        grad_send[at] = piece.astype(BF16)
-                    else:
-                        grad_keep[at] = piece
+                    at = (j,) if pick is None else (j, pick)
+                    grads[k][at] = piece.astype(grads[k].dtype)
     for copy in saves:
         copy.wait()
     if kind.turns and is_first and not is_last:
@@ -571,9 +694,9 @@
     ]
     out_specs = [HBM, HBM, VMEM, VMEM]
     if is_last:
-        piece = (count // 2,) + blocks[0].shape
-        shapes += [jax.ShapeDtypeStruct(piece, BF16), jax.ShapeDtypeStruct(piece, F32)]
-        out_specs += [VMEM] * 2
+        shape = blocks[0].shape
+        shapes += [jax.ShapeDtypeStruct(shape, BF16 if k else F32) for k in range(count)]
+        out_specs += [VMEM] * count
     else:
         shapes += [jax.ShapeDtypeStruct((n_pick, width, features), F32)]
         out_specs += [HBM]
@@ -631,11 +754,14 @@
     return results[:2], sums, (results[4], *sums, *turned)
 
 
-def finish_body(x, d, own, p1, p2, p3, first_bias, second_bias, out, grad):
+def finish_body(x, d, mine, other, p1, p2, p3, first_bias, second_bias, out, grad):
+    def total(which):
+        own = mine[0, which].astype(F32) + other[0, which].astype(F32)
+        return own + p1[which].astype(F32) + (p2[which].astype(F32) + p3[which].astype(F32))
+
     tokens = x[...].astype(F32)
-    branches = own[0].astype(F32) + p1[0].astype(F32) + p2[0].astype(F32) + p3[0].astype(F32)
-    out[...] = (tokens + branches + first_bias[...] + second_bias[...]).astype(BF16)
-    back = own[1].astype(F32) + p1[1].astype(F32) + p2[1].astype(F32) + p3[1].astype(F32)
+    out[...] = (tokens + total(0) + first_bias[...] + second_bias[...]).astype(BF16)
+    back = total(1)
     average = jnp.mean(tokens, axis=-1, keepdims=True)
     centred = tokens - average
     inverse = lax.rsqrt(jnp.mean(centred * centred, axis=-1, keepdims=True) + EPSILON)
@@ -647,18 +773,20 @@
 
 def finish(x, d, own, parts, first_bias, second_bias):
     rows, features = x.shape
-    block = min(rows, 64)
+    block = min(rows, 128)
+    mine, other, place = own
     flat = pl.BlockSpec((block, features), lambda i: (i, 0))
+    half = pl.BlockSpec((1, 2, block, features), lambda i: (place, 0, i, 0))
     pair = pl.BlockSpec((2, block, features), lambda i: (0, i, 0))
     row = pl.BlockSpec((1, features), lambda i: (0, 0))
     return pl.pallas_call(
         finish_body,
         grid=(rows // block,),
-        in_specs=[flat, flat, pair, pair, pair, pair, row, row],
+        in_specs=[flat, flat, half, half, pair, pair, pair, row, row],
         out_specs=[flat, flat],
         out_shape=[jax.ShapeDtypeStruct((rows, features), BF16)] * 2,
         name="finish",
-    )(x, d, own, *parts, first_bias, second_bias)
+    )(x, d, mine, other, *parts, first_bias, second_bias)
 
 
 def on_device(
@@ -704,6 +832,9 @@
             bit //= 2
         return [blocks[k] for k in range(count)]
 
+    def gather_direct(block):
+        return [block] + [to_layer(block, k) for k in range(1, count)]
+
     halfway = ROT // 2
     frequency = 1.0 / 10000.0 ** (jnp.arange(halfway, dtype=F32) * (2.0 / ROT))
     angles = frequency[:, None] * positions.astype(F32)[None, :]
@@ -720,7 +851,7 @@
     )
     second_parts = [second_pack[0]]
     second_parts += [to_quad(second_pack[j], j) for j in range(1, QUAD)]
-    second_blocks = gather_layers(jnp.stack(second_parts))
+    second_blocks = gather_direct(jnp.stack(second_parts))
     first_parts = [first_pack[0]] + [to_quad(first_pack[j], j) for j in range(1, QUAD)]
     first_blocks = gather_layers(jnp.stack(first_parts))
 
@@ -753,7 +884,7 @@
         (out_part, grad_part), attend_sums, carried = results
         for place, s in enumerate(group):
             partials[s] = (out_part, grad_part, place)
-    attend_send, attend_keep = carried
+    attend_grads = carried
 
     carried, sums_of = None, {}
     for group in MLP_GROUPS:
@@ -772,30 +903,26 @@
         (mine, other), mlp_sums, carried = results
         other = swap_cores(other)
         for place, s in enumerate(group):
-            both = mine[place].astype(F32) + other[place].astype(F32)
-            sums_of[s] = both.astype(BF16)
-    mlp_send, mlp_keep = carried
+            if s == 0:
+                own_halves = mine, other, place
+                continue
+            sums_of[s] = add_halves(mine, other, place)
+    mlp_grads = carried
 
     parts = [to_quad(sums_of[j], j) for j in range(1, QUAD)]
     outputs, grad_inputs = finish(
-        inputs, output_grad, sums_of[0], parts, one_row(project_bias), one_row(shrink_bias)
-    )
-
-    def reduce_layers(send, keep):
-        bit = 1
-        while True:
-            total = to_layer(send, bit).astype(F32) + keep
-            if total.shape[0] == 1:
-                break
-            send, keep = total[1::2].astype(BF16), total[0::2]
-            bit *= 2
-        parts = [to_quad(total[0, j].astype(BF16), j) for j in range(1, QUAD)]
-        return total[0, 0], parts
-
-    own, received = reduce_layers(mlp_send, mlp_keep)
+        inputs, output_grad, own_halves, parts, one_row(project_bias), one_row(shrink_bias)
+    )
+
+    def reduce_layers(grads):
+        received = [to_layer(grads[k], k) for k in range(1, count)]
+        parts = sum_layers(grads[0], received)
+        return parts[0], [to_quad(parts[j], j) for j in range(1, QUAD)]
+
+    own, received = reduce_layers(attend_grads)
+    grad_attend, grad_project = unpack_attend(meta, own, received, attend_cols, project_cols)
+    own, received = reduce_layers(mlp_grads)
     grad_expand, grad_shrink = unpack_mlp(meta, own, received, hidden_cols)
-    own, received = reduce_layers(attend_send, attend_keep)
-    grad_attend, grad_project = unpack_attend(meta, own, received, attend_cols, project_cols)
 
     place = core * QUAD + quarter
     attend_full = lax.dynamic_update_slice_in_dim(
@@ -820,30 +947,23 @@
         ]
     ).reshape(-1, 128)
     vector = vector + swap_cores(vector)
-    bit = 1
-    while bit < n_dp:
+    for bit in (1, 2):
         vector = vector + lax.ppermute(vector, "dp", xor_pairs(n_dp, bit))
-        bit *= 2
-    vector = vector.reshape(-1)
-    pieces, at = [], 0
-    for size in [features] * 5 + [2 * attend_cols, 2 * hidden_cols]:
-        pieces.append(vector[at : at + size])
-        at += size
+    vectors = [vector] + [to_layer(vector, k) for k in range(1, count)]
+    sizes = [features] * 4 + [features] * 2 + [2 * attend_cols, 2 * hidden_cols]
+    pieces = split_vector(vectors, sizes)
     return (
         outputs,
         grad_inputs,
-        pieces[0],
-        pieces[1],
-        pieces[2],
-        pieces[3],
+        *pieces[:4],
         grad_attend,
-        pieces[5],
+        pieces[6],
         grad_project.T,
         pieces[4],
         grad_expand,
-        pieces[6],
+        pieces[7],
         grad_shrink.T,
-        pieces[4],
+        pieces[5],
     )
 
 

time: 337 us -> 349 us (1.036)
  waiting for transfers between devices: 166 us -> 185 us
  Pallas kernels: 92.8 us -> 104 us
  local copies, waits for them, and re-layouts: 12.3 us -> 5.09 us
  other arithmetic: 13.7 us -> 7.82 us
  starting transfers between devices: 48 us -> 43 us
    ppermute x10 -> x15, waiting for transfers between devices: 65.4 us -> 94.1 us  [to_layer(): return lax.ppermute(value, 'dp', xor_pairs(n_dp, bits * QUAD))]
    pallas_call x0 -> x6, Pallas kernels: none -> 13.9 us  [the longest x3 7.84 us: add_halves(): pl.pallas_call(lambda *refs: add_body(place, *refs), in_specs=[HBM] * 2,...]
    ppermute x4 -> x2, waiting for transfers between devices: 12.1 us -> 3.55 us  [on_device(): vector = vector + lax.ppermute(vector, 'dp', xor_pairs(n_dp, bit))]
    ppermute x4 -> x2, starting transfers between devices: 8.4 us -> 2.17 us  [on_device(): vector = vector + lax.ppermute(vector, 'dp', xor_pairs(n_dp, bit))]
    convert_element_type x3 -> x0, other arithmetic: 4.16 us -> none  [on_device(): sums_of[s] = both.astype(BF16)]
    ppermute x10 -> x15, starting transfers between devices: 17.1 us -> 19.4 us  [to_layer(): return lax.ppermute(value, 'dp', xor_pairs(n_dp, bits * QUAD))]
  transfers between devices with their start and end apart: 40 -> 43, of which waited for: 20 -> 18; matrix products, arithmetic and copies ran while one was open for 5% -> 2% of each run, Pallas kernels for 14% -> 16%
where the time goes in v2:
time: 349 us; the launch traced here: 345 us
  waiting for transfers between devices  185 us (53%)
  Pallas kernels  104 us (30%)
  starting transfers between devices  43 us (12%)
  other arithmetic  7.82 us (2%)
  local copies, waits for them, and re-layouts  5.09 us (1%)
    ppermute x15, waiting for transfers between devices, to_layer(): return lax.ppermute(value, 'dp', xor_pairs(n_dp, bits * QUAD))  94.1 us
    ppermute x18, waiting for transfers between devices, to_quad(): return lax.ppermute(value, 'dp', xor_pairs(n_dp, j))  84.6 us
    pallas_call x6, Pallas kernels, branch(): results = call(*operands)  77.2 us
    ppermute x18, starting transfers between devices, to_quad(): return lax.ppermute(value, 'dp', xor_pairs(n_dp, j))  20.3 us
    ppermute x15, starting transfers between devices, to_layer(): return lax.ppermute(value, 'dp', xor_pairs(n_dp, bits * QUAD))  19.4 us
    pallas_call x3, Pallas kernels, add_halves(): pl.pallas_call(lambda *refs: add_body(place, *refs), in_specs=[HBM] * 2,...  7.84 us
  transfers between devices with their start and end apart: 43, of which 18 were waited for; matrix products, arithmetic and copies ran while one was open for 2% of the time, Pallas kernels for 16%

profile of v2, /device:TPU:10, one launch (start us, length us, event | category | flops | bytes accessed | tf_op | source)
XLA Modules:
  0.0 345.4 jit_solution(779518335250871466)
XLA Ops:
  0.7 1.0 convert_reduce_fusion.1
  3.8 2.3 join_message.1.refs_4_
  6.1 1.5 collective-permute-start.15
  8.2 1.4 collective-permute-start.17
  10.3 2.1 pack_weights.1
  12.9 1.5 collective-permute-start.2
  14.5 44.8 %collective-permute-done.1 = bf16[64,512]{1,0:T(8,128)(2,1)S(1)} collective-permute-done((bf16[64,512]{1,0:T(8,128)(2,1)}, bf16[64,512]{1,0:T(8,128)(2,1)S(1)}, u32[]{:S(2)}, u32[]{:S(2)}) %collective-permute-start.1) | collective-permute-done | bytes 65568 | tf_op jit(solution)/shard_map/ppermute | solution.py:821
  59.8 1.4 collective-permute-start.3
  61.2 3.9 %collective-permute-done.3 = bf16[64,512]{1,0:T(8,128)(2,1)S(1)} collective-permute-done((bf16[64,512]{1,0:T(8,128)(2,1)}, bf16[64,512]{1,0:T(8,128)(2,1)S(1)}, u32[]{:S(2)}, u32[]{:S(2)}) %collective-permute-start.3) | collective-permute-done | bytes 65568 | tf_op jit(solution)/shard_map/ppermute | solution.py:821
  65.1 1.4 collective-permute-start.8
  66.6 4.7 %collective-permute-done.8 = bf16[2,64,512]{2,1,0:T(8,128)(2,1)S(1)} collective-permute-done((bf16[2,64,512]{2,1,0:T(8,128)(2,1)}, bf16[2,64,512]{2,1,0:T(8,128)(2,1)S(1)}, u32[]{:S(2)}, u32[]{:S(2)}) %collective-permute-start.8) | collective-permute-done | bytes 131104 | tf_op jit(solution)/shard_map/ppermute | solution.py:821
  71.3 1.4 collective-permute-start.9
  73.2 0.9 pad_maximum_fusion.1.refs_6_
  74.1 3.3 collective-permute-done.9
  77.4 2.6 collective-permute-start.5
  80.0 10.0 %collective-permute-done.5.refs_8_ = bf16[4,64,512]{2,1,0:T(8,128)(2,1)S(1)} collective-permute-done((bf16[4,64,512]{2,1,0:T(8,128)(2,1)S(1)}, bf16[4,64,512]{2,1,0:T(8,128)(2,1)S(1)}, u32[]{:S(2)}, u32[]{:S(2)}) %collective-permute-start.5) | collective-permute-done | bytes 262176 | tf_op jit(solution)/shard_map/ppermute | solution.py:824
  90.0 1.4 collective-permute-start.4
  92.0 6.2 %collective-permute-done.4.refs_7_ = bf16[4,64,512]{2,1,0:T(8,128)(2,1)S(1)} collective-permute-done((bf16[4,64,512]{2,1,0:T(8,128)(2,1)S(1)}, bf16[4,64,512]{2,1,0:T(8,128)(2,1)S(1)}, u32[]{:S(2)}, u32[]{:S(2)}) %collective-permute-start.4) | collective-permute-done | bytes 262176 | tf_op jit(solution)/shard_map/ppermute | solution.py:824
  98.7 1.0 pad_maximum_fusion.refs_8_.refs_12_
  99.7 5.9 %collective-permute-done.6.refs_9_ = bf16[4,64,512]{2,1,0:T(8,128)(2,1)S(1)} collective-permute-done((bf16[4,64,512]{2,1,0:T(8,128)(2,1)S(1)}, bf16[4,64,512]{2,1,0:T(8,128)(2,1)S(1)}, u32[]{:S(2)}, u32[]{:S(2)}) %collective-permute-start.6) | collective-permute-done | bytes 262176 | tf_op jit(solution)/shard_map/ppermute | solution.py:824
  105.6 2.5 collective-permute-start.12
  108.1 1.6 collective-permute-start.11
  109.7 0.8 broadcast_in_dim.56.refs_3_
  110.5 10.0 %shard_map.263 = (bf16[1,512,1024]{2,1,0:T(8,128)(2,1)}, bf16[1,512,1024]{2,1,0:T(8,128)(2,1)}, f32[16,1024]{1,0:T(8,128)}, f32[384,128]{1,0:T(8,128)}, f32[1,51...) custom-call(s32[3]{0:T(128)} %pad_add_fusion.meta.refs_0_, f32[1,1024]{1,0:T(1,128)} %bitcast.62, f32[1,1024]{1,0:T(1,128)} %bitcast.65, ...), custom_call_target="tpu_custom_call" | custom-call | flops 2080374784 | bytes 9437184 | tf_op jit(solution)/shard_map/pallas_call | solution.py:749
  120.6 0.8 collective-permute-start.10
  121.4 15.9 %shard_map.264 = (bf16[2,512,1024]{2,1,0:T(8,128)(2,1)}, bf16[2,512,1024]{2,1,0:T(8,128)(2,1)}, f32[16,1024]{1,0:T(8,128)}, f32[384,128]{1,0:T(8,128)}, f32[1,512,1024]{2,1,0:T(8,128)}) custom-call(s32[3]{0:T(128)} %pad_add_fusion.meta.refs_0_, f32[1,1024]{1,0:T(1,128)} %bitcast.63, f32[1,1024]{1,0:T(1,128)} %bitcast.66, ...), custom_call_target="tpu_custom_call" | custom-call | flops 4160749568 | bytes 13631488 | tf_op jit(solution)/shard_map/pallas_call | solution.py:749
  137.3 10.5 %shard_map.265 = (bf16[1,512,1024]{2,1,0:T(8,128)(2,1)}, bf16[1,512,1024]{2,1,0:T(8,128)(2,1)}, f32[16,1024]{1,0:T(8,128)}, f32[384,128]{1,0:T(8,128)}, f32[4,64...) custom-call(s32[3]{0:T(128)} %pad_add_fusion.meta.refs_0_, ...), custom_call_target="tpu_custom_call" | custom-call | flops 2080374784 | bytes 9437184 | tf_op jit(solution)/shard_map/pallas_call | solution.py:749
  147.8 1.1 reduce_sum.58
  148.9 2.9 collective-permute-done.11.refs_10_.refs_14_
  151.8 0.8 copy-done.24
  152.6 10.3 %shard_map.266 = (bf16[1,2,256,1024]{3,2,1,0:T(8,128)(2,1)}, bf16[1,2,256,1024]{3,2,1,0:T(8,128)(2,1)}, f32[16,1024]{1,0:T(8,128)}, f32[8,512]{1,0:T(8,128)}, f32[2,512,1024]{2,1,0:T(8,128)}) custom-call(s32[3]{0:T(128)} %pad_add_fusion.meta.refs_0_, f32[1,1024]{1,0:T(1,128)} %bitcast.68, f32[1,1024]{1,0:T(1,128)} %bitcast.71, ...), custom_call_target="tpu_custom_call" | custom-call | flops 3221225472 | bytes 14680064 | tf_op jit(solution)/shard_map/pallas_call | solution.py:749
  162.8 18.0 %shard_map.267 = (bf16[2,2,256,1024]{3,2,1,0:T(8,128)(2,1)}, bf16[2,2,256,1024]{3,2,1,0:T(8,128)(2,1)}, f32[16,1024]{1,0:T(8,128)}, f32[8,512]{1,0:T(8,128)}, f32[2,512,1024]{2,1,0:T(8,128)}) custom-call(s32[3]{0:T(128)} %pad_add_fusion.meta.refs_0_, f32[1,1024]{1,0:T(1,128)} %bitcast.69, f32[1,1024]{1,0:T(1,128)} %bitcast.72, ...), custom_call_target="tpu_custom_call" | custom-call | flops 6442450944 | bytes 18874368 | tf_op jit(solution)/shard_map/pallas_call | solution.py:749
  180.9 12.6 %shard_map.268 = (bf16[1,2,256,1024]{3,2,1,0:T(8,128)(2,1)}, bf16[1,2,256,1024]{3,2,1,0:T(8,128)(2,1)}, f32[16,1024]{1,0:T(8,128)}, f32[8,512]{1,0:T(8,128)}, f3...) custom-call(s32[3]{0:T(128)} %pad_add_fusion.meta.refs_0_, ...), custom_call_target="tpu_custom_call" | custom-call | flops 3221225472 | bytes 14680064 | tf_op jit(solution)/shard_map/pallas_call | solution.py:749
  194.9 0.9 bitcast_reduce_fusion
  196.4 2.3 collective-permute-done.25
  198.7 1.6 collective-permute-start.26
  200.3 2.3 collective-permute-start.31
  202.6 1.2 collective-permute-start.32
  204.4 3.5 %collective-permute-done.27 = f32[96,128]{1,0:T(8,128)S(1)} collective-permute-done((f32[96,128]{1,0:T(8,128)S(1)}, f32[96,128]{1,0:T(8,128)S(1)}, u32[]{:S(2)}, u32[]{:S(2)}) %collective-permute-start.27) | collective-permute-done | bytes 49184 | tf_op jit(solution)/shard_map/ppermute | solution.py:951
  208.6 9.7 %collective-permute-done.30.refs_3_ = f32[96,128]{1,0:T(8,128)S(1)} collective-permute-done((f32[96,128]{1,0:T(8,128)S(1)}, f32[96,128]{1,0:T(8,128)S(1)}, u32[]{:S(2)}, u32[]{:S(2)}) %collective-permute-start.30) | collective-permute-done | bytes 49184 | tf_op jit(solution)/shard_map/ppermute | solution.py:824
  218.5 2.7 collective-permute-start.38
  221.8 33.0 %collective-permute-done.33.refs_2_ = bf16[4,64,512]{2,1,0:T(8,128)(2,1)} collective-permute-done((bf16[4,64,512]{2,1,0:T(8,128)(2,1)}, bf16[4,64,512]{2,1,0:T(8,128)(2,1)}, u32[]{:S(2)}, u32[]{:S(2)}) %collective-permute-start.33) | collective-permute-done | bytes 262176 | tf_op jit(solution)/shard_map/ppermute | solution.py:824
  254.8 2.0 sum_layers.2
  256.8 3.0 collective-permute-done.29.refs_2_
  260.4 1.4 collective-permute-start.35
  262.3 2.7 add_halves.5
  265.0 2.5 add_halves.4
  267.6 2.7 add_halves.3
  270.4 1.6 collective-permute-start.24
  272.5 1.4 collective-permute-start.22
  274.0 2.0 collective-permute-start.39
  276.0 23.3 %collective-permute-done.39.refs_2_ = bf16[4,2,64,512]{3,2,1,0:T(8,128)(2,1)} collective-permute-done((bf16[4,2,64,512]{3,2,1,0:T(8,128)(2,1)}, bf16[4,2,64,512]{3,2,1,0:T(8,128)(2,1)}, u32[]{:S(2)}, u32[]{:S(2)}) %collective-permute-start.39) | collective-permute-done | bytes 524320 | tf_op jit(solution)/shard_map/ppermute | solution.py:824
  299.3 1.6 collective-permute-start.36
  300.9 2.6 sum_layers.3
  303.4 17.4 %collective-permute-done.36.refs_2_ = bf16[64,512]{1,0:T(8,128)(2,1)S(1)} collective-permute-done((bf16[64,512]{1,0:T(8,128)(2,1)S(1)}, bf16[64,512]{1,0:T(8,128)(2,1)S(1)}, u32[]{:S(2)}, u32[]{:S(2)}) %collective-permute-start.36) | collective-permute-done | bytes 65568 | tf_op jit(solution)/shard_map/ppermute | solution.py:821
  321.5 4.6 %collective-permute-done.40.refs_0_ = bf16[2,64,512]{2,1,0:T(8,128)(2,1)S(1)} collective-permute-done((bf16[2,64,512]{2,1,0:T(8,128)(2,1)}, bf16[2,64,512]{2,1,0:T(8,128)(2,1)S(1)}, u32[]{:S(2)}, u32[]{:S(2)}) %collective-permute-start.40) | collective-permute-done | bytes 131104 | tf_op jit(solution)/shard_map/ppermute | solution.py:821
  326.7 4.6 %collective-permute-done.41.refs_1_ = bf16[2,64,512]{2,1,0:T(8,128)(2,1)S(1)} collective-permute-done((bf16[2,64,512]{2,1,0:T(8,128)(2,1)}, bf16[2,64,512]{2,1,0:T(8,128)(2,1)S(1)}, u32[]{:S(2)}, u32[]{:S(2)}) %collective-permute-start.41) | collective-permute-done | bytes 131104 | tf_op jit(solution)/shard_map/ppermute | solution.py:821
  331.3 1.5 collective-permute-start.42
  332.8 1.5 split_vector.1
  334.3 1.8 unpack_attend.1
  336.1 1.2 collective-permute-done.42.refs_2_
  338.0 2.2 unpack_mlp.1
  340.2 0.9 copy-done.5
  341.1 4.2 %finish.1 = (bf16[256,1024]{1,0:T(8,128)(2,1)}, bf16[256,1024]{1,0:T(8,128)(2,1)}) custom-call(bf16[256,1024]{1,0:T(8,128)(2,1)} %x.1, bf16[256,1024]{1,0:T(8,128)(2,1)} %d.1, bf16[1,2,256,1024]{3,2,1,0:T(8,128)(2,1)} %get-tuple-element.108.mine, bf16[1,2,256,1024]{3,2,1,0:T(8,128)(2,1)} %copy-done.5, bf16[2,256,1024]{2,1,0:T(8,128)(2,1)} %collective-permute-done.21.p1, ...), custom_call_target="tpu_custom_call" | custom-call | tf_op jit(solution)/shard_map/finish/pallas_call | solution.py:782
  (130 shorter events, 13.7 us)
Async XLA Ops:
  0.6 98.0 %copy-start.1 = (bf16[256,1024]{1,0:T(8,128)(2,1)S(1)}, bf16[256,1024]{1,0:T(8,128)(2,1)}, u32[]{:S(2)}) copy-start(bf16[256,1024]{1,0:T(8,128)(2,1)} %d.1) | copy-start | bytes 1572868
  0.7 90.7 %copy-start.20 = (f32[1536]{0:T(1024)S(1)}, f32[1536]{0:T(1024)}, u32[]{:S(2)}) copy-start(f32[1536]{0:T(1024)} %param.24) | copy-start | bytes 18436
  0.7 90.7 %copy-start.21 = (f32[2048]{0:T(1024)S(1)}, f32[2048]{0:T(1024)}, u32[]{:S(2)}) copy-start(f32[2048]{0:T(1024)} %param.28) | copy-start | bytes 24580
  6.1 66.6 %collective-permute-start.15 = (bf16[544,1024]{1,0:T(8,128)(2,1)}, bf16[544,1024]{1,0:T(8,128)(2,1)S(1)}, u32[]{:S(2)}, u32[]{:S(2)}) collective-permute-start(bf16[544,1024]{1,0:T(8,128)(2,1)} %join_message.1.refs_4_), channel_id=1, source_target_pairs={{0,4},{2,6},{4,0},{6,2},{8,12},{10,14},{12,8},{14,10},{16,20},{18,... | collective-permute-start | bytes 3342344 | tf_op jit(solution)/shard_map/ppermute | solution.py:821
  7.7 65.0 %collective-permute-start.13 = (bf16[544,1024]{1,0:T(8,128)(2,1)}, bf16[544,1024]{1,0:T(8,128)(2,1)}, u32[]{:S(2)}, u32[]{:S(2)}) collective-permute-start(bf16[544,1024]{1,0:T(8,128)(2,1)} %join_message.1.refs_4_), channel_id=1, source_target_pairs={{0,2},{2,0},{4,6},{6,4},{8,10},{10,8},{12,14},{14,12},{16,18},{18,... | collective-permute-start | bytes 3342344 | tf_op jit(solution)/shard_map/ppermute | solution.py:821
  8.2 71.8 %collective-permute-start.17 = (bf16[544,1024]{1,0:T(8,128)(2,1)}, bf16[544,1024]{1,0:T(8,128)(2,1)}, u32[]{:S(2)}, u32[]{:S(2)}) collective-permute-start(bf16[544,1024]{1,0:T(8,128)(2,1)} %join_message.1.refs_4_), channel_id=1, source_target_pairs={{0,6},{2,4},{4,2},{6,0},{8,14},{10,12},{12,10},{14,8},{16,22},{18,... | collective-permute-start | bytes 3342344 | tf_op jit(solution)/shard_map/ppermute | solution.py:821
  12.4 46.8 %collective-permute-start.1 = (bf16[64,512]{1,0:T(8,128)(2,1)}, bf16[64,512]{1,0:T(8,128)(2,1)S(1)}, u32[]{:S(2)}, u32[]{:S(2)}) collective-permute-start(bf16[64,512]{1,0:T(8,128)(2,1)} %get-tuple-element.82), channel_id=1, source_target_pairs={{0,2},{2,0},{4,6},{6,4},{8,10},{10,8},{12,14},{14,12},{16,18},{18,... | collective-permute-start | bytes 196616 | tf_op jit(solution)/shard_map/ppermute | solution.py:821
  12.9 46.8 %collective-permute-start.2 = (bf16[64,512]{1,0:T(8,128)(2,1)}, bf16[64,512]{1,0:T(8,128)(2,1)S(1)}, u32[]{:S(2)}, u32[]{:S(2)}) collective-permute-start(bf16[64,512]{1,0:T(8,128)(2,1)} %get-tuple-element.83), channel_id=1, source_target_pairs={{0,4},{2,6},{4,0},{6,2},{8,12},{10,14},{12,8},{14,10},{16,20},{18,... | collective-permute-start | bytes 196616 | tf_op jit(solution)/shard_map/ppermute | solution.py:821
  59.2 5.9 %collective-permute-start.7 = (bf16[2,64,512]{2,1,0:T(8,128)(2,1)}, bf16[2,64,512]{2,1,0:T(8,128)(2,1)S(1)}, u32[]{:S(2)}, u32[]{:S(2)}) collective-permute-start(bf16[2,64,512]{2,1,0:T(8,128)(2,1)} %get-tuple-element.88), channel_id=1, source_target_pairs={{0,2},{2,0},{4,6},{6,4},{8,10},{10,8},{12,14},{14,12},{16,18},{18,... | collective-permute-start | bytes 393224 | tf_op jit(solution)/shard_map/ppermute | solution.py:821
  59.8 5.4 %collective-permute-start.3 = (bf16[64,512]{1,0:T(8,128)(2,1)}, bf16[64,512]{1,0:T(8,128)(2,1)S(1)}, u32[]{:S(2)}, u32[]{:S(2)}) collective-permute-start(bf16[64,512]{1,0:T(8,128)(2,1)} %get-tuple-element.84), channel_id=1, source_target_pairs={{0,6},{2,4},{4,2},{6,0},{8,14},{10,12},{12,10},{14,8},{16,22},{18,... | collective-permute-start | bytes 196616 | tf_op jit(solution)/shard_map/ppermute | solution.py:821
  65.1 43.0 %collective-permute-start = (bf16[544,1024]{1,0:T(8,128)(2,1)}, bf16[544,1024]{1,0:T(8,128)(2,1)}, u32[]{:S(2)}, u32[]{:S(2)}) collective-permute-start(bf16[544,1024]{1,0:T(8,128)(2,1)} %join_message.1.refs_4_), channel_id=1, source_target_pairs={{0,1},{1,0},{2,3},{3,2},{4,5},{5,4},{6,7},{7,6},{8,9},{9,8},{10,11... | collective-permute-start | bytes 3342344 | tf_op jit(solution)/shard_map/ppermute | solution.py:46
  65.1 6.1 %collective-permute-start.8 = (bf16[2,64,512]{2,1,0:T(8,128)(2,1)}, bf16[2,64,512]{2,1,0:T(8,128)(2,1)S(1)}, u32[]{:S(2)}, u32[]{:S(2)}) collective-permute-start(bf16[2,64,512]{2,1,0:T(8,128)(2,1)} %get-tuple-element.89), channel_id=1, source_target_pairs={{0,4},{2,6},{4,0},{6,2},{8,12},{10,14},{12,8},{14,10},{16,20},{18,... | collective-permute-start | bytes 393224 | tf_op jit(solution)/shard_map/ppermute | solution.py:821
  71.3 6.2 %collective-permute-start.9 = (bf16[2,64,512]{2,1,0:T(8,128)(2,1)}, bf16[2,64,512]{2,1,0:T(8,128)(2,1)S(1)}, u32[]{:S(2)}, u32[]{:S(2)}) collective-permute-start(bf16[2,64,512]{2,1,0:T(8,128)(2,1)} %get-tuple-element.90), channel_id=1, source_target_pairs={{0,6},{2,4},{4,2},{6,0},{8,14},{10,12},{12,10},{14,8},{16,22},{18,... | collective-permute-start | bytes 393224 | tf_op jit(solution)/shard_map/ppermute | solution.py:821
  72.7 47.8 %copy-start.22 = (bf16[544,1024]{1,0:T(8,128)(2,1)}, bf16[544,1024]{1,0:T(8,128)(2,1)S(1)}, u32[]{:S(2)}) copy-start(bf16[544,1024]{1,0:T(8,128)(2,1)S(1)} %collective-permute-done.15.refs_6_) | copy-start | bytes 3342340
  72.7 47.8 %collective-permute-start.16 = (bf16[544,1024]{1,0:T(8,128)(2,1)S(1)}, bf16[544,1024]{1,0:T(8,128)(2,1)}, u32[]{:S(2)}, u32[]{:S(2)}) collective-permute-start(bf16[544,1024]{1,0:T(8,128)(2,1)S(1)} %collective-permute-done.15.refs_6_), channel_id=1, source_target_pairs={{0,1},{1,0},{2,3},{3,2},{4,5},{5,4},{6,7},{7,6},{8,9},{9,8},{10,11... | collective-permute-start | bytes 3342344 | tf_op jit(solution)/shard_map/ppermute | solution.py:46
  72.7 48.7 %collective-permute-start.14 = (bf16[544,1024]{1,0:T(8,128)(2,1)}, bf16[544,1024]{1,0:T(8,128)(2,1)}, u32[]{:S(2)}, u32[]{:S(2)}) collective-permute-start(bf16[544,1024]{1,0:T(8,128)(2,1)} %collective-permute-done.13.refs_4_), channel_id=1, source_target_pairs={{0,1},{1,0},{2,3},{3,2},{4,5},{5,4},{6,7},{7,6},{8,9},{9,8},{10,11... | collective-permute-start | bytes 3342344 | tf_op jit(solution)/shard_map/ppermute | solution.py:46
  74.1 36.4 %copy-start.8 = (bf16[4,64,512]{2,1,0:T(8,128)(2,1)}, bf16[4,64,512]{2,1,0:T(8,128)(2,1)S(1)}, u32[]{:S(2)}) copy-start(bf16[4,64,512]{2,1,0:T(8,128)(2,1)S(1)} %pad_maximum_fusion.1.refs_6_) | copy-start | bytes 786436
  77.4 12.6 %collective-permute-start.5 = (bf16[4,64,512]{2,1,0:T(8,128)(2,1)S(1)}, bf16[4,64,512]{2,1,0:T(8,128)(2,1)S(1)}, u32[]{:S(2)}, u32[]{:S(2)}) collective-permute-start(bf16[4,64,512]{2,1,0:T(8,128)(2,1)S(1)} %pad_maximum_fusion.1.refs_6_), channel_id=1, source_target_pairs={{0,16},{2,18},{4,20},{6,22},{8,24},{10,26},{12,28},{14,30},{16,0},... | collective-permute-start | bytes 786440 | tf_op jit(solution)/shard_map/ppermute | solution.py:824
  80.0 57.3 %collective-permute-start.18 = (bf16[544,1024]{1,0:T(8,128)(2,1)}, bf16[544,1024]{1,0:T(8,128)(2,1)}, u32[]{:S(2)}, u32[]{:S(2)}) collective-permute-start(bf16[544,1024]{1,0:T(8,128)(2,1)} %collective-permute-done.17.refs_4_), channel_id=1, source_target_pairs={{0,1},{1,0},{2,3},{3,2},{4,5},{5,4},{6,7},{7,6},{8,9},{9,8},{10,11... | collective-permute-start | bytes 3342344 | tf_op jit(solution)/shard_map/ppermute | solution.py:46
  90.0 20.5 %copy-start.25 = (bf16[4,64,512]{2,1,0:T(8,128)(2,1)}, bf16[4,64,512]{2,1,0:T(8,128)(2,1)S(1)}, u32[]{:S(2)}) copy-start(bf16[4,64,512]{2,1,0:T(8,128)(2,1)S(1)} %collective-permute-done.5.refs_8_) | copy-start | bytes 786436
  90.0 8.2 %collective-permute-start.4 = (bf16[4,64,512]{2,1,0:T(8,128)(2,1)S(1)}, bf16[4,64,512]{2,1,0:T(8,128)(2,1)S(1)}, u32[]{:S(2)}, u32[]{:S(2)}) collective-permute-start(bf16[4,64,512]{2,1,0:T(8,128)(2,1)S(1)} %pad_maximum_fusion.1.refs_6_), channel_id=1, source_target_pairs={{0,8},{2,10},{4,12},{6,14},{8,0},{10,2},{12,4},{14,6},{16,24},{18,... | collective-permute-start | bytes 786440 | tf_op jit(solution)/shard_map/ppermute | solution.py:824
  98.3 7.4 %collective-permute-start.6 = (bf16[4,64,512]{2,1,0:T(8,128)(2,1)S(1)}, bf16[4,64,512]{2,1,0:T(8,128)(2,1)S(1)}, u32[]{:S(2)}, u32[]{:S(2)}) collective-permute-start(bf16[4,64,512]{2,1,0:T(8,128)(2,1)S(1)} %collective-permute-done.5.refs_8_), channel_id=1, source_target_pairs={{0,8},{2,10},{4,12},{6,14},{8,0},{10,2},{12,4},{14,6},{16,24},{18,... | collective-permute-start | bytes 786440 | tf_op jit(solution)/shard_map/ppermute | solution.py:824
  99.7 20.9 %copy-start.6 = (bf16[4,2,64,512]{3,2,1,0:T(8,128)(2,1)}, bf16[4,2,64,512]{3,2,1,0:T(8,128)(2,1)S(1)}, u32[]{:S(2)}) copy-start(bf16[4,2,64,512]{3,2,1,0:T(8,128)(2,1)S(1)} %pad_maximum_fusion.refs_8_.refs_12_) | copy-start | bytes 1572868
  105.6 43.2 %collective-permute-start.12 = (bf16[4,2,64,512]{3,2,1,0:T(8,128)(2,1)S(1)}, bf16[4,2,64,512]{3,2,1,0:T(8,128)(2,1)S(1)}, u32[]{:S(2)}, u32[]{:S(2)}) collective-permute-start(bf16[4,2,64,512]{3,2,1,0:T(8,128)(2,1)S(1)} %pad_maximum_fusion.refs_8_.refs_12_), channel_id=1, source_target_pairs={{0,24},{2,26},{4,28},{6,30},{8,16},{10,18},{12,20},{14,22},{16,8},... | collective-permute-start | bytes 1572872 | tf_op jit(solution)/shard_map/ppermute | solution.py:824
  108.1 43.6 %collective-permute-start.11 = (bf16[4,2,64,512]{3,2,1,0:T(8,128)(2,1)S(1)}, bf16[4,2,64,512]{3,2,1,0:T(8,128)(2,1)}, u32[]{:S(2)}, u32[]{:S(2)}) collective-permute-start(bf16[4,2,64,512]{3,2,1,0:T(8,128)(2,1)S(1)} %pad_maximum_fusion.refs_8_.refs_12_), channel_id=1, source_target_pairs={{0,16},{2,18},{4,20},{6,22},{8,24},{10,26},{12,28},{14,30},{16,0},... | collective-permute-start | bytes 1572872 | tf_op jit(solution)/shard_map/ppermute | solution.py:824
  120.6 31.2 %collective-permute-start.10 = (bf16[4,2,64,512]{3,2,1,0:T(8,128)(2,1)S(1)}, bf16[4,2,64,512]{3,2,1,0:T(8,128)(2,1)S(1)}, u32[]{:S(2)}, u32[]{:S(2)}) collective-permute-start(bf16[4,2,64,512]{3,2,1,0:T(8,128)(2,1)S(1)} %pad_maximum_fusion.refs_8_.refs_12_), channel_id=1, source_target_pairs={{0,8},{2,10},{4,12},{6,14},{8,0},{10,2},{12,4},{14,6},{16,24},{18,... | collective-permute-start | bytes 1572872 | tf_op jit(solution)/shard_map/ppermute | solution.py:824
  180.8 14.0 %copy-start.16 = (f32[16,1024]{1,0:T(8,128)S(1)}, f32[16,1024]{1,0:T(8,128)}, u32[]{:S(2)}) copy-start(f32[16,1024]{1,0:T(8,128)} %get-tuple-element.116) | copy-start | bytes 196612
  194.2 67.6 %collective-permute-start.20 = (bf16[2,2,256,1024]{3,2,1,0:T(8,128)(2,1)}, bf16[2,2,256,1024]{3,2,1,0:T(8,128)(2,1)S(1)}, u32[]{:S(2)}, u32[]{:S(2)}) collective-permute-start(bf16[2,2,256,1024]{3,2,1,0:T(8,128)(2,1)} %get-tuple-element.111), channel_id=1, source_target_pairs={{0,1},{1,0},{2,3},{3,2},{4,5},{5,4},{6,7},{7,6},{8,9},{9,8},{10,11... | collective-permute-start | bytes 6291464 | tf_op jit(solution)/shard_map/ppermute | solution.py:46
  195.8 2.9 collective-permute-start.25
  196.3 64.1 %collective-permute-start.23 = (bf16[1,2,256,1024]{3,2,1,0:T(8,128)(2,1)}, bf16[1,2,256,1024]{3,2,1,0:T(8,128)(2,1)S(1)}, u32[]{:S(2)}, u32[]{:S(2)}) collective-permute-start(bf16[1,2,256,1024]{3,2,1,0:T(8,128)(2,1)} %get-tuple-element.113), channel_id=1, source_target_pairs={{0,1},{1,0},{2,3},{3,2},{4,5},{5,4},{6,7},{7,6},{8,9},{9,8},{10,11... | collective-permute-start | bytes 3145736 | tf_op jit(solution)/shard_map/ppermute | solution.py:46
  198.7 5.0 %collective-permute-start.26 = (f32[96,128]{1,0:T(8,128)S(1)}, f32[96,128]{1,0:T(8,128)S(1)}, u32[]{:S(2)}, u32[]{:S(2)}) collective-permute-start(f32[96,128]{1,0:T(8,128)S(1)} %bitcast_add_fusion), channel_id=1, source_target_pairs={{0,2},{2,0},{4,6},{6,4},{8,10},{10,8},{12,14},{14,12},{16,18},{18,... | collective-permute-start | bytes 147464 | tf_op jit(solution)/shard_map/ppermute | solution.py:951
  200.3 18.2 %collective-permute-start.31 = (bf16[4,64,512]{2,1,0:T(8,128)(2,1)}, bf16[4,64,512]{2,1,0:T(8,128)(2,1)S(1)}, u32[]{:S(2)}, u32[]{:S(2)}) collective-permute-start(bf16[4,64,512]{2,1,0:T(8,128)(2,1)} %get-tuple-element.125), channel_id=1, source_target_pairs={{0,8},{2,10},{4,12},{6,14},{8,0},{10,2},{12,4},{14,6},{16,24},{18,... | collective-permute-start | bytes 786440 | tf_op jit(solution)/shard_map/ppermute | solution.py:824
  202.6 18.6 %collective-permute-start.32 = (bf16[4,64,512]{2,1,0:T(8,128)(2,1)}, bf16[4,64,512]{2,1,0:T(8,128)(2,1)}, u32[]{:S(2)}, u32[]{:S(2)}) collective-permute-start(bf16[4,64,512]{2,1,0:T(8,128)(2,1)} %get-tuple-element.126), channel_id=1, source_target_pairs={{0,16},{2,18},{4,20},{6,22},{8,24},{10,26},{12,28},{14,30},{16,0},... | collective-permute-start | bytes 786440 | tf_op jit(solution)/shard_map/ppermute | solution.py:824
  203.8 4.2 %collective-permute-start.27 = (f32[96,128]{1,0:T(8,128)S(1)}, f32[96,128]{1,0:T(8,128)S(1)}, u32[]{:S(2)}, u32[]{:S(2)}) collective-permute-start(f32[96,128]{1,0:T(8,128)S(1)} %fusion.5), channel_id=1, source_target_pairs={{0,4},{2,6},{4,0},{6,2},{8,12},{10,14},{12,8},{14,10},{16,20},{18,... | collective-permute-start | bytes 147464 | tf_op jit(solution)/shard_map/ppermute | solution.py:951
  207.9 62.3 %copy-start.9 = (f32[96,128]{1,0:T(8,128)}, f32[96,128]{1,0:T(8,128)S(1)}, u32[]{:S(2)}) copy-start(f32[96,128]{1,0:T(8,128)S(1)} %add.48.refs_0_) | copy-start | bytes 147460
  207.9 10.3 %collective-permute-start.30 = (f32[96,128]{1,0:T(8,128)S(1)}, f32[96,128]{1,0:T(8,128)S(1)}, u32[]{:S(2)}, u32[]{:S(2)}) collective-permute-start(f32[96,128]{1,0:T(8,128)S(1)} %add.48.refs_0_), channel_id=1, source_target_pairs={{0,24},{2,26},{4,28},{6,30},{8,16},{10,18},{12,20},{14,22},{16,8},... | collective-permute-start | bytes 147464 | tf_op jit(solution)/shard_map/ppermute | solution.py:824
  218.3 3.5 %copy-start.17 = (f32[96,128]{1,0:T(8,128)}, f32[96,128]{1,0:T(8,128)S(1)}, u32[]{:S(2)}) copy-start(f32[96,128]{1,0:T(8,128)S(1)} %collective-permute-done.30.refs_3_) | copy-start | bytes 147460
  218.3 54.3 %collective-permute-start.37 = (bf16[4,2,64,512]{3,2,1,0:T(8,128)(2,1)}, bf16[4,2,64,512]{3,2,1,0:T(8,128)(2,1)}, u32[]{:S(2)}, u32[]{:S(2)}) collective-permute-start(bf16[4,2,64,512]{3,2,1,0:T(8,128)(2,1)} %get-tuple-element.137), channel_id=1, source_target_pairs={{0,8},{2,10},{4,12},{6,14},{8,0},{10,2},{12,4},{14,6},{16,24},{18,... | collective-permute-start | bytes 1572872 | tf_op jit(solution)/shard_map/ppermute | solution.py:824
  218.5 36.4 %copy-start.7 = (bf16[4,64,512]{2,1,0:T(8,128)(2,1)}, bf16[4,64,512]{2,1,0:T(8,128)(2,1)S(1)}, u32[]{:S(2)}) copy-start(bf16[4,64,512]{2,1,0:T(8,128)(2,1)S(1)} %collective-permute-done.31.refs_0_) | copy-start | bytes 786436
  218.5 55.5 %collective-permute-start.38 = (bf16[4,2,64,512]{3,2,1,0:T(8,128)(2,1)}, bf16[4,2,64,512]{3,2,1,0:T(8,128)(2,1)}, u32[]{:S(2)}, u32[]{:S(2)}) collective-permute-start(bf16[4,2,64,512]{3,2,1,0:T(8,128)(2,1)} %get-tuple-element.138), channel_id=1, source_target_pairs={{0,16},{2,18},{4,20},{6,22},{8,24},{10,26},{12,28},{14,30},{16,0},... | collective-permute-start | bytes 1572872 | tf_op jit(solution)/shard_map/ppermute | solution.py:824
  221.2 33.6 %collective-permute-start.33 = (bf16[4,64,512]{2,1,0:T(8,128)(2,1)}, bf16[4,64,512]{2,1,0:T(8,128)(2,1)}, u32[]{:S(2)}, u32[]{:S(2)}) collective-permute-start(bf16[4,64,512]{2,1,0:T(8,128)(2,1)} %get-tuple-element.127), channel_id=1, source_target_pairs={{0,24},{2,26},{4,28},{6,30},{8,16},{10,18},{12,20},{14,22},{16,8},... | collective-permute-start | bytes 786440 | tf_op jit(solution)/shard_map/ppermute | solution.py:824
  254.8 5.0 %collective-permute-start.29 = (f32[96,128]{1,0:T(8,128)S(1)}, f32[96,128]{1,0:T(8,128)S(1)}, u32[]{:S(2)}, u32[]{:S(2)}) collective-permute-start(f32[96,128]{1,0:T(8,128)S(1)} %add.48.refs_0_), channel_id=1, source_target_pairs={{0,16},{2,18},{4,20},{6,22},{8,24},{10,26},{12,28},{14,30},{16,0},... | collective-permute-start | bytes 147464 | tf_op jit(solution)/shard_map/ppermute | solution.py:824
  259.8 10.4 %copy-start.18 = (f32[96,128]{1,0:T(8,128)}, f32[96,128]{1,0:T(8,128)S(1)}, u32[]{:S(2)}) copy-start(f32[96,128]{1,0:T(8,128)S(1)} %collective-permute-done.29.refs_2_) | copy-start | bytes 147460
  259.8 10.5 %collective-permute-start.34 = (bf16[64,512]{1,0:T(8,128)(2,1)}, bf16[64,512]{1,0:T(8,128)(2,1)S(1)}, u32[]{:S(2)}, u32[]{:S(2)}) collective-permute-start(bf16[64,512]{1,0:T(8,128)(2,1)} %get-tuple-element.129), channel_id=1, source_target_pairs={{0,2},{2,0},{4,6},{6,4},{8,10},{10,8},{12,14},{14,12},{16,18},{18,... | collective-permute-start | bytes 196616 | tf_op jit(solution)/shard_map/ppermute | solution.py:821
  260.4 11.6 %collective-permute-start.35 = (bf16[64,512]{1,0:T(8,128)(2,1)}, bf16[64,512]{1,0:T(8,128)(2,1)S(1)}, u32[]{:S(2)}, u32[]{:S(2)}) collective-permute-start(bf16[64,512]{1,0:T(8,128)(2,1)} %get-tuple-element.130), channel_id=1, source_target_pairs={{0,4},{2,6},{4,0},{6,2},{8,12},{10,14},{12,8},{14,10},{16,20},{18,... | collective-permute-start | bytes 196616 | tf_op jit(solution)/shard_map/ppermute | solution.py:821
  261.8 3.2 copy-start
  261.8 8.5 %collective-permute-start.28 = (f32[96,128]{1,0:T(8,128)S(1)}, f32[96,128]{1,0:T(8,128)S(1)}, u32[]{:S(2)}, u32[]{:S(2)}) collective-permute-start(f32[96,128]{1,0:T(8,128)S(1)} %add.48.refs_0_), channel_id=1, source_target_pairs={{0,8},{2,10},{4,12},{6,14},{8,0},{10,2},{12,4},{14,6},{16,24},{18,... | collective-permute-start | bytes 147464 | tf_op jit(solution)/shard_map/ppermute | solution.py:824
  267.5 5.0 %copy-start.2 = (bf16[2,256,1024]{2,1,0:T(8,128)(2,1)S(1)}, bf16[2,256,1024]{2,1,0:T(8,128)(2,1)}, u32[]{:S(2)}) copy-start(bf16[2,256,1024]{2,1,0:T(8,128)(2,1)} %add_halves.4) | copy-start | bytes 3145732
  267.5 31.7 %copy-start.28 = (bf16[64,512]{1,0:T(8,128)(2,1)S(1)}, bf16[64,512]{1,0:T(8,128)(2,1)}, u32[]{:S(2)}) copy-start(bf16[64,512]{1,0:T(8,128)(2,1)} %get-tuple-element.131) | copy-start | bytes 196612
  270.3 29.0 %copy-start.19 = (f32[96,128]{1,0:T(8,128)}, f32[96,128]{1,0:T(8,128)S(1)}, u32[]{:S(2)}) copy-start(f32[96,128]{1,0:T(8,128)S(1)} %collective-permute-done.28.refs_1_) | copy-start | bytes 147460
  270.3 69.9 %collective-permute-start.19 = (bf16[1,2,256,1024]{3,2,1,0:T(8,128)(2,1)}, bf16[1,2,256,1024]{3,2,1,0:T(8,128)(2,1)S(1)}, u32[]{:S(2)}, u32[]{:S(2)}) collective-permute-start(bf16[1,2,256,1024]{3,2,1,0:T(8,128)(2,1)} %get-tuple-element.109), channel_id=1, source_target_pairs={{0,1},{1,0},{2,3},{3,2},{4,5},{5,4},{6,7},{7,6},{8,9},{9,8},{10,11... | collective-permute-start | bytes 3145736 | tf_op jit(solution)/shard_map/ppermute | solution.py:46
  270.4 50.4 %copy-start.13 = (bf16[64,512]{1,0:T(8,128)(2,1)}, bf16[64,512]{1,0:T(8,128)(2,1)S(1)}, u32[]{:S(2)}) copy-start(bf16[64,512]{1,0:T(8,128)(2,1)S(1)} %collective-permute-done.34.refs_0_) | copy-start | bytes 196612
  270.4 69.8 %collective-permute-start.24 = (bf16[2,256,1024]{2,1,0:T(8,128)(2,1)S(1)}, bf16[2,256,1024]{2,1,0:T(8,128)(2,1)}, u32[]{:S(2)}, u32[]{:S(2)}) collective-permute-start(bf16[2,256,1024]{2,1,0:T(8,128)(2,1)S(1)} %copy-done.3), channel_id=1, source_target_pairs={{0,6},{2,4},{4,2},{6,0},{8,14},{10,12},{12,10},{14,8},{16,22},{18,... | collective-permute-start | bytes 3145736 | tf_op jit(solution)/shard_map/ppermute | solution.py:821
  272.0 48.8 %copy-start.14 = (bf16[64,512]{1,0:T(8,128)(2,1)}, bf16[64,512]{1,0:T(8,128)(2,1)S(1)}, u32[]{:S(2)}) copy-start(bf16[64,512]{1,0:T(8,128)(2,1)S(1)} %collective-permute-done.35.refs_1_) | copy-start | bytes 196612
  272.0 68.2 %collective-permute-start.21 = (bf16[2,256,1024]{2,1,0:T(8,128)(2,1)}, bf16[2,256,1024]{2,1,0:T(8,128)(2,1)}, u32[]{:S(2)}, u32[]{:S(2)}) collective-permute-start(bf16[2,256,1024]{2,1,0:T(8,128)(2,1)} %add_halves.3), channel_id=1, source_target_pairs={{0,2},{2,0},{4,6},{6,4},{8,10},{10,8},{12,14},{14,12},{16,18},{18,... | collective-permute-start | bytes 3145736 | tf_op jit(solution)/shard_map/ppermute | solution.py:821
  272.5 67.7 %collective-permute-start.22 = (bf16[2,256,1024]{2,1,0:T(8,128)(2,1)S(1)}, bf16[2,256,1024]{2,1,0:T(8,128)(2,1)}, u32[]{:S(2)}, u32[]{:S(2)}) collective-permute-start(bf16[2,256,1024]{2,1,0:T(8,128)(2,1)S(1)} %copy-done.2), channel_id=1, source_target_pairs={{0,4},{2,6},{4,0},{6,2},{8,12},{10,14},{12,8},{14,10},{16,20},{18,... | collective-permute-start | bytes 3145736 | tf_op jit(solution)/shard_map/ppermute | solution.py:821
  274.0 25.3 %collective-permute-start.39 = (bf16[4,2,64,512]{3,2,1,0:T(8,128)(2,1)}, bf16[4,2,64,512]{3,2,1,0:T(8,128)(2,1)}, u32[]{:S(2)}, u32[]{:S(2)}) collective-permute-start(bf16[4,2,64,512]{3,2,1,0:T(8,128)(2,1)} %get-tuple-element.139), channel_id=1, source_target_pairs={{0,24},{2,26},{4,28},{6,30},{8,16},{10,18},{12,20},{14,22},{16,8},... | collective-permute-start | bytes 1572872 | tf_op jit(solution)/shard_map/ppermute | solution.py:824
  299.3 21.5 %collective-permute-start.36 = (bf16[64,512]{1,0:T(8,128)(2,1)S(1)}, bf16[64,512]{1,0:T(8,128)(2,1)S(1)}, u32[]{:S(2)}, u32[]{:S(2)}) collective-permute-start(bf16[64,512]{1,0:T(8,128)(2,1)S(1)} %copy-done.28), channel_id=1, source_target_pairs={{0,6},{2,4},{4,2},{6,0},{8,14},{10,12},{12,10},{14,8},{16,22},{18,... | collective-permute-start | bytes 196616 | tf_op jit(solution)/shard_map/ppermute | solution.py:821
  320.8 5.3 %copy-start.15 = (bf16[64,512]{1,0:T(8,128)(2,1)}, bf16[64,512]{1,0:T(8,128)(2,1)S(1)}, u32[]{:S(2)}) copy-start(bf16[64,512]{1,0:T(8,128)(2,1)S(1)} %collective-permute-done.36.refs_2_) | copy-start | bytes 196612
  320.8 5.3 %collective-permute-start.40 = (bf16[2,64,512]{2,1,0:T(8,128)(2,1)}, bf16[2,64,512]{2,1,0:T(8,128)(2,1)S(1)}, u32[]{:S(2)}, u32[]{:S(2)}) collective-permute-start(bf16[2,64,512]{2,1,0:T(8,128)(2,1)} %get-tuple-element.141), channel_id=1, source_target_pairs={{0,2},{2,0},{4,6},{6,4},{8,10},{10,8},{12,14},{14,12},{16,18},{18,... | collective-permute-start | bytes 393224 | tf_op jit(solution)/shard_map/ppermute | solution.py:821
  326.1 11.3 %copy-start.10 = (bf16[2,64,512]{2,1,0:T(8,128)(2,1)}, bf16[2,64,512]{2,1,0:T(8,128)(2,1)S(1)}, u32[]{:S(2)}) copy-start(bf16[2,64,512]{2,1,0:T(8,128)(2,1)S(1)} %collective-permute-done.40.refs_0_) | copy-start | bytes 393220
  326.1 5.2 %collective-permute-start.41 = (bf16[2,64,512]{2,1,0:T(8,128)(2,1)}, bf16[2,64,512]{2,1,0:T(8,128)(2,1)S(1)}, u32[]{:S(2)}, u32[]{:S(2)}) collective-permute-start(bf16[2,64,512]{2,1,0:T(8,128)(2,1)} %get-tuple-element.142), channel_id=1, source_target_pairs={{0,4},{2,6},{4,0},{6,2},{8,12},{10,14},{12,8},{14,10},{16,20},{18,... | collective-permute-start | bytes 393224 | tf_op jit(solution)/shard_map/ppermute | solution.py:821
  331.3 6.1 %copy-start.11 = (bf16[2,64,512]{2,1,0:T(8,128)(2,1)}, bf16[2,64,512]{2,1,0:T(8,128)(2,1)S(1)}, u32[]{:S(2)}) copy-start(bf16[2,64,512]{2,1,0:T(8,128)(2,1)S(1)} %collective-permute-done.41.refs_1_) | copy-start | bytes 393220
  331.3 6.1 %collective-permute-start.42 = (bf16[2,64,512]{2,1,0:T(8,128)(2,1)}, bf16[2,64,512]{2,1,0:T(8,128)(2,1)S(1)}, u32[]{:S(2)}, u32[]{:S(2)}) collective-permute-start(bf16[2,64,512]{2,1,0:T(8,128)(2,1)} %get-tuple-element.143), channel_id=1, source_target_pairs={{0,6},{2,4},{4,2},{6,0},{8,14},{10,12},{12,10},{14,8},{16,22},{18,... | collective-permute-start | bytes 393224 | tf_op jit(solution)/shard_map/ppermute | solution.py:821
  (8 other events, 14.1 us)

commit v3 on v2

--- a/solution.py
+++ b/solution.py
@@ -1,3 +1,5 @@
+from types import SimpleNamespace
+
 import jax
 import jax.numpy as jnp
 import numpy as np
@@ -14,14 +16,16 @@
 EPSILON = 1e-05
 NEGATIVE = -1e30
 QUERY_BLOCK = 256
+SMALL_VMEM = 12 << 20
 ROW_CHUNK = 32
 ATTEND_GROUPS = ((0,), (1, 2), (3,))
-MLP_GROUPS = ((3,), (1, 2), (0,))
+MLP_GROUPS = ((3,), (1, 2, 0))
 F32 = jnp.float32
 BF16 = jnp.bfloat16
 
 
 HBM = pl.BlockSpec(memory_space=pltpu.HBM)
+ANY = pl.BlockSpec(memory_space=pl.ANY)
 VMEM = pl.BlockSpec(memory_space=pltpu.VMEM)
 SMEM = pl.BlockSpec(memory_space=pltpu.SMEM)
 
@@ -53,6 +57,35 @@
         parts.append(part.astype(BF16))
         value = value - part
     return parts
+
+
+def staged_call(body, scalars, arrays, shapes):
+    count = len(arrays)
+
+    def whole(*refs):
+        at = len(scalars)
+        given, sources = refs[:at], refs[at : at + count]
+        outs = refs[at + count : at + count + len(shapes)]
+        targets, sems = refs[at + count + len(shapes) : -1], refs[-1]
+        copies = [
+            pltpu.make_async_copy(source, target, sems.at[k])
+            for k, (source, target) in enumerate(zip(sources, targets))
+        ]
+        for copy in copies:
+            copy.start()
+        for copy in copies:
+            copy.wait()
+        body(*given, *targets, *outs)
+
+    return pl.pallas_call(
+        whole,
+        in_specs=[SMEM] * len(scalars) + [ANY] * count,
+        out_specs=[VMEM] * len(shapes),
+        out_shape=shapes,
+        scratch_shapes=[pltpu.VMEM(array.shape, array.dtype) for array in arrays]
+        + [pltpu.SemaphoreType.DMA((count,))],
+        compiler_params=pltpu.CompilerParams(vmem_limit_bytes=SMALL_VMEM),
+    )(*scalars, *arrays)
 
 
 def pack_body(meta, attend, project, expand, shrink, *outs):
@@ -79,13 +112,14 @@
         out_specs=[VMEM] * (2 * QUAD),
         out_shape=[jax.ShapeDtypeStruct((rows, width), BF16)] * QUAD
         + [jax.ShapeDtypeStruct((2, rows, hidden), BF16)] * QUAD,
-        name="pack_weights",
     )(meta, attend, project, expand, shrink)
     return parts[:QUAD], parts[QUAD:]
 
 
 def join_body(*refs):
-    parts, message = refs[:-1], refs[-1]
+    parts, message, column_sums = refs[:-2], refs[-2], refs[-1]
+    total = fold_rows(parts[1][...].astype(F32))
+    column_sums[...] = jnp.sum(total, axis=0, keepdims=True)
     at = 0
     for part in parts:
         message[at : at + part.shape[0]] = part[...]
@@ -97,9 +131,11 @@
     return pl.pallas_call(
         join_body,
         in_specs=[VMEM] * len(parts),
-        out_specs=VMEM,
-        out_shape=jax.ShapeDtypeStruct((rows, parts[0].shape[1]), BF16),
-        name="join_message",
+        out_specs=[VMEM] * 2,
+        out_shape=[
+            jax.ShapeDtypeStruct((rows, parts[0].shape[1]), BF16),
+            jax.ShapeDtypeStruct((1, parts[0].shape[1]), F32),
+        ],
     )(*parts)
 
 
@@ -114,20 +150,15 @@
 
 def sum_layers(keep, received):
     shape = keep.shape[1:]
-    return pl.pallas_call(
-        sum_layers_body,
-        in_specs=[VMEM] * (1 + len(received)),
-        out_specs=[VMEM] * QUAD,
-        out_shape=[jax.ShapeDtypeStruct(shape, BF16 if j else F32) for j in range(QUAD)],
-        name="sum_layers",
-    )(keep, *received)
-
-
-def add_body(place, mine, other, out, mine_s, other_s, out_s, sems):
+    shapes = [jax.ShapeDtypeStruct(shape, BF16 if j else F32) for j in range(QUAD)]
+    return staged_call(sum_layers_body, [], [keep, *received], shapes)
+
+
+def add_body(mine, other, out, mine_s, other_s, out_s, sems):
     def copies(which):
         pairs = ((mine, mine_s), (other, other_s))
         return [
-            pltpu.make_async_copy(source.at[place, which], target.at[which], sems.at[which, n])
+            pltpu.make_async_copy(source.at[which], target.at[which], sems.at[which, n])
             for n, (source, target) in enumerate(pairs)
         ]
 
@@ -146,16 +177,49 @@
         save.wait()
 
 
-def add_halves(mine, other, place):
-    shape = mine.shape[1:]
+def add_halves(mine, other):
+    shape = mine.shape
     return pl.pallas_call(
-        lambda *refs: add_body(place, *refs),
-        in_specs=[HBM] * 2,
-        out_specs=HBM,
+        add_body,
+        in_specs=[ANY] * 2,
+        out_specs=ANY,
         out_shape=jax.ShapeDtypeStruct(shape, BF16),
         scratch_shapes=[pltpu.VMEM(shape, BF16)] * 3 + [pltpu.SemaphoreType.DMA((2, 3))],
-        name="add_halves",
+        compiler_params=pltpu.CompilerParams(vmem_limit_bytes=SMALL_VMEM),
     )(mine, other)
+
+
+def join_vector_body(meta, first, first_bias, second, second_bias, cotangent, out):
+    out[...] = jnp.zeros_like(out)
+    tiles = first.shape[1] // 128
+
+    def put(at, row):
+        for k in range(row.shape[1] // 128):
+            out[pl.ds(at + k, 1), :] = row[:, k * 128 : (k + 1) * 128]
+
+    at = 0
+    for sums in (first, second):
+        for part in (sums[:8], sums[8:]):
+            put(at, jnp.sum(part, axis=0, keepdims=True))
+            at += tiles
+    put(at, cotangent[...])
+    at += tiles
+    place = meta[0] * QUAD + meta[1]
+    row = jnp.sum(first_bias[...].T, axis=0, keepdims=True)
+    put(at + place * (row.shape[1] // 128), row)
+    at += 2 * QUAD * (row.shape[1] // 128)
+    row = jnp.sum(second_bias[...], axis=0, keepdims=True)
+    put(at + place * (row.shape[1] // 128), row)
+
+
+def join_vector(meta, first, first_bias, second, second_bias, cotangent, sizes):
+    rows = (sum(sizes) - cotangent.shape[1]) // 128
+    return pl.pallas_call(
+        join_vector_body,
+        in_specs=[SMEM] + [VMEM] * 5,
+        out_specs=VMEM,
+        out_shape=jax.ShapeDtypeStruct((rows, 128), F32),
+    )(meta, first, first_bias, second, second_bias, cotangent)
 
 
 def split_body(*refs):
@@ -171,13 +235,8 @@
 
 
 def split_vector(vectors, sizes):
-    pieces = pl.pallas_call(
-        split_body,
-        in_specs=[VMEM] * len(vectors),
-        out_specs=[VMEM] * len(sizes),
-        out_shape=[jax.ShapeDtypeStruct((size // 128, 128), F32) for size in sizes],
-        name="split_vector",
-    )(*vectors)
+    shapes = [jax.ShapeDtypeStruct((size // 128, 128), F32) for size in sizes]
+    pieces = staged_call(split_body, [], vectors, shapes)
     return [piece.reshape(-1) for piece in pieces]
 
 
@@ -195,16 +254,8 @@
 
 def unpack_attend(meta, own, received, attend_cols, project_cols):
     rows = own.shape[0]
-    return pl.pallas_call(
-        unpack_attend_body,
-        in_specs=[SMEM] + [VMEM] * 4,
-        out_specs=[VMEM] * 2,
-        out_shape=[
-            jax.ShapeDtypeStruct((rows, attend_cols), F32),
-            jax.ShapeDtypeStruct((rows, project_cols), F32),
-        ],
-        name="unpack_attend",
-    )(meta, own, *received)
+    shapes = [jax.ShapeDtypeStruct((rows, cols), F32) for cols in (attend_cols, project_cols)]
+    return staged_call(unpack_attend_body, [meta], [own, *received], shapes)
 
 
 def unpack_mlp_body(meta, own, *refs):
@@ -220,13 +271,8 @@
 
 def unpack_mlp(meta, own, received, hidden_cols):
     rows = own.shape[1]
-    return pl.pallas_call(
-        unpack_mlp_body,
-        in_specs=[SMEM] + [VMEM] * 4,
-        out_specs=[VMEM] * 2,
-        out_shape=[jax.ShapeDtypeStruct((rows, hidden_cols), F32)] * 2,
-        name="unpack_mlp",
-    )(meta, own, *received)
+    shapes = [jax.ShapeDtypeStruct((rows, hidden_cols), F32)] * 2
+    return staged_call(unpack_mlp_body, [meta], [own, *received], shapes)
 
 
 def row_chunks(length):
@@ -289,24 +335,24 @@
 
     @staticmethod
     def scratch(length, features, width):
-        return {
-            "mask": pltpu.VMEM((length // QUERY_BLOCK, length, QUERY_BLOCK), F32),
-            "q": pltpu.VMEM((2, 2 * HD, length), BF16),
-            "d": pltpu.VMEM((2, 2 * HD, length), BF16),
-            "kv": pltpu.VMEM((2, length, 2 * HD), BF16),
-            "kvt": pltpu.VMEM((2, 2 * HD, length), BF16),
-            "score": pltpu.VMEM((2, length, QUERY_BLOCK), F32),
-            "gprob": pltpu.VMEM((2, length, QUERY_BLOCK), F32),
-            "weight": pltpu.VMEM((2, length, QUERY_BLOCK), BF16),
-            "gprod": pltpu.VMEM((2, length, QUERY_BLOCK), BF16),
-            "dq": pltpu.VMEM((2, HD, length), F32),
-            "dk": pltpu.VMEM((2, HD, length), F32),
-            "dv": pltpu.VMEM((2, HD, length), F32),
-            "ctxt": pltpu.VMEM((2 * HD, length), BF16),
-            "ctx": pltpu.VMEM((length, 2 * HD), BF16),
-            "gmt": pltpu.VMEM((6 * HD, length), BF16),
-            "gm": pltpu.VMEM((length, 6 * HD), BF16),
-        }
+        return dict(
+            mask=pltpu.VMEM((length // QUERY_BLOCK, length, QUERY_BLOCK), F32),
+            q=pltpu.VMEM((2, 2 * HD, length), BF16),
+            d=pltpu.VMEM((2, 2 * HD, length), BF16),
+            kv=pltpu.VMEM((2, length, 2 * HD), BF16),
+            kvt=pltpu.VMEM((2, 2 * HD, length), BF16),
+            score=pltpu.VMEM((2, length, QUERY_BLOCK), F32),
+            gprob=pltpu.VMEM((2, length, QUERY_BLOCK), F32),
+            weight=pltpu.VMEM((2, length, QUERY_BLOCK), BF16),
+            gprod=pltpu.VMEM((2, length, QUERY_BLOCK), BF16),
+            dq=pltpu.VMEM((2, HD, length), F32),
+            dk=pltpu.VMEM((2, HD, length), F32),
+            dv=pltpu.VMEM((2, HD, length), F32),
+            ctxt=pltpu.VMEM((2 * HD, length), BF16),
+            ctx=pltpu.VMEM((length, 2 * HD), BF16),
+            gmt=pltpu.VMEM((6 * HD, length), BF16),
+            gm=pltpu.VMEM((length, 6 * HD), BF16),
+        )
 
     @staticmethod
     def bias_shape(width):
@@ -331,7 +377,7 @@
             query_at = lax.broadcasted_iota(jnp.int32, (width, QUERY_BLOCK), 1)
             first = start[:, lanes].astype(jnp.int32)
             allowed = (key_at >= first) & (key_at <= query_at + block * QUERY_BLOCK)
-            m["mask"][block, :width, :] = jnp.where(allowed, 0.0, NEGATIVE)
+            m.mask[block, :width, :] = jnp.where(allowed, 0.0, NEGATIVE)
 
         projected = dot_nt(w[:heads, :], norm[...]) + widen(bias[...], length)
         grad_context = dot_nt(w[heads:, :], cot[...]).astype(BF16)
@@ -340,13 +386,13 @@
             query, key, value = [
                 projected[(3 * h + k) * HD : (3 * h + k + 1) * HD] for k in range(3)
             ]
-            m["q"][h, :HD, :] = (rotate_rows(query, cosine, sine) * scale).astype(BF16)
-            m["q"][h, HD:, :] = nothing
-            m["d"][h, :HD, :] = nothing
-            m["d"][h, HD:, :] = grad_context[h * HD : (h + 1) * HD]
+            m.q[h, :HD, :] = (rotate_rows(query, cosine, sine) * scale).astype(BF16)
+            m.q[h, HD:, :] = nothing
+            m.d[h, :HD, :] = nothing
+            m.d[h, HD:, :] = grad_context[h * HD : (h + 1) * HD]
             both = jnp.concatenate([rotate_rows(key, cosine, sine), value], axis=0).astype(BF16)
-            m["kvt"][h] = both
-            m["kv"][h] = both.T
+            m.kvt[h] = both
+            m.kv[h] = both.T
 
         items = [
             (block, h) for block in reversed(range(length // QUERY_BLOCK)) for h in range(2)
@@ -359,37 +405,37 @@
 
         def products(item):
             _, h, width, lanes = place(item)
-            key_value = m["kv"][h, :width, :]
-            m["score"][item % 2, :width, :] = dot_nn(key_value, m["q"][h, :, lanes])
-            m["gprob"][item % 2, :width, :] = dot_nn(key_value, m["d"][h, :, lanes])
+            key_value = m.kv[h, :width, :]
+            m.score[item % 2, :width, :] = dot_nn(key_value, m.q[h, :, lanes])
+            m.gprob[item % 2, :width, :] = dot_nn(key_value, m.d[h, :, lanes])
 
         def softmax(item):
             block, _, width, _ = place(item)
-            scores = m["score"][item % 2, :width, :] + m["mask"][block, :width, :]
+            scores = m.score[item % 2, :width, :] + m.mask[block, :width, :]
             highest = jnp.max(scores, axis=0, keepdims=True)
             numerators = jnp.exp(scores - highest)
             weights = numerators * (1.0 / jnp.sum(numerators, axis=0, keepdims=True))
-            grad_probs = m["gprob"][item % 2, :width, :]
+            grad_probs = m.gprob[item % 2, :width, :]
             centre = jnp.sum(grad_probs * weights, axis=0, keepdims=True)
-            m["weight"][item % 2, :width, :] = weights.astype(BF16)
-            m["gprod"][item % 2, :width, :] = (weights * (grad_probs - centre)).astype(BF16)
+            m.weight[item % 2, :width, :] = weights.astype(BF16)
+            m.gprod[item % 2, :width, :] = (weights * (grad_probs - centre)).astype(BF16)
 
         def results(item):
             _, h, width, lanes = place(item)
-            weights_low = m["weight"][item % 2, :width, :]
-            grad_products = m["gprod"][item % 2, :width, :]
-            context = dot_nn(m["kvt"][h, HD:, :width], weights_low)
-            m["ctxt"][h * HD : (h + 1) * HD, lanes] = context.astype(BF16)
-            grad_query = dot_nn(m["kvt"][h, :HD, :width], grad_products)
-            m["dq"][h, :, lanes] = grad_query * scale
-            grad_key = dot_nt(m["q"][h, :HD, lanes], grad_products)
-            grad_value = dot_nt(m["d"][h, HD:, lanes], weights_low)
+            weights_low = m.weight[item % 2, :width, :]
+            grad_products = m.gprod[item % 2, :width, :]
+            context = dot_nn(m.kvt[h, HD:, :width], weights_low)
+            m.ctxt[h * HD : (h + 1) * HD, lanes] = context.astype(BF16)
+            grad_query = dot_nn(m.kvt[h, :HD, :width], grad_products)
+            m.dq[h, :, lanes] = grad_query * scale
+            grad_key = dot_nt(m.q[h, :HD, lanes], grad_products)
+            grad_value = dot_nt(m.d[h, HD:, lanes], weights_low)
             if width == length:
-                m["dk"][h] = grad_key
-                m["dv"][h] = grad_value
+                m.dk[h] = grad_key
+                m.dv[h] = grad_value
             else:
-                m["dk"][h, :, :width] += grad_key
-                m["dv"][h, :, :width] += grad_value
+                m.dk[h, :, :width] += grad_key
+                m.dv[h, :, :width] += grad_value
 
         products(0)
         for item in range(len(items)):
@@ -402,31 +448,31 @@
 
         for h in range(2):
             parts = [
-                rotate_rows(m["dq"][h], cosine, -sine),
-                rotate_rows(m["dk"][h], cosine, -sine),
-                m["dv"][h],
+                rotate_rows(m.dq[h], cosine, -sine),
+                rotate_rows(m.dk[h], cosine, -sine),
+                m.dv[h],
             ]
             for k, part in enumerate(parts):
                 rows = slice((3 * h + k) * HD, (3 * h + k + 1) * HD)
                 low = part.astype(BF16)
-                m["gmt"][rows, :] = low
+                m.gmt[rows, :] = low
                 bias_sums[rows, :] += fold_lanes(low.astype(F32))
-        m["gm"][...] = m["gmt"][...].T
-        m["ctx"][...] = m["ctxt"][...].T
+        m.gm[...] = m.gmt[...].T
+        m.ctx[...] = m.ctxt[...].T
 
     @staticmethod
     def accumulate(m, norm, cot, total):
         heads = 6 * HD
-        total[0, :heads, :] += dot_nn(m["gmt"][...], norm[...])
-        total[0, heads:, :] += dot_nn(m["ctxt"][...], cot[...])
+        total[0, :heads, :] += dot_nn(m.gmt[...], norm[...])
+        total[0, heads:, :] += dot_nn(m.ctxt[...], cot[...])
 
     @staticmethod
     def forward_out(m, w, cols):
-        return dot_nn(m["ctx"][...], w[6 * HD :, cols])
+        return dot_nn(m.ctx[...], w[6 * HD :, cols])
 
     @staticmethod
     def backward_out(m, w, cols):
-        return dot_nn(m["gm"][...], w[: 6 * HD, cols])
+        return dot_nn(m.gm[...], w[: 6 * HD, cols])
 
 
 class Mlp:
@@ -435,11 +481,11 @@
 
     @staticmethod
     def scratch(length, features, width):
-        return {
-            "hid": pltpu.VMEM((2, length, width), F32),
-            "act": pltpu.VMEM((length, width), BF16),
-            "dh": pltpu.VMEM((length, width), BF16),
-        }
+        return dict(
+            hid=pltpu.VMEM((2, length, width), F32),
+            act=pltpu.VMEM((length, width), BF16),
+            dh=pltpu.VMEM((length, width), BF16),
+        )
 
     @staticmethod
     def bias_shape(width):
@@ -451,29 +497,29 @@
 
     @staticmethod
     def compute(m, norm, cot, w, bias, bias_sums, table):
-        m["hid"][0] = dot_nn(norm[...], w[0]) + bias[...]
-        m["hid"][1] = dot_nn(cot[...], w[1])
+        m.hid[0] = dot_nn(norm[...], w[0]) + bias[...]
+        m.hid[1] = dot_nn(cot[...], w[1])
         for rows in row_chunks(norm.shape[0]):
-            hid = m["hid"][0, rows, :]
+            hid = m.hid[0, rows, :]
             below = 0.5 + 0.5 * lax.erf(hid * np.float32(0.5**0.5))
             slope = below + hid * jnp.exp(-0.5 * (hid * hid)) * np.float32((2 * np.pi) ** -0.5)
-            m["act"][rows, :] = (hid * below).astype(BF16)
-            grad_hid = (slope * m["hid"][1, rows, :]).astype(BF16)
-            m["dh"][rows, :] = grad_hid
+            m.act[rows, :] = (hid * below).astype(BF16)
+            grad_hid = (slope * m.hid[1, rows, :]).astype(BF16)
+            m.dh[rows, :] = grad_hid
             bias_sums[...] += fold_rows(grad_hid.astype(F32))
 
     @staticmethod
     def accumulate(m, norm, cot, total):
-        total[0] += dot_tn(m["dh"][...], norm[...])
-        total[1] += dot_tn(m["act"][...], cot[...])
+        total[0] += dot_tn(m.dh[...], norm[...])
+        total[1] += dot_tn(m.act[...], cot[...])
 
     @staticmethod
     def forward_out(m, w, cols):
-        return dot_nt(m["act"][...], w[1, cols, :])
+        return dot_nt(m.act[...], w[1, cols, :])
 
     @staticmethod
     def backward_out(m, w, cols):
-        return dot_nt(m["dh"][...], w[0, cols, :])
+        return dot_nt(m.dh[...], w[0, cols, :])
 
 
 def branch_body(kind, names, n_seq, count, is_first, is_last, places, *refs):
@@ -485,7 +531,8 @@
     reads_turned = kind.turns and not is_first
     blocks = take(1 if reads_turned else count)
     carried = [] if is_first else take(3)
-    out_hbm, grad_hbm, sums, bias_sums = take(4)
+    outs = take(2 * n_seq if places else 2)
+    sums, bias_sums = take(2)
     if is_last:
         grads = take(count)
     else:
@@ -495,7 +542,7 @@
     x_s, d_s, tab_s, w_s, total, norm_s, hat_s, out_st, grad_st = take(9)
     wt_s = take(1)[0] if kind.turns else None
     turned = take(1)[0] if is_last else None
-    m = dict(zip(names, take(len(names))))
+    m = SimpleNamespace(**dict(zip(names, take(len(names)))))
     token_sem, table_sem, weight_sem, part_sem, out_sem, total_sem = take(6)
 
     length, features = x_s.shape[1:]
@@ -560,14 +607,27 @@
 
     def stores(stage, i, which):
         if not places:
-            target = (out_hbm, grad_hbm)[which]
-            return [pltpu.make_async_copy(stage.at[i], target.at[i], out_sem.at[i, which, 0])]
+            return [pltpu.make_async_copy(stage.at[i], outs[which].at[i], out_sem.at[i, which, 0])]
         return [
             pltpu.make_async_copy(
-                stage.at[i, pl.ds(place, half)], target.at[i, which], out_sem.at[i, which, number]
+                stage.at[i, pl.ds(place, half)],
+                outs[2 * i + number].at[which],
+                out_sem.at[i, which, number],
             )
-            for number, (place, target) in enumerate(((mine, out_hbm), (other, grad_hbm)))
+            for number, place in enumerate((mine, other))
         ]
+
+    def start_stores(stage, i, which):
+        if not places or n_seq == 1:
+            for copy in stores(stage, i, which):
+                copy.start()
+            return
+        for k in range(n_seq):
+
+            @pl.when(i == k)
+            def _(k=k):
+                for copy in stores(stage, k, which):
+                    copy.start()
 
     def one_sequence(i, carry):
         for number in range(2):
@@ -625,8 +685,7 @@
             if places:
                 out = out + out_st[i, :, cols].astype(F32)
             out_st[i, :, cols] = out.astype(BF16)
-        for copy in stores(out_st, i, 0):
-            copy.start()
+        start_stores(out_st, i, 0)
         for cols in column_chunks(features):
             grad = kind.backward_out(m, w, cols)
             sums[0:8, cols] += fold_rows(grad * hat_s[:, cols])
@@ -635,8 +694,7 @@
             if places:
                 whole = whole + grad_st[i, :, cols].astype(F32)
             grad_st[i, :, cols] = whole.astype(BF16)
-        for copy in stores(grad_st, i, 1):
-            copy.start()
+        start_stores(grad_st, i, 1)
         return carry
 
     if n_seq == 1:
@@ -671,8 +729,11 @@
     n_pick = len(kind.picks)
     operands = [meta, gain, shift, bias]
     specs = [SMEM] + [VMEM] * 3
-    for pair in list(messages) + [part[:2] for part in partials]:
+    for pair in messages:
         operands += list(pair)
+        specs += [ANY] * 2
+    for part in partials:
+        operands += list(part[:2])
         specs += [HBM] * 2
     places = [part[2] for part in partials]
     if kind.turns and not is_first:
@@ -685,14 +746,15 @@
         operands += list(carried[:3])
         specs += [HBM, VMEM, VMEM]
     if places:
-        shapes = [jax.ShapeDtypeStruct((n_seq, 2, half, features), BF16)] * 2
+        shapes = [jax.ShapeDtypeStruct((2, half, features), BF16)] * (2 * n_seq)
     else:
         shapes = [jax.ShapeDtypeStruct((n_seq, length, features), BF16)] * 2
+    n_out = len(shapes)
     shapes += [
         jax.ShapeDtypeStruct((16, features), F32),
         jax.ShapeDtypeStruct(kind.bias_shape(width), F32),
     ]
-    out_specs = [HBM, HBM, VMEM, VMEM]
+    out_specs = [HBM] * n_out + [VMEM, VMEM]
     if is_last:
         shape = blocks[0].shape
         shapes += [jax.ShapeDtypeStruct(shape, BF16 if k else F32) for k in range(count)]
@@ -747,46 +809,43 @@
         ),
     )
     results = call(*operands)
-    sums = results[2:4]
+    outs, sums, rest = results[:n_out], results[n_out : n_out + 2], results[n_out + 2 :]
     if is_last:
-        return results[:2], sums, results[4:]
-    turned = () if not kind.turns else (results[5] if is_first else carried[3],)
-    return results[:2], sums, (results[4], *sums, *turned)
-
-
-def finish_body(x, d, mine, other, p1, p2, p3, first_bias, second_bias, out, grad):
-    def total(which):
-        own = mine[0, which].astype(F32) + other[0, which].astype(F32)
-        return own + p1[which].astype(F32) + (p2[which].astype(F32) + p3[which].astype(F32))
-
-    tokens = x[...].astype(F32)
-    out[...] = (tokens + total(0) + first_bias[...] + second_bias[...]).astype(BF16)
-    back = total(1)
-    average = jnp.mean(tokens, axis=-1, keepdims=True)
-    centred = tokens - average
-    inverse = lax.rsqrt(jnp.mean(centred * centred, axis=-1, keepdims=True) + EPSILON)
-    scaled = centred * inverse
-    level = jnp.mean(back, axis=-1, keepdims=True)
-    along = jnp.mean(back * scaled, axis=-1, keepdims=True)
-    grad[...] = (d[...].astype(F32) + (back - level - scaled * along) * inverse).astype(BF16)
+        return outs, sums, rest
+    turned = () if not kind.turns else (rest[1] if is_first else carried[3],)
+    return outs, sums, (rest[0], *sums, *turned)
+
+
+def finish_body(first_bias, second_bias, x, d, mine, other, p1, p2, p3, out, grad):
+    bias = first_bias[...] + second_bias[...]
+
+    def some_rows(number, carry):
+        rows = pl.ds(pl.multiple_of(number * ROW_CHUNK, ROW_CHUNK), ROW_CHUNK)
+
+        def total(which):
+            own = mine[which, rows, :].astype(F32) + other[which, rows, :].astype(F32)
+            pair = p2[which, rows, :].astype(F32) + p3[which, rows, :].astype(F32)
+            return own + p1[which, rows, :].astype(F32) + pair
+
+        tokens = x[rows, :].astype(F32)
+        out[rows, :] = (tokens + total(0) + bias).astype(BF16)
+        back = total(1)
+        share = np.float32(1.0 / tokens.shape[1])
+        mean = lambda value: jnp.sum(fold_lanes(value), axis=-1, keepdims=True) * share
+        centred = tokens - mean(tokens)
+        inverse = lax.rsqrt(mean(centred * centred) + EPSILON)
+        scaled = centred * inverse
+        change = (back - mean(back) - scaled * mean(back * scaled)) * inverse
+        grad[rows, :] = (d[rows, :].astype(F32) + change).astype(BF16)
+        return carry
+
+    lax.fori_loop(0, x.shape[0] // ROW_CHUNK, some_rows, 0, unroll=2)
 
 
 def finish(x, d, own, parts, first_bias, second_bias):
-    rows, features = x.shape
-    block = min(rows, 128)
-    mine, other, place = own
-    flat = pl.BlockSpec((block, features), lambda i: (i, 0))
-    half = pl.BlockSpec((1, 2, block, features), lambda i: (place, 0, i, 0))
-    pair = pl.BlockSpec((2, block, features), lambda i: (0, i, 0))
-    row = pl.BlockSpec((1, features), lambda i: (0, 0))
-    return pl.pallas_call(
-        finish_body,
-        grid=(rows // block,),
-        in_specs=[flat, flat, half, half, pair, pair, pair, row, row],
-        out_specs=[flat, flat],
-        out_shape=[jax.ShapeDtypeStruct((rows, features), BF16)] * 2,
-        name="finish",
-    )(x, d, mine, other, *parts, first_bias, second_bias)
+    shapes = [jax.ShapeDtypeStruct(x.shape, BF16)] * 2
+    arrays = [first_bias, second_bias, x, d, *own, *parts]
+    return staged_call(finish_body, [], arrays, shapes)
 
 
 def on_device(
@@ -842,7 +901,7 @@
     start = jnp.sum(earlier.astype(jnp.int32), axis=1)
     start = jnp.concatenate([start // 256, start % 256]).astype(BF16)
     turns = jnp.concatenate([jnp.cos(angles), jnp.sin(angles)], axis=1)
-    message = join_message(
+    message, cotangent_sum = join_message(
         inputs, output_grad, *low_parts(turns, 3), jnp.broadcast_to(start[None], turns.shape)
     )
 
@@ -900,13 +959,13 @@
             carried,
             group is MLP_GROUPS[-1],
         )
-        (mine, other), mlp_sums, carried = results
-        other = swap_cores(other)
+        outs, mlp_sums, carried = results
         for place, s in enumerate(group):
+            mine, other = outs[2 * place], swap_cores(outs[2 * place + 1])
             if s == 0:
-                own_halves = mine, other, place
+                own_halves = mine, other
                 continue
-            sums_of[s] = add_halves(mine, other, place)
+            sums_of[s] = add_halves(mine, other)
     mlp_grads = carried
 
     parts = [to_quad(sums_of[j], j) for j in range(1, QUAD)]
@@ -924,33 +983,12 @@
     own, received = reduce_layers(mlp_grads)
     grad_expand, grad_shrink = unpack_mlp(meta, own, received, hidden_cols)
 
-    place = core * QUAD + quarter
-    attend_full = lax.dynamic_update_slice_in_dim(
-        jnp.zeros((2 * attend_cols,), F32),
-        jnp.sum(attend_sums[1], axis=1),
-        place * (attend_cols // QUAD),
-        0,
-    )
-    hidden_full = lax.dynamic_update_slice_in_dim(
-        jnp.zeros((2 * hidden_cols,), F32),
-        jnp.sum(mlp_sums[1], axis=0),
-        place * (hidden_cols // QUAD),
-        0,
-    )
-    vector = jnp.concatenate(
-        [
-            jnp.sum(attend_sums[0].reshape(2, 8, features), axis=1).reshape(-1),
-            jnp.sum(mlp_sums[0].reshape(2, 8, features), axis=1).reshape(-1),
-            jnp.sum(output_grad.astype(F32), axis=0),
-            attend_full,
-            hidden_full,
-        ]
-    ).reshape(-1, 128)
+    sizes = [features] * 4 + [features] * 2 + [2 * attend_cols, 2 * hidden_cols]
+    vector = join_vector(meta, *attend_sums, *mlp_sums, cotangent_sum, sizes)
     vector = vector + swap_cores(vector)
     for bit in (1, 2):
         vector = vector + lax.ppermute(vector, "dp", xor_pairs(n_dp, bit))
     vectors = [vector] + [to_layer(vector, k) for k in range(1, count)]
-    sizes = [features] * 4 + [features] * 2 + [2 * attend_cols, 2 * hidden_cols]
     pieces = split_vector(vectors, sizes)
     return (
         outputs,

time: 349 us -> 332 us (0.951)
  Pallas kernels: 104 us -> 89.4 us
  waiting for transfers between devices: 185 us -> 171 us
  starting transfers between devices: 43 us -> 55.3 us
    ppermute x15, waiting for transfers between devices: 94.1 us -> 78.6 us  [to_layer(): return lax.ppermute(value, 'dp', xor_pairs(n_dp, bits * QUAD))]
    ppermute x15, starting transfers between devices: 19.4 us -> 30.6 us  [to_layer(): return lax.ppermute(value, 'dp', xor_pairs(n_dp, bits * QUAD))]
    pallas_call x10 -> x11, Pallas kernels: 24.4 us -> 15.3 us  [the longest x6 8.47 us: staged_call(): pl.pallas_call(whole, in_specs=[SMEM] * len(scalars) + [ANY] * count, out...]
    pallas_call x6 -> x5, Pallas kernels: 77.2 us -> 72 us  [branch(): results = call(*operands)]
  transfers between devices with their start and end apart: 43 -> 44, of which waited for: 18 -> 22; matrix products, arithmetic and copies ran while one was open for 2% -> 1% of each run, Pallas kernels for 16% -> 15%
where the time goes in v3:
time: 332 us; the launch traced here: 329 us
  waiting for transfers between devices  171 us (52%)
  Pallas kernels  89.4 us (27%)
  starting transfers between devices  55.3 us (17%)
  local copies, waits for them, and re-layouts  6.03 us (2%)
  other arithmetic  5.82 us (2%)
    ppermute x18, waiting for transfers between devices, to_quad(): return lax.ppermute(value, 'dp', xor_pairs(n_dp, j))  86.4 us
    ppermute x15, waiting for transfers between devices, to_layer(): return lax.ppermute(value, 'dp', xor_pairs(n_dp, bits * QUAD))  78.6 us
    pallas_call x5, Pallas kernels, branch(): results = call(*operands)  72 us
    ppermute x15, starting transfers between devices, to_layer(): return lax.ppermute(value, 'dp', xor_pairs(n_dp, bits * QUAD))  30.6 us
    ppermute x18, starting transfers between devices, to_quad(): return lax.ppermute(value, 'dp', xor_pairs(n_dp, j))  20.1 us
    pallas_call x6, Pallas kernels, staged_call(): pl.pallas_call(whole, in_specs=[SMEM] * len(scalars) + [ANY] * count, out...  8.47 us
  transfers between devices with their start and end apart: 44, of which 22 were waited for; matrix products, arithmetic and copies ran while one was open for 1% of the time, Pallas kernels for 15%

profile of v3, /device:TPU:10, one launch (start us, length us, event | category | flops | bytes accessed | tf_op | source)
XLA Modules:
  0.0 329.0 jit_solution(12413911017715603474)
XLA Ops:
  0.7 1.0 convert_reduce_fusion
  3.8 2.4 shard_map.263
  6.2 1.5 collective-permute-start.2
  8.2 1.4 collective-permute-start.17
  10.3 2.1 shard_map.264
  13.0 1.5 collective-permute-start.6
  14.5 44.8 %collective-permute-done.5 = bf16[64,512]{1,0:T(8,128)(2,1)S(1)} collective-permute-done((bf16[64,512]{1,0:T(8,128)(2,1)}, bf16[64,512]{1,0:T(8,128)(2,1)S(1)}, u32[]{:S(2)}, u32[]{:S(2)}) %collective-permute-start.5) | collective-permute-done | bytes 65568 | tf_op jit(solution)/shard_map/ppermute | solution.py:880
  59.8 1.4 collective-permute-start.7
  61.2 3.9 %collective-permute-done.7 = bf16[64,512]{1,0:T(8,128)(2,1)S(1)} collective-permute-done((bf16[64,512]{1,0:T(8,128)(2,1)}, bf16[64,512]{1,0:T(8,128)(2,1)S(1)}, u32[]{:S(2)}, u32[]{:S(2)}) %collective-permute-start.7) | collective-permute-done | bytes 65568 | tf_op jit(solution)/shard_map/ppermute | solution.py:880
  65.2 1.4 collective-permute-start.12
  67.1 4.2 %collective-permute-done.12 = bf16[2,64,512]{2,1,0:T(8,128)(2,1)S(1)} collective-permute-done((bf16[2,64,512]{2,1,0:T(8,128)(2,1)}, bf16[2,64,512]{2,1,0:T(8,128)(2,1)S(1)}, u32[]{:S(2)}, u32[]{:S(2)}) %collective-permute-start.12) | collective-permute-done | bytes 131104 | tf_op jit(solution)/shard_map/ppermute | solution.py:880
  71.3 1.4 collective-permute-start.13
  72.7 0.9 pad_maximum_fusion.1.refs_6_
  73.6 3.8 %collective-permute-done.13 = bf16[2,64,512]{2,1,0:T(8,128)(2,1)S(1)} collective-permute-done((bf16[2,64,512]{2,1,0:T(8,128)(2,1)}, bf16[2,64,512]{2,1,0:T(8,128)(2,1)S(1)}, u32[]{:S(2)}, u32[]{:S(2)}) %collective-permute-start.13) | collective-permute-done | bytes 131104 | tf_op jit(solution)/shard_map/ppermute | solution.py:880
  77.4 2.6 collective-permute-start.9
  80.0 10.0 %collective-permute-done.9.refs_8_ = bf16[4,64,512]{2,1,0:T(8,128)(2,1)} collective-permute-done((bf16[4,64,512]{2,1,0:T(8,128)(2,1)S(1)}, bf16[4,64,512]{2,1,0:T(8,128)(2,1)}, u32[]{:S(2)}, u32[]{:S(2)}) %collective-permute-start.9) | collective-permute-done | bytes 262176 | tf_op jit(solution)/shard_map/ppermute | solution.py:883
  90.1 1.5 collective-permute-start.8
  91.5 6.8 %collective-permute-done.8.refs_7_ = bf16[4,64,512]{2,1,0:T(8,128)(2,1)S(1)} collective-permute-done((bf16[4,64,512]{2,1,0:T(8,128)(2,1)S(1)}, bf16[4,64,512]{2,1,0:T(8,128)(2,1)S(1)}, u32[]{:S(2)}, u32[]{:S(2)}) %collective-permute-start.8) | collective-permute-done | bytes 262176 | tf_op jit(solution)/shard_map/ppermute | solution.py:883
  100.1 1.0 pad_maximum_fusion.refs_8_.refs_16_
  101.1 5.6 %collective-permute-done.10.refs_9_ = bf16[4,64,512]{2,1,0:T(8,128)(2,1)} collective-permute-done((bf16[4,64,512]{2,1,0:T(8,128)(2,1)}, bf16[4,64,512]{2,1,0:T(8,128)(2,1)}, u32[]{:S(2)}, u32[]{:S(2)}) %collective-permute-start.10) | collective-permute-done | bytes 262176 | tf_op jit(solution)/shard_map/ppermute | solution.py:883
  106.7 2.6 collective-permute-start.16
  109.3 0.9 collective-permute-start.15
  111.0 9.9 %shard_map.265 = (bf16[1,512,1024]{2,1,0:T(8,128)(2,1)}, bf16[1,512,1024]{2,1,0:T(8,128)(2,1)}, f32[16,1024]{1,0:T(8,128)}, f32[384,128]{1,0:T(8,128)}, f32[1,51...) custom-call(s32[3]{0:T(128)} %pad_add_fusion.meta.refs_0_, f32[1,1024]{1,0:T(1,128)} %bitcast.45, f32[1,1024]{1,0:T(1,128)} %bitcast.48, ...), custom_call_target="tpu_custom_call" | custom-call | flops 2080374784 | bytes 9437184 | tf_op jit(solution)/shard_map/pallas_call | solution.py:811
  120.9 1.5 collective-permute-start.14
  122.4 15.8 %shard_map.266 = (bf16[2,512,1024]{2,1,0:T(8,128)(2,1)}, bf16[2,512,1024]{2,1,0:T(8,128)(2,1)}, f32[16,1024]{1,0:T(8,128)}, f32[384,128]{1,0:T(8,128)}, f32[1,512,1024]{2,1,0:T(8,128)}) custom-call(s32[3]{0:T(128)} %pad_add_fusion.meta.refs_0_, f32[1,1024]{1,0:T(1,128)} %bitcast.46, f32[1,1024]{1,0:T(1,128)} %bitcast.49, ...), custom_call_target="tpu_custom_call" | custom-call | flops 4160749568 | bytes 13631488 | tf_op jit(solution)/shard_map/pallas_call | solution.py:811
  138.3 10.4 %shard_map.267 = (bf16[1,512,1024]{2,1,0:T(8,128)(2,1)}, bf16[1,512,1024]{2,1,0:T(8,128)(2,1)}, f32[16,1024]{1,0:T(8,128)}, f32[384,128]{1,0:T(8,128)}, f32[4,64...) custom-call(s32[3]{0:T(128)} %pad_add_fusion.meta.refs_0_, ...), custom_call_target="tpu_custom_call" | custom-call | flops 2080374784 | bytes 9437184 | tf_op jit(solution)/shard_map/pallas_call | solution.py:811
  148.7 4.2 %collective-permute-done.15.refs_10_.refs_18_ = bf16[4,2,64,512]{3,2,1,0:T(8,128)(2,1)} collective-permute-done((bf16[4,2,64,512]{3,2,1,0:T(8,128)(2,1)S(1)}, bf16[4,2,64,512]{3,2,1,0:T(8,128)(2,1)}, u32[]{:S(2)}, u32[]{:S(2)}) %collective-permute-start.15) | collective-permute-done | bytes 524320 | tf_op jit(solution)/shard_map/ppermute | solution.py:883
  153.7 10.2 %shard_map.268 = (bf16[2,256,1024]{2,1,0:T(8,128)(2,1)}, bf16[2,256,1024]{2,1,0:T(8,128)(2,1)}, f32[16,1024]{1,0:T(8,128)}, f32[8,512]{1,0:T(8,128)}, f32[2,512,1024]{2,1,0:T(8,128)}) custom-call(s32[3]{0:T(128)} %pad_add_fusion.meta.refs_0_, f32[1,1024]{1,0:T(1,128)} %bitcast.51, f32[1,1024]{1,0:T(1,128)} %bitcast.53, ...), custom_call_target="tpu_custom_call" | custom-call | flops 3221225472 | bytes 14680064 | tf_op jit(solution)/shard_map/pallas_call | solution.py:811
  163.9 25.7 %shard_map.269 = (bf16[2,256,1024]{2,1,0:T(8,128)(2,1)}, bf16[2,256,1024]{2,1,0:T(8,128)(2,1)}, bf16[2,256,1024]{2,1,0:T(8,128)(2,1)}, bf16[2,256,1024]{2,1,0:T(...) custom-call(s32[3]{0:T(128)} %pad_add_fusion.meta.refs_0_, ...), custom_call_target="tpu_custom_call" | custom-call | flops 9663676416 | bytes 23068672 | tf_op jit(solution)/shard_map/pallas_call | solution.py:811
  190.3 1.8 shard_map.274
  192.5 2.3 collective-permute-start.32
  194.8 0.9 collective-permute-done.26
  195.7 0.8 add.34
  196.5 1.5 collective-permute-start.27
  198.0 2.6 collective-permute-done.27
  200.6 1.5 collective-permute-start.28
  202.1 2.6 collective-permute-done.28
  204.8 0.9 collective-permute-start.31
  205.7 3.6 %collective-permute-done.31.refs_3_ = f32[96,128]{1,0:T(8,128)S(1)} collective-permute-done((f32[96,128]{1,0:T(8,128)S(1)}, f32[96,128]{1,0:T(8,128)S(1)}, u32[]{:S(2)}, u32[]{:S(2)}) %collective-permute-start.31) | collective-permute-done | bytes 49184 | tf_op jit(solution)/shard_map/ppermute | solution.py:883
  209.2 5.1 %collective-permute-start.30 = (f32[96,128]{1,0:T(8,128)S(1)}, f32[96,128]{1,0:T(8,128)S(1)}, u32[]{:S(2)}, u32[]{:S(2)}) collective-permute-start(f32[96,128]{1,0:T(8,128)S(1)} %add.36.refs_0_), channel_id=1, source_target_pairs={{0,16},{2,18},{4,20},{6,22},{8,24},{10,26},{12,28},{14,30},{16,0},... | collective-permute-start | bytes 147464 | tf_op jit(solution)/shard_map/ppermute | solution.py:883
  214.3 6.8 %collective-permute-done.30.refs_2_ = f32[96,128]{1,0:T(8,128)S(1)} collective-permute-done((f32[96,128]{1,0:T(8,128)S(1)}, f32[96,128]{1,0:T(8,128)S(1)}, u32[]{:S(2)}, u32[]{:S(2)}) %collective-permute-start.30) | collective-permute-done | bytes 49184 | tf_op jit(solution)/shard_map/ppermute | solution.py:883
  221.1 3.4 %collective-permute-start.33 = (bf16[4,64,512]{2,1,0:T(8,128)(2,1)}, bf16[4,64,512]{2,1,0:T(8,128)(2,1)S(1)}, u32[]{:S(2)}, u32[]{:S(2)}) collective-permute-start(bf16[4,64,512]{2,1,0:T(8,128)(2,1)} %get-tuple-element.128), channel_id=1, source_target_pairs={{0,16},{2,18},{4,20},{6,22},{8,24},{10,26},{12,28},{14,30},{16,0},... | collective-permute-start | bytes 786440 | tf_op jit(solution)/shard_map/ppermute | solution.py:883
  224.5 1.4 collective-permute-start.34
  225.9 8.2 %collective-permute-done.33.refs_2_ = bf16[4,64,512]{2,1,0:T(8,128)(2,1)S(1)} collective-permute-done((bf16[4,64,512]{2,1,0:T(8,128)(2,1)}, bf16[4,64,512]{2,1,0:T(8,128)(2,1)S(1)}, u32[]{:S(2)}, u32[]{:S(2)}) %collective-permute-start.33) | collective-permute-done | bytes 262176 | tf_op jit(solution)/shard_map/ppermute | solution.py:883
  234.2 4.8 %collective-permute-start.38 = (bf16[4,2,64,512]{3,2,1,0:T(8,128)(2,1)}, bf16[4,2,64,512]{3,2,1,0:T(8,128)(2,1)S(1)}, u32[]{:S(2)}, u32[]{:S(2)}) collective-permute-start(bf16[4,2,64,512]{3,2,1,0:T(8,128)(2,1)} %get-tuple-element.139), channel_id=1, source_target_pairs={{0,8},{2,10},{4,12},{6,14},{8,0},{10,2},{12,4},{14,6},{16,24},{18,... | collective-permute-start | bytes 1572872 | tf_op jit(solution)/shard_map/ppermute | solution.py:883
  238.9 9.8 %collective-permute-done.34.refs_3_ = bf16[4,64,512]{2,1,0:T(8,128)(2,1)S(1)} collective-permute-done((bf16[4,64,512]{2,1,0:T(8,128)(2,1)S(1)}, bf16[4,64,512]{2,1,0:T(8,128)(2,1)S(1)}, u32[]{:S(2)}, u32[]{:S(2)}) %collective-permute-start.34) | collective-permute-done | bytes 262176 | tf_op jit(solution)/shard_map/ppermute | solution.py:883
  248.7 1.0 copy-done.7
  250.0 1.5 collective-permute-start.35
  252.1 0.9 collective-permute-start.29
  255.4 1.6 shard_map.272
  257.5 1.5 collective-permute-start.21
  259.6 1.5 collective-permute-start.25
  261.3 2.4 collective-permute-start.40
  263.7 22.9 %collective-permute-done.40.refs_3_ = bf16[4,2,64,512]{3,2,1,0:T(8,128)(2,1)S(1)} collective-permute-done((bf16[4,2,64,512]{3,2,1,0:T(8,128)(2,1)S(1)}, bf16[4,2,64,512]{3,2,1,0:T(8,128)(2,1)S(1)}, u32[]{:S(2)}, u32[]{:S(2)}) %collective-permute-start.40) | collective-permute-done | bytes 524320 | tf_op jit(solution)/shard_map/ppermute | solution.py:883
  286.6 1.4 collective-permute-start.37
  288.5 19.4 %collective-permute-done.37.refs_4_ = bf16[64,512]{1,0:T(8,128)(2,1)S(1)} collective-permute-done((bf16[64,512]{1,0:T(8,128)(2,1)S(1)}, bf16[64,512]{1,0:T(8,128)(2,1)S(1)}, u32[]{:S(2)}, u32[]{:S(2)}) %collective-permute-start.37) | collective-permute-done | bytes 65568 | tf_op jit(solution)/shard_map/ppermute | solution.py:880
  308.5 4.4 %collective-permute-done.41.refs_2_ = bf16[2,64,512]{2,1,0:T(8,128)(2,1)S(1)} collective-permute-done((bf16[2,64,512]{2,1,0:T(8,128)(2,1)S(1)}, bf16[2,64,512]{2,1,0:T(8,128)(2,1)S(1)}, u32[]{:S(2)}, u32[]{:S(2)}) %collective-permute-start.41) | collective-permute-done | bytes 131104 | tf_op jit(solution)/shard_map/ppermute | solution.py:880
  313.5 4.4 %collective-permute-done.42.refs_3_ = bf16[2,64,512]{2,1,0:T(8,128)(2,1)S(1)} collective-permute-done((bf16[2,64,512]{2,1,0:T(8,128)(2,1)S(1)}, bf16[2,64,512]{2,1,0:T(8,128)(2,1)S(1)}, u32[]{:S(2)}, u32[]{:S(2)}) %collective-permute-start.42) | collective-permute-done | bytes 131104 | tf_op jit(solution)/shard_map/ppermute | solution.py:880
  317.8 1.5 collective-permute-start.43
  319.4 0.9 shard_map.275
  320.3 1.8 shard_map.277
  322.1 1.6 collective-permute-done.43.refs_4_
  323.7 2.1 shard_map.279
  325.9 2.9 shard_map.273
  (104 shorter events, 15.6 us)
Async XLA Ops:
  3.8 95.7 %copy-start.13 = (f32[1536]{0:T(1024)S(1)}, f32[1536]{0:T(1024)}, u32[]{:S(2)}) copy-start(f32[1536]{0:T(1024)} %param.24) | copy-start | bytes 18436
  3.8 95.7 %copy-start.14 = (f32[2048]{0:T(1024)S(1)}, f32[2048]{0:T(1024)}, u32[]{:S(2)}) copy-start(f32[2048]{0:T(1024)} %param.28) | copy-start | bytes 24580
  6.2 60.4 %collective-permute-start.2 = (bf16[544,1024]{1,0:T(8,128)(2,1)}, bf16[544,1024]{1,0:T(8,128)(2,1)S(1)}, u32[]{:S(2)}, u32[]{:S(2)}) collective-permute-start(bf16[544,1024]{1,0:T(8,128)(2,1)} %get-tuple-element.82.refs_4_.refs_8_), channel_id=1, source_target_pairs={{0,4},{2,6},{4,0},{6,2},{8,12},{10,14},{12,8},{14,10},{16,20},{18,... | collective-permute-start | bytes 3342344 | tf_op jit(solution)/shard_map/ppermute | solution.py:880
  7.7 59.1 %collective-permute-start = (bf16[544,1024]{1,0:T(8,128)(2,1)}, bf16[544,1024]{1,0:T(8,128)(2,1)S(1)}, u32[]{:S(2)}, u32[]{:S(2)}) collective-permute-start(bf16[544,1024]{1,0:T(8,128)(2,1)} %get-tuple-element.82.refs_4_.refs_8_), channel_id=1, source_target_pairs={{0,2},{2,0},{4,6},{6,4},{8,10},{10,8},{12,14},{14,12},{16,18},{18,... | collective-permute-start | bytes 3342344 | tf_op jit(solution)/shard_map/ppermute | solution.py:880
  8.2 71.8 %collective-permute-start.17 = (bf16[544,1024]{1,0:T(8,128)(2,1)}, bf16[544,1024]{1,0:T(8,128)(2,1)}, u32[]{:S(2)}, u32[]{:S(2)}) collective-permute-start(bf16[544,1024]{1,0:T(8,128)(2,1)} %get-tuple-element.82.refs_4_.refs_8_), channel_id=1, source_target_pairs={{0,6},{2,4},{4,2},{6,0},{8,14},{10,12},{12,10},{14,8},{16,22},{18,... | collective-permute-start | bytes 3342344 | tf_op jit(solution)/shard_map/ppermute | solution.py:880
  12.4 46.8 %collective-permute-start.5 = (bf16[64,512]{1,0:T(8,128)(2,1)}, bf16[64,512]{1,0:T(8,128)(2,1)S(1)}, u32[]{:S(2)}, u32[]{:S(2)}) collective-permute-start(bf16[64,512]{1,0:T(8,128)(2,1)} %get-tuple-element.84), channel_id=1, source_target_pairs={{0,2},{2,0},{4,6},{6,4},{8,10},{10,8},{12,14},{14,12},{16,18},{18,... | collective-permute-start | bytes 196616 | tf_op jit(solution)/shard_map/ppermute | solution.py:880
  13.0 46.8 %collective-permute-start.6 = (bf16[64,512]{1,0:T(8,128)(2,1)}, bf16[64,512]{1,0:T(8,128)(2,1)S(1)}, u32[]{:S(2)}, u32[]{:S(2)}) collective-permute-start(bf16[64,512]{1,0:T(8,128)(2,1)} %get-tuple-element.85), channel_id=1, source_target_pairs={{0,4},{2,6},{4,0},{6,2},{8,12},{10,14},{12,8},{14,10},{16,20},{18,... | collective-permute-start | bytes 196616 | tf_op jit(solution)/shard_map/ppermute | solution.py:880
  59.2 5.9 %collective-permute-start.11 = (bf16[2,64,512]{2,1,0:T(8,128)(2,1)}, bf16[2,64,512]{2,1,0:T(8,128)(2,1)S(1)}, u32[]{:S(2)}, u32[]{:S(2)}) collective-permute-start(bf16[2,64,512]{2,1,0:T(8,128)(2,1)} %get-tuple-element.96), channel_id=1, source_target_pairs={{0,2},{2,0},{4,6},{6,4},{8,10},{10,8},{12,14},{14,12},{16,18},{18,... | collective-permute-start | bytes 393224 | tf_op jit(solution)/shard_map/ppermute | solution.py:880
  59.8 5.4 %collective-permute-start.7 = (bf16[64,512]{1,0:T(8,128)(2,1)}, bf16[64,512]{1,0:T(8,128)(2,1)S(1)}, u32[]{:S(2)}, u32[]{:S(2)}) collective-permute-start(bf16[64,512]{1,0:T(8,128)(2,1)} %get-tuple-element.86), channel_id=1, source_target_pairs={{0,6},{2,4},{4,2},{6,0},{8,14},{10,12},{12,10},{14,8},{16,22},{18,... | collective-permute-start | bytes 196616 | tf_op jit(solution)/shard_map/ppermute | solution.py:880
  65.1 44.1 %collective-permute-start.4 = (bf16[544,1024]{1,0:T(8,128)(2,1)}, bf16[544,1024]{1,0:T(8,128)(2,1)}, u32[]{:S(2)}, u32[]{:S(2)}) collective-permute-start(bf16[544,1024]{1,0:T(8,128)(2,1)} %get-tuple-element.82.refs_4_.refs_8_), channel_id=1, source_target_pairs={{0,1},{1,0},{2,3},{3,2},{4,5},{5,4},{6,7},{7,6},{8,9},{9,8},{10,11... | collective-permute-start | bytes 3342344 | tf_op jit(solution)/shard_map/ppermute | solution.py:50
  65.2 6.1 %collective-permute-start.12 = (bf16[2,64,512]{2,1,0:T(8,128)(2,1)}, bf16[2,64,512]{2,1,0:T(8,128)(2,1)S(1)}, u32[]{:S(2)}, u32[]{:S(2)}) collective-permute-start(bf16[2,64,512]{2,1,0:T(8,128)(2,1)} %get-tuple-element.97), channel_id=1, source_target_pairs={{0,4},{2,6},{4,0},{6,2},{8,12},{10,14},{12,8},{14,10},{16,20},{18,... | collective-permute-start | bytes 393224 | tf_op jit(solution)/shard_map/ppermute | solution.py:880
  66.6 54.3 %copy-start.15 = (bf16[544,1024]{1,0:T(8,128)(2,1)}, bf16[544,1024]{1,0:T(8,128)(2,1)S(1)}, u32[]{:S(2)}) copy-start(bf16[544,1024]{1,0:T(8,128)(2,1)S(1)} %collective-permute-done.2.refs_6_) | copy-start | bytes 3342340
  66.6 54.3 %collective-permute-start.3 = (bf16[544,1024]{1,0:T(8,128)(2,1)S(1)}, bf16[544,1024]{1,0:T(8,128)(2,1)}, u32[]{:S(2)}, u32[]{:S(2)}) collective-permute-start(bf16[544,1024]{1,0:T(8,128)(2,1)S(1)} %collective-permute-done.2.refs_6_), channel_id=1, source_target_pairs={{0,1},{1,0},{2,3},{3,2},{4,5},{5,4},{6,7},{7,6},{8,9},{9,8},{10,11... | collective-permute-start | bytes 3342344 | tf_op jit(solution)/shard_map/ppermute | solution.py:50
  66.8 54.1 %copy-start.16 = (bf16[544,1024]{1,0:T(8,128)(2,1)}, bf16[544,1024]{1,0:T(8,128)(2,1)S(1)}, u32[]{:S(2)}) copy-start(bf16[544,1024]{1,0:T(8,128)(2,1)S(1)} %collective-permute-done.refs_4_) | copy-start | bytes 3342340
  66.8 55.6 %collective-permute-start.1 = (bf16[544,1024]{1,0:T(8,128)(2,1)S(1)}, bf16[544,1024]{1,0:T(8,128)(2,1)}, u32[]{:S(2)}, u32[]{:S(2)}) collective-permute-start(bf16[544,1024]{1,0:T(8,128)(2,1)S(1)} %collective-permute-done.refs_4_), channel_id=1, source_target_pairs={{0,1},{1,0},{2,3},{3,2},{4,5},{5,4},{6,7},{7,6},{8,9},{9,8},{10,11... | collective-permute-start | bytes 3342344 | tf_op jit(solution)/shard_map/ppermute | solution.py:50
  71.3 6.2 %collective-permute-start.13 = (bf16[2,64,512]{2,1,0:T(8,128)(2,1)}, bf16[2,64,512]{2,1,0:T(8,128)(2,1)S(1)}, u32[]{:S(2)}, u32[]{:S(2)}) collective-permute-start(bf16[2,64,512]{2,1,0:T(8,128)(2,1)} %get-tuple-element.98), channel_id=1, source_target_pairs={{0,6},{2,4},{4,2},{6,0},{8,14},{10,12},{12,10},{14,8},{16,22},{18,... | collective-permute-start | bytes 393224 | tf_op jit(solution)/shard_map/ppermute | solution.py:880
  73.6 37.4 %copy-start.12 = (bf16[4,64,512]{2,1,0:T(8,128)(2,1)}, bf16[4,64,512]{2,1,0:T(8,128)(2,1)S(1)}, u32[]{:S(2)}) copy-start(bf16[4,64,512]{2,1,0:T(8,128)(2,1)S(1)} %pad_maximum_fusion.1.refs_6_) | copy-start | bytes 786436
  77.4 12.6 %collective-permute-start.9 = (bf16[4,64,512]{2,1,0:T(8,128)(2,1)S(1)}, bf16[4,64,512]{2,1,0:T(8,128)(2,1)}, u32[]{:S(2)}, u32[]{:S(2)}) collective-permute-start(bf16[4,64,512]{2,1,0:T(8,128)(2,1)S(1)} %pad_maximum_fusion.1.refs_6_), channel_id=1, source_target_pairs={{0,16},{2,18},{4,20},{6,22},{8,24},{10,26},{12,28},{14,30},{16,0},... | collective-permute-start | bytes 786440 | tf_op jit(solution)/shard_map/ppermute | solution.py:883
  80.0 58.2 %collective-permute-start.18 = (bf16[544,1024]{1,0:T(8,128)(2,1)}, bf16[544,1024]{1,0:T(8,128)(2,1)}, u32[]{:S(2)}, u32[]{:S(2)}) collective-permute-start(bf16[544,1024]{1,0:T(8,128)(2,1)} %collective-permute-done.17.refs_4_), channel_id=1, source_target_pairs={{0,1},{1,0},{2,3},{3,2},{4,5},{5,4},{6,7},{7,6},{8,9},{9,8},{10,11... | collective-permute-start | bytes 3342344 | tf_op jit(solution)/shard_map/ppermute | solution.py:50
  90.1 8.2 %collective-permute-start.8 = (bf16[4,64,512]{2,1,0:T(8,128)(2,1)S(1)}, bf16[4,64,512]{2,1,0:T(8,128)(2,1)S(1)}, u32[]{:S(2)}, u32[]{:S(2)}) collective-permute-start(bf16[4,64,512]{2,1,0:T(8,128)(2,1)S(1)} %pad_maximum_fusion.1.refs_6_), channel_id=1, source_target_pairs={{0,8},{2,10},{4,12},{6,14},{8,0},{10,2},{12,4},{14,6},{16,24},{18,... | collective-permute-start | bytes 786440 | tf_op jit(solution)/shard_map/ppermute | solution.py:883
  99.0 7.7 %collective-permute-start.10 = (bf16[4,64,512]{2,1,0:T(8,128)(2,1)}, bf16[4,64,512]{2,1,0:T(8,128)(2,1)}, u32[]{:S(2)}, u32[]{:S(2)}) collective-permute-start(bf16[4,64,512]{2,1,0:T(8,128)(2,1)} %collective-permute-done.9.refs_8_), channel_id=1, source_target_pairs={{0,8},{2,10},{4,12},{6,14},{8,0},{10,2},{12,4},{14,6},{16,24},{18,... | collective-permute-start | bytes 786440 | tf_op jit(solution)/shard_map/ppermute | solution.py:883
  101.0 19.9 %copy-start.11 = (bf16[4,2,64,512]{3,2,1,0:T(8,128)(2,1)}, bf16[4,2,64,512]{3,2,1,0:T(8,128)(2,1)S(1)}, u32[]{:S(2)}) copy-start(bf16[4,2,64,512]{3,2,1,0:T(8,128)(2,1)S(1)} %pad_maximum_fusion.refs_8_.refs_16_) | copy-start | bytes 1572868
  106.7 42.1 %collective-permute-start.16 = (bf16[4,2,64,512]{3,2,1,0:T(8,128)(2,1)S(1)}, bf16[4,2,64,512]{3,2,1,0:T(8,128)(2,1)}, u32[]{:S(2)}, u32[]{:S(2)}) collective-permute-start(bf16[4,2,64,512]{3,2,1,0:T(8,128)(2,1)S(1)} %pad_maximum_fusion.refs_8_.refs_16_), channel_id=1, source_target_pairs={{0,24},{2,26},{4,28},{6,30},{8,16},{10,18},{12,20},{14,22},{16,8},... | collective-permute-start | bytes 1572872 | tf_op jit(solution)/shard_map/ppermute | solution.py:883
  109.3 43.6 %collective-permute-start.15 = (bf16[4,2,64,512]{3,2,1,0:T(8,128)(2,1)S(1)}, bf16[4,2,64,512]{3,2,1,0:T(8,128)(2,1)}, u32[]{:S(2)}, u32[]{:S(2)}) collective-permute-start(bf16[4,2,64,512]{3,2,1,0:T(8,128)(2,1)S(1)} %pad_maximum_fusion.refs_8_.refs_16_), channel_id=1, source_target_pairs={{0,16},{2,18},{4,20},{6,22},{8,24},{10,26},{12,28},{14,30},{16,0},... | collective-permute-start | bytes 1572872 | tf_op jit(solution)/shard_map/ppermute | solution.py:883
  120.9 32.0 %collective-permute-start.14 = (bf16[4,2,64,512]{3,2,1,0:T(8,128)(2,1)S(1)}, bf16[4,2,64,512]{3,2,1,0:T(8,128)(2,1)S(1)}, u32[]{:S(2)}, u32[]{:S(2)}) collective-permute-start(bf16[4,2,64,512]{3,2,1,0:T(8,128)(2,1)S(1)} %pad_maximum_fusion.refs_8_.refs_16_), channel_id=1, source_target_pairs={{0,8},{2,10},{4,12},{6,14},{8,0},{10,2},{12,4},{14,6},{16,24},{18,... | collective-permute-start | bytes 1572872 | tf_op jit(solution)/shard_map/ppermute | solution.py:883
  163.9 60.6 %copy-start.20 = (bf16[4,64,512]{2,1,0:T(8,128)(2,1)S(1)}, bf16[4,64,512]{2,1,0:T(8,128)(2,1)}, u32[]{:S(2)}) copy-start(bf16[4,64,512]{2,1,0:T(8,128)(2,1)} %get-tuple-element.129) | copy-start | bytes 786436
  189.6 63.3 %copy-start.4 = (bf16[2,256,1024]{2,1,0:T(8,128)(2,1)S(1)}, bf16[2,256,1024]{2,1,0:T(8,128)(2,1)}, u32[]{:S(2)}) copy-start(bf16[2,256,1024]{2,1,0:T(8,128)(2,1)} %get-tuple-element.109.mine) | copy-start | bytes 3145732
  189.6 60.3 %collective-permute-start.20 = (bf16[2,256,1024]{2,1,0:T(8,128)(2,1)}, bf16[2,256,1024]{2,1,0:T(8,128)(2,1)S(1)}, u32[]{:S(2)}, u32[]{:S(2)}) collective-permute-start(bf16[2,256,1024]{2,1,0:T(8,128)(2,1)} %get-tuple-element.110), channel_id=1, source_target_pairs={{0,1},{1,0},{2,3},{3,2},{4,5},{5,4},{6,7},{7,6},{8,9},{9,8},{10,11... | collective-permute-start | bytes 3145736 | tf_op jit(solution)/shard_map/ppermute | solution.py:50
  189.7 61.8 %collective-permute-start.22 = (bf16[2,256,1024]{2,1,0:T(8,128)(2,1)}, bf16[2,256,1024]{2,1,0:T(8,128)(2,1)S(1)}, u32[]{:S(2)}, u32[]{:S(2)}) collective-permute-start(bf16[2,256,1024]{2,1,0:T(8,128)(2,1)} %get-tuple-element.112), channel_id=1, source_target_pairs={{0,1},{1,0},{2,3},{3,2},{4,5},{5,4},{6,7},{7,6},{8,9},{9,8},{10,11... | collective-permute-start | bytes 3145736 | tf_op jit(solution)/shard_map/ppermute | solution.py:50
  190.2 61.8 %collective-permute-start.24 = (bf16[2,256,1024]{2,1,0:T(8,128)(2,1)}, bf16[2,256,1024]{2,1,0:T(8,128)(2,1)}, u32[]{:S(2)}, u32[]{:S(2)}) collective-permute-start(bf16[2,256,1024]{2,1,0:T(8,128)(2,1)} %get-tuple-element.114), channel_id=1, source_target_pairs={{0,1},{1,0},{2,3},{3,2},{4,5},{5,4},{6,7},{7,6},{8,9},{9,8},{10,11... | collective-permute-start | bytes 3145736 | tf_op jit(solution)/shard_map/ppermute | solution.py:50
  192.0 3.7 %collective-permute-start.26 = (f32[96,128]{1,0:T(8,128)}, f32[96,128]{1,0:T(8,128)S(1)}, u32[]{:S(2)}, u32[]{:S(2)}) collective-permute-start(f32[96,128]{1,0:T(8,128)} %shard_map.274), channel_id=1, source_target_pairs={{0,1},{1,0},{2,3},{3,2},{4,5},{5,4},{6,7},{7,6},{8,9},{9,8},{10,11... | collective-permute-start | bytes 147464 | tf_op jit(solution)/shard_map/ppermute | solution.py:50
  192.5 32.0 %collective-permute-start.32 = (bf16[4,64,512]{2,1,0:T(8,128)(2,1)}, bf16[4,64,512]{2,1,0:T(8,128)(2,1)S(1)}, u32[]{:S(2)}, u32[]{:S(2)}) collective-permute-start(bf16[4,64,512]{2,1,0:T(8,128)(2,1)} %get-tuple-element.127), channel_id=1, source_target_pairs={{0,8},{2,10},{4,12},{6,14},{8,0},{10,2},{12,4},{14,6},{16,24},{18,... | collective-permute-start | bytes 786440 | tf_op jit(solution)/shard_map/ppermute | solution.py:883
  196.5 4.1 %collective-permute-start.27 = (f32[96,128]{1,0:T(8,128)S(1)}, f32[96,128]{1,0:T(8,128)S(1)}, u32[]{:S(2)}, u32[]{:S(2)}) collective-permute-start(f32[96,128]{1,0:T(8,128)S(1)} %add.34), channel_id=1, source_target_pairs={{0,2},{2,0},{4,6},{6,4},{8,10},{10,8},{12,14},{14,12},{16,18},{18,... | collective-permute-start | bytes 147464 | tf_op jit(solution)/shard_map/ppermute | solution.py:990
  200.6 4.2 %collective-permute-start.28 = (f32[96,128]{1,0:T(8,128)S(1)}, f32[96,128]{1,0:T(8,128)S(1)}, u32[]{:S(2)}, u32[]{:S(2)}) collective-permute-start(f32[96,128]{1,0:T(8,128)S(1)} %add.35), channel_id=1, source_target_pairs={{0,4},{2,6},{4,0},{6,2},{8,12},{10,14},{12,8},{14,10},{16,20},{18,... | collective-permute-start | bytes 147464 | tf_op jit(solution)/shard_map/ppermute | solution.py:990
  204.8 4.5 %collective-permute-start.31 = (f32[96,128]{1,0:T(8,128)S(1)}, f32[96,128]{1,0:T(8,128)S(1)}, u32[]{:S(2)}, u32[]{:S(2)}) collective-permute-start(f32[96,128]{1,0:T(8,128)S(1)} %add.36.refs_0_), channel_id=1, source_target_pairs={{0,24},{2,26},{4,28},{6,30},{8,16},{10,18},{12,20},{14,22},{16,8},... | collective-permute-start | bytes 147464 | tf_op jit(solution)/shard_map/ppermute | solution.py:883
  209.2 11.8 %collective-permute-start.30 = (f32[96,128]{1,0:T(8,128)S(1)}, f32[96,128]{1,0:T(8,128)S(1)}, u32[]{:S(2)}, u32[]{:S(2)}) collective-permute-start(f32[96,128]{1,0:T(8,128)S(1)} %add.36.refs_0_), channel_id=1, source_target_pairs={{0,16},{2,18},{4,20},{6,22},{8,24},{10,26},{12,28},{14,30},{16,0},... | collective-permute-start | bytes 147464 | tf_op jit(solution)/shard_map/ppermute | solution.py:883
  221.1 13.1 %collective-permute-start.33 = (bf16[4,64,512]{2,1,0:T(8,128)(2,1)}, bf16[4,64,512]{2,1,0:T(8,128)(2,1)S(1)}, u32[]{:S(2)}, u32[]{:S(2)}) collective-permute-start(bf16[4,64,512]{2,1,0:T(8,128)(2,1)} %get-tuple-element.128), channel_id=1, source_target_pairs={{0,16},{2,18},{4,20},{6,22},{8,24},{10,26},{12,28},{14,30},{16,0},... | collective-permute-start | bytes 786440 | tf_op jit(solution)/shard_map/ppermute | solution.py:883
  224.5 24.2 %collective-permute-start.34 = (bf16[4,64,512]{2,1,0:T(8,128)(2,1)S(1)}, bf16[4,64,512]{2,1,0:T(8,128)(2,1)S(1)}, u32[]{:S(2)}, u32[]{:S(2)}) collective-permute-start(bf16[4,64,512]{2,1,0:T(8,128)(2,1)S(1)} %copy-done.20), channel_id=1, source_target_pairs={{0,24},{2,26},{4,28},{6,30},{8,16},{10,18},{12,20},{14,22},{16,8},... | collective-permute-start | bytes 786440 | tf_op jit(solution)/shard_map/ppermute | solution.py:883
  234.2 25.4 %collective-permute-start.38 = (bf16[4,2,64,512]{3,2,1,0:T(8,128)(2,1)}, bf16[4,2,64,512]{3,2,1,0:T(8,128)(2,1)S(1)}, u32[]{:S(2)}, u32[]{:S(2)}) collective-permute-start(bf16[4,2,64,512]{3,2,1,0:T(8,128)(2,1)} %get-tuple-element.139), channel_id=1, source_target_pairs={{0,8},{2,10},{4,12},{6,14},{8,0},{10,2},{12,4},{14,6},{16,24},{18,... | collective-permute-start | bytes 1572872 | tf_op jit(solution)/shard_map/ppermute | solution.py:883
  248.7 12.6 %collective-permute-start.39 = (bf16[4,2,64,512]{3,2,1,0:T(8,128)(2,1)}, bf16[4,2,64,512]{3,2,1,0:T(8,128)(2,1)S(1)}, u32[]{:S(2)}, u32[]{:S(2)}) collective-permute-start(bf16[4,2,64,512]{3,2,1,0:T(8,128)(2,1)} %get-tuple-element.140), channel_id=1, source_target_pairs={{0,16},{2,18},{4,20},{6,22},{8,24},{10,26},{12,28},{14,30},{16,0},... | collective-permute-start | bytes 1572872 | tf_op jit(solution)/shard_map/ppermute | solution.py:883
  248.7 1.0 copy-start.7
  250.0 7.5 %collective-permute-start.35 = (bf16[64,512]{1,0:T(8,128)(2,1)S(1)}, bf16[64,512]{1,0:T(8,128)(2,1)S(1)}, u32[]{:S(2)}, u32[]{:S(2)}) collective-permute-start(bf16[64,512]{1,0:T(8,128)(2,1)S(1)} %get-tuple-element.131), channel_id=1, source_target_pairs={{0,2},{2,0},{4,6},{6,4},{8,10},{10,8},{12,14},{14,12},{16,18},{18,... | collective-permute-start | bytes 196616 | tf_op jit(solution)/shard_map/ppermute | solution.py:880
  251.5 7.5 %collective-permute-start.36 = (bf16[64,512]{1,0:T(8,128)(2,1)S(1)}, bf16[64,512]{1,0:T(8,128)(2,1)S(1)}, u32[]{:S(2)}, u32[]{:S(2)}) collective-permute-start(bf16[64,512]{1,0:T(8,128)(2,1)S(1)} %get-tuple-element.132), channel_id=1, source_target_pairs={{0,4},{2,6},{4,0},{6,2},{8,12},{10,14},{12,8},{14,10},{16,20},{18,... | collective-permute-start | bytes 196616 | tf_op jit(solution)/shard_map/ppermute | solution.py:880
  252.1 5.4 %collective-permute-start.29 = (f32[96,128]{1,0:T(8,128)S(1)}, f32[96,128]{1,0:T(8,128)S(1)}, u32[]{:S(2)}, u32[]{:S(2)}) collective-permute-start(f32[96,128]{1,0:T(8,128)S(1)} %add.36.refs_0_), channel_id=1, source_target_pairs={{0,8},{2,10},{4,12},{6,14},{8,0},{10,2},{12,4},{14,6},{16,24},{18,... | collective-permute-start | bytes 147464 | tf_op jit(solution)/shard_map/ppermute | solution.py:883
  252.9 1.2 copy-start.3
  254.1 1.2 copy-start.2
  255.4 2.1 copy-start.17
  255.4 5.9 %copy-start.18 = (bf16[4,2,64,512]{3,2,1,0:T(8,128)(2,1)S(1)}, bf16[4,2,64,512]{3,2,1,0:T(8,128)(2,1)}, u32[]{:S(2)}) copy-start(bf16[4,2,64,512]{3,2,1,0:T(8,128)(2,1)} %get-tuple-element.141) | copy-start | bytes 1572868
  255.4 32.7 %copy-start.5 = (f32[4,2,64,512]{3,2,1,0:T(8,128)S(1)}, f32[4,2,64,512]{3,2,1,0:T(8,128)}, u32[]{:S(2)}) copy-start(f32[4,2,64,512]{3,2,1,0:T(8,128)} %get-tuple-element.138.refs_0_) | copy-start | bytes 3145732
  257.5 68.4 %collective-permute-start.19 = (bf16[2,256,1024]{2,1,0:T(8,128)(2,1)S(1)}, bf16[2,256,1024]{2,1,0:T(8,128)(2,1)S(1)}, u32[]{:S(2)}, u32[]{:S(2)}) collective-permute-start(bf16[2,256,1024]{2,1,0:T(8,128)(2,1)S(1)} %copy-done.17), channel_id=1, source_target_pairs={{0,1},{1,0},{2,3},{3,2},{4,5},{5,4},{6,7},{7,6},{8,9},{9,8},{10,11... | collective-permute-start | bytes 3145736 | tf_op jit(solution)/shard_map/ppermute | solution.py:50
  257.5 68.4 %collective-permute-start.21 = (bf16[2,256,1024]{2,1,0:T(8,128)(2,1)S(1)}, bf16[2,256,1024]{2,1,0:T(8,128)(2,1)S(1)}, u32[]{:S(2)}, u32[]{:S(2)}) collective-permute-start(bf16[2,256,1024]{2,1,0:T(8,128)(2,1)S(1)} %shard_map.270), channel_id=1, source_target_pairs={{0,2},{2,0},{4,6},{6,4},{8,10},{10,8},{12,14},{14,12},{16,18},{18,... | collective-permute-start | bytes 3145736 | tf_op jit(solution)/shard_map/ppermute | solution.py:880
  259.0 66.8 %collective-permute-start.23 = (bf16[2,256,1024]{2,1,0:T(8,128)(2,1)S(1)}, bf16[2,256,1024]{2,1,0:T(8,128)(2,1)S(1)}, u32[]{:S(2)}, u32[]{:S(2)}) collective-permute-start(bf16[2,256,1024]{2,1,0:T(8,128)(2,1)S(1)} %shard_map.271), channel_id=1, source_target_pairs={{0,4},{2,6},{4,0},{6,2},{8,12},{10,14},{12,8},{14,10},{16,20},{18,... | collective-permute-start | bytes 3145736 | tf_op jit(solution)/shard_map/ppermute | solution.py:880
  259.6 66.3 %collective-permute-start.25 = (bf16[2,256,1024]{2,1,0:T(8,128)(2,1)S(1)}, bf16[2,256,1024]{2,1,0:T(8,128)(2,1)S(1)}, u32[]{:S(2)}, u32[]{:S(2)}) collective-permute-start(bf16[2,256,1024]{2,1,0:T(8,128)(2,1)S(1)} %shard_map.272), channel_id=1, source_target_pairs={{0,6},{2,4},{4,2},{6,0},{8,14},{10,12},{12,10},{14,8},{16,22},{18,... | collective-permute-start | bytes 3145736 | tf_op jit(solution)/shard_map/ppermute | solution.py:880
  261.3 25.3 %collective-permute-start.40 = (bf16[4,2,64,512]{3,2,1,0:T(8,128)(2,1)S(1)}, bf16[4,2,64,512]{3,2,1,0:T(8,128)(2,1)S(1)}, u32[]{:S(2)}, u32[]{:S(2)}) collective-permute-start(bf16[4,2,64,512]{3,2,1,0:T(8,128)(2,1)S(1)} %copy-done.18), channel_id=1, source_target_pairs={{0,24},{2,26},{4,28},{6,30},{8,16},{10,18},{12,20},{14,22},{16,8},... | collective-permute-start | bytes 1572872 | tf_op jit(solution)/shard_map/ppermute | solution.py:883
  286.6 21.3 %collective-permute-start.37 = (bf16[64,512]{1,0:T(8,128)(2,1)S(1)}, bf16[64,512]{1,0:T(8,128)(2,1)S(1)}, u32[]{:S(2)}, u32[]{:S(2)}) collective-permute-start(bf16[64,512]{1,0:T(8,128)(2,1)S(1)} %get-tuple-element.133), channel_id=1, source_target_pairs={{0,6},{2,4},{4,2},{6,0},{8,14},{10,12},{12,10},{14,8},{16,22},{18,... | collective-permute-start | bytes 196616 | tf_op jit(solution)/shard_map/ppermute | solution.py:880
  288.0 32.2 %copy-start.8 = (s32[3]{0:T(128)S(1)}, s32[3]{0:T(128)}, u32[]{:S(2)}) copy-start(s32[3]{0:T(128)} %pad_add_fusion.meta.refs_0_) | copy-start | bytes 40
  288.0 37.8 %copy-start.6 = (bf16[2,256,1024]{2,1,0:T(8,128)(2,1)S(1)}, bf16[2,256,1024]{2,1,0:T(8,128)(2,1)}, u32[]{:S(2)}) copy-start(bf16[2,256,1024]{2,1,0:T(8,128)(2,1)} %get-tuple-element.107.refs_4_) | copy-start | bytes 3145732
  288.5 37.4 %copy-start = (bf16[256,1024]{1,0:T(8,128)(2,1)S(1)}, bf16[256,1024]{1,0:T(8,128)(2,1)}, u32[]{:S(2)}) copy-start(bf16[256,1024]{1,0:T(8,128)(2,1)} %refs_2_.1) | copy-start | bytes 1572868
  288.5 37.4 %copy-start.1 = (bf16[256,1024]{1,0:T(8,128)(2,1)S(1)}, bf16[256,1024]{1,0:T(8,128)(2,1)}, u32[]{:S(2)}) copy-start(bf16[256,1024]{1,0:T(8,128)(2,1)} %refs_3_.1) | copy-start | bytes 1572868
  288.5 37.4 %copy-start.9 = (f32[1024]{0:T(1024)S(1)}, f32[1024]{0:T(1024)}, u32[]{:S(2)}) copy-start(f32[1024]{0:T(1024)} %param.26) | copy-start | bytes 12292
  288.5 37.4 %copy-start.10 = (f32[1024]{0:T(1024)S(1)}, f32[1024]{0:T(1024)}, u32[]{:S(2)}) copy-start(f32[1024]{0:T(1024)} %param.30) | copy-start | bytes 12292
  307.9 5.0 %collective-permute-start.41 = (bf16[2,64,512]{2,1,0:T(8,128)(2,1)S(1)}, bf16[2,64,512]{2,1,0:T(8,128)(2,1)S(1)}, u32[]{:S(2)}, u32[]{:S(2)}) collective-permute-start(bf16[2,64,512]{2,1,0:T(8,128)(2,1)S(1)} %get-tuple-element.143), channel_id=1, source_target_pairs={{0,2},{2,0},{4,6},{6,4},{8,10},{10,8},{12,14},{14,12},{16,18},{18,... | collective-permute-start | bytes 393224 | tf_op jit(solution)/shard_map/ppermute | solution.py:880
  312.9 5.0 %collective-permute-start.42 = (bf16[2,64,512]{2,1,0:T(8,128)(2,1)S(1)}, bf16[2,64,512]{2,1,0:T(8,128)(2,1)S(1)}, u32[]{:S(2)}, u32[]{:S(2)}) collective-permute-start(bf16[2,64,512]{2,1,0:T(8,128)(2,1)S(1)} %get-tuple-element.144), channel_id=1, source_target_pairs={{0,4},{2,6},{4,0},{6,2},{8,12},{10,14},{12,8},{14,10},{16,20},{18,... | collective-permute-start | bytes 393224 | tf_op jit(solution)/shard_map/ppermute | solution.py:880
  317.8 5.9 %collective-permute-start.43 = (bf16[2,64,512]{2,1,0:T(8,128)(2,1)S(1)}, bf16[2,64,512]{2,1,0:T(8,128)(2,1)S(1)}, u32[]{:S(2)}, u32[]{:S(2)}) collective-permute-start(bf16[2,64,512]{2,1,0:T(8,128)(2,1)S(1)} %get-tuple-element.145), channel_id=1, source_target_pairs={{0,6},{2,4},{4,2},{6,0},{8,14},{10,12},{12,10},{14,8},{16,22},{18,... | collective-permute-start | bytes 393224 | tf_op jit(solution)/shard_map/ppermute | solution.py:880
  (2 other events, 1.5 us)

commit v4 on v3

--- a/solution.py
+++ b/solution.py
@@ -379,7 +379,8 @@
             allowed = (key_at >= first) & (key_at <= query_at + block * QUERY_BLOCK)
             m.mask[block, :width, :] = jnp.where(allowed, 0.0, NEGATIVE)
 
-        projected = dot_nt(w[:heads, :], norm[...]) + widen(bias[...], length)
+        column = jnp.broadcast_to(bias[...], (128, heads)).T
+        projected = dot_nt(w[:heads, :], norm[...]) + widen(column, length)
         grad_context = dot_nt(w[heads:, :], cot[...]).astype(BF16)
         nothing = jnp.zeros((HD, length), BF16)
         for h in range(2):
@@ -919,9 +920,8 @@
 
     one_row = lambda vector: vector[None, :]
     bias_part = lax.dynamic_index_in_dim(
-        attend_bias.reshape(QUAD, attend_cols // QUAD), quarter, 0, False
+        attend_bias.reshape(QUAD, attend_cols // QUAD), quarter, 0, True
     )
-    bias_part = jnp.broadcast_to(bias_part[:, None], (attend_cols // QUAD, 128))
     hidden_part = lax.dynamic_index_in_dim(
         expand_bias.reshape(QUAD, hidden_cols // QUAD), quarter, 0, True
     )
@@ -986,8 +986,8 @@
     sizes = [features] * 4 + [features] * 2 + [2 * attend_cols, 2 * hidden_cols]
     vector = join_vector(meta, *attend_sums, *mlp_sums, cotangent_sum, sizes)
     vector = vector + swap_cores(vector)
-    for bit in (1, 2):
-        vector = vector + lax.ppermute(vector, "dp", xor_pairs(n_dp, bit))
+    near = [to_quad(vector, j) for j in range(1, QUAD)]
+    vector = (vector + near[0]) + (near[1] + near[2])
     vectors = [vector] + [to_layer(vector, k) for k in range(1, count)]
     pieces = split_vector(vectors, sizes)
     return (

time: 332 us -> 322 us (0.970)
  waiting for transfers between devices: 171 us -> 165 us
    ppermute x2 -> x0, waiting for transfers between devices: 5.23 us -> none  [on_device(): vector = vector + lax.ppermute(vector, 'dp', xor_pairs(n_dp, bit))]
    ppermute x18 -> x21, starting transfers between devices: 20.1 us -> 24.5 us  [to_quad(): return lax.ppermute(value, 'dp', xor_pairs(n_dp, j))]
    ppermute x18 -> x21, waiting for transfers between devices: 86.4 us -> 87.4 us  [to_quad(): return lax.ppermute(value, 'dp', xor_pairs(n_dp, j))]
  transfers between devices with their start and end apart: 44 -> 45, of which waited for: 22 -> 20; matrix products, arithmetic and copies ran while one was open for 1% -> 1% of each run, Pallas kernels for 15% -> 14%
where the time goes in v4:
time: 322 us; the launch traced here: 320 us
  waiting for transfers between devices  165 us (51%)
  Pallas kernels  88.4 us (27%)
  starting transfers between devices  55.6 us (17%)
  other arithmetic  5.81 us (2%)
  local copies, waits for them, and re-layouts  4.07 us (1%)
    ppermute x21, waiting for transfers between devices, to_quad(): return lax.ppermute(value, 'dp', xor_pairs(n_dp, j))  87.4 us
    ppermute x15, waiting for transfers between devices, to_layer(): return lax.ppermute(value, 'dp', xor_pairs(n_dp, bits * QUAD))  76.4 us
    pallas_call x5, Pallas kernels, branch(): results = call(*operands)  72 us
    ppermute x15, starting transfers between devices, to_layer(): return lax.ppermute(value, 'dp', xor_pairs(n_dp, bits * QUAD))  30 us
    ppermute x21, starting transfers between devices, to_quad(): return lax.ppermute(value, 'dp', xor_pairs(n_dp, j))  24.5 us
    pallas_call x6, Pallas kernels, staged_call(): pl.pallas_call(whole, in_specs=[SMEM] * len(scalars) + [ANY] * count, out...  8.48 us
  transfers between devices with their start and end apart: 45, of which 20 were waited for; matrix products, arithmetic and copies ran while one was open for 1% of the time, Pallas kernels for 14%

profile of v4, /device:TPU:10, one launch (start us, length us, event | category | flops | bytes accessed | tf_op | source)
XLA Modules:
  0.0 320.3 jit_solution(4962611198222583000)
XLA Ops:
  0.7 1.0 convert_reduce_fusion
  3.8 2.4 shard_map.263
  6.1 1.5 collective-permute-start.2
  8.2 1.4 collective-permute-start.17
  10.3 2.1 shard_map.264
  12.9 1.5 collective-permute-start.6
  14.4 44.8 %collective-permute-done.5 = bf16[64,512]{1,0:T(8,128)(2,1)S(1)} collective-permute-done((bf16[64,512]{1,0:T(8,128)(2,1)}, bf16[64,512]{1,0:T(8,128)(2,1)S(1)}, u32[]{:S(2)}, u32[]{:S(2)}) %collective-permute-start.5) | collective-permute-done | bytes 65568 | tf_op jit(solution)/shard_map/ppermute | solution.py:881
  59.7 1.4 collective-permute-start.7
  61.2 3.9 %collective-permute-done.7 = bf16[64,512]{1,0:T(8,128)(2,1)S(1)} collective-permute-done((bf16[64,512]{1,0:T(8,128)(2,1)}, bf16[64,512]{1,0:T(8,128)(2,1)S(1)}, u32[]{:S(2)}, u32[]{:S(2)}) %collective-permute-start.7) | collective-permute-done | bytes 65568 | tf_op jit(solution)/shard_map/ppermute | solution.py:881
  65.1 1.4 collective-permute-start.12
  66.6 3.7 %collective-permute-done.12 = bf16[2,64,512]{2,1,0:T(8,128)(2,1)S(1)} collective-permute-done((bf16[2,64,512]{2,1,0:T(8,128)(2,1)}, bf16[2,64,512]{2,1,0:T(8,128)(2,1)S(1)}, u32[]{:S(2)}, u32[]{:S(2)}) %collective-permute-start.12) | collective-permute-done | bytes 131104 | tf_op jit(solution)/shard_map/ppermute | solution.py:881
  70.3 1.4 collective-permute-start.13
  72.3 0.9 pad_maximum_fusion.1.refs_6_
  73.1 3.2 %collective-permute-done.13 = bf16[2,64,512]{2,1,0:T(8,128)(2,1)S(1)} collective-permute-done((bf16[2,64,512]{2,1,0:T(8,128)(2,1)}, bf16[2,64,512]{2,1,0:T(8,128)(2,1)S(1)}, u32[]{:S(2)}, u32[]{:S(2)}) %collective-permute-start.13) | collective-permute-done | bytes 131104 | tf_op jit(solution)/shard_map/ppermute | solution.py:881
  76.4 2.6 collective-permute-start.9
  79.0 8.2 %collective-permute-done.9.refs_8_ = bf16[4,64,512]{2,1,0:T(8,128)(2,1)S(1)} collective-permute-done((bf16[4,64,512]{2,1,0:T(8,128)(2,1)S(1)}, bf16[4,64,512]{2,1,0:T(8,128)(2,1)S(1)}, u32[]{:S(2)}, u32[]{:S(2)}) %collective-permute-start.9) | collective-permute-done | bytes 262176 | tf_op jit(solution)/shard_map/ppermute | solution.py:884
  87.1 1.4 collective-permute-start.8
  88.5 5.6 %collective-permute-done.8.refs_7_ = bf16[4,64,512]{2,1,0:T(8,128)(2,1)S(1)} collective-permute-done((bf16[4,64,512]{2,1,0:T(8,128)(2,1)S(1)}, bf16[4,64,512]{2,1,0:T(8,128)(2,1)S(1)}, u32[]{:S(2)}, u32[]{:S(2)}) %collective-permute-start.8) | collective-permute-done | bytes 262176 | tf_op jit(solution)/shard_map/ppermute | solution.py:884
  94.1 1.5 collective-permute-start.10
  96.7 1.0 pad_maximum_fusion.refs_8_.refs_16_
  97.7 2.9 collective-permute-done.10.refs_9_
  100.6 2.6 collective-permute-start.16
  103.1 1.3 collective-permute-start.15
  104.4 9.8 %shard_map.265 = (bf16[1,512,1024]{2,1,0:T(8,128)(2,1)}, bf16[1,512,1024]{2,1,0:T(8,128)(2,1)}, f32[16,1024]{1,0:T(8,128)}, f32[384,128]{1,0:T(8,128)}, f32[1,51...) custom-call(s32[3]{0:T(128)} %pad_add_fusion.meta.refs_0_, f32[1,1024]{1,0:T(1,128)} %bitcast.45, f32[1,1024]{1,0:T(1,128)} %bitcast.48, ...), custom_call_target="tpu_custom_call" | custom-call | flops 2080374784 | bytes 9437184 | tf_op jit(solution)/shard_map/pallas_call | solution.py:812
  114.2 1.1 collective-permute-start.14
  115.3 15.7 %shard_map.266 = (bf16[2,512,1024]{2,1,0:T(8,128)(2,1)}, bf16[2,512,1024]{2,1,0:T(8,128)(2,1)}, f32[16,1024]{1,0:T(8,128)}, f32[384,128]{1,0:T(8,128)}, f32[1,512,1024]{2,1,0:T(8,128)}) custom-call(s32[3]{0:T(128)} %pad_add_fusion.meta.refs_0_, f32[1,1024]{1,0:T(1,128)} %bitcast.46, f32[1,1024]{1,0:T(1,128)} %bitcast.49, ...), custom_call_target="tpu_custom_call" | custom-call | flops 4160749568 | bytes 13631488 | tf_op jit(solution)/shard_map/pallas_call | solution.py:812
  131.1 10.4 %shard_map.267 = (bf16[1,512,1024]{2,1,0:T(8,128)(2,1)}, bf16[1,512,1024]{2,1,0:T(8,128)(2,1)}, f32[16,1024]{1,0:T(8,128)}, f32[384,128]{1,0:T(8,128)}, f32[4,64...) custom-call(s32[3]{0:T(128)} %pad_add_fusion.meta.refs_0_, ...), custom_call_target="tpu_custom_call" | custom-call | flops 2080374784 | bytes 9437184 | tf_op jit(solution)/shard_map/pallas_call | solution.py:812
  141.5 3.7 %collective-permute-done.15.refs_10_.refs_18_ = bf16[4,2,64,512]{3,2,1,0:T(8,128)(2,1)} collective-permute-done((bf16[4,2,64,512]{3,2,1,0:T(8,128)(2,1)S(1)}, bf16[4,2,64,512]{3,2,1,0:T(8,128)(2,1)}, u32[]{:S(2)}, u32[]{:S(2)}) %collective-permute-start.15) | collective-permute-done | bytes 524320 | tf_op jit(solution)/shard_map/ppermute | solution.py:884
  145.2 0.8 copy-done.20
  146.0 10.2 %shard_map.268 = (bf16[2,256,1024]{2,1,0:T(8,128)(2,1)}, bf16[2,256,1024]{2,1,0:T(8,128)(2,1)}, f32[16,1024]{1,0:T(8,128)}, f32[8,512]{1,0:T(8,128)}, f32[2,512,1024]{2,1,0:T(8,128)}) custom-call(s32[3]{0:T(128)} %pad_add_fusion.meta.refs_0_, f32[1,1024]{1,0:T(1,128)} %bitcast.51, f32[1,1024]{1,0:T(1,128)} %bitcast.53, ...), custom_call_target="tpu_custom_call" | custom-call | flops 3221225472 | bytes 14680064 | tf_op jit(solution)/shard_map/pallas_call | solution.py:812
  156.3 25.9 %shard_map.269 = (bf16[2,256,1024]{2,1,0:T(8,128)(2,1)}, bf16[2,256,1024]{2,1,0:T(8,128)(2,1)}, bf16[2,256,1024]{2,1,0:T(8,128)(2,1)}, bf16[2,256,1024]{2,1,0:T(...) custom-call(s32[3]{0:T(128)} %pad_add_fusion.meta.refs_0_, ...), custom_call_target="tpu_custom_call" | custom-call | flops 9663676416 | bytes 23068672 | tf_op jit(solution)/shard_map/pallas_call | solution.py:812
  182.2 1.8 shard_map.274
  184.0 1.4 collective-permute-done.26
  185.5 0.8 add.37
  186.3 1.7 collective-permute-start.29
  187.9 0.9 collective-permute-start.28
  188.8 1.0 collective-permute-start.27
  189.8 2.3 collective-permute-start.33
  192.9 1.6 collective-permute-start.32
  194.5 2.6 collective-permute-done.32.refs_3_
  197.1 5.3 %collective-permute-start.31 = (f32[96,128]{1,0:T(8,128)S(1)}, f32[96,128]{1,0:T(8,128)S(1)}, u32[]{:S(2)}, u32[]{:S(2)}) collective-permute-start(f32[96,128]{1,0:T(8,128)S(1)} %add_add_fusion.refs_0_), channel_id=1, source_target_pairs={{0,16},{2,18},{4,20},{6,22},{8,24},{10,26},{12,28},{14,30},{16,0},... | collective-permute-start | bytes 147464 | tf_op jit(solution)/shard_map/ppermute | solution.py:884
  202.3 2.1 collective-permute-done.31.refs_2_
  204.4 2.9 collective-permute-start.34
  208.0 12.9 %collective-permute-done.34.refs_2_ = bf16[4,64,512]{2,1,0:T(8,128)(2,1)S(1)} collective-permute-done((bf16[4,64,512]{2,1,0:T(8,128)(2,1)S(1)}, bf16[4,64,512]{2,1,0:T(8,128)(2,1)S(1)}, u32[]{:S(2)}, u32[]{:S(2)}) %collective-permute-start.34) | collective-permute-done | bytes 262176 | tf_op jit(solution)/shard_map/ppermute | solution.py:884
  220.9 3.1 collective-permute-start.39
  224.1 4.1 %collective-permute-done.35.refs_3_ = bf16[4,64,512]{2,1,0:T(8,128)(2,1)S(1)} collective-permute-done((bf16[4,64,512]{2,1,0:T(8,128)(2,1)S(1)}, bf16[4,64,512]{2,1,0:T(8,128)(2,1)S(1)}, u32[]{:S(2)}, u32[]{:S(2)}) %collective-permute-start.35) | collective-permute-done | bytes 262176 | tf_op jit(solution)/shard_map/ppermute | solution.py:884
  228.4 1.5 collective-permute-start.36
  229.9 2.2 collective-permute-start.37
  232.1 2.9 collective-permute-start.30
  238.0 10.6 %collective-permute-done.30.refs_1_ = f32[96,128]{1,0:T(8,128)S(1)} collective-permute-done((f32[96,128]{1,0:T(8,128)S(1)}, f32[96,128]{1,0:T(8,128)S(1)}, u32[]{:S(2)}, u32[]{:S(2)}) %collective-permute-start.30) | collective-permute-done | bytes 49184 | tf_op jit(solution)/shard_map/ppermute | solution.py:884
  248.6 1.5 collective-permute-start.21
  250.3 1.9 collective-permute-start.25
  252.2 0.8 collective-permute-start.41
  253.0 23.9 %collective-permute-done.41.refs_3_ = bf16[4,2,64,512]{3,2,1,0:T(8,128)(2,1)S(1)} collective-permute-done((bf16[4,2,64,512]{3,2,1,0:T(8,128)(2,1)S(1)}, bf16[4,2,64,512]{3,2,1,0:T(8,128)(2,1)S(1)}, u32[]{:S(2)}, u32[]{:S(2)}) %collective-permute-start.41) | collective-permute-done | bytes 524320 | tf_op jit(solution)/shard_map/ppermute | solution.py:884
  276.9 1.2 collective-permute-start.38
  278.6 20.6 %collective-permute-done.38.refs_4_ = bf16[64,512]{1,0:T(8,128)(2,1)S(1)} collective-permute-done((bf16[64,512]{1,0:T(8,128)(2,1)S(1)}, bf16[64,512]{1,0:T(8,128)(2,1)S(1)}, u32[]{:S(2)}, u32[]{:S(2)}) %collective-permute-start.38) | collective-permute-done | bytes 65568 | tf_op jit(solution)/shard_map/ppermute | solution.py:881
  299.4 4.7 %collective-permute-done.42.refs_2_ = bf16[2,64,512]{2,1,0:T(8,128)(2,1)S(1)} collective-permute-done((bf16[2,64,512]{2,1,0:T(8,128)(2,1)S(1)}, bf16[2,64,512]{2,1,0:T(8,128)(2,1)S(1)}, u32[]{:S(2)}, u32[]{:S(2)}) %collective-permute-start.42) | collective-permute-done | bytes 131104 | tf_op jit(solution)/shard_map/ppermute | solution.py:881
  304.6 4.5 %collective-permute-done.43.refs_3_ = bf16[2,64,512]{2,1,0:T(8,128)(2,1)S(1)} collective-permute-done((bf16[2,64,512]{2,1,0:T(8,128)(2,1)S(1)}, bf16[2,64,512]{2,1,0:T(8,128)(2,1)S(1)}, u32[]{:S(2)}, u32[]{:S(2)}) %collective-permute-start.43) | collective-permute-done | bytes 131104 | tf_op jit(solution)/shard_map/ppermute | solution.py:881
  309.1 1.4 collective-permute-start.44
  310.5 0.9 shard_map.275
  311.4 1.8 shard_map.277
  313.2 1.7 collective-permute-done.44.refs_4_
  315.0 2.1 shard_map.279
  317.2 2.9 shard_map.273
  (112 shorter events, 12.4 us)
Async XLA Ops:
  3.8 84.7 %copy-start.13 = (f32[1536]{0:T(1024)S(1)}, f32[1536]{0:T(1024)}, u32[]{:S(2)}) copy-start(f32[1536]{0:T(1024)} %param.24) | copy-start | bytes 18436
  3.8 92.4 %copy-start.14 = (f32[2048]{0:T(1024)S(1)}, f32[2048]{0:T(1024)}, u32[]{:S(2)}) copy-start(f32[2048]{0:T(1024)} %param.28) | copy-start | bytes 24580
  6.1 65.6 %collective-permute-start.2 = (bf16[544,1024]{1,0:T(8,128)(2,1)}, bf16[544,1024]{1,0:T(8,128)(2,1)S(1)}, u32[]{:S(2)}, u32[]{:S(2)}) collective-permute-start(bf16[544,1024]{1,0:T(8,128)(2,1)} %get-tuple-element.82.refs_4_.refs_8_), channel_id=1, source_target_pairs={{0,4},{2,6},{4,0},{6,2},{8,12},{10,14},{12,8},{14,10},{16,20},{18,... | collective-permute-start | bytes 3342344 | tf_op jit(solution)/shard_map/ppermute | solution.py:881
  7.6 64.1 %collective-permute-start = (bf16[544,1024]{1,0:T(8,128)(2,1)}, bf16[544,1024]{1,0:T(8,128)(2,1)}, u32[]{:S(2)}, u32[]{:S(2)}) collective-permute-start(bf16[544,1024]{1,0:T(8,128)(2,1)} %get-tuple-element.82.refs_4_.refs_8_), channel_id=1, source_target_pairs={{0,2},{2,0},{4,6},{6,4},{8,10},{10,8},{12,14},{14,12},{16,18},{18,... | collective-permute-start | bytes 3342344 | tf_op jit(solution)/shard_map/ppermute | solution.py:881
  8.2 80.3 %collective-permute-start.17 = (bf16[544,1024]{1,0:T(8,128)(2,1)}, bf16[544,1024]{1,0:T(8,128)(2,1)}, u32[]{:S(2)}, u32[]{:S(2)}) collective-permute-start(bf16[544,1024]{1,0:T(8,128)(2,1)} %get-tuple-element.82.refs_4_.refs_8_), channel_id=1, source_target_pairs={{0,6},{2,4},{4,2},{6,0},{8,14},{10,12},{12,10},{14,8},{16,22},{18,... | collective-permute-start | bytes 3342344 | tf_op jit(solution)/shard_map/ppermute | solution.py:881
  12.4 46.8 %collective-permute-start.5 = (bf16[64,512]{1,0:T(8,128)(2,1)}, bf16[64,512]{1,0:T(8,128)(2,1)S(1)}, u32[]{:S(2)}, u32[]{:S(2)}) collective-permute-start(bf16[64,512]{1,0:T(8,128)(2,1)} %get-tuple-element.84), channel_id=1, source_target_pairs={{0,2},{2,0},{4,6},{6,4},{8,10},{10,8},{12,14},{14,12},{16,18},{18,... | collective-permute-start | bytes 196616 | tf_op jit(solution)/shard_map/ppermute | solution.py:881
  12.9 46.8 %collective-permute-start.6 = (bf16[64,512]{1,0:T(8,128)(2,1)}, bf16[64,512]{1,0:T(8,128)(2,1)S(1)}, u32[]{:S(2)}, u32[]{:S(2)}) collective-permute-start(bf16[64,512]{1,0:T(8,128)(2,1)} %get-tuple-element.85), channel_id=1, source_target_pairs={{0,4},{2,6},{4,0},{6,2},{8,12},{10,14},{12,8},{14,10},{16,20},{18,... | collective-permute-start | bytes 196616 | tf_op jit(solution)/shard_map/ppermute | solution.py:881
  59.2 7.3 %collective-permute-start.11 = (bf16[2,64,512]{2,1,0:T(8,128)(2,1)}, bf16[2,64,512]{2,1,0:T(8,128)(2,1)S(1)}, u32[]{:S(2)}, u32[]{:S(2)}) collective-permute-start(bf16[2,64,512]{2,1,0:T(8,128)(2,1)} %get-tuple-element.96), channel_id=1, source_target_pairs={{0,2},{2,0},{4,6},{6,4},{8,10},{10,8},{12,14},{14,12},{16,18},{18,... | collective-permute-start | bytes 393224 | tf_op jit(solution)/shard_map/ppermute | solution.py:881
  59.7 5.4 %collective-permute-start.7 = (bf16[64,512]{1,0:T(8,128)(2,1)}, bf16[64,512]{1,0:T(8,128)(2,1)S(1)}, u32[]{:S(2)}, u32[]{:S(2)}) collective-permute-start(bf16[64,512]{1,0:T(8,128)(2,1)} %get-tuple-element.86), channel_id=1, source_target_pairs={{0,6},{2,4},{4,2},{6,0},{8,14},{10,12},{12,10},{14,8},{16,22},{18,... | collective-permute-start | bytes 196616 | tf_op jit(solution)/shard_map/ppermute | solution.py:881
  65.1 5.2 %collective-permute-start.12 = (bf16[2,64,512]{2,1,0:T(8,128)(2,1)}, bf16[2,64,512]{2,1,0:T(8,128)(2,1)S(1)}, u32[]{:S(2)}, u32[]{:S(2)}) collective-permute-start(bf16[2,64,512]{2,1,0:T(8,128)(2,1)} %get-tuple-element.97), channel_id=1, source_target_pairs={{0,4},{2,6},{4,0},{6,2},{8,12},{10,14},{12,8},{14,10},{16,20},{18,... | collective-permute-start | bytes 393224 | tf_op jit(solution)/shard_map/ppermute | solution.py:881
  66.6 36.6 %collective-permute-start.4 = (bf16[544,1024]{1,0:T(8,128)(2,1)}, bf16[544,1024]{1,0:T(8,128)(2,1)}, u32[]{:S(2)}, u32[]{:S(2)}) collective-permute-start(bf16[544,1024]{1,0:T(8,128)(2,1)} %get-tuple-element.82.refs_4_.refs_8_), channel_id=1, source_target_pairs={{0,1},{1,0},{2,3},{3,2},{4,5},{5,4},{6,7},{7,6},{8,9},{9,8},{10,11... | collective-permute-start | bytes 3342344 | tf_op jit(solution)/shard_map/ppermute | solution.py:50
  70.3 6.1 %collective-permute-start.13 = (bf16[2,64,512]{2,1,0:T(8,128)(2,1)}, bf16[2,64,512]{2,1,0:T(8,128)(2,1)S(1)}, u32[]{:S(2)}, u32[]{:S(2)}) collective-permute-start(bf16[2,64,512]{2,1,0:T(8,128)(2,1)} %get-tuple-element.98), channel_id=1, source_target_pairs={{0,6},{2,4},{4,2},{6,0},{8,14},{10,12},{12,10},{14,8},{16,22},{18,... | collective-permute-start | bytes 393224 | tf_op jit(solution)/shard_map/ppermute | solution.py:881
  71.7 42.4 %copy-start.15 = (bf16[544,1024]{1,0:T(8,128)(2,1)}, bf16[544,1024]{1,0:T(8,128)(2,1)S(1)}, u32[]{:S(2)}) copy-start(bf16[544,1024]{1,0:T(8,128)(2,1)S(1)} %collective-permute-done.2.refs_6_) | copy-start | bytes 3342340
  71.7 42.5 %collective-permute-start.3 = (bf16[544,1024]{1,0:T(8,128)(2,1)S(1)}, bf16[544,1024]{1,0:T(8,128)(2,1)}, u32[]{:S(2)}, u32[]{:S(2)}) collective-permute-start(bf16[544,1024]{1,0:T(8,128)(2,1)S(1)} %collective-permute-done.2.refs_6_), channel_id=1, source_target_pairs={{0,1},{1,0},{2,3},{3,2},{4,5},{5,4},{6,7},{7,6},{8,9},{9,8},{10,11... | collective-permute-start | bytes 3342344 | tf_op jit(solution)/shard_map/ppermute | solution.py:50
  71.8 43.6 %collective-permute-start.1 = (bf16[544,1024]{1,0:T(8,128)(2,1)}, bf16[544,1024]{1,0:T(8,128)(2,1)}, u32[]{:S(2)}, u32[]{:S(2)}) collective-permute-start(bf16[544,1024]{1,0:T(8,128)(2,1)} %collective-permute-done.refs_4_), channel_id=1, source_target_pairs={{0,1},{1,0},{2,3},{3,2},{4,5},{5,4},{6,7},{7,6},{8,9},{9,8},{10,11... | collective-permute-start | bytes 3342344 | tf_op jit(solution)/shard_map/ppermute | solution.py:50
  73.1 31.3 %copy-start.12 = (bf16[4,64,512]{2,1,0:T(8,128)(2,1)}, bf16[4,64,512]{2,1,0:T(8,128)(2,1)S(1)}, u32[]{:S(2)}) copy-start(bf16[4,64,512]{2,1,0:T(8,128)(2,1)S(1)} %pad_maximum_fusion.1.refs_6_) | copy-start | bytes 786436
  76.4 10.7 %collective-permute-start.9 = (bf16[4,64,512]{2,1,0:T(8,128)(2,1)S(1)}, bf16[4,64,512]{2,1,0:T(8,128)(2,1)S(1)}, u32[]{:S(2)}, u32[]{:S(2)}) collective-permute-start(bf16[4,64,512]{2,1,0:T(8,128)(2,1)S(1)} %pad_maximum_fusion.1.refs_6_), channel_id=1, source_target_pairs={{0,16},{2,18},{4,20},{6,22},{8,24},{10,26},{12,28},{14,30},{16,0},... | collective-permute-start | bytes 786440 | tf_op jit(solution)/shard_map/ppermute | solution.py:884
  87.1 17.3 %copy-start.24 = (bf16[4,64,512]{2,1,0:T(8,128)(2,1)}, bf16[4,64,512]{2,1,0:T(8,128)(2,1)S(1)}, u32[]{:S(2)}) copy-start(bf16[4,64,512]{2,1,0:T(8,128)(2,1)S(1)} %collective-permute-done.9.refs_8_) | copy-start | bytes 786436
  87.1 7.0 %collective-permute-start.8 = (bf16[4,64,512]{2,1,0:T(8,128)(2,1)S(1)}, bf16[4,64,512]{2,1,0:T(8,128)(2,1)S(1)}, u32[]{:S(2)}, u32[]{:S(2)}) collective-permute-start(bf16[4,64,512]{2,1,0:T(8,128)(2,1)S(1)} %pad_maximum_fusion.1.refs_6_), channel_id=1, source_target_pairs={{0,8},{2,10},{4,12},{6,14},{8,0},{10,2},{12,4},{14,6},{16,24},{18,... | collective-permute-start | bytes 786440 | tf_op jit(solution)/shard_map/ppermute | solution.py:884
  88.5 42.6 %collective-permute-start.18 = (bf16[544,1024]{1,0:T(8,128)(2,1)}, bf16[544,1024]{1,0:T(8,128)(2,1)}, u32[]{:S(2)}, u32[]{:S(2)}) collective-permute-start(bf16[544,1024]{1,0:T(8,128)(2,1)} %collective-permute-done.17.refs_4_), channel_id=1, source_target_pairs={{0,1},{1,0},{2,3},{3,2},{4,5},{5,4},{6,7},{7,6},{8,9},{9,8},{10,11... | collective-permute-start | bytes 3342344 | tf_op jit(solution)/shard_map/ppermute | solution.py:50
  94.1 6.5 %collective-permute-start.10 = (bf16[4,64,512]{2,1,0:T(8,128)(2,1)S(1)}, bf16[4,64,512]{2,1,0:T(8,128)(2,1)}, u32[]{:S(2)}, u32[]{:S(2)}) collective-permute-start(bf16[4,64,512]{2,1,0:T(8,128)(2,1)S(1)} %collective-permute-done.9.refs_8_), channel_id=1, source_target_pairs={{0,8},{2,10},{4,12},{6,14},{8,0},{10,2},{12,4},{14,6},{16,24},{18,... | collective-permute-start | bytes 786440 | tf_op jit(solution)/shard_map/ppermute | solution.py:884
  97.7 16.5 %copy-start.11 = (bf16[4,2,64,512]{3,2,1,0:T(8,128)(2,1)}, bf16[4,2,64,512]{3,2,1,0:T(8,128)(2,1)S(1)}, u32[]{:S(2)}) copy-start(bf16[4,2,64,512]{3,2,1,0:T(8,128)(2,1)S(1)} %pad_maximum_fusion.refs_8_.refs_16_) | copy-start | bytes 1572868
  100.6 40.9 %collective-permute-start.16 = (bf16[4,2,64,512]{3,2,1,0:T(8,128)(2,1)S(1)}, bf16[4,2,64,512]{3,2,1,0:T(8,128)(2,1)S(1)}, u32[]{:S(2)}, u32[]{:S(2)}) collective-permute-start(bf16[4,2,64,512]{3,2,1,0:T(8,128)(2,1)S(1)} %pad_maximum_fusion.refs_8_.refs_16_), channel_id=1, source_target_pairs={{0,24},{2,26},{4,28},{6,30},{8,16},{10,18},{12,20},{14,22},{16,8},... | collective-permute-start | bytes 1572872 | tf_op jit(solution)/shard_map/ppermute | solution.py:884
  103.1 42.1 %collective-permute-start.15 = (bf16[4,2,64,512]{3,2,1,0:T(8,128)(2,1)S(1)}, bf16[4,2,64,512]{3,2,1,0:T(8,128)(2,1)}, u32[]{:S(2)}, u32[]{:S(2)}) collective-permute-start(bf16[4,2,64,512]{3,2,1,0:T(8,128)(2,1)S(1)} %pad_maximum_fusion.refs_8_.refs_16_), channel_id=1, source_target_pairs={{0,16},{2,18},{4,20},{6,22},{8,24},{10,26},{12,28},{14,30},{16,0},... | collective-permute-start | bytes 1572872 | tf_op jit(solution)/shard_map/ppermute | solution.py:884
  114.2 31.0 %collective-permute-start.14 = (bf16[4,2,64,512]{3,2,1,0:T(8,128)(2,1)S(1)}, bf16[4,2,64,512]{3,2,1,0:T(8,128)(2,1)S(1)}, u32[]{:S(2)}, u32[]{:S(2)}) collective-permute-start(bf16[4,2,64,512]{3,2,1,0:T(8,128)(2,1)S(1)} %pad_maximum_fusion.refs_8_.refs_16_), channel_id=1, source_target_pairs={{0,8},{2,10},{4,12},{6,14},{8,0},{10,2},{12,4},{14,6},{16,24},{18,... | collective-permute-start | bytes 1572872 | tf_op jit(solution)/shard_map/ppermute | solution.py:884
  156.2 33.5 %copy-start.23 = (bf16[4,64,512]{2,1,0:T(8,128)(2,1)S(1)}, bf16[4,64,512]{2,1,0:T(8,128)(2,1)}, u32[]{:S(2)}) copy-start(bf16[4,64,512]{2,1,0:T(8,128)(2,1)} %get-tuple-element.127) | copy-start | bytes 786436
  156.3 36.3 %copy-start.17 = (bf16[2,256,1024]{2,1,0:T(8,128)(2,1)S(1)}, bf16[2,256,1024]{2,1,0:T(8,128)(2,1)}, u32[]{:S(2)}) copy-start(bf16[2,256,1024]{2,1,0:T(8,128)(2,1)} %get-tuple-element.114) | copy-start | bytes 3145732
  156.3 48.1 %copy-start.22 = (bf16[4,64,512]{2,1,0:T(8,128)(2,1)S(1)}, bf16[4,64,512]{2,1,0:T(8,128)(2,1)}, u32[]{:S(2)}) copy-start(bf16[4,64,512]{2,1,0:T(8,128)(2,1)} %get-tuple-element.128) | copy-start | bytes 786436
  156.3 51.0 %copy-start.21 = (bf16[4,64,512]{2,1,0:T(8,128)(2,1)S(1)}, bf16[4,64,512]{2,1,0:T(8,128)(2,1)}, u32[]{:S(2)}) copy-start(bf16[4,64,512]{2,1,0:T(8,128)(2,1)} %get-tuple-element.129) | copy-start | bytes 786436
  156.3 71.9 %copy-start.7 = (f32[4,64,512]{2,1,0:T(8,128)S(1)}, f32[4,64,512]{2,1,0:T(8,128)}, u32[]{:S(2)}) copy-start(f32[4,64,512]{2,1,0:T(8,128)} %get-tuple-element.126.refs_0_) | copy-start | bytes 1572868
  182.2 52.9 %copy-start.4 = (bf16[2,256,1024]{2,1,0:T(8,128)(2,1)S(1)}, bf16[2,256,1024]{2,1,0:T(8,128)(2,1)}, u32[]{:S(2)}) copy-start(bf16[2,256,1024]{2,1,0:T(8,128)(2,1)} %get-tuple-element.109.mine) | copy-start | bytes 3145732
  184.0 1.4 collective-permute-start.26
  186.3 5.8 %collective-permute-start.29 = (f32[96,128]{1,0:T(8,128)S(1)}, f32[96,128]{1,0:T(8,128)S(1)}, u32[]{:S(2)}, u32[]{:S(2)}) collective-permute-start(f32[96,128]{1,0:T(8,128)S(1)} %add.37), channel_id=1, source_target_pairs={{0,6},{2,4},{4,2},{6,0},{8,14},{10,12},{12,10},{14,8},{16,22},{18,... | collective-permute-start | bytes 147464 | tf_op jit(solution)/shard_map/ppermute | solution.py:881
  187.9 4.6 %collective-permute-start.28 = (f32[96,128]{1,0:T(8,128)S(1)}, f32[96,128]{1,0:T(8,128)S(1)}, u32[]{:S(2)}, u32[]{:S(2)}) collective-permute-start(f32[96,128]{1,0:T(8,128)S(1)} %add.37), channel_id=1, source_target_pairs={{0,4},{2,6},{4,0},{6,2},{8,12},{10,14},{12,8},{14,10},{16,20},{18,... | collective-permute-start | bytes 147464 | tf_op jit(solution)/shard_map/ppermute | solution.py:881
  188.8 4.1 %collective-permute-start.27 = (f32[96,128]{1,0:T(8,128)S(1)}, f32[96,128]{1,0:T(8,128)S(1)}, u32[]{:S(2)}, u32[]{:S(2)}) collective-permute-start(f32[96,128]{1,0:T(8,128)S(1)} %add.37), channel_id=1, source_target_pairs={{0,2},{2,0},{4,6},{6,4},{8,10},{10,8},{12,14},{14,12},{16,18},{18,... | collective-permute-start | bytes 147464 | tf_op jit(solution)/shard_map/ppermute | solution.py:881
  189.8 17.6 %collective-permute-start.33 = (bf16[4,64,512]{2,1,0:T(8,128)(2,1)S(1)}, bf16[4,64,512]{2,1,0:T(8,128)(2,1)S(1)}, u32[]{:S(2)}, u32[]{:S(2)}) collective-permute-start(bf16[4,64,512]{2,1,0:T(8,128)(2,1)S(1)} %copy-done.23), channel_id=1, source_target_pairs={{0,8},{2,10},{4,12},{6,14},{8,0},{10,2},{12,4},{14,6},{16,24},{18,... | collective-permute-start | bytes 786440 | tf_op jit(solution)/shard_map/ppermute | solution.py:884
  192.0 36.3 %collective-permute-start.20 = (bf16[2,256,1024]{2,1,0:T(8,128)(2,1)}, bf16[2,256,1024]{2,1,0:T(8,128)(2,1)S(1)}, u32[]{:S(2)}, u32[]{:S(2)}) collective-permute-start(bf16[2,256,1024]{2,1,0:T(8,128)(2,1)} %get-tuple-element.110), channel_id=1, source_target_pairs={{0,1},{1,0},{2,3},{3,2},{4,5},{5,4},{6,7},{7,6},{8,9},{9,8},{10,11... | collective-permute-start | bytes 3145736 | tf_op jit(solution)/shard_map/ppermute | solution.py:50
  192.1 37.9 %collective-permute-start.22 = (bf16[2,256,1024]{2,1,0:T(8,128)(2,1)}, bf16[2,256,1024]{2,1,0:T(8,128)(2,1)S(1)}, u32[]{:S(2)}, u32[]{:S(2)}) collective-permute-start(bf16[2,256,1024]{2,1,0:T(8,128)(2,1)} %get-tuple-element.112), channel_id=1, source_target_pairs={{0,1},{1,0},{2,3},{3,2},{4,5},{5,4},{6,7},{7,6},{8,9},{9,8},{10,11... | collective-permute-start | bytes 3145736 | tf_op jit(solution)/shard_map/ppermute | solution.py:50
  192.6 39.5 %collective-permute-start.24 = (bf16[2,256,1024]{2,1,0:T(8,128)(2,1)S(1)}, bf16[2,256,1024]{2,1,0:T(8,128)(2,1)S(1)}, u32[]{:S(2)}, u32[]{:S(2)}) collective-permute-start(bf16[2,256,1024]{2,1,0:T(8,128)(2,1)S(1)} %copy-done.17), channel_id=1, source_target_pairs={{0,1},{1,0},{2,3},{3,2},{4,5},{5,4},{6,7},{7,6},{8,9},{9,8},{10,11... | collective-permute-start | bytes 3145736 | tf_op jit(solution)/shard_map/ppermute | solution.py:50
  192.9 4.2 %collective-permute-start.32 = (f32[96,128]{1,0:T(8,128)S(1)}, f32[96,128]{1,0:T(8,128)S(1)}, u32[]{:S(2)}, u32[]{:S(2)}) collective-permute-start(f32[96,128]{1,0:T(8,128)S(1)} %add_add_fusion.refs_0_), channel_id=1, source_target_pairs={{0,24},{2,26},{4,28},{6,30},{8,16},{10,18},{12,20},{14,22},{16,8},... | collective-permute-start | bytes 147464 | tf_op jit(solution)/shard_map/ppermute | solution.py:884
  197.1 7.3 %collective-permute-start.31 = (f32[96,128]{1,0:T(8,128)S(1)}, f32[96,128]{1,0:T(8,128)S(1)}, u32[]{:S(2)}, u32[]{:S(2)}) collective-permute-start(f32[96,128]{1,0:T(8,128)S(1)} %add_add_fusion.refs_0_), channel_id=1, source_target_pairs={{0,16},{2,18},{4,20},{6,22},{8,24},{10,26},{12,28},{14,30},{16,0},... | collective-permute-start | bytes 147464 | tf_op jit(solution)/shard_map/ppermute | solution.py:884
  204.4 16.5 %collective-permute-start.34 = (bf16[4,64,512]{2,1,0:T(8,128)(2,1)S(1)}, bf16[4,64,512]{2,1,0:T(8,128)(2,1)S(1)}, u32[]{:S(2)}, u32[]{:S(2)}) collective-permute-start(bf16[4,64,512]{2,1,0:T(8,128)(2,1)S(1)} %copy-done.22), channel_id=1, source_target_pairs={{0,16},{2,18},{4,20},{6,22},{8,24},{10,26},{12,28},{14,30},{16,0},... | collective-permute-start | bytes 786440 | tf_op jit(solution)/shard_map/ppermute | solution.py:884
  207.3 20.8 %collective-permute-start.35 = (bf16[4,64,512]{2,1,0:T(8,128)(2,1)S(1)}, bf16[4,64,512]{2,1,0:T(8,128)(2,1)S(1)}, u32[]{:S(2)}, u32[]{:S(2)}) collective-permute-start(bf16[4,64,512]{2,1,0:T(8,128)(2,1)S(1)} %copy-done.21), channel_id=1, source_target_pairs={{0,24},{2,26},{4,28},{6,30},{8,16},{10,18},{12,20},{14,22},{16,8},... | collective-permute-start | bytes 786440 | tf_op jit(solution)/shard_map/ppermute | solution.py:884
  220.9 29.4 %collective-permute-start.39 = (bf16[4,2,64,512]{3,2,1,0:T(8,128)(2,1)}, bf16[4,2,64,512]{3,2,1,0:T(8,128)(2,1)S(1)}, u32[]{:S(2)}, u32[]{:S(2)}) collective-permute-start(bf16[4,2,64,512]{3,2,1,0:T(8,128)(2,1)} %get-tuple-element.139), channel_id=1, source_target_pairs={{0,8},{2,10},{4,12},{6,14},{8,0},{10,2},{12,4},{14,6},{16,24},{18,... | collective-permute-start | bytes 1572872 | tf_op jit(solution)/shard_map/ppermute | solution.py:884
  228.1 24.1 %collective-permute-start.40 = (bf16[4,2,64,512]{3,2,1,0:T(8,128)(2,1)}, bf16[4,2,64,512]{3,2,1,0:T(8,128)(2,1)S(1)}, u32[]{:S(2)}, u32[]{:S(2)}) collective-permute-start(bf16[4,2,64,512]{3,2,1,0:T(8,128)(2,1)} %get-tuple-element.140), channel_id=1, source_target_pairs={{0,16},{2,18},{4,20},{6,22},{8,24},{10,26},{12,28},{14,30},{16,0},... | collective-permute-start | bytes 1572872 | tf_op jit(solution)/shard_map/ppermute | solution.py:884
  228.4 20.2 %collective-permute-start.36 = (bf16[64,512]{1,0:T(8,128)(2,1)S(1)}, bf16[64,512]{1,0:T(8,128)(2,1)S(1)}, u32[]{:S(2)}, u32[]{:S(2)}) collective-permute-start(bf16[64,512]{1,0:T(8,128)(2,1)S(1)} %get-tuple-element.131), channel_id=1, source_target_pairs={{0,2},{2,0},{4,6},{6,4},{8,10},{10,8},{12,14},{14,12},{16,18},{18,... | collective-permute-start | bytes 196616 | tf_op jit(solution)/shard_map/ppermute | solution.py:881
  229.9 20.2 %collective-permute-start.37 = (bf16[64,512]{1,0:T(8,128)(2,1)S(1)}, bf16[64,512]{1,0:T(8,128)(2,1)S(1)}, u32[]{:S(2)}, u32[]{:S(2)}) collective-permute-start(bf16[64,512]{1,0:T(8,128)(2,1)S(1)} %get-tuple-element.132), channel_id=1, source_target_pairs={{0,4},{2,6},{4,0},{6,2},{8,12},{10,14},{12,8},{14,10},{16,20},{18,... | collective-permute-start | bytes 196616 | tf_op jit(solution)/shard_map/ppermute | solution.py:881
  232.1 16.5 %collective-permute-start.30 = (f32[96,128]{1,0:T(8,128)S(1)}, f32[96,128]{1,0:T(8,128)S(1)}, u32[]{:S(2)}, u32[]{:S(2)}) collective-permute-start(f32[96,128]{1,0:T(8,128)S(1)} %add_add_fusion.refs_0_), channel_id=1, source_target_pairs={{0,8},{2,10},{4,12},{6,14},{8,0},{10,2},{12,4},{14,6},{16,24},{18,... | collective-permute-start | bytes 147464 | tf_op jit(solution)/shard_map/ppermute | solution.py:884
  237.5 40.6 %copy-start.5 = (f32[4,2,64,512]{3,2,1,0:T(8,128)S(1)}, f32[4,2,64,512]{3,2,1,0:T(8,128)}, u32[]{:S(2)}) copy-start(f32[4,2,64,512]{3,2,1,0:T(8,128)} %get-tuple-element.138.refs_0_) | copy-start | bytes 3145732
  248.6 68.5 %collective-permute-start.19 = (bf16[2,256,1024]{2,1,0:T(8,128)(2,1)S(1)}, bf16[2,256,1024]{2,1,0:T(8,128)(2,1)S(1)}, u32[]{:S(2)}, u32[]{:S(2)}) collective-permute-start(bf16[2,256,1024]{2,1,0:T(8,128)(2,1)S(1)} %copy-done.16), channel_id=1, source_target_pairs={{0,1},{1,0},{2,3},{3,2},{4,5},{5,4},{6,7},{7,6},{8,9},{9,8},{10,11... | collective-permute-start | bytes 3145736 | tf_op jit(solution)/shard_map/ppermute | solution.py:50
  248.6 68.5 %collective-permute-start.21 = (bf16[2,256,1024]{2,1,0:T(8,128)(2,1)S(1)}, bf16[2,256,1024]{2,1,0:T(8,128)(2,1)S(1)}, u32[]{:S(2)}, u32[]{:S(2)}) collective-permute-start(bf16[2,256,1024]{2,1,0:T(8,128)(2,1)S(1)} %shard_map.270), channel_id=1, source_target_pairs={{0,2},{2,0},{4,6},{6,4},{8,10},{10,8},{12,14},{14,12},{16,18},{18,... | collective-permute-start | bytes 3145736 | tf_op jit(solution)/shard_map/ppermute | solution.py:881
  250.2 67.0 %collective-permute-start.23 = (bf16[2,256,1024]{2,1,0:T(8,128)(2,1)S(1)}, bf16[2,256,1024]{2,1,0:T(8,128)(2,1)S(1)}, u32[]{:S(2)}, u32[]{:S(2)}) collective-permute-start(bf16[2,256,1024]{2,1,0:T(8,128)(2,1)S(1)} %shard_map.271), channel_id=1, source_target_pairs={{0,4},{2,6},{4,0},{6,2},{8,12},{10,14},{12,8},{14,10},{16,20},{18,... | collective-permute-start | bytes 3145736 | tf_op jit(solution)/shard_map/ppermute | solution.py:881
  250.3 66.8 %collective-permute-start.25 = (bf16[2,256,1024]{2,1,0:T(8,128)(2,1)S(1)}, bf16[2,256,1024]{2,1,0:T(8,128)(2,1)S(1)}, u32[]{:S(2)}, u32[]{:S(2)}) collective-permute-start(bf16[2,256,1024]{2,1,0:T(8,128)(2,1)S(1)} %shard_map.272), channel_id=1, source_target_pairs={{0,6},{2,4},{4,2},{6,0},{8,14},{10,12},{12,10},{14,8},{16,22},{18,... | collective-permute-start | bytes 3145736 | tf_op jit(solution)/shard_map/ppermute | solution.py:881
  252.2 24.7 %collective-permute-start.41 = (bf16[4,2,64,512]{3,2,1,0:T(8,128)(2,1)S(1)}, bf16[4,2,64,512]{3,2,1,0:T(8,128)(2,1)S(1)}, u32[]{:S(2)}, u32[]{:S(2)}) collective-permute-start(bf16[4,2,64,512]{3,2,1,0:T(8,128)(2,1)S(1)} %copy-done.18), channel_id=1, source_target_pairs={{0,24},{2,26},{4,28},{6,30},{8,16},{10,18},{12,20},{14,22},{16,8},... | collective-permute-start | bytes 1572872 | tf_op jit(solution)/shard_map/ppermute | solution.py:884
  276.9 22.3 %collective-permute-start.38 = (bf16[64,512]{1,0:T(8,128)(2,1)S(1)}, bf16[64,512]{1,0:T(8,128)(2,1)S(1)}, u32[]{:S(2)}, u32[]{:S(2)}) collective-permute-start(bf16[64,512]{1,0:T(8,128)(2,1)S(1)} %get-tuple-element.133), channel_id=1, source_target_pairs={{0,6},{2,4},{4,2},{6,0},{8,14},{10,12},{12,10},{14,8},{16,22},{18,... | collective-permute-start | bytes 196616 | tf_op jit(solution)/shard_map/ppermute | solution.py:881
  278.1 33.3 %copy-start.8 = (s32[3]{0:T(128)S(1)}, s32[3]{0:T(128)}, u32[]{:S(2)}) copy-start(s32[3]{0:T(128)} %pad_add_fusion.meta.refs_0_) | copy-start | bytes 40
  278.1 39.1 %copy-start.6 = (bf16[2,256,1024]{2,1,0:T(8,128)(2,1)S(1)}, bf16[2,256,1024]{2,1,0:T(8,128)(2,1)}, u32[]{:S(2)}) copy-start(bf16[2,256,1024]{2,1,0:T(8,128)(2,1)} %get-tuple-element.107.refs_4_) | copy-start | bytes 3145732
  278.5 38.6 %copy-start = (bf16[256,1024]{1,0:T(8,128)(2,1)S(1)}, bf16[256,1024]{1,0:T(8,128)(2,1)}, u32[]{:S(2)}) copy-start(bf16[256,1024]{1,0:T(8,128)(2,1)} %refs_2_.1) | copy-start | bytes 1572868
  278.5 38.6 %copy-start.1 = (bf16[256,1024]{1,0:T(8,128)(2,1)S(1)}, bf16[256,1024]{1,0:T(8,128)(2,1)}, u32[]{:S(2)}) copy-start(bf16[256,1024]{1,0:T(8,128)(2,1)} %refs_3_.1) | copy-start | bytes 1572868
  278.5 38.6 %copy-start.9 = (f32[1024]{0:T(1024)S(1)}, f32[1024]{0:T(1024)}, u32[]{:S(2)}) copy-start(f32[1024]{0:T(1024)} %param.26) | copy-start | bytes 12292
  278.6 38.6 %copy-start.10 = (f32[1024]{0:T(1024)S(1)}, f32[1024]{0:T(1024)}, u32[]{:S(2)}) copy-start(f32[1024]{0:T(1024)} %param.30) | copy-start | bytes 12292
  299.1 5.0 %collective-permute-start.42 = (bf16[2,64,512]{2,1,0:T(8,128)(2,1)S(1)}, bf16[2,64,512]{2,1,0:T(8,128)(2,1)S(1)}, u32[]{:S(2)}, u32[]{:S(2)}) collective-permute-start(bf16[2,64,512]{2,1,0:T(8,128)(2,1)S(1)} %get-tuple-element.143), channel_id=1, source_target_pairs={{0,2},{2,0},{4,6},{6,4},{8,10},{10,8},{12,14},{14,12},{16,18},{18,... | collective-permute-start | bytes 393224 | tf_op jit(solution)/shard_map/ppermute | solution.py:881
  304.1 5.0 %collective-permute-start.43 = (bf16[2,64,512]{2,1,0:T(8,128)(2,1)S(1)}, bf16[2,64,512]{2,1,0:T(8,128)(2,1)S(1)}, u32[]{:S(2)}, u32[]{:S(2)}) collective-permute-start(bf16[2,64,512]{2,1,0:T(8,128)(2,1)S(1)} %get-tuple-element.144), channel_id=1, source_target_pairs={{0,4},{2,6},{4,0},{6,2},{8,12},{10,14},{12,8},{14,10},{16,20},{18,... | collective-permute-start | bytes 393224 | tf_op jit(solution)/shard_map/ppermute | solution.py:881
  309.1 5.9 %collective-permute-start.44 = (bf16[2,64,512]{2,1,0:T(8,128)(2,1)S(1)}, bf16[2,64,512]{2,1,0:T(8,128)(2,1)S(1)}, u32[]{:S(2)}, u32[]{:S(2)}) collective-permute-start(bf16[2,64,512]{2,1,0:T(8,128)(2,1)S(1)} %get-tuple-element.145), channel_id=1, source_target_pairs={{0,6},{2,4},{4,2},{6,0},{8,14},{10,12},{12,10},{14,8},{16,22},{18,... | collective-permute-start | bytes 393224 | tf_op jit(solution)/shard_map/ppermute | solution.py:881
  (7 other events, 43.1 us)

commit v5 on v4

--- a/solution.py
+++ b/solution.py
@@ -117,8 +117,8 @@
 
 
 def join_body(*refs):
-    parts, message, column_sums = refs[:-2], refs[-2], refs[-1]
-    total = fold_rows(parts[1][...].astype(F32))
+    cotangents, parts, message, column_sums = refs[0], refs[1:-2], refs[-2], refs[-1]
+    total = fold_rows(cotangents[...].astype(F32))
     column_sums[...] = jnp.sum(total, axis=0, keepdims=True)
     at = 0
     for part in parts:
@@ -126,17 +126,17 @@
         at += part.shape[0]
 
 
-def join_message(*parts):
+def join_message(cotangents, *parts):
     rows = sum(part.shape[0] for part in parts)
     return pl.pallas_call(
         join_body,
-        in_specs=[VMEM] * len(parts),
+        in_specs=[VMEM] * (1 + len(parts)),
         out_specs=[VMEM] * 2,
         out_shape=[
             jax.ShapeDtypeStruct((rows, parts[0].shape[1]), BF16),
             jax.ShapeDtypeStruct((1, parts[0].shape[1]), F32),
         ],
-    )(*parts)
+    )(cotangents, *parts)
 
 
 def sum_layers_body(keep, *refs):
@@ -527,7 +527,7 @@
     refs = list(refs)
     take = lambda number: [refs.pop(0) for _ in range(number)]
     (meta, gain, shift, bias) = take(4)
-    messages = [take(2) for _ in range(n_seq)]
+    messages = [take(4) for _ in range(n_seq)]
     partials = [take(2) for _ in places or ()]
     reads_turned = kind.turns and not is_first
     blocks = take(1 if reads_turned else count)
@@ -569,16 +569,16 @@
     def start_message(i, target, first, which):
         for number, place in enumerate((mine, other)):
             pltpu.make_async_copy(
-                messages[i][number].at[pl.ds(first, half)],
+                messages[i][first + number].at[pl.ds(0, half)],
                 target.at[i, pl.ds(place, half)],
                 token_sem.at[i, which, number],
             ).start()
 
     def start_rest(i):
-        start_message(i, d_s, half, 1)
+        start_message(i, d_s, 2, 1)
         if kind.turns:
             pltpu.make_async_copy(
-                messages[i][0].at[pl.ds(2 * half, TABLE_ROWS)], tab_s.at[i], table_sem.at[i]
+                messages[i][0].at[pl.ds(half, TABLE_ROWS)], tab_s.at[i], table_sem.at[i]
             ).start()
         if i == 0:
             for copy in weight_copies:
@@ -723,7 +723,7 @@
 
 def branch(kind, meta, gain, shift, bias, messages, partials, blocks, carried, is_last):
     n_seq, count, is_first = len(messages), len(blocks), carried is None
-    half = (messages[0][0].shape[0] - TABLE_ROWS) // 2
+    half = messages[0][2].shape[0]
     features = messages[0][0].shape[1]
     length = 2 * half
     width = blocks[0].shape[-1]
@@ -732,7 +732,7 @@
     specs = [SMEM] + [VMEM] * 3
     for pair in messages:
         operands += list(pair)
-        specs += [ANY] * 2
+        specs += [ANY] * 4
     for part in partials:
         operands += list(part[:2])
         specs += [HBM] * 2
@@ -903,7 +903,7 @@
     start = jnp.concatenate([start // 256, start % 256]).astype(BF16)
     turns = jnp.concatenate([jnp.cos(angles), jnp.sin(angles)], axis=1)
     message, cotangent_sum = join_message(
-        inputs, output_grad, *low_parts(turns, 3), jnp.broadcast_to(start[None], turns.shape)
+        output_grad, inputs, *low_parts(turns, 3), jnp.broadcast_to(start[None], turns.shape)
     )
 
     first_pack, second_pack = pack_weights(
@@ -915,8 +915,11 @@
     first_parts = [first_pack[0]] + [to_quad(first_pack[j], j) for j in range(1, QUAD)]
     first_blocks = gather_layers(jnp.stack(first_parts))
 
-    whole = [message] + [to_quad(message, j) for j in range(1, QUAD)]
-    messages = [(value, swap_cores(value)) for value in whole]
+    rows_a = [message] + [to_quad(message, j) for j in (1, 2)]
+    rows_b = [output_grad] + [to_quad(output_grad, j) for j in (1, 2)]
+    rows_a.append(to_quad(rows_a[2], 1))
+    rows_b.append(to_quad(rows_b[1], 2))
+    messages = [(a, swap_cores(a), b, swap_cores(b)) for a, b in zip(rows_a, rows_b)]
 
     one_row = lambda vector: vector[None, :]
     bias_part = lax.dynamic_index_in_dim(

time: 322 us -> 298 us (0.925)
  waiting for transfers between devices: 165 us -> 139 us
    ppermute x21 -> x24, waiting for transfers between devices: 87.4 us -> 52.7 us  [to_quad(): return lax.ppermute(value, 'dp', xor_pairs(n_dp, j))]
    ppermute x15, waiting for transfers between devices: 76.4 us -> 85.1 us  [to_layer(): return lax.ppermute(value, 'dp', xor_pairs(n_dp, bits * QUAD))]
    ppermute x21 -> x24, starting transfers between devices: 24.5 us -> 28.7 us  [to_quad(): return lax.ppermute(value, 'dp', xor_pairs(n_dp, j))]
  transfers between devices with their start and end apart: 45 -> 52, of which waited for: 20 -> 19; matrix products, arithmetic and copies ran while one was open for 1% -> 2% of each run, Pallas kernels for 14% -> 16%
where the time goes in v5:
time: 298 us; the launch traced here: 296 us
  waiting for transfers between devices  139 us (47%)
  Pallas kernels  87.8 us (29%)
  starting transfers between devices  58.5 us (20%)
  other arithmetic  5.75 us (2%)
  local copies, waits for them, and re-layouts  3.5 us (1%)
    ppermute x15, waiting for transfers between devices, to_layer(): return lax.ppermute(value, 'dp', xor_pairs(n_dp, bits * QUAD))  85.1 us
    pallas_call x5, Pallas kernels, branch(): results = call(*operands)  71.7 us
    ppermute x24, waiting for transfers between devices, to_quad(): return lax.ppermute(value, 'dp', xor_pairs(n_dp, j))  52.7 us
    ppermute x24, starting transfers between devices, to_quad(): return lax.ppermute(value, 'dp', xor_pairs(n_dp, j))  28.7 us
    ppermute x15, starting transfers between devices, to_layer(): return lax.ppermute(value, 'dp', xor_pairs(n_dp, bits * QUAD))  27.8 us
    pallas_call x6, Pallas kernels, staged_call(): pl.pallas_call(whole, in_specs=[SMEM] * len(scalars) + [ANY] * count, out...  8.48 us
  transfers between devices with their start and end apart: 52, of which 19 were waited for; matrix products, arithmetic and copies ran while one was open for 2% of the time, Pallas kernels for 16%

profile of v5, /device:TPU:10, one launch (start us, length us, event | category | flops | bytes accessed | tf_op | source)
XLA Modules:
  0.0 296.3 jit_solution(3129032943692555488)
XLA Ops:
  1.4 2.1 shard_map.264
  4.0 1.5 collective-permute-start.11
  5.5 1.4 collective-permute-start.12
  7.5 1.0 convert_reduce_fusion
  9.4 1.6 collective-permute-start.17
  11.0 1.4 collective-permute-start.18
  12.4 0.9 pad_maximum_fusion.1.refs_8_
  13.3 2.7 collective-permute-start.14
  16.6 1.5 collective-permute-start.6
  18.1 1.2 collective-permute-start.2
  19.9 2.1 shard_map.263
  22.1 1.2 collective-permute-start.4
  23.3 2.7 collective-permute-done.14.refs_10_
  26.0 1.4 collective-permute-start.13
  27.3 7.0 %collective-permute-done.13.refs_9_ = bf16[4,64,512]{2,1,0:T(8,128)(2,1)} collective-permute-done((bf16[4,64,512]{2,1,0:T(8,128)(2,1)S(1)}, bf16[4,64,512]{2,1,0:T(8,128)(2,1)}, u32[]{:S(2)}, u32[]{:S(2)}) %collective-permute-start.13) | collective-permute-done | bytes 262176 | tf_op jit(solution)/shard_map/ppermute | solution.py:884
  35.4 6.4 %collective-permute-done.4.refs_8_ = bf16[288,1024]{1,0:T(8,128)(2,1)S(1)} collective-permute-done((bf16[288,1024]{1,0:T(8,128)(2,1)}, bf16[288,1024]{1,0:T(8,128)(2,1)S(1)}, u32[]{:S(2)}, u32[]{:S(2)}) %collective-permute-start.4) | collective-permute-done | bytes 589856 | tf_op jit(solution)/shard_map/ppermute | solution.py:881
  41.8 1.0 collective-permute-start.22
  42.8 0.8 collective-permute-done.15.refs_11_
  43.7 1.5 collective-permute-start.24
  45.2 5.6 %collective-permute-done.refs_4_ = bf16[288,1024]{1,0:T(8,128)(2,1)S(1)} collective-permute-done((bf16[288,1024]{1,0:T(8,128)(2,1)}, bf16[288,1024]{1,0:T(8,128)(2,1)S(1)}, u32[]{:S(2)}, u32[]{:S(2)}) %collective-permute-start) | collective-permute-done | bytes 589856 | tf_op jit(solution)/shard_map/ppermute | solution.py:881
  52.6 10.4 %collective-permute-done.22.refs_4_ = bf16[288,1024]{1,0:T(8,128)(2,1)} collective-permute-done((bf16[288,1024]{1,0:T(8,128)(2,1)S(1)}, bf16[288,1024]{1,0:T(8,128)(2,1)}, u32[]{:S(2)}, u32[]{:S(2)}) %collective-permute-start.22) | collective-permute-done | bytes 589856 | tf_op jit(solution)/shard_map/ppermute | solution.py:881
  63.0 1.0 pad_maximum_fusion.refs_10_.refs_22_
  64.6 9.6 %shard_map.265 = (bf16[1,512,1024]{2,1,0:T(8,128)(2,1)}, bf16[1,512,1024]{2,1,0:T(8,128)(2,1)}, f32[16,1024]{1,0:T(8,128)}, f32[384,128]{1,0:T(8,128)}, f32[1,51...) custom-call(s32[3]{0:T(128)} %pad_add_fusion.meta.refs_0_, f32[1,1024]{1,0:T(1,128)} %bitcast.45, f32[1,1024]{1,0:T(1,128)} %bitcast.48, ...), custom_call_target="tpu_custom_call" | custom-call | flops 2080374784 | bytes 9437184 | tf_op jit(solution)/shard_map/pallas_call | solution.py:812
  74.3 2.3 collective-permute-start.21
  76.5 1.3 collective-permute-start.20
  77.8 1.5 collective-permute-start.19
  79.3 15.7 %shard_map.266 = (bf16[2,512,1024]{2,1,0:T(8,128)(2,1)}, bf16[2,512,1024]{2,1,0:T(8,128)(2,1)}, f32[16,1024]{1,0:T(8,128)}, f32[384,128]{1,0:T(8,128)}, f32[1,512,1024]{2,1,0:T(8,128)}) custom-call(s32[3]{0:T(128)} %pad_add_fusion.meta.refs_0_, f32[1,1024]{1,0:T(1,128)} %bitcast.46, f32[1,1024]{1,0:T(1,128)} %bitcast.49, ...), custom_call_target="tpu_custom_call" | custom-call | flops 4160749568 | bytes 13631488 | tf_op jit(solution)/shard_map/pallas_call | solution.py:812
  95.0 10.4 %shard_map.267 = (bf16[1,512,1024]{2,1,0:T(8,128)(2,1)}, bf16[1,512,1024]{2,1,0:T(8,128)(2,1)}, f32[16,1024]{1,0:T(8,128)}, f32[384,128]{1,0:T(8,128)}, f32[4,64...) custom-call(s32[3]{0:T(128)} %pad_add_fusion.meta.refs_0_, ...), custom_call_target="tpu_custom_call" | custom-call | flops 2080374784 | bytes 9437184 | tf_op jit(solution)/shard_map/pallas_call | solution.py:812
  105.5 6.3 %collective-permute-done.21.refs_13_.refs_25_ = bf16[4,2,64,512]{3,2,1,0:T(8,128)(2,1)S(1)} collective-permute-done((bf16[4,2,64,512]{3,2,1,0:T(8,128)(2,1)S(1)}, bf16[4,2,64,512]{3,2,1,0:T(8,128)(2,1)S(1)}, u32[]{:S(2)}, u32[]{:S(2)}) %collective-permute-start.21) | collective-permute-done | bytes 524320 | tf_op jit(solution)/shard_map/ppermute | solution.py:884
  111.8 9.8 %collective-permute-done.20.refs_12_.refs_24_ = bf16[4,2,64,512]{3,2,1,0:T(8,128)(2,1)S(1)} collective-permute-done((bf16[4,2,64,512]{3,2,1,0:T(8,128)(2,1)S(1)}, bf16[4,2,64,512]{3,2,1,0:T(8,128)(2,1)S(1)}, u32[]{:S(2)}, u32[]{:S(2)}) %collective-permute-start.20) | collective-permute-done | bytes 524320 | tf_op jit(solution)/shard_map/ppermute | solution.py:884
  122.6 10.3 %shard_map.268 = (bf16[2,256,1024]{2,1,0:T(8,128)(2,1)}, bf16[2,256,1024]{2,1,0:T(8,128)(2,1)}, f32[16,1024]{1,0:T(8,128)}, f32[8,512]{1,0:T(8,128)}, f32[2,512,1024]{2,1,0:T(8,128)}) custom-call(s32[3]{0:T(128)} %pad_add_fusion.meta.refs_0_, f32[1,1024]{1,0:T(1,128)} %bitcast.51, f32[1,1024]{1,0:T(1,128)} %bitcast.53, ...), custom_call_target="tpu_custom_call" | custom-call | flops 3221225472 | bytes 14680064 | tf_op jit(solution)/shard_map/pallas_call | solution.py:812
  132.9 25.7 %shard_map.269 = (bf16[2,256,1024]{2,1,0:T(8,128)(2,1)}, bf16[2,256,1024]{2,1,0:T(8,128)(2,1)}, bf16[2,256,1024]{2,1,0:T(8,128)(2,1)}, bf16[2,256,1024]{2,1,0:T(...) custom-call(s32[3]{0:T(128)} %pad_add_fusion.meta.refs_0_, ...), custom_call_target="tpu_custom_call" | custom-call | flops 9663676416 | bytes 23068672 | tf_op jit(solution)/shard_map/pallas_call | solution.py:812
  158.6 1.8 shard_map.274
  160.4 1.4 collective-permute-done.33
  161.9 0.8 add.37
  162.7 1.5 collective-permute-start.36
  164.7 1.5 collective-permute-start.34
  166.2 2.2 collective-permute-start.40
  169.0 1.8 collective-permute-start.39
  170.8 2.3 collective-permute-done.39.refs_3_
  173.1 5.0 %collective-permute-start.38 = (f32[96,128]{1,0:T(8,128)S(1)}, f32[96,128]{1,0:T(8,128)S(1)}, u32[]{:S(2)}, u32[]{:S(2)}) collective-permute-start(f32[96,128]{1,0:T(8,128)S(1)} %add_add_fusion.refs_0_), channel_id=1, source_target_pairs={{0,16},{2,18},{4,20},{6,22},{8,24},{10,26},{12,28},{14,30},{16,0},... | collective-permute-start | bytes 147464 | tf_op jit(solution)/shard_map/ppermute | solution.py:884
  178.1 2.1 collective-permute-done.38.refs_2_
  180.2 2.9 collective-permute-start.41
  183.1 1.2 collective-permute-start.42
  184.3 12.9 %collective-permute-done.41.refs_2_ = bf16[4,64,512]{2,1,0:T(8,128)(2,1)S(1)} collective-permute-done((bf16[4,64,512]{2,1,0:T(8,128)(2,1)S(1)}, bf16[4,64,512]{2,1,0:T(8,128)(2,1)S(1)}, u32[]{:S(2)}, u32[]{:S(2)}) %collective-permute-start.41) | collective-permute-done | bytes 262176 | tf_op jit(solution)/shard_map/ppermute | solution.py:884
  197.2 3.1 %collective-permute-start.46 = (bf16[4,2,64,512]{3,2,1,0:T(8,128)(2,1)}, bf16[4,2,64,512]{3,2,1,0:T(8,128)(2,1)S(1)}, u32[]{:S(2)}, u32[]{:S(2)}) collective-permute-start(bf16[4,2,64,512]{3,2,1,0:T(8,128)(2,1)} %get-tuple-element.139), channel_id=1, source_target_pairs={{0,8},{2,10},{4,12},{6,14},{8,0},{10,2},{12,4},{14,6},{16,24},{18,... | collective-permute-start | bytes 1572872 | tf_op jit(solution)/shard_map/ppermute | solution.py:884
  200.4 4.1 %collective-permute-done.42.refs_3_ = bf16[4,64,512]{2,1,0:T(8,128)(2,1)S(1)} collective-permute-done((bf16[4,64,512]{2,1,0:T(8,128)(2,1)S(1)}, bf16[4,64,512]{2,1,0:T(8,128)(2,1)S(1)}, u32[]{:S(2)}, u32[]{:S(2)}) %collective-permute-start.42) | collective-permute-done | bytes 262176 | tf_op jit(solution)/shard_map/ppermute | solution.py:884
  204.7 1.8 collective-permute-start.43
  206.5 1.5 collective-permute-start.44
  208.0 1.5 collective-permute-start.37
  211.8 13.1 %collective-permute-done.37.refs_1_ = f32[96,128]{1,0:T(8,128)S(1)} collective-permute-done((f32[96,128]{1,0:T(8,128)S(1)}, f32[96,128]{1,0:T(8,128)S(1)}, u32[]{:S(2)}, u32[]{:S(2)}) %collective-permute-start.37) | collective-permute-done | bytes 49184 | tf_op jit(solution)/shard_map/ppermute | solution.py:884
  224.9 1.8 collective-permute-start.28
  226.7 1.8 collective-permute-start.32
  229.3 23.9 %collective-permute-done.48.refs_3_ = bf16[4,2,64,512]{3,2,1,0:T(8,128)(2,1)S(1)} collective-permute-done((bf16[4,2,64,512]{3,2,1,0:T(8,128)(2,1)S(1)}, bf16[4,2,64,512]{3,2,1,0:T(8,128)(2,1)S(1)}, u32[]{:S(2)}, u32[]{:S(2)}) %collective-permute-start.48) | collective-permute-done | bytes 524320 | tf_op jit(solution)/shard_map/ppermute | solution.py:884
  253.2 1.3 collective-permute-start.45
  255.0 20.1 %collective-permute-done.45.refs_4_ = bf16[64,512]{1,0:T(8,128)(2,1)S(1)} collective-permute-done((bf16[64,512]{1,0:T(8,128)(2,1)S(1)}, bf16[64,512]{1,0:T(8,128)(2,1)S(1)}, u32[]{:S(2)}, u32[]{:S(2)}) %collective-permute-start.45) | collective-permute-done | bytes 65568 | tf_op jit(solution)/shard_map/ppermute | solution.py:881
  275.4 4.7 %collective-permute-done.49.refs_2_ = bf16[2,64,512]{2,1,0:T(8,128)(2,1)S(1)} collective-permute-done((bf16[2,64,512]{2,1,0:T(8,128)(2,1)S(1)}, bf16[2,64,512]{2,1,0:T(8,128)(2,1)S(1)}, u32[]{:S(2)}, u32[]{:S(2)}) %collective-permute-start.49) | collective-permute-done | bytes 131104 | tf_op jit(solution)/shard_map/ppermute | solution.py:881
  280.9 4.2 %collective-permute-done.50.refs_3_ = bf16[2,64,512]{2,1,0:T(8,128)(2,1)S(1)} collective-permute-done((bf16[2,64,512]{2,1,0:T(8,128)(2,1)S(1)}, bf16[2,64,512]{2,1,0:T(8,128)(2,1)S(1)}, u32[]{:S(2)}, u32[]{:S(2)}) %collective-permute-start.50) | collective-permute-done | bytes 131104 | tf_op jit(solution)/shard_map/ppermute | solution.py:881
  285.1 1.9 collective-permute-start.51
  287.0 0.9 shard_map.275
  287.9 1.8 shard_map.277
  289.7 1.2 collective-permute-done.51.refs_4_
  290.9 2.1 shard_map.279
  293.2 2.9 shard_map.273
  (134 shorter events, 14.2 us)
Async XLA Ops:
  0.6 50.2 %copy-start.13 = (f32[1536]{0:T(1024)S(1)}, f32[1536]{0:T(1024)}, u32[]{:S(2)}) copy-start(f32[1536]{0:T(1024)} %param.24) | copy-start | bytes 18436
  0.7 50.2 %copy-start.14 = (f32[2048]{0:T(1024)S(1)}, f32[2048]{0:T(1024)}, u32[]{:S(2)}) copy-start(f32[2048]{0:T(1024)} %param.28) | copy-start | bytes 24580
  0.7 33.7 %collective-permute-start.9 = (bf16[256,1024]{1,0:T(8,128)(2,1)}, bf16[256,1024]{1,0:T(8,128)(2,1)S(1)}, u32[]{:S(2)}, u32[]{:S(2)}) collective-permute-start(bf16[256,1024]{1,0:T(8,128)(2,1)} %refs_3_.1), channel_id=1, source_target_pairs={{0,1},{1,0},{2,3},{3,2},{4,5},{5,4},{6,7},{7,6},{8,9},{9,8},{10,11... | collective-permute-start | bytes 1572872 | tf_op jit(solution)/shard_map/ppermute | solution.py:50
  3.5 5.9 %collective-permute-start.10 = (bf16[64,512]{1,0:T(8,128)(2,1)}, bf16[64,512]{1,0:T(8,128)(2,1)S(1)}, u32[]{:S(2)}, u32[]{:S(2)}) collective-permute-start(bf16[64,512]{1,0:T(8,128)(2,1)} %get-tuple-element.84), channel_id=1, source_target_pairs={{0,2},{2,0},{4,6},{6,4},{8,10},{10,8},{12,14},{14,12},{16,18},{18,... | collective-permute-start | bytes 196616 | tf_op jit(solution)/shard_map/ppermute | solution.py:881
  4.0 7.0 %collective-permute-start.11 = (bf16[64,512]{1,0:T(8,128)(2,1)}, bf16[64,512]{1,0:T(8,128)(2,1)S(1)}, u32[]{:S(2)}, u32[]{:S(2)}) collective-permute-start(bf16[64,512]{1,0:T(8,128)(2,1)} %get-tuple-element.85), channel_id=1, source_target_pairs={{0,4},{2,6},{4,0},{6,2},{8,12},{10,14},{12,8},{14,10},{16,20},{18,... | collective-permute-start | bytes 196616 | tf_op jit(solution)/shard_map/ppermute | solution.py:881
  5.5 6.9 %collective-permute-start.12 = (bf16[64,512]{1,0:T(8,128)(2,1)}, bf16[64,512]{1,0:T(8,128)(2,1)S(1)}, u32[]{:S(2)}, u32[]{:S(2)}) collective-permute-start(bf16[64,512]{1,0:T(8,128)(2,1)} %get-tuple-element.86), channel_id=1, source_target_pairs={{0,6},{2,4},{4,2},{6,0},{8,14},{10,12},{12,10},{14,8},{16,22},{18,... | collective-permute-start | bytes 196616 | tf_op jit(solution)/shard_map/ppermute | solution.py:881
  7.0 9.6 %collective-permute-start.16 = (bf16[2,64,512]{2,1,0:T(8,128)(2,1)}, bf16[2,64,512]{2,1,0:T(8,128)(2,1)S(1)}, u32[]{:S(2)}, u32[]{:S(2)}) collective-permute-start(bf16[2,64,512]{2,1,0:T(8,128)(2,1)} %get-tuple-element.96), channel_id=1, source_target_pairs={{0,2},{2,0},{4,6},{6,4},{8,10},{10,8},{12,14},{14,12},{16,18},{18,... | collective-permute-start | bytes 393224 | tf_op jit(solution)/shard_map/ppermute | solution.py:881
  9.4 8.7 %collective-permute-start.17 = (bf16[2,64,512]{2,1,0:T(8,128)(2,1)}, bf16[2,64,512]{2,1,0:T(8,128)(2,1)S(1)}, u32[]{:S(2)}, u32[]{:S(2)}) collective-permute-start(bf16[2,64,512]{2,1,0:T(8,128)(2,1)} %get-tuple-element.97), channel_id=1, source_target_pairs={{0,4},{2,6},{4,0},{6,2},{8,12},{10,14},{12,8},{14,10},{16,20},{18,... | collective-permute-start | bytes 393224 | tf_op jit(solution)/shard_map/ppermute | solution.py:881
  11.0 11.1 %collective-permute-start.18 = (bf16[2,64,512]{2,1,0:T(8,128)(2,1)}, bf16[2,64,512]{2,1,0:T(8,128)(2,1)S(1)}, u32[]{:S(2)}, u32[]{:S(2)}) collective-permute-start(bf16[2,64,512]{2,1,0:T(8,128)(2,1)} %get-tuple-element.98), channel_id=1, source_target_pairs={{0,6},{2,4},{4,2},{6,0},{8,14},{10,12},{12,10},{14,8},{16,22},{18,... | collective-permute-start | bytes 393224 | tf_op jit(solution)/shard_map/ppermute | solution.py:881
  13.3 51.3 %copy-start.12 = (bf16[4,64,512]{2,1,0:T(8,128)(2,1)}, bf16[4,64,512]{2,1,0:T(8,128)(2,1)S(1)}, u32[]{:S(2)}) copy-start(bf16[4,64,512]{2,1,0:T(8,128)(2,1)S(1)} %pad_maximum_fusion.1.refs_8_) | copy-start | bytes 786436
  13.3 12.7 %collective-permute-start.14 = (bf16[4,64,512]{2,1,0:T(8,128)(2,1)S(1)}, bf16[4,64,512]{2,1,0:T(8,128)(2,1)S(1)}, u32[]{:S(2)}, u32[]{:S(2)}) collective-permute-start(bf16[4,64,512]{2,1,0:T(8,128)(2,1)S(1)} %pad_maximum_fusion.1.refs_8_), channel_id=1, source_target_pairs={{0,16},{2,18},{4,20},{6,22},{8,24},{10,26},{12,28},{14,30},{16,0},... | collective-permute-start | bytes 786440 | tf_op jit(solution)/shard_map/ppermute | solution.py:884
  16.6 18.4 %collective-permute-start.6 = (bf16[256,1024]{1,0:T(8,128)(2,1)}, bf16[256,1024]{1,0:T(8,128)(2,1)}, u32[]{:S(2)}, u32[]{:S(2)}) collective-permute-start(bf16[256,1024]{1,0:T(8,128)(2,1)} %refs_3_.1), channel_id=1, source_target_pairs={{0,4},{2,6},{4,0},{6,2},{8,12},{10,14},{12,8},{14,10},{16,20},{18,... | collective-permute-start | bytes 1572872 | tf_op jit(solution)/shard_map/ppermute | solution.py:881
  18.1 17.0 %collective-permute-start.2 = (bf16[256,1024]{1,0:T(8,128)(2,1)}, bf16[256,1024]{1,0:T(8,128)(2,1)}, u32[]{:S(2)}, u32[]{:S(2)}) collective-permute-start(bf16[256,1024]{1,0:T(8,128)(2,1)} %refs_3_.1), channel_id=1, source_target_pairs={{0,2},{2,0},{4,6},{6,4},{8,10},{10,8},{12,14},{14,12},{16,18},{18,... | collective-permute-start | bytes 1572872 | tf_op jit(solution)/shard_map/ppermute | solution.py:881
  22.1 19.7 %collective-permute-start.4 = (bf16[288,1024]{1,0:T(8,128)(2,1)}, bf16[288,1024]{1,0:T(8,128)(2,1)S(1)}, u32[]{:S(2)}, u32[]{:S(2)}) collective-permute-start(bf16[288,1024]{1,0:T(8,128)(2,1)} %get-tuple-element.82.refs_4_.refs_12_), channel_id=1, source_target_pairs={{0,4},{2,6},{4,0},{6,2},{8,12},{10,14},{12,8},{14,10},{16,20},{18,... | collective-permute-start | bytes 1769480 | tf_op jit(solution)/shard_map/ppermute | solution.py:881
  26.0 8.3 %collective-permute-start.13 = (bf16[4,64,512]{2,1,0:T(8,128)(2,1)S(1)}, bf16[4,64,512]{2,1,0:T(8,128)(2,1)}, u32[]{:S(2)}, u32[]{:S(2)}) collective-permute-start(bf16[4,64,512]{2,1,0:T(8,128)(2,1)S(1)} %pad_maximum_fusion.1.refs_8_), channel_id=1, source_target_pairs={{0,8},{2,10},{4,12},{6,14},{8,0},{10,2},{12,4},{14,6},{16,24},{18,... | collective-permute-start | bytes 786440 | tf_op jit(solution)/shard_map/ppermute | solution.py:884
  34.3 10.9 %collective-permute-start.8 = (bf16[288,1024]{1,0:T(8,128)(2,1)}, bf16[288,1024]{1,0:T(8,128)(2,1)S(1)}, u32[]{:S(2)}, u32[]{:S(2)}) collective-permute-start(bf16[288,1024]{1,0:T(8,128)(2,1)} %get-tuple-element.82.refs_4_.refs_12_), channel_id=1, source_target_pairs={{0,1},{1,0},{2,3},{3,2},{4,5},{5,4},{6,7},{7,6},{8,9},{9,8},{10,11... | collective-permute-start | bytes 1769480 | tf_op jit(solution)/shard_map/ppermute | solution.py:50
  34.3 16.5 %collective-permute-start = (bf16[288,1024]{1,0:T(8,128)(2,1)}, bf16[288,1024]{1,0:T(8,128)(2,1)S(1)}, u32[]{:S(2)}, u32[]{:S(2)}) collective-permute-start(bf16[288,1024]{1,0:T(8,128)(2,1)} %get-tuple-element.82.refs_4_.refs_12_), channel_id=1, source_target_pairs={{0,2},{2,0},{4,6},{6,4},{8,10},{10,8},{12,14},{14,12},{16,18},{18,... | collective-permute-start | bytes 1769480 | tf_op jit(solution)/shard_map/ppermute | solution.py:881
  34.9 16.0 %collective-permute-start.7 = (bf16[256,1024]{1,0:T(8,128)(2,1)}, bf16[256,1024]{1,0:T(8,128)(2,1)}, u32[]{:S(2)}, u32[]{:S(2)}) collective-permute-start(bf16[256,1024]{1,0:T(8,128)(2,1)} %collective-permute-done.6.refs_10_), channel_id=1, source_target_pairs={{0,1},{1,0},{2,3},{3,2},{4,5},{5,4},{6,7},{7,6},{8,9},{9,8},{10,11... | collective-permute-start | bytes 1572872 | tf_op jit(solution)/shard_map/ppermute | solution.py:50
  35.1 8.6 %collective-permute-start.15 = (bf16[4,64,512]{2,1,0:T(8,128)(2,1)S(1)}, bf16[4,64,512]{2,1,0:T(8,128)(2,1)S(1)}, u32[]{:S(2)}, u32[]{:S(2)}) collective-permute-start(bf16[4,64,512]{2,1,0:T(8,128)(2,1)S(1)} %collective-permute-done.14.refs_10_), channel_id=1, source_target_pairs={{0,8},{2,10},{4,12},{6,14},{8,0},{10,2},{12,4},{14,6},{16,24},{18,... | collective-permute-start | bytes 786440 | tf_op jit(solution)/shard_map/ppermute | solution.py:884
  41.8 21.3 %collective-permute-start.22 = (bf16[288,1024]{1,0:T(8,128)(2,1)S(1)}, bf16[288,1024]{1,0:T(8,128)(2,1)}, u32[]{:S(2)}, u32[]{:S(2)}) collective-permute-start(bf16[288,1024]{1,0:T(8,128)(2,1)S(1)} %collective-permute-done.4.refs_8_), channel_id=1, source_target_pairs={{0,2},{2,0},{4,6},{6,4},{8,10},{10,8},{12,14},{14,12},{16,18},{18,... | collective-permute-start | bytes 1769480 | tf_op jit(solution)/shard_map/ppermute | solution.py:881
  43.7 20.4 %collective-permute-start.24 = (bf16[256,1024]{1,0:T(8,128)(2,1)}, bf16[256,1024]{1,0:T(8,128)(2,1)}, u32[]{:S(2)}, u32[]{:S(2)}) collective-permute-start(bf16[256,1024]{1,0:T(8,128)(2,1)} %collective-permute-done.2.refs_6_), channel_id=1, source_target_pairs={{0,4},{2,6},{4,0},{6,2},{8,12},{10,14},{12,8},{14,10},{16,20},{18,... | collective-permute-start | bytes 1572872 | tf_op jit(solution)/shard_map/ppermute | solution.py:881
  45.2 31.4 %collective-permute-start.5 = (bf16[288,1024]{1,0:T(8,128)(2,1)S(1)}, bf16[288,1024]{1,0:T(8,128)(2,1)}, u32[]{:S(2)}, u32[]{:S(2)}) collective-permute-start(bf16[288,1024]{1,0:T(8,128)(2,1)S(1)} %collective-permute-done.4.refs_8_), channel_id=1, source_target_pairs={{0,1},{1,0},{2,3},{3,2},{4,5},{5,4},{6,7},{7,6},{8,9},{9,8},{10,11... | collective-permute-start | bytes 1769480 | tf_op jit(solution)/shard_map/ppermute | solution.py:50
  50.8 27.0 %collective-permute-start.1 = (bf16[288,1024]{1,0:T(8,128)(2,1)S(1)}, bf16[288,1024]{1,0:T(8,128)(2,1)}, u32[]{:S(2)}, u32[]{:S(2)}) collective-permute-start(bf16[288,1024]{1,0:T(8,128)(2,1)S(1)} %collective-permute-done.refs_4_), channel_id=1, source_target_pairs={{0,1},{1,0},{2,3},{3,2},{4,5},{5,4},{6,7},{7,6},{8,9},{9,8},{10,11... | collective-permute-start | bytes 1769480 | tf_op jit(solution)/shard_map/ppermute | solution.py:50
  50.9 23.4 %collective-permute-start.3 = (bf16[256,1024]{1,0:T(8,128)(2,1)}, bf16[256,1024]{1,0:T(8,128)(2,1)}, u32[]{:S(2)}, u32[]{:S(2)}) collective-permute-start(bf16[256,1024]{1,0:T(8,128)(2,1)} %collective-permute-done.2.refs_6_), channel_id=1, source_target_pairs={{0,1},{1,0},{2,3},{3,2},{4,5},{5,4},{6,7},{7,6},{8,9},{9,8},{10,11... | collective-permute-start | bytes 1572872 | tf_op jit(solution)/shard_map/ppermute | solution.py:50
  63.0 32.0 %collective-permute-start.23 = (bf16[288,1024]{1,0:T(8,128)(2,1)}, bf16[288,1024]{1,0:T(8,128)(2,1)}, u32[]{:S(2)}, u32[]{:S(2)}) collective-permute-start(bf16[288,1024]{1,0:T(8,128)(2,1)} %collective-permute-done.22.refs_4_), channel_id=1, source_target_pairs={{0,1},{1,0},{2,3},{3,2},{4,5},{5,4},{6,7},{7,6},{8,9},{9,8},{10,11... | collective-permute-start | bytes 1769480 | tf_op jit(solution)/shard_map/ppermute | solution.py:50
  64.0 31.0 %collective-permute-start.25 = (bf16[256,1024]{1,0:T(8,128)(2,1)}, bf16[256,1024]{1,0:T(8,128)(2,1)}, u32[]{:S(2)}, u32[]{:S(2)}) collective-permute-start(bf16[256,1024]{1,0:T(8,128)(2,1)} %collective-permute-done.24.refs_6_), channel_id=1, source_target_pairs={{0,1},{1,0},{2,3},{3,2},{4,5},{5,4},{6,7},{7,6},{8,9},{9,8},{10,11... | collective-permute-start | bytes 1572872 | tf_op jit(solution)/shard_map/ppermute | solution.py:50
  74.3 37.5 %collective-permute-start.21 = (bf16[4,2,64,512]{3,2,1,0:T(8,128)(2,1)S(1)}, bf16[4,2,64,512]{3,2,1,0:T(8,128)(2,1)S(1)}, u32[]{:S(2)}, u32[]{:S(2)}) collective-permute-start(bf16[4,2,64,512]{3,2,1,0:T(8,128)(2,1)S(1)} %pad_maximum_fusion.refs_10_.refs_22_), channel_id=1, source_target_pairs={{0,24},{2,26},{4,28},{6,30},{8,16},{10,18},{12,20},{14,22},{16,8},... | collective-permute-start | bytes 1572872 | tf_op jit(solution)/shard_map/ppermute | solution.py:884
  76.5 45.1 %collective-permute-start.20 = (bf16[4,2,64,512]{3,2,1,0:T(8,128)(2,1)S(1)}, bf16[4,2,64,512]{3,2,1,0:T(8,128)(2,1)S(1)}, u32[]{:S(2)}, u32[]{:S(2)}) collective-permute-start(bf16[4,2,64,512]{3,2,1,0:T(8,128)(2,1)S(1)} %pad_maximum_fusion.refs_10_.refs_22_), channel_id=1, source_target_pairs={{0,16},{2,18},{4,20},{6,22},{8,24},{10,26},{12,28},{14,30},{16,0},... | collective-permute-start | bytes 1572872 | tf_op jit(solution)/shard_map/ppermute | solution.py:884
  77.8 43.8 %collective-permute-start.19 = (bf16[4,2,64,512]{3,2,1,0:T(8,128)(2,1)S(1)}, bf16[4,2,64,512]{3,2,1,0:T(8,128)(2,1)S(1)}, u32[]{:S(2)}, u32[]{:S(2)}) collective-permute-start(bf16[4,2,64,512]{3,2,1,0:T(8,128)(2,1)S(1)} %pad_maximum_fusion.refs_10_.refs_22_), channel_id=1, source_target_pairs={{0,8},{2,10},{4,12},{6,14},{8,0},{10,2},{12,4},{14,6},{16,24},{18,... | collective-permute-start | bytes 1572872 | tf_op jit(solution)/shard_map/ppermute | solution.py:884
  132.9 50.2 %copy-start.25 = (bf16[4,64,512]{2,1,0:T(8,128)(2,1)S(1)}, bf16[4,64,512]{2,1,0:T(8,128)(2,1)}, u32[]{:S(2)}) copy-start(bf16[4,64,512]{2,1,0:T(8,128)(2,1)} %get-tuple-element.129) | copy-start | bytes 786436
  132.9 71.5 %copy-start.7 = (f32[4,64,512]{2,1,0:T(8,128)S(1)}, f32[4,64,512]{2,1,0:T(8,128)}, u32[]{:S(2)}) copy-start(f32[4,64,512]{2,1,0:T(8,128)} %get-tuple-element.126.refs_0_) | copy-start | bytes 1572868
  158.6 50.9 %copy-start.4 = (bf16[2,256,1024]{2,1,0:T(8,128)(2,1)S(1)}, bf16[2,256,1024]{2,1,0:T(8,128)(2,1)}, u32[]{:S(2)}) copy-start(bf16[2,256,1024]{2,1,0:T(8,128)(2,1)} %get-tuple-element.109.mine) | copy-start | bytes 3145732
  160.4 1.4 collective-permute-start.33
  162.7 5.7 %collective-permute-start.36 = (f32[96,128]{1,0:T(8,128)S(1)}, f32[96,128]{1,0:T(8,128)S(1)}, u32[]{:S(2)}, u32[]{:S(2)}) collective-permute-start(f32[96,128]{1,0:T(8,128)S(1)} %add.37), channel_id=1, source_target_pairs={{0,6},{2,4},{4,2},{6,0},{8,14},{10,12},{12,10},{14,8},{16,22},{18,... | collective-permute-start | bytes 147464 | tf_op jit(solution)/shard_map/ppermute | solution.py:881
  164.2 4.7 %collective-permute-start.35 = (f32[96,128]{1,0:T(8,128)S(1)}, f32[96,128]{1,0:T(8,128)S(1)}, u32[]{:S(2)}, u32[]{:S(2)}) collective-permute-start(f32[96,128]{1,0:T(8,128)S(1)} %add.37), channel_id=1, source_target_pairs={{0,4},{2,6},{4,0},{6,2},{8,12},{10,14},{12,8},{14,10},{16,20},{18,... | collective-permute-start | bytes 147464 | tf_op jit(solution)/shard_map/ppermute | solution.py:881
  164.7 4.3 %collective-permute-start.34 = (f32[96,128]{1,0:T(8,128)S(1)}, f32[96,128]{1,0:T(8,128)S(1)}, u32[]{:S(2)}, u32[]{:S(2)}) collective-permute-start(f32[96,128]{1,0:T(8,128)S(1)} %add.37), channel_id=1, source_target_pairs={{0,2},{2,0},{4,6},{6,4},{8,10},{10,8},{12,14},{14,12},{16,18},{18,... | collective-permute-start | bytes 147464 | tf_op jit(solution)/shard_map/ppermute | solution.py:881
  166.2 16.9 %collective-permute-start.40 = (bf16[4,64,512]{2,1,0:T(8,128)(2,1)S(1)}, bf16[4,64,512]{2,1,0:T(8,128)(2,1)S(1)}, u32[]{:S(2)}, u32[]{:S(2)}) collective-permute-start(bf16[4,64,512]{2,1,0:T(8,128)(2,1)S(1)} %copy-done.28), channel_id=1, source_target_pairs={{0,8},{2,10},{4,12},{6,14},{8,0},{10,2},{12,4},{14,6},{16,24},{18,... | collective-permute-start | bytes 786440 | tf_op jit(solution)/shard_map/ppermute | solution.py:884
  168.4 36.3 %collective-permute-start.27 = (bf16[2,256,1024]{2,1,0:T(8,128)(2,1)}, bf16[2,256,1024]{2,1,0:T(8,128)(2,1)S(1)}, u32[]{:S(2)}, u32[]{:S(2)}) collective-permute-start(bf16[2,256,1024]{2,1,0:T(8,128)(2,1)} %get-tuple-element.110), channel_id=1, source_target_pairs={{0,1},{1,0},{2,3},{3,2},{4,5},{5,4},{6,7},{7,6},{8,9},{9,8},{10,11... | collective-permute-start | bytes 3145736 | tf_op jit(solution)/shard_map/ppermute | solution.py:50
  168.4 38.1 %collective-permute-start.29 = (bf16[2,256,1024]{2,1,0:T(8,128)(2,1)}, bf16[2,256,1024]{2,1,0:T(8,128)(2,1)S(1)}, u32[]{:S(2)}, u32[]{:S(2)}) collective-permute-start(bf16[2,256,1024]{2,1,0:T(8,128)(2,1)} %get-tuple-element.112), channel_id=1, source_target_pairs={{0,1},{1,0},{2,3},{3,2},{4,5},{5,4},{6,7},{7,6},{8,9},{9,8},{10,11... | collective-permute-start | bytes 3145736 | tf_op jit(solution)/shard_map/ppermute | solution.py:50
  168.9 39.1 %collective-permute-start.31 = (bf16[2,256,1024]{2,1,0:T(8,128)(2,1)S(1)}, bf16[2,256,1024]{2,1,0:T(8,128)(2,1)S(1)}, u32[]{:S(2)}, u32[]{:S(2)}) collective-permute-start(bf16[2,256,1024]{2,1,0:T(8,128)(2,1)S(1)} %copy-done.16), channel_id=1, source_target_pairs={{0,1},{1,0},{2,3},{3,2},{4,5},{5,4},{6,7},{7,6},{8,9},{9,8},{10,11... | collective-permute-start | bytes 3145736 | tf_op jit(solution)/shard_map/ppermute | solution.py:50
  169.0 4.2 %collective-permute-start.39 = (f32[96,128]{1,0:T(8,128)S(1)}, f32[96,128]{1,0:T(8,128)S(1)}, u32[]{:S(2)}, u32[]{:S(2)}) collective-permute-start(f32[96,128]{1,0:T(8,128)S(1)} %add_add_fusion.refs_0_), channel_id=1, source_target_pairs={{0,24},{2,26},{4,28},{6,30},{8,16},{10,18},{12,20},{14,22},{16,8},... | collective-permute-start | bytes 147464 | tf_op jit(solution)/shard_map/ppermute | solution.py:884
  173.1 7.0 %collective-permute-start.38 = (f32[96,128]{1,0:T(8,128)S(1)}, f32[96,128]{1,0:T(8,128)S(1)}, u32[]{:S(2)}, u32[]{:S(2)}) collective-permute-start(f32[96,128]{1,0:T(8,128)S(1)} %add_add_fusion.refs_0_), channel_id=1, source_target_pairs={{0,16},{2,18},{4,20},{6,22},{8,24},{10,26},{12,28},{14,30},{16,0},... | collective-permute-start | bytes 147464 | tf_op jit(solution)/shard_map/ppermute | solution.py:884
  180.2 17.0 %collective-permute-start.41 = (bf16[4,64,512]{2,1,0:T(8,128)(2,1)S(1)}, bf16[4,64,512]{2,1,0:T(8,128)(2,1)S(1)}, u32[]{:S(2)}, u32[]{:S(2)}) collective-permute-start(bf16[4,64,512]{2,1,0:T(8,128)(2,1)S(1)} %copy-done.27), channel_id=1, source_target_pairs={{0,16},{2,18},{4,20},{6,22},{8,24},{10,26},{12,28},{14,30},{16,0},... | collective-permute-start | bytes 786440 | tf_op jit(solution)/shard_map/ppermute | solution.py:884
  183.1 21.3 %collective-permute-start.42 = (bf16[4,64,512]{2,1,0:T(8,128)(2,1)S(1)}, bf16[4,64,512]{2,1,0:T(8,128)(2,1)S(1)}, u32[]{:S(2)}, u32[]{:S(2)}) collective-permute-start(bf16[4,64,512]{2,1,0:T(8,128)(2,1)S(1)} %copy-done.25), channel_id=1, source_target_pairs={{0,24},{2,26},{4,28},{6,30},{8,16},{10,18},{12,20},{14,22},{16,8},... | collective-permute-start | bytes 786440 | tf_op jit(solution)/shard_map/ppermute | solution.py:884
  197.2 29.5 %collective-permute-start.46 = (bf16[4,2,64,512]{3,2,1,0:T(8,128)(2,1)}, bf16[4,2,64,512]{3,2,1,0:T(8,128)(2,1)S(1)}, u32[]{:S(2)}, u32[]{:S(2)}) collective-permute-start(bf16[4,2,64,512]{3,2,1,0:T(8,128)(2,1)} %get-tuple-element.139), channel_id=1, source_target_pairs={{0,8},{2,10},{4,12},{6,14},{8,0},{10,2},{12,4},{14,6},{16,24},{18,... | collective-permute-start | bytes 1572872 | tf_op jit(solution)/shard_map/ppermute | solution.py:884
  204.4 24.1 %collective-permute-start.47 = (bf16[4,2,64,512]{3,2,1,0:T(8,128)(2,1)}, bf16[4,2,64,512]{3,2,1,0:T(8,128)(2,1)S(1)}, u32[]{:S(2)}, u32[]{:S(2)}) collective-permute-start(bf16[4,2,64,512]{3,2,1,0:T(8,128)(2,1)} %get-tuple-element.140), channel_id=1, source_target_pairs={{0,16},{2,18},{4,20},{6,22},{8,24},{10,26},{12,28},{14,30},{16,0},... | collective-permute-start | bytes 1572872 | tf_op jit(solution)/shard_map/ppermute | solution.py:884
  204.7 20.2 %collective-permute-start.43 = (bf16[64,512]{1,0:T(8,128)(2,1)S(1)}, bf16[64,512]{1,0:T(8,128)(2,1)S(1)}, u32[]{:S(2)}, u32[]{:S(2)}) collective-permute-start(bf16[64,512]{1,0:T(8,128)(2,1)S(1)} %get-tuple-element.131), channel_id=1, source_target_pairs={{0,2},{2,0},{4,6},{6,4},{8,10},{10,8},{12,14},{14,12},{16,18},{18,... | collective-permute-start | bytes 196616 | tf_op jit(solution)/shard_map/ppermute | solution.py:881
  206.5 20.2 %collective-permute-start.44 = (bf16[64,512]{1,0:T(8,128)(2,1)S(1)}, bf16[64,512]{1,0:T(8,128)(2,1)S(1)}, u32[]{:S(2)}, u32[]{:S(2)}) collective-permute-start(bf16[64,512]{1,0:T(8,128)(2,1)S(1)} %get-tuple-element.132), channel_id=1, source_target_pairs={{0,4},{2,6},{4,0},{6,2},{8,12},{10,14},{12,8},{14,10},{16,20},{18,... | collective-permute-start | bytes 196616 | tf_op jit(solution)/shard_map/ppermute | solution.py:881
  208.0 17.0 %collective-permute-start.37 = (f32[96,128]{1,0:T(8,128)S(1)}, f32[96,128]{1,0:T(8,128)S(1)}, u32[]{:S(2)}, u32[]{:S(2)}) collective-permute-start(f32[96,128]{1,0:T(8,128)S(1)} %add_add_fusion.refs_0_), channel_id=1, source_target_pairs={{0,8},{2,10},{4,12},{6,14},{8,0},{10,2},{12,4},{14,6},{16,24},{18,... | collective-permute-start | bytes 147464 | tf_op jit(solution)/shard_map/ppermute | solution.py:884
  211.8 76.1 %copy-start.8 = (s32[3]{0:T(128)S(1)}, s32[3]{0:T(128)}, u32[]{:S(2)}) copy-start(s32[3]{0:T(128)} %pad_add_fusion.meta.refs_0_) | copy-start | bytes 40
  211.8 81.4 %copy-start = (bf16[256,1024]{1,0:T(8,128)(2,1)S(1)}, bf16[256,1024]{1,0:T(8,128)(2,1)}, u32[]{:S(2)}) copy-start(bf16[256,1024]{1,0:T(8,128)(2,1)} %refs_2_.1) | copy-start | bytes 1572868
  211.8 81.4 %copy-start.1 = (bf16[256,1024]{1,0:T(8,128)(2,1)S(1)}, bf16[256,1024]{1,0:T(8,128)(2,1)}, u32[]{:S(2)}) copy-start(bf16[256,1024]{1,0:T(8,128)(2,1)} %refs_3_.1) | copy-start | bytes 1572868
  211.8 81.3 %copy-start.6 = (bf16[2,256,1024]{2,1,0:T(8,128)(2,1)S(1)}, bf16[2,256,1024]{2,1,0:T(8,128)(2,1)}, u32[]{:S(2)}) copy-start(bf16[2,256,1024]{2,1,0:T(8,128)(2,1)} %get-tuple-element.107.refs_4_) | copy-start | bytes 3145732
  211.8 81.3 %copy-start.9 = (f32[1024]{0:T(1024)S(1)}, f32[1024]{0:T(1024)}, u32[]{:S(2)}) copy-start(f32[1024]{0:T(1024)} %param.26) | copy-start | bytes 12292
  211.8 81.3 %copy-start.10 = (f32[1024]{0:T(1024)S(1)}, f32[1024]{0:T(1024)}, u32[]{:S(2)}) copy-start(f32[1024]{0:T(1024)} %param.30) | copy-start | bytes 12292
  224.9 68.2 %collective-permute-start.26 = (bf16[2,256,1024]{2,1,0:T(8,128)(2,1)S(1)}, bf16[2,256,1024]{2,1,0:T(8,128)(2,1)S(1)}, u32[]{:S(2)}, u32[]{:S(2)}) collective-permute-start(bf16[2,256,1024]{2,1,0:T(8,128)(2,1)S(1)} %copy-done.15), channel_id=1, source_target_pairs={{0,1},{1,0},{2,3},{3,2},{4,5},{5,4},{6,7},{7,6},{8,9},{9,8},{10,11... | collective-permute-start | bytes 3145736 | tf_op jit(solution)/shard_map/ppermute | solution.py:50
  224.9 68.2 %collective-permute-start.28 = (bf16[2,256,1024]{2,1,0:T(8,128)(2,1)S(1)}, bf16[2,256,1024]{2,1,0:T(8,128)(2,1)S(1)}, u32[]{:S(2)}, u32[]{:S(2)}) collective-permute-start(bf16[2,256,1024]{2,1,0:T(8,128)(2,1)S(1)} %shard_map.270), channel_id=1, source_target_pairs={{0,2},{2,0},{4,6},{6,4},{8,10},{10,8},{12,14},{14,12},{16,18},{18,... | collective-permute-start | bytes 3145736 | tf_op jit(solution)/shard_map/ppermute | solution.py:881
  226.7 66.4 %collective-permute-start.30 = (bf16[2,256,1024]{2,1,0:T(8,128)(2,1)S(1)}, bf16[2,256,1024]{2,1,0:T(8,128)(2,1)S(1)}, u32[]{:S(2)}, u32[]{:S(2)}) collective-permute-start(bf16[2,256,1024]{2,1,0:T(8,128)(2,1)S(1)} %shard_map.271), channel_id=1, source_target_pairs={{0,4},{2,6},{4,0},{6,2},{8,12},{10,14},{12,8},{14,10},{16,20},{18,... | collective-permute-start | bytes 3145736 | tf_op jit(solution)/shard_map/ppermute | solution.py:881
  226.7 66.4 %collective-permute-start.32 = (bf16[2,256,1024]{2,1,0:T(8,128)(2,1)S(1)}, bf16[2,256,1024]{2,1,0:T(8,128)(2,1)S(1)}, u32[]{:S(2)}, u32[]{:S(2)}) collective-permute-start(bf16[2,256,1024]{2,1,0:T(8,128)(2,1)S(1)} %shard_map.272), channel_id=1, source_target_pairs={{0,6},{2,4},{4,2},{6,0},{8,14},{10,12},{12,10},{14,8},{16,22},{18,... | collective-permute-start | bytes 3145736 | tf_op jit(solution)/shard_map/ppermute | solution.py:881
  228.5 24.7 %collective-permute-start.48 = (bf16[4,2,64,512]{3,2,1,0:T(8,128)(2,1)S(1)}, bf16[4,2,64,512]{3,2,1,0:T(8,128)(2,1)S(1)}, u32[]{:S(2)}, u32[]{:S(2)}) collective-permute-start(bf16[4,2,64,512]{3,2,1,0:T(8,128)(2,1)S(1)} %copy-done.21), channel_id=1, source_target_pairs={{0,24},{2,26},{4,28},{6,30},{8,16},{10,18},{12,20},{14,22},{16,8},... | collective-permute-start | bytes 1572872 | tf_op jit(solution)/shard_map/ppermute | solution.py:884
  253.2 21.9 %collective-permute-start.45 = (bf16[64,512]{1,0:T(8,128)(2,1)S(1)}, bf16[64,512]{1,0:T(8,128)(2,1)S(1)}, u32[]{:S(2)}, u32[]{:S(2)}) collective-permute-start(bf16[64,512]{1,0:T(8,128)(2,1)S(1)} %get-tuple-element.133), channel_id=1, source_target_pairs={{0,6},{2,4},{4,2},{6,0},{8,14},{10,12},{12,10},{14,8},{16,22},{18,... | collective-permute-start | bytes 196616 | tf_op jit(solution)/shard_map/ppermute | solution.py:881
  275.1 5.0 %collective-permute-start.49 = (bf16[2,64,512]{2,1,0:T(8,128)(2,1)S(1)}, bf16[2,64,512]{2,1,0:T(8,128)(2,1)S(1)}, u32[]{:S(2)}, u32[]{:S(2)}) collective-permute-start(bf16[2,64,512]{2,1,0:T(8,128)(2,1)S(1)} %get-tuple-element.143), channel_id=1, source_target_pairs={{0,2},{2,0},{4,6},{6,4},{8,10},{10,8},{12,14},{14,12},{16,18},{18,... | collective-permute-start | bytes 393224 | tf_op jit(solution)/shard_map/ppermute | solution.py:881
  280.1 5.0 %collective-permute-start.50 = (bf16[2,64,512]{2,1,0:T(8,128)(2,1)S(1)}, bf16[2,64,512]{2,1,0:T(8,128)(2,1)S(1)}, u32[]{:S(2)}, u32[]{:S(2)}) collective-permute-start(bf16[2,64,512]{2,1,0:T(8,128)(2,1)S(1)} %get-tuple-element.144), channel_id=1, source_target_pairs={{0,4},{2,6},{4,0},{6,2},{8,12},{10,14},{12,8},{14,10},{16,20},{18,... | collective-permute-start | bytes 393224 | tf_op jit(solution)/shard_map/ppermute | solution.py:881
  285.1 5.9 %collective-permute-start.51 = (bf16[2,64,512]{2,1,0:T(8,128)(2,1)S(1)}, bf16[2,64,512]{2,1,0:T(8,128)(2,1)S(1)}, u32[]{:S(2)}, u32[]{:S(2)}) collective-permute-start(bf16[2,64,512]{2,1,0:T(8,128)(2,1)S(1)} %get-tuple-element.145), channel_id=1, source_target_pairs={{0,6},{2,4},{4,2},{6,0},{8,14},{10,12},{12,10},{14,8},{16,22},{18,... | collective-permute-start | bytes 393224 | tf_op jit(solution)/shard_map/ppermute | solution.py:881
  (18 other events, 362.8 us)

commit v6 on v5

--- a/solution.py
+++ b/solution.py
@@ -976,14 +976,20 @@
         inputs, output_grad, own_halves, parts, one_row(project_bias), one_row(shrink_bias)
     )
 
-    def reduce_layers(grads):
-        received = [to_layer(grads[k], k) for k in range(1, count)]
+    def reduce_layers(grads, relayed):
+        if relayed:
+            far = to_layer(grads[3], 1)
+            near = to_layer(grads[1], 1)
+            middle = (far.astype(F32) + grads[2].astype(F32)).astype(BF16)
+            received = [near, to_layer(middle, 2)]
+        else:
+            received = [to_layer(grads[k], k) for k in range(1, count)]
         parts = sum_layers(grads[0], received)
         return parts[0], [to_quad(parts[j], j) for j in range(1, QUAD)]
 
-    own, received = reduce_layers(attend_grads)
+    own, received = reduce_layers(attend_grads, False)
     grad_attend, grad_project = unpack_attend(meta, own, received, attend_cols, project_cols)
-    own, received = reduce_layers(mlp_grads)
+    own, received = reduce_layers(mlp_grads, count == 4)
     grad_expand, grad_shrink = unpack_mlp(meta, own, received, hidden_cols)
 
     sizes = [features] * 4 + [features] * 2 + [2 * attend_cols, 2 * hidden_cols]

time: 298 us -> 293 us (0.983)
  waiting for transfers between devices: 139 us -> 129 us
  starting transfers between devices: 58.5 us -> 62.1 us
    ppermute x15, waiting for transfers between devices: 85.1 us -> 70.2 us  [to_layer(): return lax.ppermute(value, 'dp', xor_pairs(n_dp, bits * QUAD))]
    ppermute x15, starting transfers between devices: 27.8 us -> 33.7 us  [to_layer(): return lax.ppermute(value, 'dp', xor_pairs(n_dp, bits * QUAD))]
    ppermute x24, waiting for transfers between devices: 52.7 us -> 57.7 us  [to_quad(): return lax.ppermute(value, 'dp', xor_pairs(n_dp, j))]
  transfers between devices with their start and end apart: 52 -> 52, of which waited for: 19 -> 21; matrix products, arithmetic and copies ran while one was open for 2% -> 2% of each run, Pallas kernels for 16% -> 16%
where the time goes in v6:
time: 293 us; the launch traced here: 290 us
  waiting for transfers between devices  129 us (44%)
  Pallas kernels  87.7 us (30%)
  starting transfers between devices  62.1 us (21%)
  other arithmetic  5.89 us (2%)
  local copies, waits for them, and re-layouts  3.5 us (1%)
    pallas_call x5, Pallas kernels, branch(): results = call(*operands)  71.6 us
    ppermute x15, waiting for transfers between devices, to_layer(): return lax.ppermute(value, 'dp', xor_pairs(n_dp, bits * QUAD))  70.2 us
    ppermute x24, waiting for transfers between devices, to_quad(): return lax.ppermute(value, 'dp', xor_pairs(n_dp, j))  57.7 us
    ppermute x15, starting transfers between devices, to_layer(): return lax.ppermute(value, 'dp', xor_pairs(n_dp, bits * QUAD))  33.7 us
    ppermute x24, starting transfers between devices, to_quad(): return lax.ppermute(value, 'dp', xor_pairs(n_dp, j))  26.5 us
    pallas_call x6, Pallas kernels, staged_call(): pl.pallas_call(whole, in_specs=[SMEM] * len(scalars) + [ANY] * count, out...  8.36 us
  transfers between devices with their start and end apart: 52, of which 21 were waited for; matrix products, arithmetic and copies ran while one was open for 2% of the time, Pallas kernels for 16%

profile of v6, /device:TPU:10, one launch (start us, length us, event | category | flops | bytes accessed | tf_op | source)
XLA Modules:
  0.0 290.0 jit_solution(8767233560253459139)
XLA Ops:
  1.4 2.1 shard_map.264
  4.0 1.5 collective-permute-start.11
  5.5 1.4 collective-permute-start.12
  7.5 1.0 convert_reduce_fusion
  9.4 1.6 collective-permute-start.17
  11.0 1.4 collective-permute-start.18
  12.4 0.9 pad_maximum_fusion.1.refs_8_
  13.3 2.7 collective-permute-start.14
  16.6 1.5 collective-permute-start.6
  18.1 1.2 collective-permute-start.2
  19.9 2.1 shard_map.263
  22.1 1.2 collective-permute-start.4
  23.3 2.7 collective-permute-done.14.refs_10_
  26.0 1.4 collective-permute-start.13
  27.3 6.9 %collective-permute-done.13.refs_9_ = bf16[4,64,512]{2,1,0:T(8,128)(2,1)S(1)} collective-permute-done((bf16[4,64,512]{2,1,0:T(8,128)(2,1)S(1)}, bf16[4,64,512]{2,1,0:T(8,128)(2,1)S(1)}, u32[]{:S(2)}, u32[]{:S(2)}) %collective-permute-start.13) | collective-permute-done | bytes 262176 | tf_op jit(solution)/shard_map/ppermute | solution.py:884
  35.3 6.5 %collective-permute-done.4.refs_8_ = bf16[288,1024]{1,0:T(8,128)(2,1)S(1)} collective-permute-done((bf16[288,1024]{1,0:T(8,128)(2,1)}, bf16[288,1024]{1,0:T(8,128)(2,1)S(1)}, u32[]{:S(2)}, u32[]{:S(2)}) %collective-permute-start.4) | collective-permute-done | bytes 589856 | tf_op jit(solution)/shard_map/ppermute | solution.py:881
  41.8 1.0 collective-permute-start.22
  42.8 0.7 collective-permute-done.15.refs_11_
  43.5 1.5 collective-permute-start.24
  45.1 5.6 %collective-permute-done.refs_4_ = bf16[288,1024]{1,0:T(8,128)(2,1)S(1)} collective-permute-done((bf16[288,1024]{1,0:T(8,128)(2,1)}, bf16[288,1024]{1,0:T(8,128)(2,1)S(1)}, u32[]{:S(2)}, u32[]{:S(2)}) %collective-permute-start) | collective-permute-done | bytes 589856 | tf_op jit(solution)/shard_map/ppermute | solution.py:881
  52.5 10.4 %collective-permute-done.22.refs_4_ = bf16[288,1024]{1,0:T(8,128)(2,1)} collective-permute-done((bf16[288,1024]{1,0:T(8,128)(2,1)S(1)}, bf16[288,1024]{1,0:T(8,128)(2,1)}, u32[]{:S(2)}, u32[]{:S(2)}) %collective-permute-start.22) | collective-permute-done | bytes 589856 | tf_op jit(solution)/shard_map/ppermute | solution.py:881
  62.9 1.0 pad_maximum_fusion.refs_10_.refs_22_
  64.5 9.6 %shard_map.265 = (bf16[1,512,1024]{2,1,0:T(8,128)(2,1)}, bf16[1,512,1024]{2,1,0:T(8,128)(2,1)}, f32[16,1024]{1,0:T(8,128)}, f32[384,128]{1,0:T(8,128)}, f32[1,51...) custom-call(s32[3]{0:T(128)} %pad_add_fusion.meta.refs_0_, f32[1,1024]{1,0:T(1,128)} %bitcast.45, f32[1,1024]{1,0:T(1,128)} %bitcast.48, ...), custom_call_target="tpu_custom_call" | custom-call | flops 2080374784 | bytes 9437184 | tf_op jit(solution)/shard_map/pallas_call | solution.py:812
  74.2 2.3 collective-permute-start.21
  76.4 1.3 collective-permute-start.20
  77.7 1.5 collective-permute-start.19
  79.2 15.7 %shard_map.266 = (bf16[2,512,1024]{2,1,0:T(8,128)(2,1)}, bf16[2,512,1024]{2,1,0:T(8,128)(2,1)}, f32[16,1024]{1,0:T(8,128)}, f32[384,128]{1,0:T(8,128)}, f32[1,512,1024]{2,1,0:T(8,128)}) custom-call(s32[3]{0:T(128)} %pad_add_fusion.meta.refs_0_, f32[1,1024]{1,0:T(1,128)} %bitcast.46, f32[1,1024]{1,0:T(1,128)} %bitcast.49, ...), custom_call_target="tpu_custom_call" | custom-call | flops 4160749568 | bytes 13631488 | tf_op jit(solution)/shard_map/pallas_call | solution.py:812
  94.9 10.4 %shard_map.267 = (bf16[1,512,1024]{2,1,0:T(8,128)(2,1)}, bf16[1,512,1024]{2,1,0:T(8,128)(2,1)}, f32[16,1024]{1,0:T(8,128)}, f32[384,128]{1,0:T(8,128)}, f32[4,64...) custom-call(s32[3]{0:T(128)} %pad_add_fusion.meta.refs_0_, ...), custom_call_target="tpu_custom_call" | custom-call | flops 2080374784 | bytes 9437184 | tf_op jit(solution)/shard_map/pallas_call | solution.py:812
  105.3 6.3 %collective-permute-done.21.refs_13_.refs_25_ = bf16[4,2,64,512]{3,2,1,0:T(8,128)(2,1)S(1)} collective-permute-done((bf16[4,2,64,512]{3,2,1,0:T(8,128)(2,1)S(1)}, bf16[4,2,64,512]{3,2,1,0:T(8,128)(2,1)S(1)}, u32[]{:S(2)}, u32[]{:S(2)}) %collective-permute-start.21) | collective-permute-done | bytes 524320 | tf_op jit(solution)/shard_map/ppermute | solution.py:884
  111.7 9.8 %collective-permute-done.20.refs_12_.refs_24_ = bf16[4,2,64,512]{3,2,1,0:T(8,128)(2,1)S(1)} collective-permute-done((bf16[4,2,64,512]{3,2,1,0:T(8,128)(2,1)S(1)}, bf16[4,2,64,512]{3,2,1,0:T(8,128)(2,1)S(1)}, u32[]{:S(2)}, u32[]{:S(2)}) %collective-permute-start.20) | collective-permute-done | bytes 524320 | tf_op jit(solution)/shard_map/ppermute | solution.py:884
  121.5 0.8 copy-done.22
  122.5 10.3 %shard_map.268 = (bf16[2,256,1024]{2,1,0:T(8,128)(2,1)}, bf16[2,256,1024]{2,1,0:T(8,128)(2,1)}, f32[16,1024]{1,0:T(8,128)}, f32[8,512]{1,0:T(8,128)}, f32[2,512,1024]{2,1,0:T(8,128)}) custom-call(s32[3]{0:T(128)} %pad_add_fusion.meta.refs_0_, f32[1,1024]{1,0:T(1,128)} %bitcast.51, f32[1,1024]{1,0:T(1,128)} %bitcast.53, ...), custom_call_target="tpu_custom_call" | custom-call | flops 3221225472 | bytes 14680064 | tf_op jit(solution)/shard_map/pallas_call | solution.py:812
  132.8 25.6 %shard_map.269 = (bf16[2,256,1024]{2,1,0:T(8,128)(2,1)}, bf16[2,256,1024]{2,1,0:T(8,128)(2,1)}, bf16[2,256,1024]{2,1,0:T(8,128)(2,1)}, bf16[2,256,1024]{2,1,0:T(...) custom-call(s32[3]{0:T(128)} %pad_add_fusion.meta.refs_0_, ...), custom_call_target="tpu_custom_call" | custom-call | flops 9663676416 | bytes 23068672 | tf_op jit(solution)/shard_map/pallas_call | solution.py:812
  158.4 1.8 shard_map.274
  160.3 1.4 collective-permute-done.33
  161.7 0.8 add.40
  162.5 1.5 collective-permute-start.36
  164.5 1.5 collective-permute-start.34
  166.5 1.0 collective-permute-done.36
  167.5 0.8 collective-permute-done.35
  169.0 4.3 %collective-permute-start.38 = (f32[96,128]{1,0:T(8,128)S(1)}, f32[96,128]{1,0:T(8,128)S(1)}, u32[]{:S(2)}, u32[]{:S(2)}) collective-permute-start(f32[96,128]{1,0:T(8,128)S(1)} %add_add_fusion.refs_0_), channel_id=1, source_target_pairs={{0,16},{2,18},{4,20},{6,22},{8,24},{10,26},{12,28},{14,30},{16,0},... | collective-permute-start | bytes 147464 | tf_op jit(solution)/shard_map/ppermute | solution.py:884
  173.2 3.6 %collective-permute-start.40 = (bf16[4,64,512]{2,1,0:T(8,128)(2,1)S(1)}, bf16[4,64,512]{2,1,0:T(8,128)(2,1)S(1)}, u32[]{:S(2)}, u32[]{:S(2)}) collective-permute-start(bf16[4,64,512]{2,1,0:T(8,128)(2,1)S(1)} %copy-done.27), channel_id=1, source_target_pairs={{0,8},{2,10},{4,12},{6,14},{8,0},{10,2},{12,4},{14,6},{16,24},{18,... | collective-permute-start | bytes 786440 | tf_op jit(solution)/shard_map/ppermute | solution.py:884
  176.9 2.2 collective-permute-start.41
  179.1 6.4 %collective-permute-done.40.refs_1_ = bf16[4,64,512]{2,1,0:T(8,128)(2,1)S(1)} collective-permute-done((bf16[4,64,512]{2,1,0:T(8,128)(2,1)S(1)}, bf16[4,64,512]{2,1,0:T(8,128)(2,1)S(1)}, u32[]{:S(2)}, u32[]{:S(2)}) %collective-permute-start.40) | collective-permute-done | bytes 262176 | tf_op jit(solution)/shard_map/ppermute | solution.py:884
  185.5 2.5 collective-permute-start.47
  188.0 2.8 collective-permute-done.41.refs_2_
  191.2 6.1 %collective-permute-done.42.refs_3_ = bf16[4,64,512]{2,1,0:T(8,128)(2,1)S(1)} collective-permute-done((bf16[4,64,512]{2,1,0:T(8,128)(2,1)S(1)}, bf16[4,64,512]{2,1,0:T(8,128)(2,1)S(1)}, u32[]{:S(2)}, u32[]{:S(2)}) %collective-permute-start.42) | collective-permute-done | bytes 262176 | tf_op jit(solution)/shard_map/ppermute | solution.py:884
  197.2 9.6 %collective-permute-start.46 = (bf16[4,2,64,512]{3,2,1,0:T(8,128)(2,1)}, bf16[4,2,64,512]{3,2,1,0:T(8,128)(2,1)S(1)}, u32[]{:S(2)}, u32[]{:S(2)}) collective-permute-start(bf16[4,2,64,512]{3,2,1,0:T(8,128)(2,1)} %get-tuple-element.139), channel_id=1, source_target_pairs={{0,8},{2,10},{4,12},{6,14},{8,0},{10,2},{12,4},{14,6},{16,24},{18,... | collective-permute-start | bytes 1572872 | tf_op jit(solution)/shard_map/ppermute | solution.py:884
  207.1 1.5 collective-permute-start.43
  208.5 0.9 collective-permute-start.44
  211.8 6.2 %collective-permute-done.37.refs_1_ = f32[96,128]{1,0:T(8,128)S(1)} collective-permute-done((f32[96,128]{1,0:T(8,128)S(1)}, f32[96,128]{1,0:T(8,128)S(1)}, u32[]{:S(2)}, u32[]{:S(2)}) %collective-permute-start.37) | collective-permute-done | bytes 49184 | tf_op jit(solution)/shard_map/ppermute | solution.py:884
  218.6 1.7 collective-permute-start.30
  220.3 1.3 collective-permute-start.32
  221.7 1.6 collective-permute-start.48
  223.3 22.3 %collective-permute-done.48.refs_2_ = bf16[4,2,64,512]{3,2,1,0:T(8,128)(2,1)S(1)} collective-permute-done((bf16[4,2,64,512]{3,2,1,0:T(8,128)(2,1)S(1)}, bf16[4,2,64,512]{3,2,1,0:T(8,128)(2,1)S(1)}, u32[]{:S(2)}, u32[]{:S(2)}) %collective-permute-start.48) | collective-permute-done | bytes 524320 | tf_op jit(solution)/shard_map/ppermute | solution.py:884
  245.6 2.3 collective-permute-start.45
  248.2 20.7 %collective-permute-done.45.refs_4_ = bf16[64,512]{1,0:T(8,128)(2,1)S(1)} collective-permute-done((bf16[64,512]{1,0:T(8,128)(2,1)S(1)}, bf16[64,512]{1,0:T(8,128)(2,1)S(1)}, u32[]{:S(2)}, u32[]{:S(2)}) %collective-permute-start.45) | collective-permute-done | bytes 65568 | tf_op jit(solution)/shard_map/ppermute | solution.py:881
  269.2 4.6 %collective-permute-done.49.refs_2_ = bf16[2,64,512]{2,1,0:T(8,128)(2,1)S(1)} collective-permute-done((bf16[2,64,512]{2,1,0:T(8,128)(2,1)S(1)}, bf16[2,64,512]{2,1,0:T(8,128)(2,1)S(1)}, u32[]{:S(2)}, u32[]{:S(2)}) %collective-permute-start.49) | collective-permute-done | bytes 131104 | tf_op jit(solution)/shard_map/ppermute | solution.py:881
  273.9 4.8 %collective-permute-done.50.refs_3_ = bf16[2,64,512]{2,1,0:T(8,128)(2,1)S(1)} collective-permute-done((bf16[2,64,512]{2,1,0:T(8,128)(2,1)S(1)}, bf16[2,64,512]{2,1,0:T(8,128)(2,1)S(1)}, u32[]{:S(2)}, u32[]{:S(2)}) %collective-permute-start.50) | collective-permute-done | bytes 131104 | tf_op jit(solution)/shard_map/ppermute | solution.py:881
  278.9 0.9 shard_map.275
  279.8 1.8 shard_map.277
  281.6 3.0 %collective-permute-done.51.refs_4_ = bf16[2,64,512]{2,1,0:T(8,128)(2,1)S(1)} collective-permute-done((bf16[2,64,512]{2,1,0:T(8,128)(2,1)S(1)}, bf16[2,64,512]{2,1,0:T(8,128)(2,1)S(1)}, u32[]{:S(2)}, u32[]{:S(2)}) %collective-permute-start.51) | collective-permute-done | bytes 131104 | tf_op jit(solution)/shard_map/ppermute | solution.py:881
  284.6 2.1 shard_map.279
  286.9 2.9 %shard_map.273 = (bf16[256,1024]{1,0:T(8,128)(2,1)}, bf16[256,1024]{1,0:T(8,128)(2,1)}) custom-call(f32[1,1024]{1,0:T(1,128)S(1)} %bitcast.29, f32[1,1024]{1,0:T(1,128)S(1)} %bitcast.30, bf16[256,1024]{1,0:T(8,128)(2,1)S(1)} %copy-done, bf16[256,1024]{1,0:T(8,128)(2,1)S(1)} %copy-done.1, bf16[2,256,1024]{2,1,0:T(8,128)(2,1)S(1)} %copy-done.6, ...), custom_call_target="tpu_custom_call" | custom-call | tf_op jit(solution)/shard_map/pallas_call | solution.py:80
  (135 shorter events, 13.8 us)
Async XLA Ops:
  0.6 50.1 %copy-start.14 = (f32[1536]{0:T(1024)S(1)}, f32[1536]{0:T(1024)}, u32[]{:S(2)}) copy-start(f32[1536]{0:T(1024)} %param.24) | copy-start | bytes 18436
  0.7 50.1 %copy-start.15 = (f32[2048]{0:T(1024)S(1)}, f32[2048]{0:T(1024)}, u32[]{:S(2)}) copy-start(f32[2048]{0:T(1024)} %param.28) | copy-start | bytes 24580
  0.7 33.5 %collective-permute-start.9 = (bf16[256,1024]{1,0:T(8,128)(2,1)}, bf16[256,1024]{1,0:T(8,128)(2,1)}, u32[]{:S(2)}, u32[]{:S(2)}) collective-permute-start(bf16[256,1024]{1,0:T(8,128)(2,1)} %refs_3_.1), channel_id=1, source_target_pairs={{0,1},{1,0},{2,3},{3,2},{4,5},{5,4},{6,7},{7,6},{8,9},{9,8},{10,11... | collective-permute-start | bytes 1572872 | tf_op jit(solution)/shard_map/ppermute | solution.py:50
  3.5 5.9 %collective-permute-start.10 = (bf16[64,512]{1,0:T(8,128)(2,1)}, bf16[64,512]{1,0:T(8,128)(2,1)S(1)}, u32[]{:S(2)}, u32[]{:S(2)}) collective-permute-start(bf16[64,512]{1,0:T(8,128)(2,1)} %get-tuple-element.84), channel_id=1, source_target_pairs={{0,2},{2,0},{4,6},{6,4},{8,10},{10,8},{12,14},{14,12},{16,18},{18,... | collective-permute-start | bytes 196616 | tf_op jit(solution)/shard_map/ppermute | solution.py:881
  4.0 7.0 %collective-permute-start.11 = (bf16[64,512]{1,0:T(8,128)(2,1)}, bf16[64,512]{1,0:T(8,128)(2,1)S(1)}, u32[]{:S(2)}, u32[]{:S(2)}) collective-permute-start(bf16[64,512]{1,0:T(8,128)(2,1)} %get-tuple-element.85), channel_id=1, source_target_pairs={{0,4},{2,6},{4,0},{6,2},{8,12},{10,14},{12,8},{14,10},{16,20},{18,... | collective-permute-start | bytes 196616 | tf_op jit(solution)/shard_map/ppermute | solution.py:881
  5.5 6.9 %collective-permute-start.12 = (bf16[64,512]{1,0:T(8,128)(2,1)}, bf16[64,512]{1,0:T(8,128)(2,1)S(1)}, u32[]{:S(2)}, u32[]{:S(2)}) collective-permute-start(bf16[64,512]{1,0:T(8,128)(2,1)} %get-tuple-element.86), channel_id=1, source_target_pairs={{0,6},{2,4},{4,2},{6,0},{8,14},{10,12},{12,10},{14,8},{16,22},{18,... | collective-permute-start | bytes 196616 | tf_op jit(solution)/shard_map/ppermute | solution.py:881
  7.0 9.6 %collective-permute-start.16 = (bf16[2,64,512]{2,1,0:T(8,128)(2,1)}, bf16[2,64,512]{2,1,0:T(8,128)(2,1)S(1)}, u32[]{:S(2)}, u32[]{:S(2)}) collective-permute-start(bf16[2,64,512]{2,1,0:T(8,128)(2,1)} %get-tuple-element.96), channel_id=1, source_target_pairs={{0,2},{2,0},{4,6},{6,4},{8,10},{10,8},{12,14},{14,12},{16,18},{18,... | collective-permute-start | bytes 393224 | tf_op jit(solution)/shard_map/ppermute | solution.py:881
  9.4 8.7 %collective-permute-start.17 = (bf16[2,64,512]{2,1,0:T(8,128)(2,1)}, bf16[2,64,512]{2,1,0:T(8,128)(2,1)S(1)}, u32[]{:S(2)}, u32[]{:S(2)}) collective-permute-start(bf16[2,64,512]{2,1,0:T(8,128)(2,1)} %get-tuple-element.97), channel_id=1, source_target_pairs={{0,4},{2,6},{4,0},{6,2},{8,12},{10,14},{12,8},{14,10},{16,20},{18,... | collective-permute-start | bytes 393224 | tf_op jit(solution)/shard_map/ppermute | solution.py:881
  11.0 11.1 %collective-permute-start.18 = (bf16[2,64,512]{2,1,0:T(8,128)(2,1)}, bf16[2,64,512]{2,1,0:T(8,128)(2,1)S(1)}, u32[]{:S(2)}, u32[]{:S(2)}) collective-permute-start(bf16[2,64,512]{2,1,0:T(8,128)(2,1)} %get-tuple-element.98), channel_id=1, source_target_pairs={{0,6},{2,4},{4,2},{6,0},{8,14},{10,12},{12,10},{14,8},{16,22},{18,... | collective-permute-start | bytes 393224 | tf_op jit(solution)/shard_map/ppermute | solution.py:881
  13.3 51.2 %copy-start.13 = (bf16[4,64,512]{2,1,0:T(8,128)(2,1)}, bf16[4,64,512]{2,1,0:T(8,128)(2,1)S(1)}, u32[]{:S(2)}) copy-start(bf16[4,64,512]{2,1,0:T(8,128)(2,1)S(1)} %pad_maximum_fusion.1.refs_8_) | copy-start | bytes 786436
  13.3 12.7 %collective-permute-start.14 = (bf16[4,64,512]{2,1,0:T(8,128)(2,1)S(1)}, bf16[4,64,512]{2,1,0:T(8,128)(2,1)S(1)}, u32[]{:S(2)}, u32[]{:S(2)}) collective-permute-start(bf16[4,64,512]{2,1,0:T(8,128)(2,1)S(1)} %pad_maximum_fusion.1.refs_8_), channel_id=1, source_target_pairs={{0,16},{2,18},{4,20},{6,22},{8,24},{10,26},{12,28},{14,30},{16,0},... | collective-permute-start | bytes 786440 | tf_op jit(solution)/shard_map/ppermute | solution.py:884
  16.6 18.2 %collective-permute-start.6 = (bf16[256,1024]{1,0:T(8,128)(2,1)}, bf16[256,1024]{1,0:T(8,128)(2,1)}, u32[]{:S(2)}, u32[]{:S(2)}) collective-permute-start(bf16[256,1024]{1,0:T(8,128)(2,1)} %refs_3_.1), channel_id=1, source_target_pairs={{0,4},{2,6},{4,0},{6,2},{8,12},{10,14},{12,8},{14,10},{16,20},{18,... | collective-permute-start | bytes 1572872 | tf_op jit(solution)/shard_map/ppermute | solution.py:881
  18.1 16.9 %collective-permute-start.2 = (bf16[256,1024]{1,0:T(8,128)(2,1)}, bf16[256,1024]{1,0:T(8,128)(2,1)}, u32[]{:S(2)}, u32[]{:S(2)}) collective-permute-start(bf16[256,1024]{1,0:T(8,128)(2,1)} %refs_3_.1), channel_id=1, source_target_pairs={{0,2},{2,0},{4,6},{6,4},{8,10},{10,8},{12,14},{14,12},{16,18},{18,... | collective-permute-start | bytes 1572872 | tf_op jit(solution)/shard_map/ppermute | solution.py:881
  22.1 19.7 %collective-permute-start.4 = (bf16[288,1024]{1,0:T(8,128)(2,1)}, bf16[288,1024]{1,0:T(8,128)(2,1)S(1)}, u32[]{:S(2)}, u32[]{:S(2)}) collective-permute-start(bf16[288,1024]{1,0:T(8,128)(2,1)} %get-tuple-element.82.refs_4_.refs_12_), channel_id=1, source_target_pairs={{0,4},{2,6},{4,0},{6,2},{8,12},{10,14},{12,8},{14,10},{16,20},{18,... | collective-permute-start | bytes 1769480 | tf_op jit(solution)/shard_map/ppermute | solution.py:881
  26.0 8.2 %collective-permute-start.13 = (bf16[4,64,512]{2,1,0:T(8,128)(2,1)S(1)}, bf16[4,64,512]{2,1,0:T(8,128)(2,1)S(1)}, u32[]{:S(2)}, u32[]{:S(2)}) collective-permute-start(bf16[4,64,512]{2,1,0:T(8,128)(2,1)S(1)} %pad_maximum_fusion.1.refs_8_), channel_id=1, source_target_pairs={{0,8},{2,10},{4,12},{6,14},{8,0},{10,2},{12,4},{14,6},{16,24},{18,... | collective-permute-start | bytes 786440 | tf_op jit(solution)/shard_map/ppermute | solution.py:884
  34.2 10.9 %collective-permute-start.8 = (bf16[288,1024]{1,0:T(8,128)(2,1)}, bf16[288,1024]{1,0:T(8,128)(2,1)S(1)}, u32[]{:S(2)}, u32[]{:S(2)}) collective-permute-start(bf16[288,1024]{1,0:T(8,128)(2,1)} %get-tuple-element.82.refs_4_.refs_12_), channel_id=1, source_target_pairs={{0,1},{1,0},{2,3},{3,2},{4,5},{5,4},{6,7},{7,6},{8,9},{9,8},{10,11... | collective-permute-start | bytes 1769480 | tf_op jit(solution)/shard_map/ppermute | solution.py:50
  34.2 16.5 %collective-permute-start = (bf16[288,1024]{1,0:T(8,128)(2,1)}, bf16[288,1024]{1,0:T(8,128)(2,1)S(1)}, u32[]{:S(2)}, u32[]{:S(2)}) collective-permute-start(bf16[288,1024]{1,0:T(8,128)(2,1)} %get-tuple-element.82.refs_4_.refs_12_), channel_id=1, source_target_pairs={{0,2},{2,0},{4,6},{6,4},{8,10},{10,8},{12,14},{14,12},{16,18},{18,... | collective-permute-start | bytes 1769480 | tf_op jit(solution)/shard_map/ppermute | solution.py:881
  34.8 15.9 %collective-permute-start.7 = (bf16[256,1024]{1,0:T(8,128)(2,1)}, bf16[256,1024]{1,0:T(8,128)(2,1)}, u32[]{:S(2)}, u32[]{:S(2)}) collective-permute-start(bf16[256,1024]{1,0:T(8,128)(2,1)} %collective-permute-done.6.refs_10_), channel_id=1, source_target_pairs={{0,1},{1,0},{2,3},{3,2},{4,5},{5,4},{6,7},{7,6},{8,9},{9,8},{10,11... | collective-permute-start | bytes 1572872 | tf_op jit(solution)/shard_map/ppermute | solution.py:50
  35.0 8.6 %collective-permute-start.15 = (bf16[4,64,512]{2,1,0:T(8,128)(2,1)S(1)}, bf16[4,64,512]{2,1,0:T(8,128)(2,1)S(1)}, u32[]{:S(2)}, u32[]{:S(2)}) collective-permute-start(bf16[4,64,512]{2,1,0:T(8,128)(2,1)S(1)} %collective-permute-done.14.refs_10_), channel_id=1, source_target_pairs={{0,8},{2,10},{4,12},{6,14},{8,0},{10,2},{12,4},{14,6},{16,24},{18,... | collective-permute-start | bytes 786440 | tf_op jit(solution)/shard_map/ppermute | solution.py:884
  41.8 21.1 %collective-permute-start.22 = (bf16[288,1024]{1,0:T(8,128)(2,1)S(1)}, bf16[288,1024]{1,0:T(8,128)(2,1)}, u32[]{:S(2)}, u32[]{:S(2)}) collective-permute-start(bf16[288,1024]{1,0:T(8,128)(2,1)S(1)} %collective-permute-done.4.refs_8_), channel_id=1, source_target_pairs={{0,2},{2,0},{4,6},{6,4},{8,10},{10,8},{12,14},{14,12},{16,18},{18,... | collective-permute-start | bytes 1769480 | tf_op jit(solution)/shard_map/ppermute | solution.py:881
  43.5 20.4 %collective-permute-start.24 = (bf16[256,1024]{1,0:T(8,128)(2,1)}, bf16[256,1024]{1,0:T(8,128)(2,1)}, u32[]{:S(2)}, u32[]{:S(2)}) collective-permute-start(bf16[256,1024]{1,0:T(8,128)(2,1)} %collective-permute-done.2.refs_6_), channel_id=1, source_target_pairs={{0,4},{2,6},{4,0},{6,2},{8,12},{10,14},{12,8},{14,10},{16,20},{18,... | collective-permute-start | bytes 1572872 | tf_op jit(solution)/shard_map/ppermute | solution.py:881
  45.1 31.4 %collective-permute-start.5 = (bf16[288,1024]{1,0:T(8,128)(2,1)S(1)}, bf16[288,1024]{1,0:T(8,128)(2,1)}, u32[]{:S(2)}, u32[]{:S(2)}) collective-permute-start(bf16[288,1024]{1,0:T(8,128)(2,1)S(1)} %collective-permute-done.4.refs_8_), channel_id=1, source_target_pairs={{0,1},{1,0},{2,3},{3,2},{4,5},{5,4},{6,7},{7,6},{8,9},{9,8},{10,11... | collective-permute-start | bytes 1769480 | tf_op jit(solution)/shard_map/ppermute | solution.py:50
  50.7 27.0 %collective-permute-start.1 = (bf16[288,1024]{1,0:T(8,128)(2,1)S(1)}, bf16[288,1024]{1,0:T(8,128)(2,1)}, u32[]{:S(2)}, u32[]{:S(2)}) collective-permute-start(bf16[288,1024]{1,0:T(8,128)(2,1)S(1)} %collective-permute-done.refs_4_), channel_id=1, source_target_pairs={{0,1},{1,0},{2,3},{3,2},{4,5},{5,4},{6,7},{7,6},{8,9},{9,8},{10,11... | collective-permute-start | bytes 1769480 | tf_op jit(solution)/shard_map/ppermute | solution.py:50
  50.8 23.4 %collective-permute-start.3 = (bf16[256,1024]{1,0:T(8,128)(2,1)}, bf16[256,1024]{1,0:T(8,128)(2,1)}, u32[]{:S(2)}, u32[]{:S(2)}) collective-permute-start(bf16[256,1024]{1,0:T(8,128)(2,1)} %collective-permute-done.2.refs_6_), channel_id=1, source_target_pairs={{0,1},{1,0},{2,3},{3,2},{4,5},{5,4},{6,7},{7,6},{8,9},{9,8},{10,11... | collective-permute-start | bytes 1572872 | tf_op jit(solution)/shard_map/ppermute | solution.py:50
  62.9 32.0 %collective-permute-start.23 = (bf16[288,1024]{1,0:T(8,128)(2,1)}, bf16[288,1024]{1,0:T(8,128)(2,1)}, u32[]{:S(2)}, u32[]{:S(2)}) collective-permute-start(bf16[288,1024]{1,0:T(8,128)(2,1)} %collective-permute-done.22.refs_4_), channel_id=1, source_target_pairs={{0,1},{1,0},{2,3},{3,2},{4,5},{5,4},{6,7},{7,6},{8,9},{9,8},{10,11... | collective-permute-start | bytes 1769480 | tf_op jit(solution)/shard_map/ppermute | solution.py:50
  63.9 31.0 %collective-permute-start.25 = (bf16[256,1024]{1,0:T(8,128)(2,1)}, bf16[256,1024]{1,0:T(8,128)(2,1)}, u32[]{:S(2)}, u32[]{:S(2)}) collective-permute-start(bf16[256,1024]{1,0:T(8,128)(2,1)} %collective-permute-done.24.refs_6_), channel_id=1, source_target_pairs={{0,1},{1,0},{2,3},{3,2},{4,5},{5,4},{6,7},{7,6},{8,9},{9,8},{10,11... | collective-permute-start | bytes 1572872 | tf_op jit(solution)/shard_map/ppermute | solution.py:50
  74.2 37.5 %collective-permute-start.21 = (bf16[4,2,64,512]{3,2,1,0:T(8,128)(2,1)S(1)}, bf16[4,2,64,512]{3,2,1,0:T(8,128)(2,1)S(1)}, u32[]{:S(2)}, u32[]{:S(2)}) collective-permute-start(bf16[4,2,64,512]{3,2,1,0:T(8,128)(2,1)S(1)} %pad_maximum_fusion.refs_10_.refs_22_), channel_id=1, source_target_pairs={{0,24},{2,26},{4,28},{6,30},{8,16},{10,18},{12,20},{14,22},{16,8},... | collective-permute-start | bytes 1572872 | tf_op jit(solution)/shard_map/ppermute | solution.py:884
  76.4 45.1 %collective-permute-start.20 = (bf16[4,2,64,512]{3,2,1,0:T(8,128)(2,1)S(1)}, bf16[4,2,64,512]{3,2,1,0:T(8,128)(2,1)S(1)}, u32[]{:S(2)}, u32[]{:S(2)}) collective-permute-start(bf16[4,2,64,512]{3,2,1,0:T(8,128)(2,1)S(1)} %pad_maximum_fusion.refs_10_.refs_22_), channel_id=1, source_target_pairs={{0,16},{2,18},{4,20},{6,22},{8,24},{10,26},{12,28},{14,30},{16,0},... | collective-permute-start | bytes 1572872 | tf_op jit(solution)/shard_map/ppermute | solution.py:884
  77.7 43.8 %collective-permute-start.19 = (bf16[4,2,64,512]{3,2,1,0:T(8,128)(2,1)S(1)}, bf16[4,2,64,512]{3,2,1,0:T(8,128)(2,1)S(1)}, u32[]{:S(2)}, u32[]{:S(2)}) collective-permute-start(bf16[4,2,64,512]{3,2,1,0:T(8,128)(2,1)S(1)} %pad_maximum_fusion.refs_10_.refs_22_), channel_id=1, source_target_pairs={{0,8},{2,10},{4,12},{6,14},{8,0},{10,2},{12,4},{14,6},{16,24},{18,... | collective-permute-start | bytes 1572872 | tf_op jit(solution)/shard_map/ppermute | solution.py:884
  132.8 58.0 %copy-start.24 = (bf16[4,64,512]{2,1,0:T(8,128)(2,1)S(1)}, bf16[4,64,512]{2,1,0:T(8,128)(2,1)}, u32[]{:S(2)}) copy-start(bf16[4,64,512]{2,1,0:T(8,128)(2,1)} %get-tuple-element.129) | copy-start | bytes 786436
  132.8 74.0 %copy-start.7 = (f32[4,64,512]{2,1,0:T(8,128)S(1)}, f32[4,64,512]{2,1,0:T(8,128)}, u32[]{:S(2)}) copy-start(f32[4,64,512]{2,1,0:T(8,128)} %get-tuple-element.126.refs_0_) | copy-start | bytes 1572868
  158.4 51.0 %copy-start.4 = (bf16[2,256,1024]{2,1,0:T(8,128)(2,1)S(1)}, bf16[2,256,1024]{2,1,0:T(8,128)(2,1)}, u32[]{:S(2)}) copy-start(bf16[2,256,1024]{2,1,0:T(8,128)(2,1)} %get-tuple-element.109.mine) | copy-start | bytes 3145732
  160.3 1.4 collective-permute-start.33
  162.5 5.0 %collective-permute-start.36 = (f32[96,128]{1,0:T(8,128)S(1)}, f32[96,128]{1,0:T(8,128)S(1)}, u32[]{:S(2)}, u32[]{:S(2)}) collective-permute-start(f32[96,128]{1,0:T(8,128)S(1)} %add.40), channel_id=1, source_target_pairs={{0,6},{2,4},{4,2},{6,0},{8,14},{10,12},{12,10},{14,8},{16,22},{18,... | collective-permute-start | bytes 147464 | tf_op jit(solution)/shard_map/ppermute | solution.py:881
  164.0 4.3 %collective-permute-start.35 = (f32[96,128]{1,0:T(8,128)S(1)}, f32[96,128]{1,0:T(8,128)S(1)}, u32[]{:S(2)}, u32[]{:S(2)}) collective-permute-start(f32[96,128]{1,0:T(8,128)S(1)} %add.40), channel_id=1, source_target_pairs={{0,4},{2,6},{4,0},{6,2},{8,12},{10,14},{12,8},{14,10},{16,20},{18,... | collective-permute-start | bytes 147464 | tf_op jit(solution)/shard_map/ppermute | solution.py:881
  164.5 4.1 %collective-permute-start.34 = (f32[96,128]{1,0:T(8,128)S(1)}, f32[96,128]{1,0:T(8,128)S(1)}, u32[]{:S(2)}, u32[]{:S(2)}) collective-permute-start(f32[96,128]{1,0:T(8,128)S(1)} %add.40), channel_id=1, source_target_pairs={{0,2},{2,0},{4,6},{6,4},{8,10},{10,8},{12,14},{14,12},{16,18},{18,... | collective-permute-start | bytes 147464 | tf_op jit(solution)/shard_map/ppermute | solution.py:881
  166.0 41.0 %collective-permute-start.27 = (bf16[2,256,1024]{2,1,0:T(8,128)(2,1)}, bf16[2,256,1024]{2,1,0:T(8,128)(2,1)S(1)}, u32[]{:S(2)}, u32[]{:S(2)}) collective-permute-start(bf16[2,256,1024]{2,1,0:T(8,128)(2,1)} %get-tuple-element.110), channel_id=1, source_target_pairs={{0,1},{1,0},{2,3},{3,2},{4,5},{5,4},{6,7},{7,6},{8,9},{9,8},{10,11... | collective-permute-start | bytes 3145736 | tf_op jit(solution)/shard_map/ppermute | solution.py:50
  166.0 42.5 %collective-permute-start.29 = (bf16[2,256,1024]{2,1,0:T(8,128)(2,1)}, bf16[2,256,1024]{2,1,0:T(8,128)(2,1)S(1)}, u32[]{:S(2)}, u32[]{:S(2)}) collective-permute-start(bf16[2,256,1024]{2,1,0:T(8,128)(2,1)} %get-tuple-element.112), channel_id=1, source_target_pairs={{0,1},{1,0},{2,3},{3,2},{4,5},{5,4},{6,7},{7,6},{8,9},{9,8},{10,11... | collective-permute-start | bytes 3145736 | tf_op jit(solution)/shard_map/ppermute | solution.py:50
  167.5 41.9 %collective-permute-start.31 = (bf16[2,256,1024]{2,1,0:T(8,128)(2,1)S(1)}, bf16[2,256,1024]{2,1,0:T(8,128)(2,1)S(1)}, u32[]{:S(2)}, u32[]{:S(2)}) collective-permute-start(bf16[2,256,1024]{2,1,0:T(8,128)(2,1)S(1)} %copy-done.17), channel_id=1, source_target_pairs={{0,1},{1,0},{2,3},{3,2},{4,5},{5,4},{6,7},{7,6},{8,9},{9,8},{10,11... | collective-permute-start | bytes 3145736 | tf_op jit(solution)/shard_map/ppermute | solution.py:50
  168.6 4.6 %collective-permute-start.39 = (f32[96,128]{1,0:T(8,128)S(1)}, f32[96,128]{1,0:T(8,128)S(1)}, u32[]{:S(2)}, u32[]{:S(2)}) collective-permute-start(f32[96,128]{1,0:T(8,128)S(1)} %add_add_fusion.refs_0_), channel_id=1, source_target_pairs={{0,24},{2,26},{4,28},{6,30},{8,16},{10,18},{12,20},{14,22},{16,8},... | collective-permute-start | bytes 147464 | tf_op jit(solution)/shard_map/ppermute | solution.py:884
  169.0 7.9 %collective-permute-start.38 = (f32[96,128]{1,0:T(8,128)S(1)}, f32[96,128]{1,0:T(8,128)S(1)}, u32[]{:S(2)}, u32[]{:S(2)}) collective-permute-start(f32[96,128]{1,0:T(8,128)S(1)} %add_add_fusion.refs_0_), channel_id=1, source_target_pairs={{0,16},{2,18},{4,20},{6,22},{8,24},{10,26},{12,28},{14,30},{16,0},... | collective-permute-start | bytes 147464 | tf_op jit(solution)/shard_map/ppermute | solution.py:884
  173.2 12.2 %collective-permute-start.40 = (bf16[4,64,512]{2,1,0:T(8,128)(2,1)S(1)}, bf16[4,64,512]{2,1,0:T(8,128)(2,1)S(1)}, u32[]{:S(2)}, u32[]{:S(2)}) collective-permute-start(bf16[4,64,512]{2,1,0:T(8,128)(2,1)S(1)} %copy-done.27), channel_id=1, source_target_pairs={{0,8},{2,10},{4,12},{6,14},{8,0},{10,2},{12,4},{14,6},{16,24},{18,... | collective-permute-start | bytes 786440 | tf_op jit(solution)/shard_map/ppermute | solution.py:884
  176.9 13.9 %collective-permute-start.41 = (bf16[4,64,512]{2,1,0:T(8,128)(2,1)S(1)}, bf16[4,64,512]{2,1,0:T(8,128)(2,1)S(1)}, u32[]{:S(2)}, u32[]{:S(2)}) collective-permute-start(bf16[4,64,512]{2,1,0:T(8,128)(2,1)S(1)} %copy-done.26), channel_id=1, source_target_pairs={{0,16},{2,18},{4,20},{6,22},{8,24},{10,26},{12,28},{14,30},{16,0},... | collective-permute-start | bytes 786440 | tf_op jit(solution)/shard_map/ppermute | solution.py:884
  185.5 34.8 %collective-permute-start.47 = (bf16[4,2,64,512]{3,2,1,0:T(8,128)(2,1)}, bf16[4,2,64,512]{3,2,1,0:T(8,128)(2,1)S(1)}, u32[]{:S(2)}, u32[]{:S(2)}) collective-permute-start(bf16[4,2,64,512]{3,2,1,0:T(8,128)(2,1)} %get-tuple-element.140), channel_id=1, source_target_pairs={{0,8},{2,10},{4,12},{6,14},{8,0},{10,2},{12,4},{14,6},{16,24},{18,... | collective-permute-start | bytes 1572872 | tf_op jit(solution)/shard_map/ppermute | solution.py:884
  190.8 6.4 %collective-permute-start.42 = (bf16[4,64,512]{2,1,0:T(8,128)(2,1)S(1)}, bf16[4,64,512]{2,1,0:T(8,128)(2,1)S(1)}, u32[]{:S(2)}, u32[]{:S(2)}) collective-permute-start(bf16[4,64,512]{2,1,0:T(8,128)(2,1)S(1)} %copy-done.24), channel_id=1, source_target_pairs={{0,24},{2,26},{4,28},{6,30},{8,16},{10,18},{12,20},{14,22},{16,8},... | collective-permute-start | bytes 786440 | tf_op jit(solution)/shard_map/ppermute | solution.py:884
  197.2 24.5 %collective-permute-start.46 = (bf16[4,2,64,512]{3,2,1,0:T(8,128)(2,1)}, bf16[4,2,64,512]{3,2,1,0:T(8,128)(2,1)S(1)}, u32[]{:S(2)}, u32[]{:S(2)}) collective-permute-start(bf16[4,2,64,512]{3,2,1,0:T(8,128)(2,1)} %get-tuple-element.139), channel_id=1, source_target_pairs={{0,8},{2,10},{4,12},{6,14},{8,0},{10,2},{12,4},{14,6},{16,24},{18,... | collective-permute-start | bytes 1572872 | tf_op jit(solution)/shard_map/ppermute | solution.py:884
  207.1 10.9 %collective-permute-start.43 = (bf16[64,512]{1,0:T(8,128)(2,1)S(1)}, bf16[64,512]{1,0:T(8,128)(2,1)S(1)}, u32[]{:S(2)}, u32[]{:S(2)}) collective-permute-start(bf16[64,512]{1,0:T(8,128)(2,1)S(1)} %get-tuple-element.131), channel_id=1, source_target_pairs={{0,2},{2,0},{4,6},{6,4},{8,10},{10,8},{12,14},{14,12},{16,18},{18,... | collective-permute-start | bytes 196616 | tf_op jit(solution)/shard_map/ppermute | solution.py:881
  208.5 10.0 %collective-permute-start.44 = (bf16[64,512]{1,0:T(8,128)(2,1)S(1)}, bf16[64,512]{1,0:T(8,128)(2,1)S(1)}, u32[]{:S(2)}, u32[]{:S(2)}) collective-permute-start(bf16[64,512]{1,0:T(8,128)(2,1)S(1)} %get-tuple-element.132), channel_id=1, source_target_pairs={{0,4},{2,6},{4,0},{6,2},{8,12},{10,14},{12,8},{14,10},{16,20},{18,... | collective-permute-start | bytes 196616 | tf_op jit(solution)/shard_map/ppermute | solution.py:881
  209.4 8.5 %collective-permute-start.37 = (f32[96,128]{1,0:T(8,128)S(1)}, f32[96,128]{1,0:T(8,128)S(1)}, u32[]{:S(2)}, u32[]{:S(2)}) collective-permute-start(f32[96,128]{1,0:T(8,128)S(1)} %add_add_fusion.refs_0_), channel_id=1, source_target_pairs={{0,8},{2,10},{4,12},{6,14},{8,0},{10,2},{12,4},{14,6},{16,24},{18,... | collective-permute-start | bytes 147464 | tf_op jit(solution)/shard_map/ppermute | solution.py:884
  211.7 68.1 %copy-start.8 = (s32[3]{0:T(128)S(1)}, s32[3]{0:T(128)}, u32[]{:S(2)}) copy-start(s32[3]{0:T(128)} %pad_add_fusion.meta.refs_0_) | copy-start | bytes 40
  218.0 68.8 %collective-permute-start.26 = (bf16[2,256,1024]{2,1,0:T(8,128)(2,1)S(1)}, bf16[2,256,1024]{2,1,0:T(8,128)(2,1)S(1)}, u32[]{:S(2)}, u32[]{:S(2)}) collective-permute-start(bf16[2,256,1024]{2,1,0:T(8,128)(2,1)S(1)} %copy-done.16), channel_id=1, source_target_pairs={{0,1},{1,0},{2,3},{3,2},{4,5},{5,4},{6,7},{7,6},{8,9},{9,8},{10,11... | collective-permute-start | bytes 3145736 | tf_op jit(solution)/shard_map/ppermute | solution.py:50
  218.0 68.8 %collective-permute-start.28 = (bf16[2,256,1024]{2,1,0:T(8,128)(2,1)S(1)}, bf16[2,256,1024]{2,1,0:T(8,128)(2,1)S(1)}, u32[]{:S(2)}, u32[]{:S(2)}) collective-permute-start(bf16[2,256,1024]{2,1,0:T(8,128)(2,1)S(1)} %shard_map.270), channel_id=1, source_target_pairs={{0,2},{2,0},{4,6},{6,4},{8,10},{10,8},{12,14},{14,12},{16,18},{18,... | collective-permute-start | bytes 3145736 | tf_op jit(solution)/shard_map/ppermute | solution.py:881
  218.6 68.2 %collective-permute-start.30 = (bf16[2,256,1024]{2,1,0:T(8,128)(2,1)S(1)}, bf16[2,256,1024]{2,1,0:T(8,128)(2,1)S(1)}, u32[]{:S(2)}, u32[]{:S(2)}) collective-permute-start(bf16[2,256,1024]{2,1,0:T(8,128)(2,1)S(1)} %shard_map.271), channel_id=1, source_target_pairs={{0,4},{2,6},{4,0},{6,2},{8,12},{10,14},{12,8},{14,10},{16,20},{18,... | collective-permute-start | bytes 3145736 | tf_op jit(solution)/shard_map/ppermute | solution.py:881
  220.3 66.6 %collective-permute-start.32 = (bf16[2,256,1024]{2,1,0:T(8,128)(2,1)S(1)}, bf16[2,256,1024]{2,1,0:T(8,128)(2,1)S(1)}, u32[]{:S(2)}, u32[]{:S(2)}) collective-permute-start(bf16[2,256,1024]{2,1,0:T(8,128)(2,1)S(1)} %shard_map.272), channel_id=1, source_target_pairs={{0,6},{2,4},{4,2},{6,0},{8,14},{10,12},{12,10},{14,8},{16,22},{18,... | collective-permute-start | bytes 3145736 | tf_op jit(solution)/shard_map/ppermute | solution.py:881
  221.5 65.3 %copy-start = (bf16[256,1024]{1,0:T(8,128)(2,1)S(1)}, bf16[256,1024]{1,0:T(8,128)(2,1)}, u32[]{:S(2)}) copy-start(bf16[256,1024]{1,0:T(8,128)(2,1)} %refs_2_.1) | copy-start | bytes 1572868
  221.5 65.3 %copy-start.1 = (bf16[256,1024]{1,0:T(8,128)(2,1)S(1)}, bf16[256,1024]{1,0:T(8,128)(2,1)}, u32[]{:S(2)}) copy-start(bf16[256,1024]{1,0:T(8,128)(2,1)} %refs_3_.1) | copy-start | bytes 1572868
  221.5 65.3 %copy-start.6 = (bf16[2,256,1024]{2,1,0:T(8,128)(2,1)S(1)}, bf16[2,256,1024]{2,1,0:T(8,128)(2,1)}, u32[]{:S(2)}) copy-start(bf16[2,256,1024]{2,1,0:T(8,128)(2,1)} %get-tuple-element.107.refs_4_) | copy-start | bytes 3145732
  221.6 65.3 %copy-start.9 = (f32[1024]{0:T(1024)S(1)}, f32[1024]{0:T(1024)}, u32[]{:S(2)}) copy-start(f32[1024]{0:T(1024)} %param.26) | copy-start | bytes 12292
  221.6 65.3 %copy-start.10 = (f32[1024]{0:T(1024)S(1)}, f32[1024]{0:T(1024)}, u32[]{:S(2)}) copy-start(f32[1024]{0:T(1024)} %param.30) | copy-start | bytes 12292
  221.7 23.8 %collective-permute-start.48 = (bf16[4,2,64,512]{3,2,1,0:T(8,128)(2,1)S(1)}, bf16[4,2,64,512]{3,2,1,0:T(8,128)(2,1)S(1)}, u32[]{:S(2)}, u32[]{:S(2)}) collective-permute-start(bf16[4,2,64,512]{3,2,1,0:T(8,128)(2,1)S(1)} %add_convert_fusion), channel_id=1, source_target_pairs={{0,16},{2,18},{4,20},{6,22},{8,24},{10,26},{12,28},{14,30},{16,0},... | collective-permute-start | bytes 1572872 | tf_op jit(solution)/shard_map/ppermute | solution.py:884
  245.6 23.3 %collective-permute-start.45 = (bf16[64,512]{1,0:T(8,128)(2,1)S(1)}, bf16[64,512]{1,0:T(8,128)(2,1)S(1)}, u32[]{:S(2)}, u32[]{:S(2)}) collective-permute-start(bf16[64,512]{1,0:T(8,128)(2,1)S(1)} %get-tuple-element.133), channel_id=1, source_target_pairs={{0,6},{2,4},{4,2},{6,0},{8,14},{10,12},{12,10},{14,8},{16,22},{18,... | collective-permute-start | bytes 196616 | tf_op jit(solution)/shard_map/ppermute | solution.py:881
  268.8 5.0 %collective-permute-start.49 = (bf16[2,64,512]{2,1,0:T(8,128)(2,1)S(1)}, bf16[2,64,512]{2,1,0:T(8,128)(2,1)S(1)}, u32[]{:S(2)}, u32[]{:S(2)}) collective-permute-start(bf16[2,64,512]{2,1,0:T(8,128)(2,1)S(1)} %get-tuple-element.143), channel_id=1, source_target_pairs={{0,2},{2,0},{4,6},{6,4},{8,10},{10,8},{12,14},{14,12},{16,18},{18,... | collective-permute-start | bytes 393224 | tf_op jit(solution)/shard_map/ppermute | solution.py:881
  273.8 5.0 %collective-permute-start.50 = (bf16[2,64,512]{2,1,0:T(8,128)(2,1)S(1)}, bf16[2,64,512]{2,1,0:T(8,128)(2,1)S(1)}, u32[]{:S(2)}, u32[]{:S(2)}) collective-permute-start(bf16[2,64,512]{2,1,0:T(8,128)(2,1)S(1)} %get-tuple-element.144), channel_id=1, source_target_pairs={{0,4},{2,6},{4,0},{6,2},{8,12},{10,14},{12,8},{14,10},{16,20},{18,... | collective-permute-start | bytes 393224 | tf_op jit(solution)/shard_map/ppermute | solution.py:881
  278.8 5.9 %collective-permute-start.51 = (bf16[2,64,512]{2,1,0:T(8,128)(2,1)S(1)}, bf16[2,64,512]{2,1,0:T(8,128)(2,1)S(1)}, u32[]{:S(2)}, u32[]{:S(2)}) collective-permute-start(bf16[2,64,512]{2,1,0:T(8,128)(2,1)S(1)} %get-tuple-element.145), channel_id=1, source_target_pairs={{0,6},{2,4},{4,2},{6,0},{8,14},{10,12},{12,10},{14,8},{16,22},{18,... | collective-permute-start | bytes 393224 | tf_op jit(solution)/shard_map/ppermute | solution.py:881
  (18 other events, 353.8 us)
